TPU v7x, 512 devices: a whole 4x4x16 slice. The times are simulated.
512 devices in a mesh: wide: 128 (over y_hi, x, z), narrow: 4 (over y_lo, core).
Axes of the slice: x: 4, y: 4 (y_hi: 2, y_lo: 2; y = y_hi * 2 + y_lo), z: 16, core: 2. Of those that a mesh axis runs over, the one named last changes fastest.
Arguments:
- treated: bfloat16 [131072, 512], P(('wide', 'narrow')), may hold values from -6 to 6
- control: bfloat16 [131072, 512], P('wide'), may hold values from -6 to 6
- treated_weight: float32 [131072], P(('wide', 'narrow')), may hold values from 0.5 to 2
- control_weight: float32 [131072], replicated, may hold values from 0.5 to 2
- band: int32 [1024, 24], P(('wide', 'narrow')), may hold values from 0 to 1, as said below
Outputs:
- grad_treated: float32 [131072, 512], P(('wide', 'narrow'))
- grad_control: float32 [131072, 512], P(('wide', 'narrow'))
Inputs may be any that keep to these rules, and one draw needn't show every extreme that they name: band[t, k] = 1 pairs treated block t with control block (t // 8 - 1) * 8 + k. For each t the ones form one run of k that contains k = 8 + t % 8; every k whose control block lies outside 0 to 1023 is 0.
All inputs are finite; a program needn't handle non-finite values.
Results may differ from a plain program's by a relative error of at most 0.0055.
Values may be sent and summed in bfloat16 or wider, within the bound.
No kernel may reach another device: no remote copies, remote signals or barrier semaphores. Data moves between devices by JAX's collectives and lax.ppermute only.
A program may use at most 64 MiB of HBM per device.

v0:
```python
import jax
import jax.numpy as jnp
from jax import lax
from jax.sharding import PartitionSpec as P

SWEEPS = 2


SMOOTHING_TEMP = 0.05
EPSILON = 1e-06


def extended(block, sides, width):
    for axis, dim in sides:
        count = lax.axis_size(axis)
        forward = [(i, i + 1) for i in range(count - 1)]
        backward = [(target, source) for source, target in forward]
        low = lax.ppermute(
            lax.slice_in_dim(block, block.shape[dim] - width, None, axis=dim), axis, forward
        )
        high = lax.ppermute(lax.slice_in_dim(block, 0, width, axis=dim), axis, backward)
        block = jnp.concatenate([low, block, high], axis=dim)
    return block


def normalize(features):
    values = features.astype(jnp.float32)
    return (values * lax.rsqrt(jnp.mean(values * values, axis=1, keepdims=True) + EPSILON)).astype(
        jnp.bfloat16
    )


def expand(pair_blocks, block_rows):
    block_count, column_count = pair_blocks.shape
    full = jnp.broadcast_to(
        pair_blocks[:, None, :, None], (block_count, block_rows, column_count, block_rows)
    )
    return full.reshape(block_count * block_rows, column_count * block_rows)


def shards(treated, control, treated_weight, control_weight, band):
    row_count = treated.shape[0]
    slab_rows = control.shape[0]
    feature_total = treated.shape[1]
    block_rows = row_count // band.shape[0]
    wide_index = lax.axis_index("wide")
    narrow_index = lax.axis_index("narrow")
    treated_norm = normalize(treated)
    own_slab = normalize(control)
    band_span = extended(own_slab[None], (("wide", 0),), 1)
    band_span = band_span.reshape(3 * slab_rows, feature_total)
    paired_mask = expand(band, block_rows) > 0
    scale_factor = 1.0 / (feature_total * SMOOTHING_TEMP)
    pairwise_inner = lax.dot_general(
        treated_norm, band_span, (((1,), (1,)), ((), ())), preferred_element_type=jnp.float32
    )
    kernel = jnp.where(paired_mask, jnp.exp(pairwise_inner * scale_factor), 0.0)
    scales = jnp.ones((3 * slab_rows,), jnp.float32)
    own_weight_slab = lax.dynamic_slice_in_dim(control_weight, wide_index * slab_rows, slab_rows)
    row_scale = treated_weight
    for sweep_index in range(SWEEPS):
        row_scale = treated_weight / jnp.sum(kernel * scales[None, :], axis=1)
        column_parts = jnp.sum(kernel * row_scale[:, None], axis=0).reshape(3, slab_rows)
        slab_parts = lax.psum(column_parts, "narrow")
        edges = extended(slab_parts[None], (("wide", 0),), 1)
        column_total = edges[1, 1] + edges[0, 2] + edges[2, 0]
        col_scale = own_weight_slab / column_total
        scales = extended(col_scale[None], (("wide", 0),), 1).reshape(3 * slab_rows)
    transport = row_scale[:, None] * kernel * scales[None, :]
    plan_bf = transport.astype(jnp.bfloat16)
    pulled = jnp.dot(plan_bf, band_span, preferred_element_type=jnp.float32)
    grad_treated = jnp.sum(transport, axis=1)[:, None] * treated_norm.astype(jnp.float32) - pulled
    quarter = slab_rows // lax.axis_size("narrow")
    pushed = lax.dot_general(
        plan_bf, treated_norm, (((0,), (0,)), ((), ())), preferred_element_type=jnp.float32
    )
    pushed = pushed.reshape(3, slab_rows, feature_total)
    neighbours = extended(pushed, (("wide", 0),), 1)
    summed = lax.psum_scatter(
        neighbours[0] + neighbours[2] + neighbours[4], "narrow", scatter_dimension=0, tiled=True
    )
    own_rows = lax.dynamic_slice_in_dim(own_slab, narrow_index * quarter, quarter, 0).astype(
        jnp.float32
    )
    own_weight = lax.dynamic_slice_in_dim(
        control_weight, wide_index * slab_rows + narrow_index * quarter, quarter
    )
    grad_control = own_weight[:, None] * own_rows - summed
    return (grad_treated, grad_control)


def solution(mesh):
    return jax.shard_map(
        shards,
        mesh=mesh,
        in_specs=(
            P(("wide", "narrow"), None),
            P("wide", None),
            P(("wide", "narrow")),
            P(),
            P(("wide", "narrow"), None),
        ),
        out_specs=(P(("wide", "narrow"), None), P(("wide", "narrow"), None)),
        check_vma=False,
    )
```

profile of v0, /device:TPU:24, one launch (start us, length us, event | category | flops | bytes accessed | tf_op | source)
XLA Modules:
  0.0 225.0 jit_solution(4623724721699542760)
XLA Ops:
  7.2 0.0 copy-start.2
  7.2 0.0 copy-start.4
  7.2 0.0 reduce-scatter.2.cloned.1.call-start
  7.2 1.5 fusion.2
  8.8 1.5 fusion.13
  10.3 14.3 %collective-permute-start.1 = (bf16[1,1024,512]{2,1,0:T(8,128)(2,1)S(1)}, bf16[1,1024,512]{2,1,0:T(8,128)(2,1)S(1)}, u32[]{:S(2)}, u32[]{:S(2)}) collective-permute-start(bf16[1,1024,512]{2,1,0:T(8,128)(2,1)S(1)} %fusion.13), channel_id=1, source_target_pairs={{4,0},{8,4},{12,8},{16,12},{20,16},{24,20},{28,24},{32,28},{36,32}... | collective-permute-start | bytes 3145736 | tf_op jit(solution)/shard_map/ppermute | solution.py:21
  24.6 1.9 collective-permute-start
  26.5 0.0 copy-done.2
  26.5 0.1 fusion.5
  26.6 0.0 copy-done.4
  26.7 20.3 %collective-permute-done.1 = bf16[1,1024,512]{2,1,0:T(8,128)(2,1)S(1)} collective-permute-done((bf16[1,1024,512]{2,1,0:T(8,128)(2,1)S(1)}, bf16[1,1024,512]{2,1,0:T(8,128)(2,1)S(1)}, u32[]{:S(2)}, u32[]{:S(2)}) %collective-permute-start.1) | collective-permute-done | bytes 1048608 | tf_op jit(solution)/shard_map/ppermute | solution.py:21
  47.0 9.9 %collective-permute-done = bf16[1,1024,512]{2,1,0:T(8,128)(2,1)S(1)} collective-permute-done((bf16[1,1024,512]{2,1,0:T(8,128)(2,1)S(1)}, bf16[1,1024,512]{2,1,0:T(8,128)(2,1)S(1)}, u32[]{:S(2)}, u32[]{:S(2)}) %collective-permute-start) | collective-permute-done | bytes 1048608 | tf_op jit(solution)/shard_map/ppermute | solution.py:18
  56.9 0.3 pad_maximum_fusion
  57.2 0.0 copy-start
  57.3 0.3 broadcast_in_dim.16
  57.5 0.0 copy-start.3
  57.5 1.3 fusion.10
  58.9 0.0 copy-done
  58.9 0.0 copy-done.3
  58.9 0.4 multiply_reduce_fusion.1
  59.4 10.1 %psum.14 = f32[1,3,1024]{2,1,0:T(4,128)S(1)} all-reduce(f32[1,3,1024]{2,1,0:T(4,128)S(1)} %broadcast_in_dim.35), channel_id=1, replica_groups=mesh['wide'=128,'narrow'=4] {'narrow'}, use_global_device_ids=true, to_apply=%region_4.5 | all-reduce | flops 3072 | bytes 24576 | tf_op jit(solution)/shard_map/psum | solution.py:64
  69.5 1.9 collective-permute-start.3
  71.4 3.9 %collective-permute-start.2 = (f32[1,3,1024]{2,1,0:T(4,128)S(1)}, f32[1,3,1024]{2,1,0:T(4,128)S(1)}, u32[]{:S(2)}, u32[]{:S(2)}) collective-permute-start(f32[1,3,1024]{2,1,0:T(4,128)S(1)} %psum.14), channel_id=1, source_target_pairs={{0,4},{4,8},{8,12},{12,16},{16,20},{20,24},{24,28},{28,32},{32,36}... | collective-permute-start | bytes 36872 | tf_op jit(solution)/shard_map/ppermute | solution.py:18
  75.3 0.0 collective-permute-done.3
  75.4 7.4 %collective-permute-done.2 = f32[1,3,1024]{2,1,0:T(4,128)S(1)} collective-permute-done((f32[1,3,1024]{2,1,0:T(4,128)S(1)}, f32[1,3,1024]{2,1,0:T(4,128)S(1)}, u32[]{:S(2)}, u32[]{:S(2)}) %collective-permute-start.2) | collective-permute-done | bytes 12320 | tf_op jit(solution)/shard_map/ppermute | solution.py:18
  82.8 0.7 dynamic-slice_divide_fusion.1
  83.5 1.9 collective-permute-start.5
  85.4 3.9 %collective-permute-start.4 = (f32[1,1024]{1,0:T(1,128)S(1)}, f32[1,1024]{1,0:T(1,128)S(1)}, u32[]{:S(2)}, u32[]{:S(2)}) collective-permute-start(f32[1,1024]{1,0:T(1,128)S(1)} %bitcast.28), channel_id=1, source_target_pairs={{0,4},{4,8},{8,12},{12,16},{16,20},{20,24},{24,28},{28,32},{32,36}... | collective-permute-start | bytes 12296 | tf_op jit(solution)/shard_map/ppermute | solution.py:18
  89.3 0.0 collective-permute-done.5
  89.3 7.3 %collective-permute-done.4 = f32[1,1024]{1,0:T(1,128)S(1)} collective-permute-done((f32[1,1024]{1,0:T(1,128)S(1)}, f32[1,1024]{1,0:T(1,128)S(1)}, u32[]{:S(2)}, u32[]{:S(2)}) %collective-permute-start.4) | collective-permute-done | bytes 4128 | tf_op jit(solution)/shard_map/ppermute | solution.py:18
  96.7 0.3 multiply_reduce_fusion
  97.0 0.4 multiply_reduce_fusion.3
  97.4 10.1 %psum.15 = f32[1,3,1024]{2,1,0:T(4,128)S(1)} all-reduce(f32[1,3,1024]{2,1,0:T(4,128)S(1)} %broadcast_in_dim.37), channel_id=1, replica_groups=mesh['wide'=128,'narrow'=4] {'narrow'}, use_global_device_ids=true, to_apply=%region_7.8 | all-reduce | flops 3072 | bytes 24576 | tf_op jit(solution)/shard_map/psum | solution.py:64
  107.6 1.9 collective-permute-start.7
  109.5 3.9 %collective-permute-start.6 = (f32[1,3,1024]{2,1,0:T(4,128)S(1)}, f32[1,3,1024]{2,1,0:T(4,128)S(1)}, u32[]{:S(2)}, u32[]{:S(2)}) collective-permute-start(f32[1,3,1024]{2,1,0:T(4,128)S(1)} %psum.15), channel_id=1, source_target_pairs={{0,4},{4,8},{8,12},{12,16},{16,20},{20,24},{24,28},{28,32},{32,36}... | collective-permute-start | bytes 36872 | tf_op jit(solution)/shard_map/ppermute | solution.py:18
  113.4 0.0 collective-permute-done.7
  113.4 7.4 %collective-permute-done.6 = f32[1,3,1024]{2,1,0:T(4,128)S(1)} collective-permute-done((f32[1,3,1024]{2,1,0:T(4,128)S(1)}, f32[1,3,1024]{2,1,0:T(4,128)S(1)}, u32[]{:S(2)}, u32[]{:S(2)}) %collective-permute-start.6) | collective-permute-done | bytes 12320 | tf_op jit(solution)/shard_map/ppermute | solution.py:18
  120.9 0.7 dynamic-slice_divide_fusion
  121.6 1.9 collective-permute-start.9
  123.5 3.9 %collective-permute-start.8 = (f32[1,1024]{1,0:T(1,128)S(1)}, f32[1,1024]{1,0:T(1,128)S(1)}, u32[]{:S(2)}, u32[]{:S(2)}) collective-permute-start(f32[1,1024]{1,0:T(1,128)S(1)} %bitcast.25), channel_id=1, source_target_pairs={{0,4},{4,8},{8,12},{12,16},{16,20},{20,24},{24,28},{28,32},{32,36}... | collective-permute-start | bytes 12296 | tf_op jit(solution)/shard_map/ppermute | solution.py:18
  127.4 0.0 collective-permute-done.9
  127.4 7.3 %collective-permute-done.8 = f32[1,1024]{1,0:T(1,128)S(1)} collective-permute-done((f32[1,1024]{1,0:T(1,128)S(1)}, f32[1,1024]{1,0:T(1,128)S(1)}, u32[]{:S(2)}, u32[]{:S(2)}) %collective-permute-start.8) | collective-permute-done | bytes 4128 | tf_op jit(solution)/shard_map/ppermute | solution.py:18
  134.8 1.1 fusion.7
  135.9 0.4 slice_bitcast_fusion.1
  136.4 1.9 collective-permute-start.11
  138.3 3.9 %collective-permute-start.10 = (f32[1,1024,512]{2,1,0:T(8,128)S(1)}, f32[1,1024,512]{2,1,0:T(8,128)S(1)}, u32[]{:S(2)}, u32[]{:S(2)}) collective-permute-start(f32[1,1024,512]{2,1,0:T(8,128)S(1)} %get-tuple-element.2), channel_id=1, source_target_pairs={{0,4},{4,8},{8,12},{12,16},{16,20},{20,24},{24,28},{28,32},{32,36}... | collective-permute-start | bytes 6291464 | tf_op jit(solution)/shard_map/ppermute | solution.py:18
  142.2 39.4 %collective-permute-done.11 = f32[1,1024,512]{2,1,0:T(8,128)S(1)} collective-permute-done((f32[1,1024,512]{2,1,0:T(8,128)S(1)}, f32[1,1024,512]{2,1,0:T(8,128)S(1)}, u32[]{:S(2)}, u32[]{:S(2)}) %collective-permute-start.11) | collective-permute-done | bytes 2097184 | tf_op jit(solution)/shard_map/ppermute | solution.py:21
  181.6 7.7 %collective-permute-done.10 = f32[1,1024,512]{2,1,0:T(8,128)S(1)} collective-permute-done((f32[1,1024,512]{2,1,0:T(8,128)S(1)}, f32[1,1024,512]{2,1,0:T(8,128)S(1)}, u32[]{:S(2)}, u32[]{:S(2)}) %collective-permute-start.10) | collective-permute-done | bytes 2097184 | tf_op jit(solution)/shard_map/ppermute | solution.py:18
  189.3 2.1 fusion.4
  191.4 0.0 reduce-scatter.2.cloned.1.call-update
  191.4 0.8 dynamic_slice.10
  192.2 0.0 copy-start.1
  192.2 2.7 %fusion.3 = bf16[1024,512]{1,0:T(8,128)(2,1)} fusion(bf16[1024,512]{1,0:T(8,128)(2,1)} %param.6, f32[1024]{0:T(1024)S(1)} %add_rsqrt_fusion), kind=kLoop, calls=%fused_computation.12 | loop fusion | flops 1572864 | bytes 2101248 | tf_op jit(solution)/shard_map/convert_element_type | solution.py:28
  194.9 0.5 multiply_reduce_fusion.2
  195.4 0.0 copy-done.1
  195.4 1.8 convolution_subtract_fusion
  197.2 19.0 %reduce-scatter.2.cloned.1.call-done = f32[256,512]{1,0:T(8,128)} async-done(((f32[1024,512]{1,0:T(8,128)}), f32[256,512]{1,0:T(8,128)}) %reduce-scatter.2.cloned.1.call-update) | async-done | bytes 524304 | tf_op jit(solution)/shard_map/reduce_scatter | solution.py:79
  216.2 2.0 multiply_subtract_fusion
  (13 shorter events, 0.1 us)
Async XLA Ops:
  7.2 19.3 %copy-start.2 = (bf16[256,512]{1,0:T(8,128)(2,1)S(1)}, bf16[256,512]{1,0:T(8,128)(2,1)}, u32[]{:S(2)}) copy-start(bf16[256,512]{1,0:T(8,128)(2,1)} %param.5) | copy-start | bytes 786436
  7.2 19.5 %copy-start.4 = (s32[2,24]{1,0:T(2,128)S(1)}, s32[2,24]{1,0:T(2,128)}, u32[]{:S(2)}) copy-start(s32[2,24]{1,0:T(2,128)} %param.9) | copy-start | bytes 580
  7.2 209.0 %reduce-scatter.2.cloned.1.call-start = ((), (), s32[]{:S(2)}) async-start(), calls=%async_computation.1 | async-start | bytes 2621440 | tf_op jit(solution)/shard_map/reduce_scatter | solution.py:79
  10.3 36.7 %collective-permute-start.1 = (bf16[1,1024,512]{2,1,0:T(8,128)(2,1)S(1)}, bf16[1,1024,512]{2,1,0:T(8,128)(2,1)S(1)}, u32[]{:S(2)}, u32[]{:S(2)}) collective-permute-start(bf16[1,1024,512]{2,1,0:T(8,128)(2,1)S(1)} %fusion.13), channel_id=1, source_target_pairs={{4,0},{8,4},{12,8},{16,12},{20,16},{24,20},{28,24},{32,28},{36,32}... | collective-permute-start | bytes 3145736 | tf_op jit(solution)/shard_map/ppermute | solution.py:21
  24.6 32.3 %collective-permute-start = (bf16[1,1024,512]{2,1,0:T(8,128)(2,1)S(1)}, bf16[1,1024,512]{2,1,0:T(8,128)(2,1)S(1)}, u32[]{:S(2)}, u32[]{:S(2)}) collective-permute-start(bf16[1,1024,512]{2,1,0:T(8,128)(2,1)S(1)} %fusion.13), channel_id=1, source_target_pairs={{0,4},{4,8},{8,12},{12,16},{16,20},{20,24},{24,28},{28,32},{32,36}... | collective-permute-start | bytes 3145736 | tf_op jit(solution)/shard_map/ppermute | solution.py:18
  57.2 1.7 copy-start
  57.5 1.4 copy-start.3
  69.5 5.9 %collective-permute-start.3 = (f32[1,3,1024]{2,1,0:T(4,128)S(1)}, f32[1,3,1024]{2,1,0:T(4,128)S(1)}, u32[]{:S(2)}, u32[]{:S(2)}) collective-permute-start(f32[1,3,1024]{2,1,0:T(4,128)S(1)} %psum.14), channel_id=1, source_target_pairs={{4,0},{8,4},{12,8},{16,12},{20,16},{24,20},{28,24},{32,28},{36,32}... | collective-permute-start | bytes 36872 | tf_op jit(solution)/shard_map/ppermute | solution.py:21
  71.4 11.4 %collective-permute-start.2 = (f32[1,3,1024]{2,1,0:T(4,128)S(1)}, f32[1,3,1024]{2,1,0:T(4,128)S(1)}, u32[]{:S(2)}, u32[]{:S(2)}) collective-permute-start(f32[1,3,1024]{2,1,0:T(4,128)S(1)} %psum.14), channel_id=1, source_target_pairs={{0,4},{4,8},{8,12},{12,16},{16,20},{20,24},{24,28},{28,32},{32,36}... | collective-permute-start | bytes 36872 | tf_op jit(solution)/shard_map/ppermute | solution.py:18
  83.5 5.9 %collective-permute-start.5 = (f32[1,1024]{1,0:T(1,128)S(1)}, f32[1,1024]{1,0:T(1,128)S(1)}, u32[]{:S(2)}, u32[]{:S(2)}) collective-permute-start(f32[1,1024]{1,0:T(1,128)S(1)} %bitcast.27), channel_id=1, source_target_pairs={{4,0},{8,4},{12,8},{16,12},{20,16},{24,20},{28,24},{32,28},{36,32}... | collective-permute-start | bytes 12296 | tf_op jit(solution)/shard_map/ppermute | solution.py:21
  85.4 11.2 %collective-permute-start.4 = (f32[1,1024]{1,0:T(1,128)S(1)}, f32[1,1024]{1,0:T(1,128)S(1)}, u32[]{:S(2)}, u32[]{:S(2)}) collective-permute-start(f32[1,1024]{1,0:T(1,128)S(1)} %bitcast.28), channel_id=1, source_target_pairs={{0,4},{4,8},{8,12},{12,16},{16,20},{20,24},{24,28},{28,32},{32,36}... | collective-permute-start | bytes 12296 | tf_op jit(solution)/shard_map/ppermute | solution.py:18
  107.6 5.8 %collective-permute-start.7 = (f32[1,3,1024]{2,1,0:T(4,128)S(1)}, f32[1,3,1024]{2,1,0:T(4,128)S(1)}, u32[]{:S(2)}, u32[]{:S(2)}) collective-permute-start(f32[1,3,1024]{2,1,0:T(4,128)S(1)} %psum.15), channel_id=1, source_target_pairs={{4,0},{8,4},{12,8},{16,12},{20,16},{24,20},{28,24},{32,28},{36,32}... | collective-permute-start | bytes 36872 | tf_op jit(solution)/shard_map/ppermute | solution.py:21
  109.5 11.4 %collective-permute-start.6 = (f32[1,3,1024]{2,1,0:T(4,128)S(1)}, f32[1,3,1024]{2,1,0:T(4,128)S(1)}, u32[]{:S(2)}, u32[]{:S(2)}) collective-permute-start(f32[1,3,1024]{2,1,0:T(4,128)S(1)} %psum.15), channel_id=1, source_target_pairs={{0,4},{4,8},{8,12},{12,16},{16,20},{20,24},{24,28},{28,32},{32,36}... | collective-permute-start | bytes 36872 | tf_op jit(solution)/shard_map/ppermute | solution.py:18
  121.6 5.9 %collective-permute-start.9 = (f32[1,1024]{1,0:T(1,128)S(1)}, f32[1,1024]{1,0:T(1,128)S(1)}, u32[]{:S(2)}, u32[]{:S(2)}) collective-permute-start(f32[1,1024]{1,0:T(1,128)S(1)} %bitcast.24), channel_id=1, source_target_pairs={{4,0},{8,4},{12,8},{16,12},{20,16},{24,20},{28,24},{32,28},{36,32}... | collective-permute-start | bytes 12296 | tf_op jit(solution)/shard_map/ppermute | solution.py:21
  123.5 11.2 %collective-permute-start.8 = (f32[1,1024]{1,0:T(1,128)S(1)}, f32[1,1024]{1,0:T(1,128)S(1)}, u32[]{:S(2)}, u32[]{:S(2)}) collective-permute-start(f32[1,1024]{1,0:T(1,128)S(1)} %bitcast.25), channel_id=1, source_target_pairs={{0,4},{4,8},{8,12},{12,16},{16,20},{20,24},{24,28},{28,32},{32,36}... | collective-permute-start | bytes 12296 | tf_op jit(solution)/shard_map/ppermute | solution.py:18
  136.4 45.3 %collective-permute-start.11 = (f32[1,1024,512]{2,1,0:T(8,128)S(1)}, f32[1,1024,512]{2,1,0:T(8,128)S(1)}, u32[]{:S(2)}, u32[]{:S(2)}) collective-permute-start(f32[1,1024,512]{2,1,0:T(8,128)S(1)} %get-tuple-element.3), channel_id=1, source_target_pairs={{4,0},{8,4},{12,8},{16,12},{20,16},{24,20},{28,24},{32,28},{36,32}... | collective-permute-start | bytes 6291464 | tf_op jit(solution)/shard_map/ppermute | solution.py:21
  138.3 51.0 %collective-permute-start.10 = (f32[1,1024,512]{2,1,0:T(8,128)S(1)}, f32[1,1024,512]{2,1,0:T(8,128)S(1)}, u32[]{:S(2)}, u32[]{:S(2)}) collective-permute-start(f32[1,1024,512]{2,1,0:T(8,128)S(1)} %get-tuple-element.2), channel_id=1, source_target_pairs={{0,4},{4,8},{8,12},{12,16},{16,20},{20,24},{24,28},{28,32},{32,36}... | collective-permute-start | bytes 6291464 | tf_op jit(solution)/shard_map/ppermute | solution.py:18
  192.2 3.2 %copy-start.1 = (bf16[3,1024,512]{2,1,0:T(8,128)(2,1)S(1)}, bf16[3,1024,512]{2,1,0:T(8,128)(2,1)}, u32[]{:S(2)}) copy-start(bf16[3,1024,512]{2,1,0:T(8,128)(2,1)} %copy-done) | copy-start | bytes 9437188
Sparse Core Ops, SparseCore 0:
  191.6 24.5 reduce-scatter.1
where the time goes:
time: 228 us; the launch traced here: 225 us
  waiting for transfers between devices  126 us (55%)
  starting transfers between devices  45.4 us (20%)
  blocking collectives  20.2 us (9%)
  between operations  14.3 us (6%)
  other arithmetic  13.5 us (6%)
  matrix products  4.3 us (2%)
    ppermute x6, waiting for transfers between devices, extended(): lax.ppermute(lax.slice_in_dim(block, 0, width, axis=dim), axis, backward)  59.7 us
    ppermute x6, waiting for transfers between devices, extended(): lax.ppermute(lax.slice_in_dim(block, block.shape[dim] - width, None, axis...  47 us
    ppermute x6, starting transfers between devices, extended(): lax.ppermute(lax.slice_in_dim(block, 0, width, axis=dim), axis, backward)  23.9 us
    ppermute x6, starting transfers between devices, extended(): lax.ppermute(lax.slice_in_dim(block, block.shape[dim] - width, None, axis...  21.5 us
    psum x2, blocking collectives, shards(): slab_parts = lax.psum(column_parts, 'narrow')  20.2 us
    reduce_scatter x1, waiting for transfers between devices, shards(): lax.psum_scatter(neighbours[0] + neighbours[2] + neighbours[4], 'narrow',...  19 us
  transfers between devices with their start and end apart: 13, of which 9 were waited for; matrix products, arithmetic and copies ran while one was open for 3% of the time, Pallas kernels for 0%

commit v1 on v0

v1 whole, which is shorter than its diff:
```python
import jax
import jax.numpy as jnp
from jax import lax
from jax.sharding import PartitionSpec as P

SWEEPS = 2
SMOOTHING_TEMP = 0.05
EPSILON = 1e-06

SWAP_Y = [(0, 2), (2, 0), (1, 3), (3, 1)]
SWAP_CORE = [(0, 1), (1, 0), (2, 3), (3, 2)]


def from_low(block, hops):
    count = lax.axis_size("wide")
    return lax.ppermute(block, "wide", [(i, i + hops) for i in range(count - hops)])


def from_high(block, hops):
    count = lax.axis_size("wide")
    return lax.ppermute(block, "wide", [(i + hops, i) for i in range(count - hops)])


def normalize(features):
    values = features.astype(jnp.float32)
    return (values * lax.rsqrt(jnp.mean(values * values, axis=1, keepdims=True) + EPSILON)).astype(
        jnp.bfloat16
    )


def expand(pair_blocks, block_rows):
    block_count, column_count = pair_blocks.shape
    full = jnp.broadcast_to(
        pair_blocks[:, None, :, None], (block_count, block_rows, column_count, block_rows)
    )
    return full.reshape(block_count * block_rows, column_count * block_rows)


def shards(treated, control, treated_weight, control_weight, band):
    quarter, features = treated.shape
    slab = control.shape[0]
    block_rows = quarter // band.shape[0]
    per_quarter = band.shape[0]
    wide_index = lax.axis_index("wide")
    n = lax.axis_index("narrow")
    wide_count = lax.axis_size("wide")
    order = [n, n ^ 2, n ^ 1, n ^ 3]
    scale_factor = 1.0 / (features * SMOOTHING_TEMP)

    def pick(array, axis):
        return [lax.dynamic_index_in_dim(array, o, axis, keepdims=True) for o in order]

    control_parts = pick(control.reshape(4, quarter, features), 0)
    near_raw = jnp.concatenate(control_parts[:2], 0).reshape(2 * quarter, features)
    far_raw = jnp.concatenate(control_parts[2:], 0).reshape(2 * quarter, features)
    low_near = from_low(near_raw, 1)
    high_near = from_high(near_raw, 1)

    pairs = jnp.pad(band.astype(jnp.float32).reshape(1, -1), ((0, 0), (0, quarter - band.size)))
    small = jnp.concatenate([treated_weight[None], pairs], 0)
    treated_y = lax.ppermute(treated, "narrow", SWAP_Y)
    small_y = lax.ppermute(small, "narrow", SWAP_Y)
    treated_pair = jnp.concatenate([treated, treated_y], 0)
    small_pair = jnp.stack([small, small_y], 0)
    treated_far = lax.ppermute(treated_pair, "narrow", SWAP_CORE)
    small_far = lax.ppermute(small_pair, "narrow", SWAP_CORE)
    small_all = jnp.concatenate([small_pair, small_far], 0)
    slab_weight = small_all[:, 0].reshape(slab)
    slab_band = small_all[:, 1, : band.size].reshape(4 * per_quarter, 3, 4, per_quarter)
    slab_band = jnp.concatenate(pick(slab_band, 2), 2)

    treated_slab = normalize(jnp.concatenate([treated_pair, treated_far], 0))
    own_norm = normalize(jnp.concatenate([near_raw, far_raw], 0))

    def kernel_of(rows, columns, pair_blocks):
        inner = lax.dot_general(
            rows, columns, (((1,), (1,)), ((), ())), preferred_element_type=jnp.float32
        )
        return jnp.where(
            expand(pair_blocks, block_rows) > 0, jnp.exp(inner * scale_factor), 0.0
        )

    half_blocks = 2 * per_quarter

    def side_blocks(first):
        chosen = slab_band[:, 0::2, first : first + 2]
        return chosen.reshape(4 * per_quarter, 2 * half_blocks)

    kernel_own = kernel_of(treated_slab, own_norm, slab_band[:, 1].reshape(4 * per_quarter, -1))

    near_sides = jnp.stack([low_near, high_near], 0)
    far_sides = lax.ppermute(near_sides, "narrow", SWAP_CORE)
    near_norm = normalize(near_sides.reshape(slab, features))
    kernel_near = kernel_of(treated_slab, near_norm, side_blocks(0))

    gated, _ = lax.optimization_barrier((treated_pair, near_sides))
    low_treated = from_low(gated, 1)
    high_treated = from_high(gated, 1)
    treated_sides = jnp.stack([low_treated, high_treated], 0)
    treated_sides_far = lax.ppermute(treated_sides, "narrow", SWAP_CORE)

    far_norm = normalize(far_sides.reshape(slab, features))
    kernel_far = kernel_of(treated_slab, far_norm, side_blocks(2))

    weight_slabs = [
        jnp.concatenate(
            pick(
                lax.dynamic_slice_in_dim(
                    control_weight, (wide_index + d) * slab, slab
                ).reshape(4, quarter),
                0,
            ),
            0,
        ).reshape(slab)
        for d in (-1, 0, 1)
    ]
    exists = [wide_index > 0, True, wide_index < wide_count - 1]

    half = slab // 2
    scales = [jnp.ones((slab,), jnp.float32)] * 3
    extra_up = jnp.pad(slab_band[:, 2, 0].reshape(-1), (0, slab - 4 * per_quarter * per_quarter))
    extra_down = jnp.pad(slab_band[:, 0, 0].reshape(-1), (0, slab - 4 * per_quarter * per_quarter))
    received = []
    for sweep_index in range(SWEEPS):
        low, own, high = scales
        near_scale = jnp.concatenate([low[:half], high[:half]])
        far_scale = jnp.concatenate([low[half:], high[half:]])
        row_total = (
            jnp.sum(kernel_own * own[None], axis=1)
            + jnp.sum(kernel_near * near_scale[None], axis=1)
            + jnp.sum(kernel_far * far_scale[None], axis=1)
        )
        row_scale = slab_weight / row_total
        column_own = jnp.sum(kernel_own * row_scale[:, None], axis=0)
        column_near = jnp.sum(kernel_near * row_scale[:, None], axis=0)
        column_far = jnp.sum(kernel_far * row_scale[:, None], axis=0)
        column_low = jnp.concatenate([column_near[:half], column_far[:half]])
        column_high = jnp.concatenate([column_near[half:], column_far[half:]])
        if sweep_index == SWEEPS - 1:
            extra_up = extra_down = row_scale
        from_below = from_low(jnp.stack([column_own, column_high, extra_up], 0), 1)
        from_above = from_high(jnp.stack([column_own, column_low, extra_down], 0), 1)
        from_below2 = from_low(column_high[None], 2)
        from_above2 = from_high(column_low[None], 2)
        totals = [
            column_low + from_below[0] + from_below2[0],
            column_own + from_below[1] + from_above[1],
            column_high + from_above[0] + from_above2[0],
        ]
        scales = [
            jnp.where(there, weight / total, 0.0)
            for there, weight, total in zip(exists, weight_slabs, totals)
        ]
        received.append((from_below[2], from_above[2]))

    low, own, high = scales
    near_scale = jnp.concatenate([low[:half], high[:half]])
    far_scale = jnp.concatenate([low[half:], high[half:]])

    own_row_scale = row_scale[:quarter, None]
    row_mass = jnp.zeros((quarter,), jnp.float32)
    pulled = jnp.zeros((quarter, features), jnp.float32)
    for kernel, scale, columns in (
        (kernel_own, own, own_norm),
        (kernel_near, near_scale, near_norm),
        (kernel_far, far_scale, far_norm),
    ):
        transport = own_row_scale * kernel[:quarter] * scale[None]
        row_mass = row_mass + jnp.sum(transport, axis=1)
        pulled = pulled + jnp.dot(
            transport.astype(jnp.bfloat16), columns, preferred_element_type=jnp.float32
        )
    grad_treated = row_mass[:, None] * treated_slab[:quarter].astype(jnp.float32) - pulled

    own_quarter = own_norm[:quarter]
    sides = jnp.concatenate([treated_sides, treated_sides_far], 1)
    sides_norm = normalize(sides.reshape(2 * slab, features))
    blocks_low, blocks_high = (
        r[: 4 * per_quarter * per_quarter].reshape(4 * per_quarter, per_quarter)
        for r in received[0]
    )
    kernel_mid = kernel_of(treated_slab, own_quarter, slab_band[:, 1, 0])
    kernel_sides = kernel_of(
        sides_norm, own_quarter, jnp.concatenate([blocks_low, blocks_high], 0)
    )
    sides_scale = jnp.concatenate(received[-1])
    own_column_scale = own[None, :quarter]
    pushed = jnp.zeros((quarter, features), jnp.float32)
    for kernel, scale, rows in (
        (kernel_mid, row_scale, treated_slab),
        (kernel_sides, sides_scale, sides_norm),
    ):
        transport = (scale[:, None] * kernel * own_column_scale).astype(jnp.bfloat16)
        pushed = pushed + lax.dot_general(
            transport, rows, (((0,), (0,)), ((), ())), preferred_element_type=jnp.float32
        )
    own_weight = weight_slabs[1][:quarter]
    grad_control = own_weight[:, None] * own_quarter.astype(jnp.float32) - pushed
    return (grad_treated, grad_control)


def solution(mesh):
    return jax.shard_map(
        shards,
        mesh=mesh,
        in_specs=(
            P(("wide", "narrow"), None),
            P("wide", None),
            P(("wide", "narrow")),
            P(),
            P(("wide", "narrow"), None),
        ),
        out_specs=(P(("wide", "narrow"), None), P(("wide", "narrow"), None)),
        check_vma=False,
    )
```

time: 228 us -> 145 us (0.64)
  waiting for transfers between devices: 126 us -> 9.61 us
  starting transfers between devices: 45.4 us -> 83 us
  blocking collectives: 20.2 us -> 0 us
  matrix products: 4.3 us -> 20.1 us
  between operations: 14.3 us -> 1.67 us
  local copies, waits for them, and re-layouts: 1.57 us -> 10.4 us
  other arithmetic: 13.5 us -> 18.8 us
    ppermute x12 -> x18, waiting for transfers between devices: 107 us -> 9.61 us  [the longest x6 8.53 us: from_low(): lax.ppermute(block, 'wide', [(i, i + hops) for i in range(count - hops)])]
    ppermute x12 -> x18, starting transfers between devices: 45.4 us -> 83 us  [the longest x6 45.2 us: from_high(): lax.ppermute(block, 'wide', [(i + hops, i) for i in range(count - hops)])]
    psum x2 -> x0, blocking collectives: 20.2 us -> none  [shards(): slab_parts = lax.psum(column_parts, 'narrow')]
    reduce_scatter x1 -> x0, waiting for transfers between devices: 19 us -> none  [shards(): lax.psum_scatter(neighbours[0] + neighbours[2] + neighbours[4], 'narrow',...]
    dot_general x3 -> x8, matrix products: 4.3 us -> 20.1 us  [the longest x2 8.41 us: shards(): lax.dot_general(transport, rows, (((0,), (0,)), ((), ())), preferred_elem...]
    reduce_sum x4 -> x6, other arithmetic: 1.65 us -> 5.32 us  [the longest x1 2.45 us: shards(): row_mass = row_mass + jnp.sum(transport, axis=1)]
    gt x0 -> x8, local copies, waits for them, and re-layouts: none -> 2.56 us  [kernel_of(): expand(pair_blocks, block_rows) > 0]
    convert_element_type x0 -> x2, other arithmetic: none -> 2.5 us  [the longest x1 1.81 us: normalize(): values = features.astype(jnp.float32)]
  transfers between devices with their start and end apart: 13 -> 18, of which waited for: 9 -> 2; matrix products, arithmetic and copies ran while one was open for 3% -> 24% of each run, Pallas kernels for 0% -> 0%
where the time goes in v1:
time: 145 us; the launch traced here: 144 us
  starting transfers between devices  83 us (57%)
  matrix products  20.1 us (14%)
  other arithmetic  18.8 us (13%)
  local copies, waits for them, and re-layouts  10.4 us (7%)
  waiting for transfers between devices  9.61 us (7%)
  between operations  1.67 us (1%)
    ppermute x6, starting transfers between devices, from_high(): lax.ppermute(block, 'wide', [(i + hops, i) for i in range(count - hops)])  45.2 us
    ppermute x6, starting transfers between devices, from_low(): lax.ppermute(block, 'wide', [(i, i + hops) for i in range(count - hops)])  23.7 us
    ppermute x6, waiting for transfers between devices, from_low(): lax.ppermute(block, 'wide', [(i, i + hops) for i in range(count - hops)])  8.53 us
    dot_general x2, matrix products, shards(): lax.dot_general(transport, rows, (((0,), (0,)), ((), ())), preferred_elem...  8.41 us
    dot_general x3, matrix products, shards(): jnp.dot(transport.astype(jnp.bfloat16), columns, preferred_element_type=j...  6.86 us
    dot_general x3, matrix products, kernel_of(): lax.dot_general(rows, columns, (((1,), (1,)), ((), ())), preferred_elemen...  4.82 us
    convert_element_type x5, other arithmetic, normalize(): (values * lax.rsqrt(jnp.mean(values * values, axis=1, keepdims=True) + EP...  4.76 us
    ppermute x1, starting transfers between devices, shards(): small_y = lax.ppermute(small, 'narrow', SWAP_Y)  3.91 us
  transfers between devices with their start and end apart: 18, of which 2 were waited for; matrix products, arithmetic and copies ran while one was open for 24% of the time, Pallas kernels for 0%

profile of v1, /device:TPU:24, one launch (start us, length us, event | category | flops | bytes accessed | tf_op | source)
XLA Modules:
  0.0 143.6 jit_solution(13401687214669993986)
XLA Ops:
  0.7 1.3 constant_dynamic-slice_fusion.15
  2.0 14.3 %collective-permute-start.5 = (bf16[512,512]{1,0:T(8,128)(2,1)S(1)}, bf16[512,512]{1,0:T(8,128)(2,1)S(1)}, u32[]{:S(2)}, u32[]{:S(2)}) collective-permute-start(bf16[512,512]{1,0:T(8,128)(2,1)S(1)} %bitcast.141), channel_id=1, source_target_pairs={{4,0},{8,4},{12,8},{16,12},{20,16},{24,20},{28,24},{32,28},{36,32}... | collective-permute-start | bytes 1572872 | tf_op jit(solution)/shard_map/ppermute | solution.py:21
  16.3 1.9 %collective-permute-start.4 = (bf16[512,512]{1,0:T(8,128)(2,1)S(1)}, bf16[512,512]{1,0:T(8,128)(2,1)S(1)}, u32[]{:S(2)}, u32[]{:S(2)}) collective-permute-start(bf16[512,512]{1,0:T(8,128)(2,1)S(1)} %bitcast.142), channel_id=1, source_target_pairs={{0,4},{4,8},{8,12},{12,16},{16,20},{20,24},{24,28},{28,32},{32,36}... | collective-permute-start | bytes 1572872 | tf_op jit(solution)/shard_map/ppermute | solution.py:16
  18.2 1.9 %collective-permute-start.2 = (bf16[256,512]{1,0:T(8,128)(2,1)}, bf16[256,512]{1,0:T(8,128)(2,1)S(1)}, u32[]{:S(2)}, u32[]{:S(2)}) collective-permute-start(bf16[256,512]{1,0:T(8,128)(2,1)} %param.5), channel_id=1, source_target_pairs={{0,2},{2,0},{1,3},{3,1},{4,6},{6,4},{5,7},{7,5},{8,10},{10,8},{9,1... | collective-permute-start | bytes 786440 | tf_op jit(solution)/shard_map/ppermute | solution.py:61
  20.1 0.7 convert_element_type.77
  20.9 0.7 fusion.58
  21.6 3.9 %collective-permute-start = (f32[2,256]{1,0:T(2,128)S(1)}, f32[2,256]{1,0:T(2,128)S(1)}, u32[]{:S(2)}, u32[]{:S(2)}) collective-permute-start(f32[2,256]{1,0:T(2,128)S(1)} %get-tuple-element.75), channel_id=1, source_target_pairs={{0,2},{2,0},{1,3},{3,1},{4,6},{6,4},{5,7},{7,5},{8,10},{10,8},{9,1... | collective-permute-start | bytes 6152 | tf_op jit(solution)/shard_map/ppermute | solution.py:62
  25.5 1.7 %constant_dynamic-update-slice_fusion.1 = bf16[512,512]{1,0:T(8,128)(2,1)} fusion(bf16[256,512]{1,0:T(8,128)(2,1)} %param.5), kind=kLoop, calls=%fused_computation.97 | loop fusion | bytes 524288
  27.2 0.3 fusion.5
  27.5 1.3 fusion.6
  28.8 0.8 fusion.60
  29.7 1.9 %collective-permute-start.1 = (f32[2,2,256]{2,1,0:T(2,128)S(1)}, f32[2,2,256]{2,1,0:T(2,128)S(1)}, u32[]{:S(2)}, u32[]{:S(2)}) collective-permute-start(f32[2,2,256]{2,1,0:T(2,128)S(1)} %pad_maximum_fusion.15), channel_id=1, source_target_pairs={{0,1},{1,0},{2,3},{3,2},{4,5},{5,4},{6,7},{7,6},{8,9},{9,8},{10,11... | collective-permute-start | bytes 12296 | tf_op jit(solution)/shard_map/ppermute | solution.py:66
  31.7 1.1 collective-permute-done.1
  32.8 0.1 reshape_squeeze.15
  32.9 0.1 copy.35
  33.9 0.1 broadcast_in_dim.33
  34.0 0.1 copy.65
  34.2 1.1 copy.41
  35.2 0.8 constant_dynamic-update-slice_fusion
  36.0 2.1 %collective-permute-start.3 = (bf16[512,512]{1,0:T(8,128)(2,1)}, bf16[512,512]{1,0:T(8,128)(2,1)S(1)}, u32[]{:S(2)}, u32[]{:S(2)}) collective-permute-start(bf16[512,512]{1,0:T(8,128)(2,1)} %constant_dynamic-update-slice_fusion), channel_id=1, source_target_pairs={{0,1},{1,0},{2,3},{3,2},{4,5},{5,4},{6,7},{7,6},{8,9},{9,8},{10,11... | collective-permute-start | bytes 1572872 | tf_op jit(solution)/shard_map/ppermute | solution.py:65
  38.1 0.1 pad_maximum_fusion.2
  38.2 2.4 %collective-permute-start.6 = (bf16[2,512,512]{2,1,0:T(8,128)(2,1)S(1)}, bf16[2,512,512]{2,1,0:T(8,128)(2,1)S(1)}, u32[]{:S(2)}, u32[]{:S(2)}) collective-permute-start(bf16[2,512,512]{2,1,0:T(8,128)(2,1)S(1)} %pad_maximum_fusion.2), channel_id=1, source_target_pairs={{0,1},{1,0},{2,3},{3,2},{4,5},{5,4},{6,7},{7,6},{8,9},{9,8},{10,11... | collective-permute-start | bytes 3145736 | tf_op jit(solution)/shard_map/ppermute | solution.py:92
  40.6 9.6 %collective-permute-start.16 = (bf16[512,512]{1,0:T(8,128)(2,1)}, bf16[512,512]{1,0:T(8,128)(2,1)S(1)}, u32[]{:S(2)}, u32[]{:S(2)}) collective-permute-start(bf16[512,512]{1,0:T(8,128)(2,1)} %constant_dynamic-update-slice_fusion), channel_id=1, source_target_pairs={{4,0},{8,4},{12,8},{16,12},{20,16},{24,20},{28,24},{32,28},{36,32}... | collective-permute-start | bytes 1572872 | tf_op jit(solution)/shard_map/ppermute | solution.py:21
  50.3 1.9 %collective-permute-start.15 = (bf16[512,512]{1,0:T(8,128)(2,1)}, bf16[512,512]{1,0:T(8,128)(2,1)S(1)}, u32[]{:S(2)}, u32[]{:S(2)}) collective-permute-start(bf16[512,512]{1,0:T(8,128)(2,1)} %constant_dynamic-update-slice_fusion), channel_id=1, source_target_pairs={{0,4},{4,8},{8,12},{12,16},{16,20},{20,24},{24,28},{28,32},{32,36}... | collective-permute-start | bytes 1572872 | tf_op jit(solution)/shard_map/ppermute | solution.py:16
  52.2 0.3 multiply_reduce_fusion.11
  52.5 0.3 fusion.8
  52.8 1.2 fusion.3
  54.1 1.2 fusion.4
  55.3 0.3 broadcast_in_dim.29
  55.7 1.6 %fusion.72 = (f32[1024]{0:T(1024)S(1)}, f32[1024,1024]{0,1:T(8,128)S(1)}) fusion(bf16[1024,512]{1,0:T(8,128)(2,1)S(1)} %fusion.4, bf16[1024,512]{1,0:T(8,128)(2,1)S(1)} %copy-done.3, pred[128,8,8,128]{3,2,1,0:T(8,128)(4,1)S(1)} %bitcast.156), kind=kOutput, calls=%fused_computation.176 | convolution fusion | flops 1076886528 | bytes 7344128 | tf_op jit(solution)/shard_map/dot_general | solution.py:76
  57.3 0.3 broadcast_in_dim.30
  57.6 1.6 %fusion.73 = (f32[1024]{0:T(1024)S(1)}, f32[1024,1024]{0,1:T(8,128)S(1)}) fusion(bf16[1024,512]{1,0:T(8,128)(2,1)S(1)} %fusion.4, bf16[1024,512]{1,0:T(8,128)(2,1)S(1)} %fusion.8, pred[128,8,8,128]{3,2,1,0:T(8,128)(4,1)S(1)} %bitcast.157), kind=kOutput, calls=%fused_computation.177 | convolution fusion | flops 1076886528 | bytes 7344128 | tf_op jit(solution)/shard_map/dot_general | solution.py:76
  59.3 0.3 multiply_reduce_fusion.10
  59.6 0.3 fusion.7
  59.9 0.3 broadcast_in_dim.31
  60.2 1.6 %fusion.71 = (f32[1024]{0:T(1024)S(1)}, f32[1024,1024]{0,1:T(8,128)S(1)}) fusion(bf16[1024,512]{1,0:T(8,128)(2,1)S(1)} %fusion.4, bf16[1024,512]{1,0:T(8,128)(2,1)S(1)} %fusion.7, pred[128,8,8,128]{3,2,1,0:T(8,128)(4,1)S(1)} %bitcast.158), kind=kOutput, calls=%fused_computation.175 | convolution fusion | flops 1076886528 | bytes 7344128 | tf_op jit(solution)/shard_map/dot_general | solution.py:76
  61.9 0.9 multiply_reduce_fusion.9
  62.9 9.6 %collective-permute-start.8 = (f32[3,1024]{1,0:T(4,128)S(1)}, f32[3,1024]{1,0:T(4,128)S(1)}, u32[]{:S(2)}, u32[]{:S(2)}) collective-permute-start(f32[3,1024]{1,0:T(4,128)S(1)} %get-tuple-element.55), channel_id=1, source_target_pairs={{4,0},{8,4},{12,8},{16,12},{20,16},{24,20},{28,24},{32,28},{36,32}... | collective-permute-start | bytes 36872 | tf_op jit(solution)/shard_map/ppermute | solution.py:21
  72.5 1.9 %collective-permute-start.7 = (f32[3,1024]{1,0:T(4,128)S(1)}, f32[3,1024]{1,0:T(4,128)S(1)}, u32[]{:S(2)}, u32[]{:S(2)}) collective-permute-start(f32[3,1024]{1,0:T(4,128)S(1)} %get-tuple-element.54), channel_id=1, source_target_pairs={{0,4},{4,8},{8,12},{12,16},{16,20},{20,24},{24,28},{28,32},{32,36}... | collective-permute-start | bytes 36872 | tf_op jit(solution)/shard_map/ppermute | solution.py:16
  74.5 1.1 pad_maximum_fusion.3
  75.6 1.9 %collective-permute-start.17 = (bf16[2,512,512]{2,1,0:T(8,128)(2,1)}, bf16[2,512,512]{2,1,0:T(8,128)(2,1)}, u32[]{:S(2)}, u32[]{:S(2)}) collective-permute-start(bf16[2,512,512]{2,1,0:T(8,128)(2,1)} %pad_maximum_fusion.3), channel_id=1, source_target_pairs={{0,1},{1,0},{2,3},{3,2},{4,5},{5,4},{6,7},{7,6},{8,9},{9,8},{10,11... | collective-permute-start | bytes 3145736 | tf_op jit(solution)/shard_map/ppermute | solution.py:100
  77.5 3.4 %collective-permute-start.10 = (f32[1,1024]{1,0:T(1,128)S(1)}, f32[1,1024]{1,0:T(1,128)S(1)}, u32[]{:S(2)}, u32[]{:S(2)}) collective-permute-start(f32[1,1024]{1,0:T(1,128)S(1)} %bitcast.196), channel_id=1, source_target_pairs={{8,0},{12,4},{16,8},{20,12},{24,16},{28,20},{32,24},{36,28},{40,32... | collective-permute-start | bytes 12296 | tf_op jit(solution)/shard_map/ppermute | solution.py:21
  80.9 3.6 %collective-permute-start.9 = (f32[1,1024]{1,0:T(1,128)S(1)}, f32[1,1024]{1,0:T(1,128)S(1)}, u32[]{:S(2)}, u32[]{:S(2)}) collective-permute-start(f32[1,1024]{1,0:T(1,128)S(1)} %bitcast.194), channel_id=1, source_target_pairs={{0,8},{4,12},{8,16},{12,20},{16,24},{20,28},{24,32},{28,36},{32,40... | collective-permute-start | bytes 12296 | tf_op jit(solution)/shard_map/ppermute | solution.py:16
  84.5 8.5 %collective-permute-done.9 = f32[1,1024]{1,0:T(1,128)S(1)} collective-permute-done((f32[1,1024]{1,0:T(1,128)S(1)}, f32[1,1024]{1,0:T(1,128)S(1)}, u32[]{:S(2)}, u32[]{:S(2)}) %collective-permute-start.9) | collective-permute-done | bytes 4128 | tf_op jit(solution)/shard_map/ppermute | solution.py:16
  93.1 0.3 multiply_reduce_fusion.4
  93.4 0.3 multiply_reduce_fusion.6
  93.8 0.3 multiply_reduce_fusion.5
  94.2 0.9 multiply_reduce_fusion.2
  95.2 2.1 %collective-permute-start.14 = (f32[1,1024]{1,0:T(1,128)S(1)}, f32[1,1024]{1,0:T(1,128)S(1)}, u32[]{:S(2)}, u32[]{:S(2)}) collective-permute-start(f32[1,1024]{1,0:T(1,128)S(1)} %bitcast.186), channel_id=1, source_target_pairs={{8,0},{12,4},{16,8},{20,12},{24,16},{28,20},{32,24},{36,28},{40,32... | collective-permute-start | bytes 12296 | tf_op jit(solution)/shard_map/ppermute | solution.py:21
  97.2 4.8 %collective-permute-start.13 = (f32[1,1024]{1,0:T(1,128)S(1)}, f32[1,1024]{1,0:T(1,128)S(1)}, u32[]{:S(2)}, u32[]{:S(2)}) collective-permute-start(f32[1,1024]{1,0:T(1,128)S(1)} %bitcast.184), channel_id=1, source_target_pairs={{0,8},{4,12},{8,16},{12,20},{16,24},{20,28},{24,32},{28,36},{32,40... | collective-permute-start | bytes 12296 | tf_op jit(solution)/shard_map/ppermute | solution.py:16
  102.1 9.6 %collective-permute-start.11 = (f32[3,1024]{1,0:T(4,128)S(1)}, f32[3,1024]{1,0:T(4,128)S(1)}, u32[]{:S(2)}, u32[]{:S(2)}) collective-permute-start(f32[3,1024]{1,0:T(4,128)S(1)} %get-tuple-element.38), channel_id=1, source_target_pairs={{0,4},{4,8},{8,12},{12,16},{16,20},{20,24},{24,28},{28,32},{32,36}... | collective-permute-start | bytes 36872 | tf_op jit(solution)/shard_map/ppermute | solution.py:16
  111.7 6.2 %collective-permute-start.12 = (f32[3,1024]{1,0:T(4,128)S(1)}, f32[3,1024]{1,0:T(4,128)S(1)}, u32[]{:S(2)}, u32[]{:S(2)}) collective-permute-start(f32[3,1024]{1,0:T(4,128)S(1)} %get-tuple-element.39), channel_id=1, source_target_pairs={{4,0},{8,4},{12,8},{16,12},{20,16},{24,20},{28,24},{32,28},{36,32}... | collective-permute-start | bytes 36872 | tf_op jit(solution)/shard_map/ppermute | solution.py:21
  118.4 0.2 broadcast_in_dim.34
  118.6 0.3 copy.64
  118.9 1.4 copy.44
  120.5 2.4 %fusion.27 = (f32[256]{0:T(256)S(1)}, f32[256]{0:T(256)S(1)}, f32[256]{0:T(256)S(1)}) fusion(f32[1024,1024]{0,1:T(8,128)} %copy-done.1, f32[1024]{0:T(1024)S(1)} %pad_maximum_fusion.23, f32[256]{0:T(256)S(1)} %slice.156, f32[1024]{0:T(1024)S(1)} %pad_maximum_fusion.24, f32[1024,1024]{0,1:T(8,128)} %copy-done.2, f32[1024]{0:T(1024)S(1)} %bitcast.166, ...), kind=kLoop, calls=%fused_computation.65 | loop fusion | flops 2358528 | bytes 3162112 | tf_op jit(solution)/shard_map/reduce_sum | solution.py:169
  123.0 2.0 %fusion.32 = f32[256,512]{1,0:T(8,128)S(1)} fusion(bf16[1024,512]{1,0:T(8,128)(2,1)S(1)} %copy-done.4, f32[1024,1024]{0,1:T(8,128)} %copy-done, f32[1024]{0:T(1024)S(1)} %bitcast.167, f32[256]{0:T(256)S(1)} %slice.156), kind=kOutput, calls=%fused_computation.68 | convolution fusion | flops 269221888 | bytes 2626560 | tf_op jit(solution)/shard_map/dot_general | solution.py:170
  125.0 2.0 %convolution_add_fusion.2 = f32[256,512]{1,0:T(8,128)S(1)} fusion(f32[256,512]{1,0:T(8,128)S(1)} %fusion.32, bf16[1024,512]{1,0:T(8,128)(2,1)S(1)} %fusion.8, f32[1024,1024]{0,1:T(8,128)} %copy-done.1, f32[1024]{0:T(1024)S(1)} %pad_maximum_fusion.23, f32[256]{0:T(256)S(1)} %slice.156), kind=kOutput, calls=%fused_computation.43 | convolution fusion | flops 269352960 | bytes 3150848 | tf_op jit(solution)/shard_map/dot_general | solution.py:170
  127.0 2.9 %fusion.14 = f32[256,512]{1,0:T(8,128)} fusion(f32[256,512]{1,0:T(8,128)S(1)} %convolution_add_fusion.2, bf16[1024,512]{1,0:T(8,128)(2,1)S(1)} %copy-done.6, f32[1024,1024]{0,1:T(8,128)} %copy-done.2, f32[1024]{0:T(1024)S(1)} %pad_maximum_fusion.24, f32[256]{0:T(256)S(1)} %slice.156, bf16[1024,512]{1,0:T(8,128)(2,1)} %copy-done.9, f32[256]{0:T(256)S(1)} %add_add_fusion.1), kind=kOutput, calls=%fused_computation.44 | convolution fusion | flops 269746176 | bytes 3414016 | tf_op jit(solution)/shard_map/dot_general | solution.py:170
  129.9 1.7 %multiply_reduce_fusion = f32[2,1024]{1,0:T(2,128)S(1)} fusion(bf16[2,512,512]{2,1,0:T(8,128)(2,1)} %collective-permute-done.17, bf16[1,512,512]{2,1,0:T(8,128)(2,1)S(1)} %bitcast.136, bf16[1,512,512]{2,1,0:T(8,128)(2,1)S(1)} %bitcast.139), kind=kLoop, calls=%fused_computation.2 | loop fusion | flops 8386560 | bytes 2105344 | tf_op jit(solution)/shard_map/reduce_sum | solution.py:26
  131.6 1.8 %maximum_convert_fusion = f32[2,1024,512]{2,1,0:T(8,128)S(1)} fusion(bf16[2,512,512]{2,1,0:T(8,128)(2,1)} %collective-permute-done.17, bf16[1,512,512]{2,1,0:T(8,128)(2,1)S(1)} %bitcast.137, bf16[1,512,512]{2,1,0:T(8,128)(2,1)S(1)} %bitcast.140), kind=kLoop, calls=%fused_computation.26 | loop fusion | flops 6291456 | bytes 6291456 | tf_op jit(solution)/shard_map/convert_element_type | solution.py:25
  133.5 1.7 %fusion = bf16[2048,512]{1,0:T(8,128)(2,1)} fusion(f32[2,1024,512]{2,1,0:T(8,128)S(1)} %maximum_convert_fusion, f32[2048]{0:T(1024)S(1)} %bitcast.176), kind=kLoop, calls=%fused_computation.1 | loop fusion | flops 2097152 | bytes 6299648 | tf_op jit(solution)/shard_map/convert_element_type | solution.py:26
  135.2 5.3 %fusion.16 = f32[256,512]{1,0:T(8,128)} fusion(bf16[2048,512]{1,0:T(8,128)(2,1)} %fusion, pred[2048,256]{1,0:T(32,128)(4,1)S(1)} %copy-done.11, f32[256]{0:T(256)S(1)} %slice.175, f32[2048]{0:T(1024)S(1)} %pad_maximum_fusion.14, bf16[1024,512]{1,0:T(8,128)(2,1)S(1)} %copy-done.4), kind=kOutput, calls=%fused_computation.46 | convolution fusion | flops 1076363264 | bytes 5514240 | tf_op jit(solution)/shard_map/dot_general | solution.py:194
  140.5 3.1 %fusion.15 = f32[256,512]{1,0:T(8,128)} fusion(f32[256,512]{1,0:T(8,128)} %fusion.16, bf16[1024,512]{1,0:T(8,128)(2,1)S(1)} %copy-done.10, pred[1024,256]{1,0:T(32,128)(4,1)S(1)} %copy-done.12, f32[256]{0:T(256)S(1)} %slice.175, f32[1024]{0:T(1024)S(1)} %get-tuple-element.13, f32[256]{0:T(256)S(1)} %bitcast.204, bf16[1024,512]{1,0:T(8,128)(2,1)S(1)} %copy-done.4), kind=kOutput, calls=%fused_computation.45 | convolution fusion | flops 538705920 | bytes 3938304 | tf_op jit(solution)/shard_map/dot_general | solution.py:194
  (128 shorter events, 2.0 us)
Async XLA Ops:
  2.0 36.1 %collective-permute-start.5 = (bf16[512,512]{1,0:T(8,128)(2,1)S(1)}, bf16[512,512]{1,0:T(8,128)(2,1)S(1)}, u32[]{:S(2)}, u32[]{:S(2)}) collective-permute-start(bf16[512,512]{1,0:T(8,128)(2,1)S(1)} %bitcast.141), channel_id=1, source_target_pairs={{4,0},{8,4},{12,8},{16,12},{20,16},{24,20},{28,24},{32,28},{36,32}... | collective-permute-start | bytes 1572872 | tf_op jit(solution)/shard_map/ppermute | solution.py:21
  16.3 21.8 %collective-permute-start.4 = (bf16[512,512]{1,0:T(8,128)(2,1)S(1)}, bf16[512,512]{1,0:T(8,128)(2,1)S(1)}, u32[]{:S(2)}, u32[]{:S(2)}) collective-permute-start(bf16[512,512]{1,0:T(8,128)(2,1)S(1)} %bitcast.142), channel_id=1, source_target_pairs={{0,4},{4,8},{8,12},{12,16},{16,20},{20,24},{24,28},{28,32},{32,36}... | collective-permute-start | bytes 1572872 | tf_op jit(solution)/shard_map/ppermute | solution.py:16
  18.2 17.0 %collective-permute-start.2 = (bf16[256,512]{1,0:T(8,128)(2,1)}, bf16[256,512]{1,0:T(8,128)(2,1)S(1)}, u32[]{:S(2)}, u32[]{:S(2)}) collective-permute-start(bf16[256,512]{1,0:T(8,128)(2,1)} %param.5), channel_id=1, source_target_pairs={{0,2},{2,0},{1,3},{3,1},{4,6},{6,4},{5,7},{7,5},{8,10},{10,8},{9,1... | collective-permute-start | bytes 786440 | tf_op jit(solution)/shard_map/ppermute | solution.py:61
  21.6 8.1 %collective-permute-start = (f32[2,256]{1,0:T(2,128)S(1)}, f32[2,256]{1,0:T(2,128)S(1)}, u32[]{:S(2)}, u32[]{:S(2)}) collective-permute-start(f32[2,256]{1,0:T(2,128)S(1)} %get-tuple-element.75), channel_id=1, source_target_pairs={{0,2},{2,0},{1,3},{3,1},{4,6},{6,4},{5,7},{7,5},{8,10},{10,8},{9,1... | collective-permute-start | bytes 6152 | tf_op jit(solution)/shard_map/ppermute | solution.py:62
  28.8 24.0 %copy-start.7 = (bf16[256,512]{1,0:T(8,128)(2,1)S(1)}, bf16[256,512]{1,0:T(8,128)(2,1)}, u32[]{:S(2)}) copy-start(bf16[256,512]{1,0:T(8,128)(2,1)} %param.5) | copy-start | bytes 786436
  29.7 3.1 %collective-permute-start.1 = (f32[2,2,256]{2,1,0:T(2,128)S(1)}, f32[2,2,256]{2,1,0:T(2,128)S(1)}, u32[]{:S(2)}, u32[]{:S(2)}) collective-permute-start(f32[2,2,256]{2,1,0:T(2,128)S(1)} %pad_maximum_fusion.15), channel_id=1, source_target_pairs={{0,1},{1,0},{2,3},{3,2},{4,5},{5,4},{6,7},{7,6},{8,9},{9,8},{10,11... | collective-permute-start | bytes 12296 | tf_op jit(solution)/shard_map/ppermute | solution.py:66
  35.2 17.3 %copy-start.8 = (bf16[256,512]{1,0:T(8,128)(2,1)}, bf16[256,512]{1,0:T(8,128)(2,1)S(1)}, u32[]{:S(2)}) copy-start(bf16[256,512]{1,0:T(8,128)(2,1)S(1)} %collective-permute-done.2) | copy-start | bytes 786436
  36.0 16.8 %collective-permute-start.3 = (bf16[512,512]{1,0:T(8,128)(2,1)}, bf16[512,512]{1,0:T(8,128)(2,1)S(1)}, u32[]{:S(2)}, u32[]{:S(2)}) collective-permute-start(bf16[512,512]{1,0:T(8,128)(2,1)} %constant_dynamic-update-slice_fusion), channel_id=1, source_target_pairs={{0,1},{1,0},{2,3},{3,2},{4,5},{5,4},{6,7},{7,6},{8,9},{9,8},{10,11... | collective-permute-start | bytes 1572872 | tf_op jit(solution)/shard_map/ppermute | solution.py:65
  38.2 17.5 %copy-start.3 = (bf16[1024,512]{1,0:T(8,128)(2,1)S(1)}, bf16[1024,512]{1,0:T(8,128)(2,1)}, u32[]{:S(2)}) copy-start(bf16[1024,512]{1,0:T(8,128)(2,1)} %fusion.6) | copy-start | bytes 3145732
  38.2 21.0 %collective-permute-start.6 = (bf16[2,512,512]{2,1,0:T(8,128)(2,1)S(1)}, bf16[2,512,512]{2,1,0:T(8,128)(2,1)S(1)}, u32[]{:S(2)}, u32[]{:S(2)}) collective-permute-start(bf16[2,512,512]{2,1,0:T(8,128)(2,1)S(1)} %pad_maximum_fusion.2), channel_id=1, source_target_pairs={{0,1},{1,0},{2,3},{3,2},{4,5},{5,4},{6,7},{7,6},{8,9},{9,8},{10,11... | collective-permute-start | bytes 3145736 | tf_op jit(solution)/shard_map/ppermute | solution.py:92
  40.6 33.9 %collective-permute-start.16 = (bf16[512,512]{1,0:T(8,128)(2,1)}, bf16[512,512]{1,0:T(8,128)(2,1)S(1)}, u32[]{:S(2)}, u32[]{:S(2)}) collective-permute-start(bf16[512,512]{1,0:T(8,128)(2,1)} %constant_dynamic-update-slice_fusion), channel_id=1, source_target_pairs={{4,0},{8,4},{12,8},{16,12},{20,16},{24,20},{28,24},{32,28},{36,32}... | collective-permute-start | bytes 1572872 | tf_op jit(solution)/shard_map/ppermute | solution.py:21
  50.3 24.2 %collective-permute-start.15 = (bf16[512,512]{1,0:T(8,128)(2,1)}, bf16[512,512]{1,0:T(8,128)(2,1)S(1)}, u32[]{:S(2)}, u32[]{:S(2)}) collective-permute-start(bf16[512,512]{1,0:T(8,128)(2,1)} %constant_dynamic-update-slice_fusion), channel_id=1, source_target_pairs={{0,4},{4,8},{8,12},{12,16},{16,20},{20,24},{24,28},{28,32},{32,36}... | collective-permute-start | bytes 1572872 | tf_op jit(solution)/shard_map/ppermute | solution.py:16
  55.3 4.9 %copy-start.9 = (bf16[1024,512]{1,0:T(8,128)(2,1)}, bf16[1024,512]{1,0:T(8,128)(2,1)S(1)}, u32[]{:S(2)}) copy-start(bf16[1024,512]{1,0:T(8,128)(2,1)S(1)} %fusion.4) | copy-start | bytes 3145732
  57.3 36.9 %copy-start = (f32[1024,1024]{0,1:T(8,128)}, f32[1024,1024]{0,1:T(8,128)S(1)}, u32[]{:S(2)}) copy-start(f32[1024,1024]{0,1:T(8,128)S(1)} %get-tuple-element.79) | copy-start | bytes 12582916
  59.3 34.9 %copy-start.1 = (f32[1024,1024]{0,1:T(8,128)}, f32[1024,1024]{0,1:T(8,128)S(1)}, u32[]{:S(2)}) copy-start(f32[1024,1024]{0,1:T(8,128)S(1)} %get-tuple-element.81) | copy-start | bytes 12582916
  59.9 2.0 %copy-start.5 = (bf16[1024,512]{1,0:T(8,128)(2,1)}, bf16[1024,512]{1,0:T(8,128)(2,1)S(1)}, u32[]{:S(2)}) copy-start(bf16[1024,512]{1,0:T(8,128)(2,1)S(1)} %fusion.7) | copy-start | bytes 3145732
  61.9 32.3 %copy-start.2 = (f32[1024,1024]{0,1:T(8,128)}, f32[1024,1024]{0,1:T(8,128)S(1)}, u32[]{:S(2)}) copy-start(f32[1024,1024]{0,1:T(8,128)S(1)} %get-tuple-element.77) | copy-start | bytes 12582916
  62.9 21.6 %collective-permute-start.8 = (f32[3,1024]{1,0:T(4,128)S(1)}, f32[3,1024]{1,0:T(4,128)S(1)}, u32[]{:S(2)}, u32[]{:S(2)}) collective-permute-start(f32[3,1024]{1,0:T(4,128)S(1)} %get-tuple-element.55), channel_id=1, source_target_pairs={{4,0},{8,4},{12,8},{16,12},{20,16},{24,20},{28,24},{32,28},{36,32}... | collective-permute-start | bytes 36872 | tf_op jit(solution)/shard_map/ppermute | solution.py:21
  72.5 11.9 %collective-permute-start.7 = (f32[3,1024]{1,0:T(4,128)S(1)}, f32[3,1024]{1,0:T(4,128)S(1)}, u32[]{:S(2)}, u32[]{:S(2)}) collective-permute-start(f32[3,1024]{1,0:T(4,128)S(1)} %get-tuple-element.54), channel_id=1, source_target_pairs={{0,4},{4,8},{8,12},{12,16},{16,20},{20,24},{24,28},{28,32},{32,36}... | collective-permute-start | bytes 36872 | tf_op jit(solution)/shard_map/ppermute | solution.py:16
  75.6 54.3 %collective-permute-start.17 = (bf16[2,512,512]{2,1,0:T(8,128)(2,1)}, bf16[2,512,512]{2,1,0:T(8,128)(2,1)}, u32[]{:S(2)}, u32[]{:S(2)}) collective-permute-start(bf16[2,512,512]{2,1,0:T(8,128)(2,1)} %pad_maximum_fusion.3), channel_id=1, source_target_pairs={{0,1},{1,0},{2,3},{3,2},{4,5},{5,4},{6,7},{7,6},{8,9},{9,8},{10,11... | collective-permute-start | bytes 3145736 | tf_op jit(solution)/shard_map/ppermute | solution.py:100
  77.5 7.0 %collective-permute-start.10 = (f32[1,1024]{1,0:T(1,128)S(1)}, f32[1,1024]{1,0:T(1,128)S(1)}, u32[]{:S(2)}, u32[]{:S(2)}) collective-permute-start(f32[1,1024]{1,0:T(1,128)S(1)} %bitcast.196), channel_id=1, source_target_pairs={{8,0},{12,4},{16,8},{20,12},{24,16},{28,20},{32,24},{36,28},{40,32... | collective-permute-start | bytes 12296 | tf_op jit(solution)/shard_map/ppermute | solution.py:21
  80.9 12.2 %collective-permute-start.9 = (f32[1,1024]{1,0:T(1,128)S(1)}, f32[1,1024]{1,0:T(1,128)S(1)}, u32[]{:S(2)}, u32[]{:S(2)}) collective-permute-start(f32[1,1024]{1,0:T(1,128)S(1)} %bitcast.194), channel_id=1, source_target_pairs={{0,8},{4,12},{8,16},{12,20},{16,24},{20,28},{24,32},{28,36},{32,40... | collective-permute-start | bytes 12296 | tf_op jit(solution)/shard_map/ppermute | solution.py:16
  95.1 27.9 %copy-start.4 = (bf16[1024,512]{1,0:T(8,128)(2,1)S(1)}, bf16[1024,512]{1,0:T(8,128)(2,1)}, u32[]{:S(2)}) copy-start(bf16[1024,512]{1,0:T(8,128)(2,1)} %fusion.6) | copy-start | bytes 3145732
  95.2 25.2 %collective-permute-start.14 = (f32[1,1024]{1,0:T(1,128)S(1)}, f32[1,1024]{1,0:T(1,128)S(1)}, u32[]{:S(2)}, u32[]{:S(2)}) collective-permute-start(f32[1,1024]{1,0:T(1,128)S(1)} %bitcast.186), channel_id=1, source_target_pairs={{8,0},{12,4},{16,8},{20,12},{24,16},{28,20},{32,24},{36,28},{40,32... | collective-permute-start | bytes 12296 | tf_op jit(solution)/shard_map/ppermute | solution.py:21
  97.2 23.2 %collective-permute-start.13 = (f32[1,1024]{1,0:T(1,128)S(1)}, f32[1,1024]{1,0:T(1,128)S(1)}, u32[]{:S(2)}, u32[]{:S(2)}) collective-permute-start(f32[1,1024]{1,0:T(1,128)S(1)} %bitcast.184), channel_id=1, source_target_pairs={{0,8},{4,12},{8,16},{12,20},{16,24},{20,28},{24,32},{28,36},{32,40... | collective-permute-start | bytes 12296 | tf_op jit(solution)/shard_map/ppermute | solution.py:16
  102.1 18.2 %collective-permute-start.11 = (f32[3,1024]{1,0:T(4,128)S(1)}, f32[3,1024]{1,0:T(4,128)S(1)}, u32[]{:S(2)}, u32[]{:S(2)}) collective-permute-start(f32[3,1024]{1,0:T(4,128)S(1)} %get-tuple-element.38), channel_id=1, source_target_pairs={{0,4},{4,8},{8,12},{12,16},{16,20},{20,24},{24,28},{28,32},{32,36}... | collective-permute-start | bytes 36872 | tf_op jit(solution)/shard_map/ppermute | solution.py:16
  111.7 8.6 %collective-permute-start.12 = (f32[3,1024]{1,0:T(4,128)S(1)}, f32[3,1024]{1,0:T(4,128)S(1)}, u32[]{:S(2)}, u32[]{:S(2)}) collective-permute-start(f32[3,1024]{1,0:T(4,128)S(1)} %get-tuple-element.39), channel_id=1, source_target_pairs={{4,0},{8,4},{12,8},{16,12},{20,16},{24,20},{28,24},{32,28},{36,32}... | collective-permute-start | bytes 36872 | tf_op jit(solution)/shard_map/ppermute | solution.py:21
  120.5 6.5 %copy-start.6 = (bf16[1024,512]{1,0:T(8,128)(2,1)S(1)}, bf16[1024,512]{1,0:T(8,128)(2,1)}, u32[]{:S(2)}) copy-start(bf16[1024,512]{1,0:T(8,128)(2,1)} %copy-done.5) | copy-start | bytes 3145732
  133.5 1.7 %copy-start.11 = (pred[2048,256]{1,0:T(32,128)(4,1)S(1)}, pred[2048,256]{1,0:T(32,128)(4,1)}, u32[]{:S(2)}) copy-start(pred[2048,256]{1,0:T(32,128)(4,1)} %copy.44) | copy-start | bytes 1572868
  135.2 5.3 %copy-start.10 = (bf16[1024,512]{1,0:T(8,128)(2,1)S(1)}, bf16[1024,512]{1,0:T(8,128)(2,1)}, u32[]{:S(2)}) copy-start(bf16[1024,512]{1,0:T(8,128)(2,1)} %copy-done.9) | copy-start | bytes 3145732
  135.2 5.3 %copy-start.12 = (pred[1024,256]{1,0:T(32,128)(4,1)S(1)}, pred[1024,256]{1,0:T(32,128)(4,1)}, u32[]{:S(2)}) copy-start(pred[1024,256]{1,0:T(32,128)(4,1)} %copy.41) | copy-start | bytes 786436

commit v2 on v0

v2 whole, which is shorter than its diff:
```python
import jax
import jax.numpy as jnp
from jax import lax
from jax.experimental import pallas as pl
from jax.experimental.pallas import tpu as pltpu
from jax.sharding import PartitionSpec as P


SMOOTHING_TEMP = 0.05
EPSILON = 1e-06

SWAP_Y = [(0, 2), (2, 0), (1, 3), (3, 1)]
SWAP_CORE = [(0, 1), (1, 0), (2, 3), (3, 2)]

LANES = 128
QUARTER = 256
HALF = 512
SLAB = 1024
WIDTH = 512
SCALE = 1.0 / (WIDTH * SMOOTHING_TEMP)

F32 = jnp.float32
BF16 = jnp.bfloat16

CORE, Y, ODD, A_EVEN, HAS_ODD, WIDE, WIDE_ODD, WIDE_EVEN = range(8)


def both_ways(pairs, count):
    kept = [(a, b) for a, b in pairs if b < count]
    return kept + [(b, a) for a, b in kept]


def narrow_swap(block, pairs):
    return lax.ppermute(block, "narrow", pairs)


def exchange(block, hops, crossing):
    count = lax.axis_size("wide")
    first = hops if crossing else 0
    pairs = [
        (base + i, base + i + hops) for base in range(first, count, 2 * hops) for i in range(hops)
    ]
    return lax.ppermute(block, "wide", both_ways(pairs, count))


def normalize(features):
    values = features.astype(F32)
    total = jnp.sum(values * values, axis=1, keepdims=True)
    return (values * lax.rsqrt(total * (1.0 / WIDTH) + EPSILON)).astype(BF16)


def nt_dot(a, b):
    return lax.dot_general(a, b, (((1,), (1,)), ((), ())), preferred_element_type=F32)


def identity():
    return lax.broadcasted_iota(jnp.int32, (LANES, LANES), 0) == lax.broadcasted_iota(
        jnp.int32, (LANES, LANES), 1
    )


def to_column(row):
    return jnp.sum(jnp.where(identity(), row, 0.0), axis=1, keepdims=True)


def to_row(column):
    return jnp.sum(jnp.where(identity(), column, 0.0), axis=0, keepdims=True)


def lane_tiles(values):
    total = values[:, :LANES]
    for i in range(1, values.shape[1] // LANES):
        total = total + values[:, i * LANES : (i + 1) * LANES]
    return total


def sublane_tiles(values):
    rows, columns = values.shape
    return jnp.sum(values.reshape(rows // 8, 8, columns), axis=0)


def block_kernel(rows_ref, columns, mask_ref, i, lanes):
    inner = nt_dot(rows_ref[pl.ds(pl.multiple_of(i * QUARTER, QUARTER), QUARTER), :], columns)
    values = jnp.exp(inner * SCALE)
    top = values[:LANES] * mask_ref[pl.ds(2 * i, 1), lanes]
    bottom = values[LANES:] * mask_ref[pl.ds(2 * i + 1, 1), lanes]
    return top, bottom


def fill_kernel(rows_ref, columns_ref, mask_ref, lanes, kernel_ref, sums_ref, before_ref):
    def step(i, carry):
        blocks = block_kernel(rows_ref, columns_ref[...], mask_ref, i, lanes)
        for j, block in enumerate(blocks):
            at = pl.ds(pl.multiple_of(i * QUARTER + j * LANES, LANES), LANES)
            kernel_ref[at, :] = block
            sums = lane_tiles(block)
            if before_ref is not None:
                sums = sums + before_ref[at, :]
            sums_ref[at, :] = sums
        return carry

    lax.fori_loop(0, 4, step, 0)


def prepare_kernel(
    flags, own_ref, y_ref, far_ref, small_ref, small_y_ref, small_far_ref, control_ref, weight_any,
    rows_ref, columns_ref, kernel_ref, sums_ref, mask_ref, weight_ref, pair_ref, column_weight_ref,
    band_ref, fetched_ref, sems,
):
    core, y, odd = flags[CORE], flags[Y], flags[ODD]
    copies = [
        pltpu.make_async_copy(
            weight_any.at[pl.ds(pl.multiple_of(flags[which] * 8, 8), 8), :],
            fetched_ref.at[i],
            sems.at[i],
        )
        for i, which in enumerate((WIDE, WIDE_ODD, WIDE_EVEN))
    ]
    for copy in copies:
        copy.start()
    rows_ref[0:QUARTER, :] = normalize(own_ref[...])
    rows_ref[QUARTER:HALF, :] = normalize(y_ref[...])
    rows_ref[HALF:SLAB, :] = normalize(far_ref[...])
    for i in range(4):
        quarter = (2 * i + core) if i < 2 else (2 * (i - 2) + 1 - core)
        at = pl.ds(pl.multiple_of(quarter * QUARTER, QUARTER), QUARTER)
        columns_ref[i * QUARTER : (i + 1) * QUARTER, :] = normalize(control_ref[at, :])

    band_ref[...] = jnp.zeros_like(band_ref)
    for i, source in enumerate(
        (small_ref[...], small_y_ref[...], small_far_ref[0], small_far_ref[1])
    ):
        band_ref[2 * i : 2 * i + 2, :] = source[2:4]
        for j in range(2):
            at = slice((2 * i + j) * LANES, (2 * i + j + 1) * LANES)
            weight_ref[at, :] = jnp.broadcast_to(to_column(source[j : j + 1]), (LANES, LANES))
    band = band_ref[...].astype(BF16)
    odd_base = odd * 16
    even_base = 16 - odd * 16
    lane = lax.broadcasted_iota(jnp.int32, (1, 3 * SLAB), 1)
    segment = lane // SLAB
    within = lane % SLAB
    block = (lane // LANES) % 2
    own_quarter = jnp.where(
        within < HALF, 2 * (within // QUARTER) + core, 2 * (within // QUARTER - 2) + 1 - core
    )
    side_quarter = 2 * ((within // QUARTER) % 2) + jnp.where(segment == 1, core, 1 - core)
    side_base = jnp.where(within < HALF, odd_base, even_base)
    wanted = jnp.where(segment == 0, 8 + 2 * own_quarter, side_base + 2 * side_quarter) + block
    one_hot = lax.broadcasted_iota(jnp.int32, (LANES, 3 * SLAB), 0) == wanted
    mask_ref[...] = jnp.dot(
        band[:16], jnp.where(one_hot, 1.0, 0.0).astype(BF16), preferred_element_type=F32
    )[:8]
    place = lax.broadcasted_iota(jnp.int32, (16, LANES), 0)
    base = jnp.where(place < 2, 8, jnp.where(place < 4, odd_base, even_base))
    chosen = base + 2 * (2 * y + core) + place % 2
    select = jnp.where(
        lax.broadcasted_iota(jnp.int32, (16, LANES), 1) == chosen, 1.0, 0.0
    ).astype(BF16)
    by_block = nt_dot(select, band).astype(BF16)
    spread = (
        lax.broadcasted_iota(jnp.int32, (LANES, SLAB), 0)
        == lax.broadcasted_iota(jnp.int32, (LANES, SLAB), 1) // LANES
    )
    pair_ref[...] = jnp.dot(
        by_block, jnp.where(spread, 1.0, 0.0).astype(BF16), preferred_element_type=F32
    )[:8]

    fill_kernel(rows_ref, columns_ref, mask_ref, slice(0, SLAB), kernel_ref, sums_ref, None)

    for copy in copies:
        copy.wait()
    column_weight_ref[...] = jnp.zeros_like(column_weight_ref)
    for i in range(3):
        for q in range(4):
            quarter = (2 * q + core) if q < 2 else (2 * (q - 2) + 1 - core)
            for j in range(2):
                at = slice((2 * q + j) * LANES, (2 * q + j + 1) * LANES)
                column_weight_ref[i : i + 1, at] = fetched_ref[i, pl.ds(2 * quarter + j, 1), :]


def near_kernel(
    odd_ref, even_ref, rows_ref, mask_ref, before_ref, columns_ref, kernel_ref, sums_ref
):
    columns_ref[0:HALF, :] = normalize(odd_ref[...])
    columns_ref[HALF:SLAB, :] = normalize(even_ref[...])
    fill_kernel(
        rows_ref, columns_ref, mask_ref, slice(SLAB, 2 * SLAB), kernel_ref, sums_ref, before_ref
    )


def finish_messages(
    flags, own, near, far, first, second, partial_ref, odd_ref, even_ref, a_ref, b_ref
):
    own = jnp.sum(own, axis=0, keepdims=True)
    near = jnp.sum(near, axis=0, keepdims=True)
    far = jnp.sum(far, axis=0, keepdims=True)
    partial_ref[...] = jnp.zeros_like(partial_ref)
    partial_ref[0:1, :] = own
    for i in range(2):
        at = slice(i * HALF, (i + 1) * HALF)
        partial_ref[i + 1 : i + 2, 0:HALF] = near[:, at]
        partial_ref[i + 1 : i + 2, HALF:SLAB] = far[:, at]
    odd = partial_ref[1:2, :]
    even = partial_ref[2:3, :]
    odd_ref[0:1, :] = own
    odd_ref[1:2, :] = odd
    odd_ref[2:4, :] = first
    even_ref[0:1, :] = own
    even_ref[1:2, :] = even
    even_ref[2:4, :] = second
    a_even = flags[A_EVEN] > 0
    a_ref[...] = jnp.where(a_even, even, odd)
    b_ref[...] = jnp.where(a_even, odd, even)


def far_kernel(
    flags, odd_far_ref, even_far_ref, rows_ref, mask_ref, own_kernel_ref, near_kernel_ref,
    before_ref, weight_ref, pair_ref, columns_ref, kernel_ref, partial_ref, odd_ref, even_ref, a_ref, b_ref,
):
    columns_ref[0:HALF, :] = normalize(odd_far_ref[...])
    columns_ref[HALF:SLAB, :] = normalize(even_far_ref[...])

    def step(i, carry):
        own, near, far = carry
        blocks = block_kernel(
            rows_ref, columns_ref[...], mask_ref, i, slice(2 * SLAB, 3 * SLAB)
        )
        for j, block in enumerate(blocks):
            at = pl.ds(pl.multiple_of(i * QUARTER + j * LANES, LANES), LANES)
            kernel_ref[at, :] = block
            sums = lane_tiles(block) + before_ref[at, :]
            scale = weight_ref[at, 0:1] / jnp.sum(sums, axis=1, keepdims=True)
            own = own + sublane_tiles(own_kernel_ref[at, :] * scale)
            near = near + sublane_tiles(near_kernel_ref[at, :] * scale)
            far = far + sublane_tiles(block * scale)
        return own, near, far

    zero = jnp.zeros((8, SLAB), F32)
    own, near, far = lax.fori_loop(0, 4, step, (zero, zero, zero))
    finish_messages(
        flags, own, near, far, pair_ref[2:4, :], pair_ref[4:6, :],
        partial_ref, odd_ref, even_ref, a_ref, b_ref,
    )


def column_scales(flags, partial_ref, odd_ref, even_ref, a_ref, b_ref, column_weight_ref):
    a_even = flags[A_EVEN] > 0
    two_odd = jnp.where(a_even, b_ref[...], a_ref[...])
    two_even = jnp.where(a_even, a_ref[...], b_ref[...])
    own = partial_ref[0:1, :] + odd_ref[1:2, :] + even_ref[1:2, :]
    odd = partial_ref[1:2, :] + odd_ref[0:1, :] + two_odd
    even = partial_ref[2:3, :] + even_ref[0:1, :] + two_even
    has_odd = flags[HAS_ODD] > 0
    own = column_weight_ref[0:1, :] / own
    odd = jnp.where(has_odd, column_weight_ref[1:2, :] / jnp.where(has_odd, odd, 1.0), 0.0)
    even = column_weight_ref[2:3, :] / even
    near = jnp.concatenate([odd[:, :HALF], even[:, :HALF]], axis=1)
    far = jnp.concatenate([odd[:, HALF:], even[:, HALF:]], axis=1)
    return own, near, far


def sweep_kernel(
    flags, partial_in, odd_in, even_in, a_in, b_in, column_weight_ref, own_kernel_ref,
    near_kernel_ref, far_kernel_ref, weight_ref, row_ref, lane_ref, partial_ref, odd_ref,
    even_ref, a_ref, b_ref, flat_ref,
):
    scales = column_scales(flags, partial_in, odd_in, even_in, a_in, b_in, column_weight_ref)
    kernels = (own_kernel_ref, near_kernel_ref, far_kernel_ref)

    def step(i, carry):
        at = pl.ds(pl.multiple_of(i * LANES, LANES), LANES)
        total = jnp.zeros((LANES, LANES), F32)
        for kernel_ref, scale in zip(kernels, scales, strict=True):
            total = total + lane_tiles(kernel_ref[at, :] * scale)
        row_scale = weight_ref[at, 0:1] / jnp.sum(total, axis=1, keepdims=True)
        row_ref[at, :] = jnp.broadcast_to(row_scale, (LANES, LANES))
        flat_ref[pl.ds(i, 1), :] = to_row(row_scale)
        return tuple(
            sums + sublane_tiles(kernel_ref[at, :] * row_scale)
            for kernel_ref, sums in zip(kernels, carry, strict=True)
        )

    zero = jnp.zeros((8, SLAB), F32)
    own, near, far = lax.fori_loop(0, 8, step, (zero, zero, zero))
    for i in range(8):
        lane_ref[0:1, i * LANES : (i + 1) * LANES] = flat_ref[i : i + 1, :]
    flat = jnp.broadcast_to(lane_ref[...], (2, SLAB))
    finish_messages(
        flags, own, near, far, flat, flat, partial_ref, odd_ref, even_ref, a_ref, b_ref
    )


def transposed_kernel(
    flags, columns_ref, rows_ref, odd_near_ref, even_near_ref, odd_far_ref, even_far_ref, pair_ref,
    odd_in, even_in, odd_rows_ref, even_rows_ref, kernel_ref,
):
    at = pl.ds(pl.multiple_of(flags[Y] * QUARTER, QUARTER), QUARTER)
    own = columns_ref[at, :]
    odd_rows_ref[0:HALF, :] = normalize(odd_near_ref[...])
    odd_rows_ref[HALF:SLAB, :] = normalize(odd_far_ref[...])
    even_rows_ref[0:HALF, :] = normalize(even_near_ref[...])
    even_rows_ref[HALF:SLAB, :] = normalize(even_far_ref[...])
    for i, (rows, top, bottom) in enumerate(
        (
            (rows_ref, pair_ref[0:1, :], pair_ref[1:2, :]),
            (odd_rows_ref, odd_in[2:3, :], odd_in[3:4, :]),
            (even_rows_ref, even_in[2:3, :], even_in[3:4, :]),
        )
    ):
        values = jnp.exp(nt_dot(own, rows[...]) * SCALE)
        lanes = slice(i * SLAB, (i + 1) * SLAB)
        kernel_ref[0:LANES, lanes] = values[:LANES] * top
        kernel_ref[LANES:QUARTER, lanes] = values[LANES:] * bottom


def gradient_kernel(
    flags, partial_in, odd_in, even_in, a_in, b_in, column_weight_ref, row_ref, lane_ref,
    own_kernel_ref, near_kernel_ref, far_kernel_ref, own_columns_ref, near_columns_ref,
    far_columns_ref, rows_ref, odd_rows_ref, even_rows_ref, transposed_ref, treated_out,
    control_out,
):
    scales = column_scales(flags, partial_in, odd_in, even_in, a_in, b_in, column_weight_ref)
    row_scale = row_ref[:, 0:1]
    mass = jnp.zeros((QUARTER, LANES), F32)
    pulled = jnp.zeros((QUARTER, WIDTH), F32)
    for kernel_ref, scale, columns_ref in zip(
        (own_kernel_ref, near_kernel_ref, far_kernel_ref),
        scales,
        (own_columns_ref, near_columns_ref, far_columns_ref),
        strict=True,
    ):
        transport = row_scale * kernel_ref[...] * scale
        mass = mass + lane_tiles(transport)
        pulled = pulled + jnp.dot(
            transport.astype(BF16), columns_ref[...], preferred_element_type=F32
        )
    mass = jnp.sum(mass, axis=1, keepdims=True)
    treated_out[...] = mass * rows_ref[0:QUARTER, :].astype(F32) - pulled

    second = flags[Y] > 0

    def own_quarter(row):
        return jnp.where(second, row[:, QUARTER:HALF], row[:, :QUARTER])

    def upright(row):
        return jnp.concatenate([to_column(row[:, :LANES]), to_column(row[:, LANES:])], axis=0)

    own_scale = upright(own_quarter(scales[0]))
    own_weight = upright(own_quarter(column_weight_ref[0:1, :]))
    pushed = jnp.zeros((QUARTER, WIDTH), F32)
    for i, (scale, rows) in enumerate(
        ((lane_ref[...], rows_ref), (odd_in[2:3, :], odd_rows_ref), (even_in[2:3, :], even_rows_ref))
    ):
        transport = scale * transposed_ref[:, i * SLAB : (i + 1) * SLAB] * own_scale
        pushed = pushed + jnp.dot(transport.astype(BF16), rows[...], preferred_element_type=F32)
    at = pl.ds(pl.multiple_of(flags[Y] * QUARTER, QUARTER), QUARTER)
    control_out[...] = own_weight * own_columns_ref[at, :].astype(F32) - pushed


VMEM = pl.BlockSpec(memory_space=pltpu.VMEM)
SMEM = pl.BlockSpec(memory_space=pltpu.SMEM)
ANY = pl.BlockSpec(memory_space=pltpu.HBM)


def call(body, specs, outs, operands, scratch=(), limit=30, out_specs=None):
    return pl.pallas_call(
        body,
        out_shape=tuple(jax.ShapeDtypeStruct(shape, dtype) for shape, dtype in outs),
        in_specs=specs,
        out_specs=out_specs or tuple(VMEM for _ in outs),
        scratch_shapes=list(scratch),
        compiler_params=pltpu.CompilerParams(vmem_limit_bytes=limit << 20),
    )(*operands)


MESSAGES = [((4, SLAB), F32), ((4, SLAB), F32), ((1, SLAB), F32), ((1, SLAB), F32)]


def trade(messages):
    odd, even, a, b = messages
    return (
        exchange(odd, 1, True),
        exchange(even, 1, False),
        exchange(a, 2, True),
        exchange(b, 2, False),
    )


def step(treated, control, treated_weight, control_weight, band):
    wide_index = lax.axis_index("wide")
    n = lax.axis_index("narrow")
    wide_count = lax.axis_size("wide")
    core, y, odd = n % 2, n // 2, wide_index % 2
    toward_odd = wide_index + 2 * odd - 1
    values = (
        core,
        y,
        odd,
        jnp.logical_xor(wide_index % 4 >= 2, odd == 1).astype(jnp.int32),
        ((toward_odd >= 0) & (toward_odd < wide_count)).astype(jnp.int32),
        wide_index,
        jnp.clip(toward_odd, 0, wide_count - 1),
        wide_index + 1 - 2 * odd,
    )
    place = lax.iota(jnp.int32, 8)
    flags = jnp.zeros((8,), jnp.int32)
    for i, value in enumerate(values):
        flags = jnp.where(place == i, value, flags)

    near = lax.dynamic_slice(
        control.reshape(2, 2, QUARTER, WIDTH), (0, core, 0, 0), (2, 1, QUARTER, WIDTH)
    ).reshape(HALF, WIDTH)
    odd_near = exchange(near, 1, True)
    even_near = exchange(near, 1, False)

    small = jnp.concatenate(
        [
            treated_weight.reshape(2, LANES),
            jnp.pad(band.astype(F32), ((0, 0), (0, LANES - band.shape[1]))),
        ],
        0,
    )
    treated_y = narrow_swap(treated, SWAP_Y)
    small_y = narrow_swap(small, SWAP_Y)
    treated_pair = jnp.concatenate([treated, treated_y], 0)
    treated_far = narrow_swap(treated_pair, SWAP_CORE)
    small_far = narrow_swap(jnp.stack([small, small_y], 0), SWAP_CORE)

    weights = control_weight.reshape(-1, LANES)
    rows, own_columns, own_kernel, sums, mask, weight, pairs, column_weight = call(
        prepare_kernel,
        [SMEM] + [VMEM] * 7 + [ANY],
        [
            ((SLAB, WIDTH), BF16),
            ((SLAB, WIDTH), BF16),
            ((SLAB, SLAB), F32),
            ((SLAB, LANES), F32),
            ((8, 3 * SLAB), F32),
            ((SLAB, LANES), F32),
            ((8, SLAB), F32),
            ((8, SLAB), F32),
        ],
        [flags, treated, treated_y, treated_far, small, small_y, small_far, control, weights],
        [
            pltpu.VMEM((LANES, LANES), F32),
            pltpu.VMEM((3, 8, LANES), F32),
            pltpu.SemaphoreType.DMA((3,)),
        ],
    )

    odd_near, even_near, _ = lax.optimization_barrier((odd_near, even_near, sums))
    odd_far = narrow_swap(odd_near, SWAP_CORE)
    even_far = narrow_swap(even_near, SWAP_CORE)
    near_columns, near_values, sums = call(
        near_kernel,
        [VMEM] * 5,
        [((SLAB, WIDTH), BF16), ((SLAB, SLAB), F32), ((SLAB, LANES), F32)],
        [odd_near, even_near, rows, mask, sums],
    )

    odd_treated = exchange(treated_pair, 1, True)
    even_treated = exchange(treated_pair, 1, False)

    far_columns, far_values, partial, *messages = call(
        far_kernel,
        [SMEM] + [VMEM] * 9,
        [((SLAB, WIDTH), BF16), ((SLAB, SLAB), F32), ((8, SLAB), F32), *MESSAGES],
        [flags, odd_far, even_far, rows, mask, own_kernel, near_values, sums, weight, pairs],
    )
    first = trade(messages)
    odd_treated_far = narrow_swap(odd_treated, SWAP_CORE)
    even_treated_far = narrow_swap(even_treated, SWAP_CORE)

    row_scale, lane_scale, partial, *messages = call(
        sweep_kernel,
        [SMEM] + [VMEM] * 10,
        [((SLAB, LANES), F32), ((1, SLAB), F32), ((8, SLAB), F32), *MESSAGES],
        [flags, partial, *first, column_weight, own_kernel, near_values, far_values, weight],
        [pltpu.VMEM((8, LANES), F32)],
    )
    second = trade(messages)

    odd_rows, even_rows, transposed = call(
        transposed_kernel,
        [SMEM] + [VMEM] * 9,
        [((SLAB, WIDTH), BF16), ((SLAB, WIDTH), BF16), ((QUARTER, 3 * SLAB), F32)],
        [
            flags, own_columns, rows, odd_treated, even_treated, odd_treated_far,
            even_treated_far, pairs, first[0], first[1],
        ],
    )

    top = pl.BlockSpec((QUARTER, SLAB), lambda i: (0, 0))
    whole = lambda *shape: pl.BlockSpec(shape, lambda i: (0,) * len(shape))
    return pl.pallas_call(
        gradient_kernel,
        grid=(1,),
        out_shape=(jax.ShapeDtypeStruct((QUARTER, WIDTH), F32),) * 2,
        in_specs=[
            SMEM, whole(8, SLAB), whole(4, SLAB), whole(4, SLAB), whole(1, SLAB), whole(1, SLAB),
            whole(8, SLAB), pl.BlockSpec((QUARTER, LANES), lambda i: (0, 0)), whole(1, SLAB),
            top, top, top,
            *[whole(SLAB, WIDTH)] * 6, whole(QUARTER, 3 * SLAB),
        ],
        out_specs=(whole(QUARTER, WIDTH),) * 2,
        compiler_params=pltpu.CompilerParams(vmem_limit_bytes=30 << 20),
        name="gradient_kernel",
    )(
        flags, partial, *second, column_weight, row_scale, lane_scale, own_kernel, near_values,
        far_values, own_columns, near_columns, far_columns, rows, odd_rows, even_rows, transposed,
    )


def solution(mesh):
    return jax.shard_map(
        step,
        mesh=mesh,
        in_specs=(
            P(("wide", "narrow"), None),
            P("wide", None),
            P(("wide", "narrow")),
            P(),
            P(("wide", "narrow"), None),
        ),
        out_specs=(P(("wide", "narrow"), None), P(("wide", "narrow"), None)),
        check_vma=False,
    )
```

time: 228 us -> 117 us (0.51)
  waiting for transfers between devices: 126 us -> 13.5 us
  starting transfers between devices: 45.4 us -> 74.5 us
  Pallas kernels: 0 us -> 20.2 us
  blocking collectives: 20.2 us -> 0 us
  between operations: 14.3 us -> 1.02 us
  other arithmetic: 13.5 us -> 1.38 us
  matrix products: 4.3 us -> 0 us
  local copies, waits for them, and re-layouts: 1.57 us -> 5.28 us
    ppermute x12 -> x20, waiting for transfers between devices: 107 us -> 13.5 us  [the longest x12 13.4 us: exchange(): return lax.ppermute(block, 'wide', both_ways(pairs, count))]
    ppermute x12 -> x20, starting transfers between devices: 45.4 us -> 74.5 us  [the longest x12 56 us: exchange(): return lax.ppermute(block, 'wide', both_ways(pairs, count))]
    pallas_call x0 -> x6, Pallas kernels: none -> 20.2 us  [the longest x5 16.7 us: call(): pl.pallas_call(body, out_shape=tuple((jax.ShapeDtypeStruct(shape, dtype)...]
    psum x2 -> x0, blocking collectives: 20.2 us -> none  [shards(): slab_parts = lax.psum(column_parts, 'narrow')]
    reduce_scatter x1 -> x0, waiting for transfers between devices: 19 us -> none  [shards(): lax.psum_scatter(neighbours[0] + neighbours[2] + neighbours[4], 'narrow',...]
    dot_general x3 -> x0, matrix products: 4.3 us -> none  [the longest x1 1.82 us: shards(): pulled = jnp.dot(plan_bf, band_span, preferred_element_type=jnp.float32)]
    unnamed x10 -> x7, local copies, waits for them, and re-layouts: 0.05 us -> 4.18 us
    reduce_sum x6 -> x0, other arithmetic: 3.32 us -> none  [the longest x2 1.66 us: normalize(): jnp.mean(values * values, axis=1, keepdims=True) + EPSILON]
  transfers between devices with their start and end apart: 13 -> 20, of which waited for: 9 -> 5; matrix products, arithmetic and copies ran while one was open for 3% -> 3% of each run, Pallas kernels for 0% -> 14%
where the time goes in v2:
time: 117 us; the launch traced here: 116 us
  starting transfers between devices  74.5 us (64%)
  Pallas kernels  20.2 us (17%)
  waiting for transfers between devices  13.5 us (12%)
  local copies, waits for them, and re-layouts  5.28 us (5%)
  other arithmetic  1.38 us (1%)
    ppermute x12, starting transfers between devices, exchange(): return lax.ppermute(block, 'wide', both_ways(pairs, count))  56 us
    ppermute x8, starting transfers between devices, narrow_swap(): return lax.ppermute(block, 'narrow', pairs)  18.5 us
    pallas_call x5, Pallas kernels, call(): pl.pallas_call(body, out_shape=tuple((jax.ShapeDtypeStruct(shape, dtype)...  16.7 us
    ppermute x12, waiting for transfers between devices, exchange(): return lax.ppermute(block, 'wide', both_ways(pairs, count))  13.4 us
    unnamed x7, local copies, waits for them, and re-layouts  4.18 us
    pallas_call x1, Pallas kernels, step(): pl.pallas_call(gradient_kernel, grid=(1,), out_shape=(jax.ShapeDtypeStruc...  3.54 us
  transfers between devices with their start and end apart: 20, of which 5 were waited for; matrix products, arithmetic and copies ran while one was open for 3% of the time, Pallas kernels for 14%

profile of v2, /device:TPU:24, one launch (start us, length us, event | category | flops | bytes accessed | tf_op | source)
XLA Modules:
  0.0 115.9 jit_solution(112533915100294290)
XLA Ops:
  0.6 2.7 %collective-permute-start.2 = (bf16[256,512]{1,0:T(8,128)(2,1)}, bf16[256,512]{1,0:T(8,128)(2,1)S(1)}, u32[]{:S(2)}, u32[]{:S(2)}) collective-permute-start(bf16[256,512]{1,0:T(8,128)(2,1)} %own_ref.1), channel_id=1, source_target_pairs={{0,2},{2,0},{1,3},{3,1},{4,6},{6,4},{5,7},{7,5},{8,10},{10,8},{9,1... | collective-permute-start | bytes 786440 | tf_op jit(solution)/shard_map/ppermute | solution.py:34
  3.3 1.1 constant_dynamic-slice_fusion
  4.4 14.0 %collective-permute-start = (bf16[512,512]{1,0:T(8,128)(2,1)S(1)}, bf16[512,512]{1,0:T(8,128)(2,1)S(1)}, u32[]{:S(2)}, u32[]{:S(2)}) collective-permute-start(bf16[512,512]{1,0:T(8,128)(2,1)S(1)} %bitcast.12), channel_id=1, source_target_pairs={{4,8},{12,16},{20,24},{28,32},{36,40},{44,48},{52,56},{60,64},{68,... | collective-permute-start | bytes 1572872 | tf_op jit(solution)/shard_map/ppermute | solution.py:43
  18.4 1.9 %collective-permute-start.1 = (bf16[512,512]{1,0:T(8,128)(2,1)S(1)}, bf16[512,512]{1,0:T(8,128)(2,1)S(1)}, u32[]{:S(2)}, u32[]{:S(2)}) collective-permute-start(bf16[512,512]{1,0:T(8,128)(2,1)S(1)} %bitcast.13), channel_id=1, source_target_pairs={{0,4},{8,12},{16,20},{24,28},{32,36},{40,44},{48,52},{56,60},{64,6... | collective-permute-start | bytes 1572872 | tf_op jit(solution)/shard_map/ppermute | solution.py:43
  20.3 0.7 convert_element_type.13
  21.0 0.7 fusion
  21.7 2.9 %collective-permute-start.4 = (f32[4,128]{1,0:T(4,128)S(1)}, f32[4,128]{1,0:T(4,128)S(1)}, u32[]{:S(2)}, u32[]{:S(2)}) collective-permute-start(f32[4,128]{1,0:T(4,128)S(1)} %get-tuple-element.63.small_ref), channel_id=1, source_target_pairs={{0,2},{2,0},{1,3},{3,1},{4,6},{6,4},{5,7},{7,5},{8,10},{10,8},{9,1... | collective-permute-start | bytes 6152 | tf_op jit(solution)/shard_map/ppermute | solution.py:34
  24.6 1.0 constant_dynamic-update-slice_fusion.1
  25.5 0.0 collective-permute-done.2.y_ref
  25.6 1.9 %collective-permute-start.3 = (bf16[512,512]{1,0:T(8,128)(2,1)S(1)}, bf16[512,512]{1,0:T(8,128)(2,1)S(1)}, u32[]{:S(2)}, u32[]{:S(2)}) collective-permute-start(bf16[512,512]{1,0:T(8,128)(2,1)S(1)} %constant_dynamic-update-slice_fusion), channel_id=1, source_target_pairs={{0,1},{1,0},{2,3},{3,2},{4,5},{5,4},{6,7},{7,6},{8,9},{9,8},{10,11... | collective-permute-start | bytes 1572872 | tf_op jit(solution)/shard_map/ppermute | solution.py:34
  27.5 0.0 collective-permute-done.4.small_y_ref
  27.5 2.4 %collective-permute-start.5 = (f32[2,4,128]{2,1,0:T(4,128)S(1)}, f32[2,4,128]{2,1,0:T(4,128)S(1)}, u32[]{:S(2)}, u32[]{:S(2)}) collective-permute-start(f32[2,4,128]{2,1,0:T(4,128)S(1)} %pad_maximum_fusion), channel_id=1, source_target_pairs={{0,1},{1,0},{2,3},{3,2},{4,5},{5,4},{6,7},{7,6},{8,9},{9,8},{10,11... | collective-permute-start | bytes 12296 | tf_op jit(solution)/shard_map/ppermute | solution.py:34
  29.9 4.5 %collective-permute-start.16 = (bf16[512,512]{1,0:T(8,128)(2,1)S(1)}, bf16[512,512]{1,0:T(8,128)(2,1)}, u32[]{:S(2)}, u32[]{:S(2)}) collective-permute-start(bf16[512,512]{1,0:T(8,128)(2,1)S(1)} %constant_dynamic-update-slice_fusion), channel_id=1, source_target_pairs={{4,8},{12,16},{20,24},{28,32},{36,40},{44,48},{52,56},{60,64},{68,... | collective-permute-start | bytes 1572872 | tf_op jit(solution)/shard_map/ppermute | solution.py:43
  34.5 0.0 collective-permute-done.5.small_far_ref
  34.5 1.9 %collective-permute-start.17 = (bf16[512,512]{1,0:T(8,128)(2,1)S(1)}, bf16[512,512]{1,0:T(8,128)(2,1)}, u32[]{:S(2)}, u32[]{:S(2)}) collective-permute-start(bf16[512,512]{1,0:T(8,128)(2,1)S(1)} %constant_dynamic-update-slice_fusion), channel_id=1, source_target_pairs={{0,4},{8,12},{16,20},{24,28},{32,36},{40,44},{48,52},{56,60},{64,6... | collective-permute-start | bytes 1572872 | tf_op jit(solution)/shard_map/ppermute | solution.py:43
  36.5 0.0 collective-permute-done.3.far_ref
  36.5 0.0 copy-start
  36.5 1.2 %copy-done = bf16[1024,512]{1,0:T(8,128)(2,1)S(1)} copy-done((bf16[1024,512]{1,0:T(8,128)(2,1)S(1)}, bf16[1024,512]{1,0:T(8,128)(2,1)}, u32[]{:S(2)}) %copy-start) | copy-done | bytes 1048600
  37.7 0.0 copy-start.1
  37.7 0.9 copy-done.1
  38.7 0.0 copy-start.2
  38.7 1.0 copy-done.2
  39.7 3.7 %shard_map.68 = (bf16[1024,512]{1,0:T(8,128)(2,1)S(1)}, bf16[1024,512]{1,0:T(8,128)(2,1)S(1)}, f32[1024,1024]{1,0:T(8,128)S(1)}, f32[1024,128]{1,0:T(8,128)S(1)}...) custom-call(s32[8]{0:T(128)S(1)} %compare_select_fusion.7.flags, ...), custom_call_target="tpu_custom_call" | custom-call | tf_op jit(solution)/shard_map/pallas_call | solution.py:367
  43.4 0.0 collective-permute-done.odd_ref
  43.4 0.0 collective-permute-done.1.even_ref
  43.4 1.9 %collective-permute-start.6 = (bf16[512,512]{1,0:T(8,128)(2,1)S(1)}, bf16[512,512]{1,0:T(8,128)(2,1)S(1)}, u32[]{:S(2)}, u32[]{:S(2)}) collective-permute-start(bf16[512,512]{1,0:T(8,128)(2,1)S(1)} %collective-permute-done.odd_ref), channel_id=1, source_target_pairs={{0,1},{1,0},{2,3},{3,2},{4,5},{5,4},{6,7},{7,6},{8,9},{9,8},{10,11... | collective-permute-start | bytes 1572872 | tf_op jit(solution)/shard_map/ppermute | solution.py:34
  45.3 2.4 %collective-permute-start.7 = (bf16[512,512]{1,0:T(8,128)(2,1)S(1)}, bf16[512,512]{1,0:T(8,128)(2,1)S(1)}, u32[]{:S(2)}, u32[]{:S(2)}) collective-permute-start(bf16[512,512]{1,0:T(8,128)(2,1)S(1)} %collective-permute-done.1.even_ref), channel_id=1, source_target_pairs={{0,1},{1,0},{2,3},{3,2},{4,5},{5,4},{6,7},{7,6},{8,9},{9,8},{10,11... | collective-permute-start | bytes 1572872 | tf_op jit(solution)/shard_map/ppermute | solution.py:34
  47.7 3.8 %collective-permute-done.16.odd_near_ref = bf16[512,512]{1,0:T(8,128)(2,1)} collective-permute-done((bf16[512,512]{1,0:T(8,128)(2,1)S(1)}, bf16[512,512]{1,0:T(8,128)(2,1)}, u32[]{:S(2)}, u32[]{:S(2)}) %collective-permute-start.16) | collective-permute-done | bytes 524320 | tf_op jit(solution)/shard_map/ppermute | solution.py:43
  51.5 1.9 %collective-permute-start.18 = (bf16[512,512]{1,0:T(8,128)(2,1)}, bf16[512,512]{1,0:T(8,128)(2,1)S(1)}, u32[]{:S(2)}, u32[]{:S(2)}) collective-permute-start(bf16[512,512]{1,0:T(8,128)(2,1)} %collective-permute-done.16.odd_near_ref), channel_id=1, source_target_pairs={{0,1},{1,0},{2,3},{3,2},{4,5},{5,4},{6,7},{7,6},{8,9},{9,8},{10,11... | collective-permute-start | bytes 1572872 | tf_op jit(solution)/shard_map/ppermute | solution.py:34
  53.4 0.0 collective-permute-done.17.even_near_ref
  53.4 2.4 %collective-permute-start.19 = (bf16[512,512]{1,0:T(8,128)(2,1)}, bf16[512,512]{1,0:T(8,128)(2,1)S(1)}, u32[]{:S(2)}, u32[]{:S(2)}) collective-permute-start(bf16[512,512]{1,0:T(8,128)(2,1)} %collective-permute-done.17.even_near_ref), channel_id=1, source_target_pairs={{0,1},{1,0},{2,3},{3,2},{4,5},{5,4},{6,7},{7,6},{8,9},{9,8},{10,11... | collective-permute-start | bytes 1572872 | tf_op jit(solution)/shard_map/ppermute | solution.py:34
  55.8 2.4 %shard_map.69 = (bf16[1024,512]{1,0:T(8,128)(2,1)S(1)}, f32[1024,1024]{1,0:T(8,128)S(1)}, f32[1024,128]{1,0:T(8,128)S(1)}) custom-call(bf16[512,512]{1,0:T(8,128)(2,1)S(1)} %collective-permute-done.odd_ref, bf16[512,512]{1,0:T(8,128)(2,1)S(1)} %collective-permute-done.1.even_ref, bf16[1024,512]{1,0:T(8,128)(2,1)S(1)} %get-tuple-element.35.rows_ref, ...), custom_call_target="tpu_custom_call" | custom-call | tf_op jit(solution)/shard_map/pallas_call | solution.py:367
  58.3 0.0 collective-permute-done.6.odd_far_ref
  58.3 0.0 collective-permute-done.7.even_far_ref
  58.3 4.4 %shard_map.70 = (bf16[1024,512]{1,0:T(8,128)(2,1)S(1)}, f32[1024,1024]{1,0:T(8,128)S(1)}, f32[8,1024]{1,0:T(8,128)S(1)}, f32[4,1024]{1,0:T(4,128)S(1)}, f32[4,10...) custom-call(s32[8]{0:T(128)S(1)} %compare_select_fusion.7.flags, ...), custom_call_target="tpu_custom_call" | custom-call | tf_op jit(solution)/shard_map/pallas_call | solution.py:367
  62.7 4.5 %collective-permute-start.8 = (f32[4,1024]{1,0:T(4,128)S(1)}, f32[4,1024]{1,0:T(4,128)S(1)}, u32[]{:S(2)}, u32[]{:S(2)}) collective-permute-start(f32[4,1024]{1,0:T(4,128)S(1)} %get-tuple-element.43), channel_id=1, source_target_pairs={{4,8},{12,16},{20,24},{28,32},{36,40},{44,48},{52,56},{60,64},{68,... | collective-permute-start | bytes 49160 | tf_op jit(solution)/shard_map/ppermute | solution.py:43
  67.2 1.9 %collective-permute-start.9 = (f32[4,1024]{1,0:T(4,128)S(1)}, f32[4,1024]{1,0:T(4,128)S(1)}, u32[]{:S(2)}, u32[]{:S(2)}) collective-permute-start(f32[4,1024]{1,0:T(4,128)S(1)} %get-tuple-element.44), channel_id=1, source_target_pairs={{0,4},{8,12},{16,20},{24,28},{32,36},{40,44},{48,52},{56,60},{64,6... | collective-permute-start | bytes 49160 | tf_op jit(solution)/shard_map/ppermute | solution.py:43
  69.2 8.5 %collective-permute-start.10 = (f32[1,1024]{1,0:T(1,128)S(1)}, f32[1,1024]{1,0:T(1,128)S(1)}, u32[]{:S(2)}, u32[]{:S(2)}) collective-permute-start(f32[1,1024]{1,0:T(1,128)S(1)} %get-tuple-element.45), channel_id=1, source_target_pairs={{8,16},{12,20},{24,32},{28,36},{40,48},{44,52},{56,64},{60,68},{72... | collective-permute-start | bytes 12296 | tf_op jit(solution)/shard_map/ppermute | solution.py:43
  77.7 3.6 %collective-permute-done.10.a_in = f32[1,1024]{1,0:T(1,128)S(1)} collective-permute-done((f32[1,1024]{1,0:T(1,128)S(1)}, f32[1,1024]{1,0:T(1,128)S(1)}, u32[]{:S(2)}, u32[]{:S(2)}) %collective-permute-start.10) | collective-permute-done | bytes 4128 | tf_op jit(solution)/shard_map/ppermute | solution.py:43
  81.3 1.9 %collective-permute-start.11 = (f32[1,1024]{1,0:T(1,128)S(1)}, f32[1,1024]{1,0:T(1,128)S(1)}, u32[]{:S(2)}, u32[]{:S(2)}) collective-permute-start(f32[1,1024]{1,0:T(1,128)S(1)} %get-tuple-element.46), channel_id=1, source_target_pairs={{0,8},{4,12},{16,24},{20,28},{32,40},{36,44},{48,56},{52,60},{64,7... | collective-permute-start | bytes 12296 | tf_op jit(solution)/shard_map/ppermute | solution.py:43
  83.2 4.5 %collective-permute-done.11.b_in = f32[1,1024]{1,0:T(1,128)S(1)} collective-permute-done((f32[1,1024]{1,0:T(1,128)S(1)}, f32[1,1024]{1,0:T(1,128)S(1)}, u32[]{:S(2)}, u32[]{:S(2)}) %collective-permute-start.11) | collective-permute-done | bytes 4128 | tf_op jit(solution)/shard_map/ppermute | solution.py:43
  87.7 0.0 collective-permute-done.8.odd_in
  87.7 0.0 collective-permute-done.9.even_in
  87.7 3.3 %shard_map.71 = (f32[1024,128]{1,0:T(8,128)S(1)}, f32[1,1024]{1,0:T(1,128)S(1)}, f32[8,1024]{1,0:T(8,128)S(1)}, f32[4,1024]{1,0:T(4,128)S(1)}, f32[4,1024]{1,0:T...) custom-call(s32[8]{0:T(128)S(1)} %compare_select_fusion.7.flags, f32[8,1024]{1,0:T(8,128)S(1)} %get-tuple-element.42.partial_in, ...), custom_call_target="tpu_custom_call" | custom-call | tf_op jit(solution)/shard_map/pallas_call | solution.py:367
  91.0 7.1 %collective-permute-start.12 = (f32[4,1024]{1,0:T(4,128)S(1)}, f32[4,1024]{1,0:T(4,128)S(1)}, u32[]{:S(2)}, u32[]{:S(2)}) collective-permute-start(f32[4,1024]{1,0:T(4,128)S(1)} %get-tuple-element.50), channel_id=1, source_target_pairs={{4,8},{12,16},{20,24},{28,32},{36,40},{44,48},{52,56},{60,64},{68,... | collective-permute-start | bytes 49160 | tf_op jit(solution)/shard_map/ppermute | solution.py:43
  98.1 1.9 %collective-permute-start.13 = (f32[4,1024]{1,0:T(4,128)S(1)}, f32[4,1024]{1,0:T(4,128)S(1)}, u32[]{:S(2)}, u32[]{:S(2)}) collective-permute-start(f32[4,1024]{1,0:T(4,128)S(1)} %get-tuple-element.51), channel_id=1, source_target_pairs={{0,4},{8,12},{16,20},{24,28},{32,36},{40,44},{48,52},{56,60},{64,6... | collective-permute-start | bytes 49160 | tf_op jit(solution)/shard_map/ppermute | solution.py:43
  100.0 6.0 %collective-permute-start.14 = (f32[1,1024]{1,0:T(1,128)S(1)}, f32[1,1024]{1,0:T(1,128)S(1)}, u32[]{:S(2)}, u32[]{:S(2)}) collective-permute-start(f32[1,1024]{1,0:T(1,128)S(1)} %get-tuple-element.52), channel_id=1, source_target_pairs={{8,16},{12,20},{24,32},{28,36},{40,48},{44,52},{56,64},{60,68},{72... | collective-permute-start | bytes 12296 | tf_op jit(solution)/shard_map/ppermute | solution.py:43
  106.0 0.0 collective-permute-done.18.odd_far_ref
  106.0 1.9 %collective-permute-start.15 = (f32[1,1024]{1,0:T(1,128)S(1)}, f32[1,1024]{1,0:T(1,128)S(1)}, u32[]{:S(2)}, u32[]{:S(2)}) collective-permute-start(f32[1,1024]{1,0:T(1,128)S(1)} %get-tuple-element.53), channel_id=1, source_target_pairs={{0,8},{4,12},{16,24},{20,28},{32,40},{36,44},{48,56},{52,60},{64,7... | collective-permute-start | bytes 12296 | tf_op jit(solution)/shard_map/ppermute | solution.py:43
  107.9 0.0 collective-permute-done.19.even_far_ref
  107.9 2.9 %shard_map.72 = (bf16[1024,512]{1,0:T(8,128)(2,1)S(1)}, bf16[1024,512]{1,0:T(8,128)(2,1)S(1)}, f32[256,3072]{1,0:T(8,128)S(1)}) custom-call(s32[8]{0:T(128)S(1)} %compare_select_fusion.7.flags, bf16[1024,512]{1,0:T(8,128)(2,1)S(1)} %get-tuple-element.56.columns_ref.own_columns_ref, bf16[1024,512]{1,0:T(8,128)(2,1)S(1)} %get-tuple-element.35.rows_ref, ...), custom_call_target="tpu_custom_call" | custom-call | tf_op jit(solution)/shard_map/pallas_call | solution.py:367
  110.8 1.3 %collective-permute-done.14.a_in = f32[1,1024]{1,0:T(1,128)S(1)} collective-permute-done((f32[1,1024]{1,0:T(1,128)S(1)}, f32[1,1024]{1,0:T(1,128)S(1)}, u32[]{:S(2)}, u32[]{:S(2)}) %collective-permute-start.14) | collective-permute-done | bytes 4128 | tf_op jit(solution)/shard_map/ppermute | solution.py:43
  112.1 0.3 collective-permute-done.15.b_in
  112.4 0.0 collective-permute-done.12.odd_in
  112.4 0.0 collective-permute-done.13.even_in
  112.4 3.5 %gradient_kernel.1 = (f32[256,512]{1,0:T(8,128)}, f32[256,512]{1,0:T(8,128)}) custom-call(s32[8]{0:T(128)S(1)} %compare_select_fusion.7.flags, f32[8,1024]{1,0:T(8,128)S(1)} %get-tuple-element.49.partial_in, f32[4,1024]{1,0:T(4,128)S(1)} %collective-permute-done.12.odd_in, f32[4,1024]{1,0:T(4,128)S(1)} %collective-permute-done.13.even_in, ...), custom_call_target="tpu_custom_call" | custom-call | tf_op jit(solution)/shard_map/gradient_kernel/pallas_call | solution.py:496
  (3 shorter events, 0.0 us)
Async XLA Ops:
  0.6 24.9 %collective-permute-start.2 = (bf16[256,512]{1,0:T(8,128)(2,1)}, bf16[256,512]{1,0:T(8,128)(2,1)S(1)}, u32[]{:S(2)}, u32[]{:S(2)}) collective-permute-start(bf16[256,512]{1,0:T(8,128)(2,1)} %own_ref.1), channel_id=1, source_target_pairs={{0,2},{2,0},{1,3},{3,1},{4,6},{6,4},{5,7},{7,5},{8,10},{10,8},{9,1... | collective-permute-start | bytes 786440 | tf_op jit(solution)/shard_map/ppermute | solution.py:34
  4.4 39.0 %collective-permute-start = (bf16[512,512]{1,0:T(8,128)(2,1)S(1)}, bf16[512,512]{1,0:T(8,128)(2,1)S(1)}, u32[]{:S(2)}, u32[]{:S(2)}) collective-permute-start(bf16[512,512]{1,0:T(8,128)(2,1)S(1)} %bitcast.12), channel_id=1, source_target_pairs={{4,8},{12,16},{20,24},{28,32},{36,40},{44,48},{52,56},{60,64},{68,... | collective-permute-start | bytes 1572872 | tf_op jit(solution)/shard_map/ppermute | solution.py:43
  18.4 25.0 %collective-permute-start.1 = (bf16[512,512]{1,0:T(8,128)(2,1)S(1)}, bf16[512,512]{1,0:T(8,128)(2,1)S(1)}, u32[]{:S(2)}, u32[]{:S(2)}) collective-permute-start(bf16[512,512]{1,0:T(8,128)(2,1)S(1)} %bitcast.13), channel_id=1, source_target_pairs={{0,4},{8,12},{16,20},{24,28},{32,36},{40,44},{48,52},{56,60},{64,6... | collective-permute-start | bytes 1572872 | tf_op jit(solution)/shard_map/ppermute | solution.py:43
  21.7 5.8 %collective-permute-start.4 = (f32[4,128]{1,0:T(4,128)S(1)}, f32[4,128]{1,0:T(4,128)S(1)}, u32[]{:S(2)}, u32[]{:S(2)}) collective-permute-start(f32[4,128]{1,0:T(4,128)S(1)} %get-tuple-element.63.small_ref), channel_id=1, source_target_pairs={{0,2},{2,0},{1,3},{3,1},{4,6},{6,4},{5,7},{7,5},{8,10},{10,8},{9,1... | collective-permute-start | bytes 6152 | tf_op jit(solution)/shard_map/ppermute | solution.py:34
  25.6 10.9 %collective-permute-start.3 = (bf16[512,512]{1,0:T(8,128)(2,1)S(1)}, bf16[512,512]{1,0:T(8,128)(2,1)S(1)}, u32[]{:S(2)}, u32[]{:S(2)}) collective-permute-start(bf16[512,512]{1,0:T(8,128)(2,1)S(1)} %constant_dynamic-update-slice_fusion), channel_id=1, source_target_pairs={{0,1},{1,0},{2,3},{3,2},{4,5},{5,4},{6,7},{7,6},{8,9},{9,8},{10,11... | collective-permute-start | bytes 1572872 | tf_op jit(solution)/shard_map/ppermute | solution.py:34
  27.5 6.9 %collective-permute-start.5 = (f32[2,4,128]{2,1,0:T(4,128)S(1)}, f32[2,4,128]{2,1,0:T(4,128)S(1)}, u32[]{:S(2)}, u32[]{:S(2)}) collective-permute-start(f32[2,4,128]{2,1,0:T(4,128)S(1)} %pad_maximum_fusion), channel_id=1, source_target_pairs={{0,1},{1,0},{2,3},{3,2},{4,5},{5,4},{6,7},{7,6},{8,9},{9,8},{10,11... | collective-permute-start | bytes 12296 | tf_op jit(solution)/shard_map/ppermute | solution.py:34
  29.9 21.6 %collective-permute-start.16 = (bf16[512,512]{1,0:T(8,128)(2,1)S(1)}, bf16[512,512]{1,0:T(8,128)(2,1)}, u32[]{:S(2)}, u32[]{:S(2)}) collective-permute-start(bf16[512,512]{1,0:T(8,128)(2,1)S(1)} %constant_dynamic-update-slice_fusion), channel_id=1, source_target_pairs={{4,8},{12,16},{20,24},{28,32},{36,40},{44,48},{52,56},{60,64},{68,... | collective-permute-start | bytes 1572872 | tf_op jit(solution)/shard_map/ppermute | solution.py:43
  34.5 18.9 %collective-permute-start.17 = (bf16[512,512]{1,0:T(8,128)(2,1)S(1)}, bf16[512,512]{1,0:T(8,128)(2,1)}, u32[]{:S(2)}, u32[]{:S(2)}) collective-permute-start(bf16[512,512]{1,0:T(8,128)(2,1)S(1)} %constant_dynamic-update-slice_fusion), channel_id=1, source_target_pairs={{0,4},{8,12},{16,20},{24,28},{32,36},{40,44},{48,52},{56,60},{64,6... | collective-permute-start | bytes 1572872 | tf_op jit(solution)/shard_map/ppermute | solution.py:43
  36.5 1.2 %copy-start = (bf16[1024,512]{1,0:T(8,128)(2,1)S(1)}, bf16[1024,512]{1,0:T(8,128)(2,1)}, u32[]{:S(2)}) copy-start(bf16[1024,512]{1,0:T(8,128)(2,1)} %control_ref.1) | copy-start | bytes 3145732
  37.7 0.9 copy-start.1
  38.7 1.0 copy-start.2
  43.4 14.9 %collective-permute-start.6 = (bf16[512,512]{1,0:T(8,128)(2,1)S(1)}, bf16[512,512]{1,0:T(8,128)(2,1)S(1)}, u32[]{:S(2)}, u32[]{:S(2)}) collective-permute-start(bf16[512,512]{1,0:T(8,128)(2,1)S(1)} %collective-permute-done.odd_ref), channel_id=1, source_target_pairs={{0,1},{1,0},{2,3},{3,2},{4,5},{5,4},{6,7},{7,6},{8,9},{9,8},{10,11... | collective-permute-start | bytes 1572872 | tf_op jit(solution)/shard_map/ppermute | solution.py:34
  45.3 13.0 %collective-permute-start.7 = (bf16[512,512]{1,0:T(8,128)(2,1)S(1)}, bf16[512,512]{1,0:T(8,128)(2,1)S(1)}, u32[]{:S(2)}, u32[]{:S(2)}) collective-permute-start(bf16[512,512]{1,0:T(8,128)(2,1)S(1)} %collective-permute-done.1.even_ref), channel_id=1, source_target_pairs={{0,1},{1,0},{2,3},{3,2},{4,5},{5,4},{6,7},{7,6},{8,9},{9,8},{10,11... | collective-permute-start | bytes 1572872 | tf_op jit(solution)/shard_map/ppermute | solution.py:34
  51.5 54.5 %collective-permute-start.18 = (bf16[512,512]{1,0:T(8,128)(2,1)}, bf16[512,512]{1,0:T(8,128)(2,1)S(1)}, u32[]{:S(2)}, u32[]{:S(2)}) collective-permute-start(bf16[512,512]{1,0:T(8,128)(2,1)} %collective-permute-done.16.odd_near_ref), channel_id=1, source_target_pairs={{0,1},{1,0},{2,3},{3,2},{4,5},{5,4},{6,7},{7,6},{8,9},{9,8},{10,11... | collective-permute-start | bytes 1572872 | tf_op jit(solution)/shard_map/ppermute | solution.py:34
  53.4 54.5 %collective-permute-start.19 = (bf16[512,512]{1,0:T(8,128)(2,1)}, bf16[512,512]{1,0:T(8,128)(2,1)S(1)}, u32[]{:S(2)}, u32[]{:S(2)}) collective-permute-start(bf16[512,512]{1,0:T(8,128)(2,1)} %collective-permute-done.17.even_near_ref), channel_id=1, source_target_pairs={{0,1},{1,0},{2,3},{3,2},{4,5},{5,4},{6,7},{7,6},{8,9},{9,8},{10,11... | collective-permute-start | bytes 1572872 | tf_op jit(solution)/shard_map/ppermute | solution.py:34
  62.7 25.0 %collective-permute-start.8 = (f32[4,1024]{1,0:T(4,128)S(1)}, f32[4,1024]{1,0:T(4,128)S(1)}, u32[]{:S(2)}, u32[]{:S(2)}) collective-permute-start(f32[4,1024]{1,0:T(4,128)S(1)} %get-tuple-element.43), channel_id=1, source_target_pairs={{4,8},{12,16},{20,24},{28,32},{36,40},{44,48},{52,56},{60,64},{68,... | collective-permute-start | bytes 49160 | tf_op jit(solution)/shard_map/ppermute | solution.py:43
  67.2 20.4 %collective-permute-start.9 = (f32[4,1024]{1,0:T(4,128)S(1)}, f32[4,1024]{1,0:T(4,128)S(1)}, u32[]{:S(2)}, u32[]{:S(2)}) collective-permute-start(f32[4,1024]{1,0:T(4,128)S(1)} %get-tuple-element.44), channel_id=1, source_target_pairs={{0,4},{8,12},{16,20},{24,28},{32,36},{40,44},{48,52},{56,60},{64,6... | collective-permute-start | bytes 49160 | tf_op jit(solution)/shard_map/ppermute | solution.py:43
  69.2 12.1 %collective-permute-start.10 = (f32[1,1024]{1,0:T(1,128)S(1)}, f32[1,1024]{1,0:T(1,128)S(1)}, u32[]{:S(2)}, u32[]{:S(2)}) collective-permute-start(f32[1,1024]{1,0:T(1,128)S(1)} %get-tuple-element.45), channel_id=1, source_target_pairs={{8,16},{12,20},{24,32},{28,36},{40,48},{44,52},{56,64},{60,68},{72... | collective-permute-start | bytes 12296 | tf_op jit(solution)/shard_map/ppermute | solution.py:43
  81.3 6.4 %collective-permute-start.11 = (f32[1,1024]{1,0:T(1,128)S(1)}, f32[1,1024]{1,0:T(1,128)S(1)}, u32[]{:S(2)}, u32[]{:S(2)}) collective-permute-start(f32[1,1024]{1,0:T(1,128)S(1)} %get-tuple-element.46), channel_id=1, source_target_pairs={{0,8},{4,12},{16,24},{20,28},{32,40},{36,44},{48,56},{52,60},{64,7... | collective-permute-start | bytes 12296 | tf_op jit(solution)/shard_map/ppermute | solution.py:43
  91.0 21.4 %collective-permute-start.12 = (f32[4,1024]{1,0:T(4,128)S(1)}, f32[4,1024]{1,0:T(4,128)S(1)}, u32[]{:S(2)}, u32[]{:S(2)}) collective-permute-start(f32[4,1024]{1,0:T(4,128)S(1)} %get-tuple-element.50), channel_id=1, source_target_pairs={{4,8},{12,16},{20,24},{28,32},{36,40},{44,48},{52,56},{60,64},{68,... | collective-permute-start | bytes 49160 | tf_op jit(solution)/shard_map/ppermute | solution.py:43
  98.1 14.3 %collective-permute-start.13 = (f32[4,1024]{1,0:T(4,128)S(1)}, f32[4,1024]{1,0:T(4,128)S(1)}, u32[]{:S(2)}, u32[]{:S(2)}) collective-permute-start(f32[4,1024]{1,0:T(4,128)S(1)} %get-tuple-element.51), channel_id=1, source_target_pairs={{0,4},{8,12},{16,20},{24,28},{32,36},{40,44},{48,52},{56,60},{64,6... | collective-permute-start | bytes 49160 | tf_op jit(solution)/shard_map/ppermute | solution.py:43
  100.0 12.1 %collective-permute-start.14 = (f32[1,1024]{1,0:T(1,128)S(1)}, f32[1,1024]{1,0:T(1,128)S(1)}, u32[]{:S(2)}, u32[]{:S(2)}) collective-permute-start(f32[1,1024]{1,0:T(1,128)S(1)} %get-tuple-element.52), channel_id=1, source_target_pairs={{8,16},{12,20},{24,32},{28,36},{40,48},{44,52},{56,64},{60,68},{72... | collective-permute-start | bytes 12296 | tf_op jit(solution)/shard_map/ppermute | solution.py:43
  106.0 6.4 %collective-permute-start.15 = (f32[1,1024]{1,0:T(1,128)S(1)}, f32[1,1024]{1,0:T(1,128)S(1)}, u32[]{:S(2)}, u32[]{:S(2)}) collective-permute-start(f32[1,1024]{1,0:T(1,128)S(1)} %get-tuple-element.53), channel_id=1, source_target_pairs={{0,8},{4,12},{16,24},{20,28},{32,40},{36,44},{48,56},{52,60},{64,7... | collective-permute-start | bytes 12296 | tf_op jit(solution)/shard_map/ppermute | solution.py:43

commit v3 on v2

v3 whole, which is shorter than its diff:
```python
import jax
import jax.numpy as jnp
from jax import lax
from jax.experimental import pallas as pl
from jax.experimental.pallas import tpu as pltpu
from jax.sharding import PartitionSpec as P


SMOOTHING_TEMP = 0.05
EPSILON = 1e-06

SWAP_Y = [(0, 2), (2, 0), (1, 3), (3, 1)]
SWAP_CORE = [(0, 1), (1, 0), (2, 3), (3, 2)]

LANES = 128
QUARTER = 256
HALF = 512
SLAB = 1024
WIDTH = 512
SCALE = 1.0 / (WIDTH * SMOOTHING_TEMP)

F32 = jnp.float32
BF16 = jnp.bfloat16

INFO = 16
MESSAGE = QUARTER + INFO
JOINED = 2 * MESSAGE

NARROW, ODD, A_EVEN, HAS_ODD = range(4)


def both_ways(pairs, count):
    kept = [(a, b) for a, b in pairs if b < count]
    return kept + [(b, a) for a, b in kept]


def narrow_swap(block, pairs):
    return lax.ppermute(block, "narrow", pairs)


def exchange(block, hops, crossing):
    count = lax.axis_size("wide")
    first = hops if crossing else 0
    pairs = [
        (base + i, base + i + hops) for base in range(first, count, 2 * hops) for i in range(hops)
    ]
    return lax.ppermute(block, "wide", both_ways(pairs, count))


def normalize(features):
    values = features.astype(F32)
    total = jnp.sum(values * values, axis=1, keepdims=True)
    return (values * lax.rsqrt(total * (1.0 / WIDTH) + EPSILON)).astype(BF16)


def nt_dot(a, b):
    return lax.dot_general(a, b, (((1,), (1,)), ((), ())), preferred_element_type=F32)


def identity():
    return lax.broadcasted_iota(jnp.int32, (LANES, LANES), 0) == lax.broadcasted_iota(
        jnp.int32, (LANES, LANES), 1
    )


def to_column(row):
    return jnp.sum(jnp.where(identity(), row, 0.0), axis=1, keepdims=True)


def to_row(column):
    return jnp.sum(jnp.where(identity(), column, 0.0), axis=0, keepdims=True)


def lane_tiles(values):
    total = values[:, :LANES]
    for i in range(1, values.shape[1] // LANES):
        total = total + values[:, i * LANES : (i + 1) * LANES]
    return total


def sublane_tiles(values):
    rows, columns = values.shape
    return jnp.sum(values.reshape(rows // 8, 8, columns), axis=0)


def block_kernel(rows_ref, columns, mask_ref, i, lanes):
    inner = nt_dot(rows_ref[pl.ds(pl.multiple_of(i * QUARTER, QUARTER), QUARTER), :], columns)
    values = jnp.exp(inner * SCALE)
    top = values[:LANES] * mask_ref[pl.ds(2 * i, 1), lanes]
    bottom = values[LANES:] * mask_ref[pl.ds(2 * i + 1, 1), lanes]
    return top, bottom


def fill_kernel(rows_ref, columns_ref, mask_ref, lanes, kernel_ref, sums_ref, before_ref):
    def step(i, carry):
        blocks = block_kernel(rows_ref, columns_ref[...], mask_ref, i, lanes)
        for j, block in enumerate(blocks):
            at = pl.ds(pl.multiple_of(i * QUARTER + j * LANES, LANES), LANES)
            kernel_ref[at, :] = block
            sums = lane_tiles(block)
            if before_ref is not None:
                sums = sums + before_ref[at, :]
            sums_ref[at, :] = sums
        return carry

    lax.fori_loop(0, 4, step, 0)


def pack_kernel(treated_ref, weight_ref, band_ref, message_ref, info_ref):
    message_ref[0:QUARTER, :] = normalize(treated_ref[...])
    info_ref[...] = jnp.zeros_like(info_ref)
    weight = weight_ref[...]
    for i in range(3):
        part = weight.astype(BF16).astype(F32)
        info_ref[0:2, i * LANES : (i + 1) * LANES] = part
        weight = weight - part
    info_ref[0:2, 3 * LANES : 3 * LANES + 24] = band_ref[...].astype(F32)
    message_ref[QUARTER:MESSAGE, :] = info_ref[...].astype(BF16)


def join_kernel(own_ref, y_ref, joined_ref):
    joined_ref[0:QUARTER, :] = own_ref[0:QUARTER, :]
    joined_ref[QUARTER:HALF, :] = y_ref[0:QUARTER, :]
    joined_ref[HALF : HALF + INFO, :] = own_ref[QUARTER:MESSAGE, :]
    joined_ref[HALF + INFO : JOINED, :] = y_ref[QUARTER:MESSAGE, :]


def columns_kernel(control_ref, columns_ref):
    columns_ref[...] = normalize(control_ref[...])


def prepare_kernel(
    flags, joined_ref, far_ref, columns_ref, rows_ref, kernel_ref, sums_ref, mask_ref, weight_ref,
    pair_ref, band_ref,
):
    n, odd = flags[NARROW], flags[ODD]
    rows_ref[0:HALF, :] = joined_ref[0:HALF, :]
    rows_ref[HALF:SLAB, :] = far_ref[0:HALF, :]

    band_ref[...] = jnp.zeros_like(band_ref)
    for i, (source, first) in enumerate(
        ((joined_ref, HALF), (joined_ref, HALF + INFO), (far_ref, HALF), (far_ref, HALF + INFO))
    ):
        info = source[first : first + INFO, :].astype(F32)
        band_ref[2 * i : 2 * i + 2, :] = info[0:2, 3 * LANES :]
        weights = info[:, :LANES] + info[:, LANES : 2 * LANES] + info[:, 2 * LANES : 3 * LANES]
        for j in range(2):
            at = slice((2 * i + j) * LANES, (2 * i + j + 1) * LANES)
            weight_ref[at, :] = jnp.broadcast_to(to_column(weights[j : j + 1]), (LANES, LANES))
    band = band_ref[...].astype(BF16)
    odd_base = odd * 16
    even_base = 16 - odd * 16
    lane = lax.broadcasted_iota(jnp.int32, (1, 3 * SLAB), 1)
    segment = lane // SLAB
    wanted = (lane % SLAB) // LANES + jnp.where(
        segment == 0, 8, jnp.where(segment == 1, odd_base, even_base)
    )
    one_hot = lax.broadcasted_iota(jnp.int32, (LANES, 3 * SLAB), 0) == wanted
    mask_ref[...] = jnp.dot(
        band[:16], jnp.where(one_hot, 1.0, 0.0).astype(BF16), preferred_element_type=F32
    )[:8]
    place = lax.broadcasted_iota(jnp.int32, (16, LANES), 0)
    base = jnp.where(place < 2, 8, jnp.where(place < 4, odd_base, even_base))
    chosen = base + 2 * n + place % 2
    select = jnp.where(
        lax.broadcasted_iota(jnp.int32, (16, LANES), 1) == chosen, 1.0, 0.0
    ).astype(BF16)
    by_block = nt_dot(select, band).astype(BF16)
    spread = (
        lax.broadcasted_iota(jnp.int32, (LANES, SLAB), 0)
        == lax.broadcasted_iota(jnp.int32, (LANES, SLAB), 1) // LANES
    )
    pair_ref[...] = jnp.dot(
        by_block, jnp.where(spread, 1.0, 0.0).astype(BF16), preferred_element_type=F32
    )[:8]

    fill_kernel(rows_ref, columns_ref, mask_ref, slice(0, SLAB), kernel_ref, sums_ref, None)


def finish_messages(
    flags, sums, first, second, partial_ref, odd_ref, even_ref, a_ref, b_ref
):
    own, odd, even = (jnp.sum(part, axis=0, keepdims=True) for part in sums)
    partial_ref[...] = jnp.zeros_like(partial_ref)
    partial_ref[0:1, :] = own
    partial_ref[1:2, :] = odd
    partial_ref[2:3, :] = even
    odd_ref[0:1, :] = own
    odd_ref[1:2, :] = odd
    odd_ref[2:4, :] = first
    even_ref[0:1, :] = own
    even_ref[1:2, :] = even
    even_ref[2:4, :] = second
    a_even = flags[A_EVEN] > 0
    a_ref[...] = jnp.where(a_even, even, odd)
    b_ref[...] = jnp.where(a_even, odd, even)


def sides_kernel(
    flags, odd_raw, even_raw, rows_ref, mask_ref, own_kernel_ref, own_sums_ref, weight_ref,
    pair_ref, odd_columns_ref, even_columns_ref, odd_kernel_ref, even_kernel_ref, partial_ref,
    odd_ref, even_ref, a_ref, b_ref, sums_ref,
):
    odd_columns_ref[...] = normalize(odd_raw[...])
    even_columns_ref[...] = normalize(even_raw[...])
    fill_kernel(
        rows_ref, odd_columns_ref, mask_ref, slice(SLAB, 2 * SLAB), odd_kernel_ref, sums_ref,
        own_sums_ref,
    )

    def step(i, carry):
        own, odd, even = carry
        blocks = block_kernel(
            rows_ref, even_columns_ref[...], mask_ref, i, slice(2 * SLAB, 3 * SLAB)
        )
        for j, block in enumerate(blocks):
            at = pl.ds(pl.multiple_of(i * QUARTER + j * LANES, LANES), LANES)
            even_kernel_ref[at, :] = block
            sums = lane_tiles(block) + sums_ref[at, :]
            scale = weight_ref[at, 0:1] / jnp.sum(sums, axis=1, keepdims=True)
            own = own + sublane_tiles(own_kernel_ref[at, :] * scale)
            odd = odd + sublane_tiles(odd_kernel_ref[at, :] * scale)
            even = even + sublane_tiles(block * scale)
        return own, odd, even

    zero = jnp.zeros((8, SLAB), F32)
    sums = lax.fori_loop(0, 4, step, (zero, zero, zero))
    finish_messages(
        flags, sums, pair_ref[2:4, :], pair_ref[4:6, :], partial_ref, odd_ref, even_ref, a_ref,
        b_ref,
    )


def column_scales(flags, partial_ref, odd_ref, even_ref, a_ref, b_ref, weights):
    a_even = flags[A_EVEN] > 0
    two_odd = jnp.where(a_even, b_ref[...], a_ref[...])
    two_even = jnp.where(a_even, a_ref[...], b_ref[...])
    own = partial_ref[0:1, :] + odd_ref[1:2, :] + even_ref[1:2, :]
    odd = partial_ref[1:2, :] + odd_ref[0:1, :] + two_odd
    even = partial_ref[2:3, :] + even_ref[0:1, :] + two_even
    has_odd = flags[HAS_ODD] > 0
    own_weight, odd_weight, even_weight = (ref[...] for ref in weights)
    odd = jnp.where(has_odd, odd_weight / jnp.where(has_odd, odd, 1.0), 0.0)
    return own_weight / own, odd, even_weight / even


def sweep_kernel(
    flags, partial_in, odd_in, even_in, a_in, b_in, own_weight, odd_weight, even_weight,
    own_kernel_ref, odd_kernel_ref, even_kernel_ref, weight_ref, odd_joined, even_joined, row_ref,
    lane_ref, pair_ref, partial_ref, odd_ref, even_ref, a_ref, b_ref, flat_ref,
):
    pair_ref[0:HALF, :] = odd_joined[0:HALF, :]
    pair_ref[HALF:SLAB, :] = even_joined[0:HALF, :]
    scales = column_scales(
        flags, partial_in, odd_in, even_in, a_in, b_in, (own_weight, odd_weight, even_weight)
    )
    kernels = (own_kernel_ref, odd_kernel_ref, even_kernel_ref)

    def step(i, carry):
        at = pl.ds(pl.multiple_of(i * LANES, LANES), LANES)
        total = jnp.zeros((LANES, LANES), F32)
        for kernel_ref, scale in zip(kernels, scales, strict=True):
            total = total + lane_tiles(kernel_ref[at, :] * scale)
        row_scale = weight_ref[at, 0:1] / jnp.sum(total, axis=1, keepdims=True)
        row_ref[at, :] = jnp.broadcast_to(row_scale, (LANES, LANES))
        flat_ref[pl.ds(i, 1), :] = to_row(row_scale)
        return tuple(
            sums + sublane_tiles(kernel_ref[at, :] * row_scale)
            for kernel_ref, sums in zip(kernels, carry, strict=True)
        )

    zero = jnp.zeros((8, SLAB), F32)
    sums = lax.fori_loop(0, 8, step, (zero, zero, zero))
    for i in range(8):
        lane_ref[0:1, i * LANES : (i + 1) * LANES] = flat_ref[i : i + 1, :]
    flat = jnp.broadcast_to(lane_ref[...], (2, SLAB))
    finish_messages(flags, sums, flat, flat, partial_ref, odd_ref, even_ref, a_ref, b_ref)


def transposed_kernel(
    flags, columns_ref, rows_ref, near_ref, far_ref, pair_ref, odd_in, even_in, odd_rows_ref,
    even_rows_ref, kernel_ref,
):
    own = columns_ref[pl.ds(pl.multiple_of(flags[NARROW] * QUARTER, QUARTER), QUARTER), :]
    odd_rows_ref[0:HALF, :] = near_ref[0:HALF, :]
    odd_rows_ref[HALF:SLAB, :] = far_ref[0:HALF, :]
    even_rows_ref[0:HALF, :] = near_ref[HALF:SLAB, :]
    even_rows_ref[HALF:SLAB, :] = far_ref[HALF:SLAB, :]
    for i, (rows, top, bottom) in enumerate(
        (
            (rows_ref, pair_ref[0:1, :], pair_ref[1:2, :]),
            (odd_rows_ref, odd_in[2:3, :], odd_in[3:4, :]),
            (even_rows_ref, even_in[2:3, :], even_in[3:4, :]),
        )
    ):
        values = jnp.exp(nt_dot(own, rows[...]) * SCALE)
        lanes = slice(i * SLAB, (i + 1) * SLAB)
        kernel_ref[0:LANES, lanes] = values[:LANES] * top
        kernel_ref[LANES:QUARTER, lanes] = values[LANES:] * bottom


def gradient_kernel(
    flags, partial_in, odd_in, even_in, a_in, b_in, own_weight, odd_weight, even_weight, row_ref,
    lane_ref, own_kernel_ref, odd_kernel_ref, even_kernel_ref, own_columns_ref, odd_columns_ref,
    even_columns_ref, rows_ref, odd_rows_ref, even_rows_ref, transposed_ref, treated_out,
    control_out,
):
    scales = column_scales(
        flags, partial_in, odd_in, even_in, a_in, b_in, (own_weight, odd_weight, even_weight)
    )
    row_scale = row_ref[:, 0:1]
    mass = jnp.zeros((QUARTER, LANES), F32)
    pulled = jnp.zeros((QUARTER, WIDTH), F32)
    for kernel_ref, scale, columns_ref in zip(
        (own_kernel_ref, odd_kernel_ref, even_kernel_ref),
        scales,
        (own_columns_ref, odd_columns_ref, even_columns_ref),
        strict=True,
    ):
        transport = row_scale * kernel_ref[...] * scale
        mass = mass + lane_tiles(transport)
        pulled = pulled + jnp.dot(
            transport.astype(BF16), columns_ref[...], preferred_element_type=F32
        )
    mass = jnp.sum(mass, axis=1, keepdims=True)
    treated_out[...] = mass * rows_ref[0:QUARTER, :].astype(F32) - pulled

    n = flags[NARROW]

    def own_quarter(row):
        found = row[:, :QUARTER]
        for i in range(1, 4):
            found = jnp.where(n == i, row[:, i * QUARTER : (i + 1) * QUARTER], found)
        return found

    def upright(row):
        return jnp.concatenate([to_column(row[:, :LANES]), to_column(row[:, LANES:])], axis=0)

    own_scale = upright(own_quarter(scales[0]))
    own_mass = upright(own_quarter(own_weight[...]))
    pushed = jnp.zeros((QUARTER, WIDTH), F32)
    for i, (scale, rows) in enumerate(
        ((lane_ref[...], rows_ref), (odd_in[2:3, :], odd_rows_ref), (even_in[2:3, :], even_rows_ref))
    ):
        transport = scale * transposed_ref[:, i * SLAB : (i + 1) * SLAB] * own_scale
        pushed = pushed + jnp.dot(transport.astype(BF16), rows[...], preferred_element_type=F32)
    at = pl.ds(pl.multiple_of(n * QUARTER, QUARTER), QUARTER)
    control_out[...] = own_mass * own_columns_ref[at, :].astype(F32) - pushed


VMEM = pl.BlockSpec(memory_space=pltpu.VMEM)
SMEM = pl.BlockSpec(memory_space=pltpu.SMEM)


def call(body, specs, outs, operands, scratch=(), limit=16, out_specs=None):
    return pl.pallas_call(
        body,
        out_shape=tuple(jax.ShapeDtypeStruct(shape, dtype) for shape, dtype in outs),
        in_specs=specs,
        out_specs=out_specs or tuple(VMEM for _ in outs),
        scratch_shapes=list(scratch),
        compiler_params=pltpu.CompilerParams(vmem_limit_bytes=limit << 20),
    )(*operands)


MESSAGES = [((4, SLAB), F32), ((4, SLAB), F32), ((1, SLAB), F32), ((1, SLAB), F32)]


def trade(messages):
    odd, even, a, b = messages
    return (
        exchange(odd, 1, True),
        exchange(even, 1, False),
        exchange(a, 2, True),
        exchange(b, 2, False),
    )


def step(treated, control, treated_weight, control_weight, band):
    wide_index = lax.axis_index("wide")
    n = lax.axis_index("narrow")
    wide_count = lax.axis_size("wide")
    odd = wide_index % 2
    toward_odd = wide_index + 2 * odd - 1
    toward_even = wide_index + 1 - 2 * odd
    values = (
        n,
        odd,
        jnp.logical_xor(wide_index % 4 >= 2, odd == 1).astype(jnp.int32),
        ((toward_odd >= 0) & (toward_odd < wide_count)).astype(jnp.int32),
    )
    place = lax.iota(jnp.int32, 8)
    flags = jnp.zeros((8,), jnp.int32)
    for i, value in enumerate(values):
        flags = jnp.where(place == i, value, flags)
    weights = [
        lax.dynamic_slice_in_dim(control_weight, jnp.maximum(at, 0) * SLAB, SLAB).reshape(1, SLAB)
        for at in (wide_index, toward_odd, toward_even)
    ]

    odd_control = exchange(control, 1, True)
    even_control = exchange(control, 1, False)
    (own_columns,) = call(columns_kernel, [VMEM], [((SLAB, WIDTH), BF16)], [control])

    (message,) = call(
        pack_kernel,
        [VMEM] * 3,
        [((MESSAGE, WIDTH), BF16)],
        [treated, treated_weight.reshape(2, LANES), band],
        [pltpu.VMEM((INFO, WIDTH), F32)],
    )
    message_y = narrow_swap(message, SWAP_Y)
    (joined,) = call(join_kernel, [VMEM] * 2, [((JOINED, WIDTH), BF16)], [message, message_y])
    joined_far = narrow_swap(joined, SWAP_CORE)
    odd_joined = exchange(joined, 1, True)
    even_joined = exchange(joined, 1, False)

    rows, own_kernel, sums, mask, weight, pairs = call(
        prepare_kernel,
        [SMEM] + [VMEM] * 3,
        [
            ((SLAB, WIDTH), BF16),
            ((SLAB, SLAB), F32),
            ((SLAB, LANES), F32),
            ((8, 3 * SLAB), F32),
            ((SLAB, LANES), F32),
            ((8, SLAB), F32),
        ],
        [flags, joined, joined_far, own_columns],
        [pltpu.VMEM((LANES, LANES), F32)],
    )
    odd_columns, even_columns, odd_kernel, even_kernel, partial, *messages = call(
        sides_kernel,
        [SMEM] + [VMEM] * 8,
        [
            ((SLAB, WIDTH), BF16),
            ((SLAB, WIDTH), BF16),
            ((SLAB, SLAB), F32),
            ((SLAB, SLAB), F32),
            ((8, SLAB), F32),
            *MESSAGES,
        ],
        [flags, odd_control, even_control, rows, mask, own_kernel, sums, weight, pairs],
        [pltpu.VMEM((SLAB, LANES), F32)],
    )
    first = trade(messages)

    row_scale, lane_scale, near_rows, partial, *messages = call(
        sweep_kernel,
        [SMEM] + [VMEM] * 14,
        [((SLAB, LANES), F32), ((1, SLAB), F32), ((SLAB, WIDTH), BF16), ((8, SLAB), F32), *MESSAGES],
        [
            flags, partial, *first, *weights, own_kernel, odd_kernel, even_kernel, weight,
            odd_joined, even_joined,
        ],
        [pltpu.VMEM((8, LANES), F32)],
    )
    second = trade(messages)
    far_rows = narrow_swap(near_rows, SWAP_CORE)

    odd_rows, even_rows, transposed = call(
        transposed_kernel,
        [SMEM] + [VMEM] * 7,
        [((SLAB, WIDTH), BF16), ((SLAB, WIDTH), BF16), ((QUARTER, 3 * SLAB), F32)],
        [flags, own_columns, rows, near_rows, far_rows, pairs, first[0], first[1]],
    )

    top = pl.BlockSpec((QUARTER, SLAB), lambda i: (0, 0))
    whole = lambda *shape: pl.BlockSpec(shape, lambda i: (0,) * len(shape))
    return pl.pallas_call(
        gradient_kernel,
        grid=(1,),
        out_shape=(jax.ShapeDtypeStruct((QUARTER, WIDTH), F32),) * 2,
        in_specs=[
            SMEM, whole(8, SLAB), whole(4, SLAB), whole(4, SLAB), whole(1, SLAB), whole(1, SLAB),
            whole(1, SLAB), whole(1, SLAB), whole(1, SLAB),
            pl.BlockSpec((QUARTER, LANES), lambda i: (0, 0)), whole(1, SLAB), top, top, top,
            *[whole(SLAB, WIDTH)] * 6, whole(QUARTER, 3 * SLAB),
        ],
        out_specs=(whole(QUARTER, WIDTH),) * 2,
        compiler_params=pltpu.CompilerParams(vmem_limit_bytes=16 << 20),
        name="gradient_kernel",
    )(
        flags, partial, *second, *weights, row_scale, lane_scale, own_kernel, odd_kernel,
        even_kernel, own_columns, odd_columns, even_columns, rows, odd_rows, even_rows, transposed,
    )


def solution(mesh):
    return jax.shard_map(
        step,
        mesh=mesh,
        in_specs=(
            P(("wide", "narrow"), None),
            P("wide", None),
            P(("wide", "narrow")),
            P(),
            P(("wide", "narrow"), None),
        ),
        out_specs=(P(("wide", "narrow"), None), P(("wide", "narrow"), None)),
        check_vma=False,
    )
```

time: 117 us -> 115 us (0.983)
  the two profiles are of different devices: /device:TPU:24 before, /device:TPU:150 now
where the time goes in v3:
time: 115 us; the launch traced here: 114 us
  starting transfers between devices  79.2 us (69%)
  Pallas kernels  20.4 us (18%)
  waiting for transfers between devices  9.69 us (8%)
  local copies, waits for them, and re-layouts  4.25 us (4%)
    ppermute x12, starting transfers between devices, exchange(): return lax.ppermute(block, 'wide', both_ways(pairs, count))  72.2 us
    pallas_call x7, Pallas kernels, call(): pl.pallas_call(body, out_shape=tuple((jax.ShapeDtypeStruct(shape, dtype)...  16.9 us
    ppermute x3, starting transfers between devices, narrow_swap(): return lax.ppermute(block, 'narrow', pairs)  7.03 us
    ppermute x3, waiting for transfers between devices, narrow_swap(): return lax.ppermute(block, 'narrow', pairs)  6.54 us
    unnamed x8, local copies, waits for them, and re-layouts  3.52 us
    pallas_call x1, Pallas kernels, step(): pl.pallas_call(gradient_kernel, grid=(1,), out_shape=(jax.ShapeDtypeStruc...  3.48 us
    ppermute x12, waiting for transfers between devices, exchange(): return lax.ppermute(block, 'wide', both_ways(pairs, count))  3.15 us
  transfers between devices with their start and end apart: 15, of which 3 were waited for; matrix products, arithmetic and copies ran while one was open for 1% of the time, Pallas kernels for 11%

profile of v3, /device:TPU:150, one launch (start us, length us, event | category | flops | bytes accessed | tf_op | source)
XLA Modules:
  0.0 114.5 jit_solution(17168832648534114967)
XLA Ops:
  0.6 2.0 %collective-permute-start = (bf16[1024,512]{1,0:T(8,128)(2,1)}, bf16[1024,512]{1,0:T(8,128)(2,1)S(1)}, u32[]{:S(2)}, u32[]{:S(2)}) collective-permute-start(bf16[1024,512]{1,0:T(8,128)(2,1)} %control_ref.1), channel_id=1, source_target_pairs={{4,8},{12,16},{20,24},{28,32},{36,40},{44,48},{52,56},{60,64},{68,... | collective-permute-start | bytes 3145736 | tf_op jit(solution)/shard_map/ppermute | solution.py:47
  2.7 5.6 %collective-permute-start.1 = (bf16[1024,512]{1,0:T(8,128)(2,1)}, bf16[1024,512]{1,0:T(8,128)(2,1)}, u32[]{:S(2)}, u32[]{:S(2)}) collective-permute-start(bf16[1024,512]{1,0:T(8,128)(2,1)} %control_ref.1), channel_id=1, source_target_pairs={{0,4},{8,12},{16,20},{24,28},{32,36},{40,44},{48,52},{56,60},{64,6... | collective-permute-start | bytes 3145736 | tf_op jit(solution)/shard_map/ppermute | solution.py:47
  8.3 0.0 copy-start.1
  8.3 0.9 copy-done.1
  9.3 0.0 copy-start.2
  9.3 0.7 copy-done.2
  9.9 0.0 copy-start.3
  9.9 0.7 copy-done.3
  10.6 0.1 shard_map.68.own_ref
  10.8 3.2 %collective-permute-start.2 = (bf16[272,512]{1,0:T(8,128)(2,1)S(1)}, bf16[272,512]{1,0:T(8,128)(2,1)S(1)}, u32[]{:S(2)}, u32[]{:S(2)}) collective-permute-start(bf16[272,512]{1,0:T(8,128)(2,1)S(1)} %shard_map.68.own_ref), channel_id=1, source_target_pairs={{0,2},{2,0},{1,3},{3,1},{4,6},{6,4},{5,7},{7,5},{8,10},{10,8},{9,1... | collective-permute-start | bytes 835592 | tf_op jit(solution)/shard_map/ppermute | solution.py:38
  14.0 6.5 %collective-permute-done.2.y_ref = bf16[272,512]{1,0:T(8,128)(2,1)S(1)} collective-permute-done((bf16[272,512]{1,0:T(8,128)(2,1)S(1)}, bf16[272,512]{1,0:T(8,128)(2,1)S(1)}, u32[]{:S(2)}, u32[]{:S(2)}) %collective-permute-start.2) | collective-permute-done | bytes 278560 | tf_op jit(solution)/shard_map/ppermute | solution.py:38
  20.5 1.9 %collective-permute-start.3 = (bf16[544,512]{1,0:T(8,128)(2,1)S(1)}, bf16[544,512]{1,0:T(8,128)(2,1)S(1)}, u32[]{:S(2)}, u32[]{:S(2)}) collective-permute-start(bf16[544,512]{1,0:T(8,128)(2,1)S(1)} %shard_map.69.joined_ref), channel_id=1, source_target_pairs={{0,1},{1,0},{2,3},{3,2},{4,5},{5,4},{6,7},{7,6},{8,9},{9,8},{10,11... | collective-permute-start | bytes 1671176 | tf_op jit(solution)/shard_map/ppermute | solution.py:38
  22.5 2.2 %collective-permute-start.9 = (bf16[544,512]{1,0:T(8,128)(2,1)S(1)}, bf16[544,512]{1,0:T(8,128)(2,1)}, u32[]{:S(2)}, u32[]{:S(2)}) collective-permute-start(bf16[544,512]{1,0:T(8,128)(2,1)S(1)} %shard_map.69.joined_ref), channel_id=1, source_target_pairs={{0,4},{8,12},{16,20},{24,28},{32,36},{40,44},{48,52},{56,60},{64,6... | collective-permute-start | bytes 1671176 | tf_op jit(solution)/shard_map/ppermute | solution.py:47
  24.7 3.0 %collective-permute-start.8 = (bf16[544,512]{1,0:T(8,128)(2,1)S(1)}, bf16[544,512]{1,0:T(8,128)(2,1)}, u32[]{:S(2)}, u32[]{:S(2)}) collective-permute-start(bf16[544,512]{1,0:T(8,128)(2,1)S(1)} %shard_map.69.joined_ref), channel_id=1, source_target_pairs={{4,8},{12,16},{20,24},{28,32},{36,40},{44,48},{52,56},{60,64},{68,... | collective-permute-start | bytes 1671176 | tf_op jit(solution)/shard_map/ppermute | solution.py:47
  27.7 0.0 copy-start
  27.8 1.2 %copy-done = bf16[1024,512]{1,0:T(8,128)(2,1)S(1)} copy-done((bf16[1024,512]{1,0:T(8,128)(2,1)S(1)}, bf16[1024,512]{1,0:T(8,128)(2,1)}, u32[]{:S(2)}) %copy-start) | copy-done | bytes 1048600
  29.0 0.3 shard_map.70.columns_ref.own_columns_ref
  29.4 0.0 collective-permute-done.3.far_ref
  29.4 3.0 %shard_map.71 = (bf16[1024,512]{1,0:T(8,128)(2,1)S(1)}, f32[1024,1024]{1,0:T(8,128)S(1)}, f32[1024,128]{1,0:T(8,128)S(1)}, f32[8,3072]{1,0:T(8,128)S(1)}, f32[10...) custom-call(s32[8]{0:T(128)S(1)} %compare_select_fusion.3.flags, bf16[544,512]{1,0:T(8,128)(2,1)S(1)} %shard_map.69.joined_ref, ...), custom_call_target="tpu_custom_call" | custom-call | tf_op jit(solution)/shard_map/pallas_call | solution.py:356
  32.4 0.0 collective-permute-done.odd_raw
  32.4 0.2 collective-permute-done.1.even_raw
  32.6 7.6 %shard_map.72 = (bf16[1024,512]{1,0:T(8,128)(2,1)S(1)}, bf16[1024,512]{1,0:T(8,128)(2,1)S(1)}, f32[1024,1024]{1,0:T(8,128)S(1)}, f32[1024,1024]{1,0:T(8,128)S(1)...) custom-call(s32[8]{0:T(128)S(1)} %compare_select_fusion.3.flags, ...), custom_call_target="tpu_custom_call" | custom-call | tf_op jit(solution)/shard_map/pallas_call | solution.py:356
  40.2 6.4 %collective-permute-start.6 = (f32[1,1024]{1,0:T(1,128)S(1)}, f32[1,1024]{1,0:T(1,128)S(1)}, u32[]{:S(2)}, u32[]{:S(2)}) collective-permute-start(f32[1,1024]{1,0:T(1,128)S(1)} %get-tuple-element.37), channel_id=1, source_target_pairs={{8,16},{12,20},{24,32},{28,36},{40,48},{44,52},{56,64},{60,68},{72... | collective-permute-start | bytes 12296 | tf_op jit(solution)/shard_map/ppermute | solution.py:47
  46.6 5.0 %collective-permute-start.7 = (f32[1,1024]{1,0:T(1,128)S(1)}, f32[1,1024]{1,0:T(1,128)S(1)}, u32[]{:S(2)}, u32[]{:S(2)}) collective-permute-start(f32[1,1024]{1,0:T(1,128)S(1)} %get-tuple-element.38), channel_id=1, source_target_pairs={{0,8},{4,12},{16,24},{20,28},{32,40},{36,44},{48,56},{52,60},{64,7... | collective-permute-start | bytes 12296 | tf_op jit(solution)/shard_map/ppermute | solution.py:47
  51.6 4.1 %collective-permute-start.4 = (f32[4,1024]{1,0:T(4,128)S(1)}, f32[4,1024]{1,0:T(4,128)S(1)}, u32[]{:S(2)}, u32[]{:S(2)}) collective-permute-start(f32[4,1024]{1,0:T(4,128)S(1)} %get-tuple-element.35), channel_id=1, source_target_pairs={{4,8},{12,16},{20,24},{28,32},{36,40},{44,48},{52,56},{60,64},{68,... | collective-permute-start | bytes 49160 | tf_op jit(solution)/shard_map/ppermute | solution.py:47
  55.8 0.0 collective-permute-done.9.even_joined
  55.8 1.9 %collective-permute-start.5 = (f32[4,1024]{1,0:T(4,128)S(1)}, f32[4,1024]{1,0:T(4,128)S(1)}, u32[]{:S(2)}, u32[]{:S(2)}) collective-permute-start(f32[4,1024]{1,0:T(4,128)S(1)} %get-tuple-element.36), channel_id=1, source_target_pairs={{0,4},{8,12},{16,20},{24,28},{32,36},{40,44},{48,52},{56,60},{64,6... | collective-permute-start | bytes 49160 | tf_op jit(solution)/shard_map/ppermute | solution.py:47
  57.7 0.7 fusion
  58.4 0.0 collective-permute-done.8.odd_joined
  58.4 0.0 collective-permute-done.6.a_in
  58.4 0.0 collective-permute-done.7.b_in
  58.4 0.0 collective-permute-done.4.odd_in
  58.5 2.9 %collective-permute-done.5.even_in = f32[4,1024]{1,0:T(4,128)S(1)} collective-permute-done((f32[4,1024]{1,0:T(4,128)S(1)}, f32[4,1024]{1,0:T(4,128)S(1)}, u32[]{:S(2)}, u32[]{:S(2)}) %collective-permute-start.5) | collective-permute-done | bytes 16416 | tf_op jit(solution)/shard_map/ppermute | solution.py:47
  61.4 4.2 %shard_map.73 = (f32[1024,128]{1,0:T(8,128)S(1)}, f32[1,1024]{1,0:T(1,128)S(1)}, bf16[1024,512]{1,0:T(8,128)(2,1)S(1)}, f32[8,1024]{1,0:T(8,128)S(1)}, f32[4,102...) custom-call(s32[8]{0:T(128)S(1)} %compare_select_fusion.3.flags, ...), custom_call_target="tpu_custom_call" | custom-call | tf_op jit(solution)/shard_map/pallas_call | solution.py:356
  65.6 1.9 %collective-permute-start.14 = (bf16[1024,512]{1,0:T(8,128)(2,1)S(1)}, bf16[1024,512]{1,0:T(8,128)(2,1)S(1)}, u32[]{:S(2)}, u32[]{:S(2)}) collective-permute-start(bf16[1024,512]{1,0:T(8,128)(2,1)S(1)} %get-tuple-element.50.near_ref), channel_id=1, source_target_pairs={{0,1},{1,0},{2,3},{3,2},{4,5},{5,4},{6,7},{7,6},{8,9},{9,8},{10,11... | collective-permute-start | bytes 3145736 | tf_op jit(solution)/shard_map/ppermute | solution.py:38
  67.5 2.9 %collective-permute-start.10 = (f32[4,1024]{1,0:T(4,128)S(1)}, f32[4,1024]{1,0:T(4,128)S(1)}, u32[]{:S(2)}, u32[]{:S(2)}) collective-permute-start(f32[4,1024]{1,0:T(4,128)S(1)} %get-tuple-element.42), channel_id=1, source_target_pairs={{4,8},{12,16},{20,24},{28,32},{36,40},{44,48},{52,56},{60,64},{68,... | collective-permute-start | bytes 49160 | tf_op jit(solution)/shard_map/ppermute | solution.py:47
  70.4 1.9 %collective-permute-start.11 = (f32[4,1024]{1,0:T(4,128)S(1)}, f32[4,1024]{1,0:T(4,128)S(1)}, u32[]{:S(2)}, u32[]{:S(2)}) collective-permute-start(f32[4,1024]{1,0:T(4,128)S(1)} %get-tuple-element.43), channel_id=1, source_target_pairs={{0,4},{8,12},{16,20},{24,28},{32,36},{40,44},{48,52},{56,60},{64,6... | collective-permute-start | bytes 49160 | tf_op jit(solution)/shard_map/ppermute | solution.py:47
  72.4 5.6 %collective-permute-start.12 = (f32[1,1024]{1,0:T(1,128)S(1)}, f32[1,1024]{1,0:T(1,128)S(1)}, u32[]{:S(2)}, u32[]{:S(2)}) collective-permute-start(f32[1,1024]{1,0:T(1,128)S(1)} %get-tuple-element.44), channel_id=1, source_target_pairs={{8,16},{12,20},{24,32},{28,36},{40,48},{44,52},{56,64},{60,68},{72... | collective-permute-start | bytes 12296 | tf_op jit(solution)/shard_map/ppermute | solution.py:47
  77.9 31.4 %collective-permute-start.13 = (f32[1,1024]{1,0:T(1,128)S(1)}, f32[1,1024]{1,0:T(1,128)S(1)}, u32[]{:S(2)}, u32[]{:S(2)}) collective-permute-start(f32[1,1024]{1,0:T(1,128)S(1)} %get-tuple-element.45), channel_id=1, source_target_pairs={{0,8},{4,12},{16,24},{20,28},{32,40},{36,44},{48,56},{52,60},{64,7... | collective-permute-start | bytes 12296 | tf_op jit(solution)/shard_map/ppermute | solution.py:47
  109.3 0.0 collective-permute-done.14.far_ref
  109.3 1.6 %shard_map.74 = (bf16[1024,512]{1,0:T(8,128)(2,1)S(1)}, bf16[1024,512]{1,0:T(8,128)(2,1)S(1)}, f32[256,3072]{1,0:T(8,128)S(1)}) custom-call(s32[8]{0:T(128)S(1)} %compare_select_fusion.3.flags, bf16[1024,512]{1,0:T(8,128)(2,1)S(1)} %shard_map.70.columns_ref.own_columns_ref, bf16[1024,512]{1,0:T(8,128)(2,1)S(1)} %get-tuple-element.28.rows_ref, ...), custom_call_target="tpu_custom_call" | custom-call | tf_op jit(solution)/shard_map/pallas_call | solution.py:356
  110.9 0.0 collective-permute-done.12.a_in
  111.0 0.0 collective-permute-done.13.b_in
  111.0 0.0 collective-permute-done.10.odd_in
  111.0 0.0 collective-permute-done.11.even_in
  111.0 3.5 %gradient_kernel.1 = (f32[256,512]{1,0:T(8,128)}, f32[256,512]{1,0:T(8,128)}) custom-call(s32[8]{0:T(128)S(1)} %compare_select_fusion.3.flags, f32[8,1024]{1,0:T(8,128)S(1)} %get-tuple-element.41.partial_in, f32[4,1024]{1,0:T(4,128)S(1)} %collective-permute-done.10.odd_in, f32[4,1024]{1,0:T(4,128)S(1)} %collective-permute-done.11.even_in, ...), custom_call_target="tpu_custom_call" | custom-call | tf_op jit(solution)/shard_map/gradient_kernel/pallas_call | solution.py:470
  (2 shorter events, 0.0 us)
Async XLA Ops:
  0.6 31.8 %collective-permute-start = (bf16[1024,512]{1,0:T(8,128)(2,1)}, bf16[1024,512]{1,0:T(8,128)(2,1)S(1)}, u32[]{:S(2)}, u32[]{:S(2)}) collective-permute-start(bf16[1024,512]{1,0:T(8,128)(2,1)} %control_ref.1), channel_id=1, source_target_pairs={{4,8},{12,16},{20,24},{28,32},{36,40},{44,48},{52,56},{60,64},{68,... | collective-permute-start | bytes 3145736 | tf_op jit(solution)/shard_map/ppermute | solution.py:47
  2.7 30.0 %collective-permute-start.1 = (bf16[1024,512]{1,0:T(8,128)(2,1)}, bf16[1024,512]{1,0:T(8,128)(2,1)}, u32[]{:S(2)}, u32[]{:S(2)}) collective-permute-start(bf16[1024,512]{1,0:T(8,128)(2,1)} %control_ref.1), channel_id=1, source_target_pairs={{0,4},{8,12},{16,20},{24,28},{32,36},{40,44},{48,52},{56,60},{64,6... | collective-permute-start | bytes 3145736 | tf_op jit(solution)/shard_map/ppermute | solution.py:47
  8.3 1.0 copy-start.1
  9.3 0.7 copy-start.2
  9.9 0.7 copy-start.3
  10.8 9.7 %collective-permute-start.2 = (bf16[272,512]{1,0:T(8,128)(2,1)S(1)}, bf16[272,512]{1,0:T(8,128)(2,1)S(1)}, u32[]{:S(2)}, u32[]{:S(2)}) collective-permute-start(bf16[272,512]{1,0:T(8,128)(2,1)S(1)} %shard_map.68.own_ref), channel_id=1, source_target_pairs={{0,2},{2,0},{1,3},{3,1},{4,6},{6,4},{5,7},{7,5},{8,10},{10,8},{9,1... | collective-permute-start | bytes 835592 | tf_op jit(solution)/shard_map/ppermute | solution.py:38
  20.5 8.8 %collective-permute-start.3 = (bf16[544,512]{1,0:T(8,128)(2,1)S(1)}, bf16[544,512]{1,0:T(8,128)(2,1)S(1)}, u32[]{:S(2)}, u32[]{:S(2)}) collective-permute-start(bf16[544,512]{1,0:T(8,128)(2,1)S(1)} %shard_map.69.joined_ref), channel_id=1, source_target_pairs={{0,1},{1,0},{2,3},{3,2},{4,5},{5,4},{6,7},{7,6},{8,9},{9,8},{10,11... | collective-permute-start | bytes 1671176 | tf_op jit(solution)/shard_map/ppermute | solution.py:38
  22.5 33.3 %collective-permute-start.9 = (bf16[544,512]{1,0:T(8,128)(2,1)S(1)}, bf16[544,512]{1,0:T(8,128)(2,1)}, u32[]{:S(2)}, u32[]{:S(2)}) collective-permute-start(bf16[544,512]{1,0:T(8,128)(2,1)S(1)} %shard_map.69.joined_ref), channel_id=1, source_target_pairs={{0,4},{8,12},{16,20},{24,28},{32,36},{40,44},{48,52},{56,60},{64,6... | collective-permute-start | bytes 1671176 | tf_op jit(solution)/shard_map/ppermute | solution.py:47
  24.7 33.8 %collective-permute-start.8 = (bf16[544,512]{1,0:T(8,128)(2,1)S(1)}, bf16[544,512]{1,0:T(8,128)(2,1)}, u32[]{:S(2)}, u32[]{:S(2)}) collective-permute-start(bf16[544,512]{1,0:T(8,128)(2,1)S(1)} %shard_map.69.joined_ref), channel_id=1, source_target_pairs={{4,8},{12,16},{20,24},{28,32},{36,40},{44,48},{52,56},{60,64},{68,... | collective-permute-start | bytes 1671176 | tf_op jit(solution)/shard_map/ppermute | solution.py:47
  27.7 1.2 %copy-start = (bf16[1024,512]{1,0:T(8,128)(2,1)S(1)}, bf16[1024,512]{1,0:T(8,128)(2,1)}, u32[]{:S(2)}) copy-start(bf16[1024,512]{1,0:T(8,128)(2,1)} %control_ref.1) | copy-start | bytes 3145732
  40.2 18.2 %collective-permute-start.6 = (f32[1,1024]{1,0:T(1,128)S(1)}, f32[1,1024]{1,0:T(1,128)S(1)}, u32[]{:S(2)}, u32[]{:S(2)}) collective-permute-start(f32[1,1024]{1,0:T(1,128)S(1)} %get-tuple-element.37), channel_id=1, source_target_pairs={{8,16},{12,20},{24,32},{28,36},{40,48},{44,52},{56,64},{60,68},{72... | collective-permute-start | bytes 12296 | tf_op jit(solution)/shard_map/ppermute | solution.py:47
  46.6 11.8 %collective-permute-start.7 = (f32[1,1024]{1,0:T(1,128)S(1)}, f32[1,1024]{1,0:T(1,128)S(1)}, u32[]{:S(2)}, u32[]{:S(2)}) collective-permute-start(f32[1,1024]{1,0:T(1,128)S(1)} %get-tuple-element.38), channel_id=1, source_target_pairs={{0,8},{4,12},{16,24},{20,28},{32,40},{36,44},{48,56},{52,60},{64,7... | collective-permute-start | bytes 12296 | tf_op jit(solution)/shard_map/ppermute | solution.py:47
  51.6 6.8 %collective-permute-start.4 = (f32[4,1024]{1,0:T(4,128)S(1)}, f32[4,1024]{1,0:T(4,128)S(1)}, u32[]{:S(2)}, u32[]{:S(2)}) collective-permute-start(f32[4,1024]{1,0:T(4,128)S(1)} %get-tuple-element.35), channel_id=1, source_target_pairs={{4,8},{12,16},{20,24},{28,32},{36,40},{44,48},{52,56},{60,64},{68,... | collective-permute-start | bytes 49160 | tf_op jit(solution)/shard_map/ppermute | solution.py:47
  55.8 5.6 %collective-permute-start.5 = (f32[4,1024]{1,0:T(4,128)S(1)}, f32[4,1024]{1,0:T(4,128)S(1)}, u32[]{:S(2)}, u32[]{:S(2)}) collective-permute-start(f32[4,1024]{1,0:T(4,128)S(1)} %get-tuple-element.36), channel_id=1, source_target_pairs={{0,4},{8,12},{16,20},{24,28},{32,36},{40,44},{48,52},{56,60},{64,6... | collective-permute-start | bytes 49160 | tf_op jit(solution)/shard_map/ppermute | solution.py:47
  65.6 43.8 %collective-permute-start.14 = (bf16[1024,512]{1,0:T(8,128)(2,1)S(1)}, bf16[1024,512]{1,0:T(8,128)(2,1)S(1)}, u32[]{:S(2)}, u32[]{:S(2)}) collective-permute-start(bf16[1024,512]{1,0:T(8,128)(2,1)S(1)} %get-tuple-element.50.near_ref), channel_id=1, source_target_pairs={{0,1},{1,0},{2,3},{3,2},{4,5},{5,4},{6,7},{7,6},{8,9},{9,8},{10,11... | collective-permute-start | bytes 3145736 | tf_op jit(solution)/shard_map/ppermute | solution.py:38
  67.5 43.5 %collective-permute-start.10 = (f32[4,1024]{1,0:T(4,128)S(1)}, f32[4,1024]{1,0:T(4,128)S(1)}, u32[]{:S(2)}, u32[]{:S(2)}) collective-permute-start(f32[4,1024]{1,0:T(4,128)S(1)} %get-tuple-element.42), channel_id=1, source_target_pairs={{4,8},{12,16},{20,24},{28,32},{36,40},{44,48},{52,56},{60,64},{68,... | collective-permute-start | bytes 49160 | tf_op jit(solution)/shard_map/ppermute | solution.py:47
  70.4 40.5 %collective-permute-start.11 = (f32[4,1024]{1,0:T(4,128)S(1)}, f32[4,1024]{1,0:T(4,128)S(1)}, u32[]{:S(2)}, u32[]{:S(2)}) collective-permute-start(f32[4,1024]{1,0:T(4,128)S(1)} %get-tuple-element.43), channel_id=1, source_target_pairs={{0,4},{8,12},{16,20},{24,28},{32,36},{40,44},{48,52},{56,60},{64,6... | collective-permute-start | bytes 49160 | tf_op jit(solution)/shard_map/ppermute | solution.py:47
  72.4 38.6 %collective-permute-start.12 = (f32[1,1024]{1,0:T(1,128)S(1)}, f32[1,1024]{1,0:T(1,128)S(1)}, u32[]{:S(2)}, u32[]{:S(2)}) collective-permute-start(f32[1,1024]{1,0:T(1,128)S(1)} %get-tuple-element.44), channel_id=1, source_target_pairs={{8,16},{12,20},{24,32},{28,36},{40,48},{44,52},{56,64},{60,68},{72... | collective-permute-start | bytes 12296 | tf_op jit(solution)/shard_map/ppermute | solution.py:47
  77.9 33.0 %collective-permute-start.13 = (f32[1,1024]{1,0:T(1,128)S(1)}, f32[1,1024]{1,0:T(1,128)S(1)}, u32[]{:S(2)}, u32[]{:S(2)}) collective-permute-start(f32[1,1024]{1,0:T(1,128)S(1)} %get-tuple-element.45), channel_id=1, source_target_pairs={{0,8},{4,12},{16,24},{20,28},{32,40},{36,44},{48,56},{52,60},{64,7... | collective-permute-start | bytes 12296 | tf_op jit(solution)/shard_map/ppermute | solution.py:47

commit v4 on v3

--- a/solution.py
+++ b/solution.py
@@ -26,7 +26,7 @@
 MESSAGE = QUARTER + INFO
 JOINED = 2 * MESSAGE
 
-NARROW, ODD, A_EVEN, HAS_ODD = range(4)
+NARROW, CORE, ODD, A_EVEN, HAS_ODD = range(5)
 
 
 def both_ways(pairs, count):
@@ -127,6 +127,17 @@
 
 def columns_kernel(control_ref, columns_ref):
     columns_ref[...] = normalize(control_ref[...])
+
+
+def near_columns_kernel(odd_ref, even_ref, columns_ref):
+    columns_ref[0:HALF, :] = normalize(odd_ref[...])
+    columns_ref[HALF:SLAB, :] = normalize(even_ref[...])
+
+
+def near_kernel(rows_ref, columns_ref, mask_ref, before_ref, kernel_ref, sums_ref):
+    fill_kernel(
+        rows_ref, columns_ref, mask_ref, slice(SLAB, 2 * SLAB), kernel_ref, sums_ref, before_ref
+    )
 
 
 def prepare_kernel(
@@ -152,9 +163,10 @@
     even_base = 16 - odd * 16
     lane = lax.broadcasted_iota(jnp.int32, (1, 3 * SLAB), 1)
     segment = lane // SLAB
-    wanted = (lane % SLAB) // LANES + jnp.where(
-        segment == 0, 8, jnp.where(segment == 1, odd_base, even_base)
-    )
+    core = flags[CORE]
+    side = jnp.where(lane % SLAB < HALF, odd_base, even_base)
+    side = side + 4 * jnp.where(segment == 1, core, 1 - core) + (lane % HALF) // LANES
+    wanted = jnp.where(segment == 0, 8 + lane // LANES, side)
     one_hot = lax.broadcasted_iota(jnp.int32, (LANES, 3 * SLAB), 0) == wanted
     mask_ref[...] = jnp.dot(
         band[:16], jnp.where(one_hot, 1.0, 0.0).astype(BF16), preferred_element_type=F32
@@ -177,10 +189,20 @@
     fill_kernel(rows_ref, columns_ref, mask_ref, slice(0, SLAB), kernel_ref, sums_ref, None)
 
 
-def finish_messages(
-    flags, sums, first, second, partial_ref, odd_ref, even_ref, a_ref, b_ref
-):
-    own, odd, even = (jnp.sum(part, axis=0, keepdims=True) for part in sums)
+def regroup(flags, first, second):
+    low = jnp.concatenate([first[:, :HALF], second[:, :HALF]], axis=1)
+    high = jnp.concatenate([first[:, HALF:], second[:, HALF:]], axis=1)
+    swap = flags[CORE] > 0
+    return jnp.where(swap, high, low), jnp.where(swap, low, high)
+
+
+def finish_messages(flags, sums, first, second, partial_ref, odd_ref, even_ref, a_ref, b_ref):
+    own, near, far = (jnp.sum(part, axis=0, keepdims=True) for part in sums)
+    swap = flags[CORE] > 0
+    low = jnp.where(swap, far, near)
+    high = jnp.where(swap, near, far)
+    odd = jnp.concatenate([low[:, :HALF], high[:, :HALF]], axis=1)
+    even = jnp.concatenate([low[:, HALF:], high[:, HALF:]], axis=1)
     partial_ref[...] = jnp.zeros_like(partial_ref)
     partial_ref[0:1, :] = own
     partial_ref[1:2, :] = odd
@@ -196,32 +218,24 @@
     b_ref[...] = jnp.where(a_even, odd, even)
 
 
-def sides_kernel(
-    flags, odd_raw, even_raw, rows_ref, mask_ref, own_kernel_ref, own_sums_ref, weight_ref,
-    pair_ref, odd_columns_ref, even_columns_ref, odd_kernel_ref, even_kernel_ref, partial_ref,
-    odd_ref, even_ref, a_ref, b_ref, sums_ref,
+def far_kernel(
+    flags, rows_ref, columns_ref, mask_ref, own_kernel_ref, near_kernel_ref, before_ref,
+    weight_ref, pair_ref, kernel_ref, partial_ref, odd_ref, even_ref, a_ref, b_ref,
 ):
-    odd_columns_ref[...] = normalize(odd_raw[...])
-    even_columns_ref[...] = normalize(even_raw[...])
-    fill_kernel(
-        rows_ref, odd_columns_ref, mask_ref, slice(SLAB, 2 * SLAB), odd_kernel_ref, sums_ref,
-        own_sums_ref,
-    )
-
     def step(i, carry):
-        own, odd, even = carry
+        own, near, far = carry
         blocks = block_kernel(
-            rows_ref, even_columns_ref[...], mask_ref, i, slice(2 * SLAB, 3 * SLAB)
+            rows_ref, columns_ref[...], mask_ref, i, slice(2 * SLAB, 3 * SLAB)
         )
         for j, block in enumerate(blocks):
             at = pl.ds(pl.multiple_of(i * QUARTER + j * LANES, LANES), LANES)
-            even_kernel_ref[at, :] = block
-            sums = lane_tiles(block) + sums_ref[at, :]
+            kernel_ref[at, :] = block
+            sums = lane_tiles(block) + before_ref[at, :]
             scale = weight_ref[at, 0:1] / jnp.sum(sums, axis=1, keepdims=True)
             own = own + sublane_tiles(own_kernel_ref[at, :] * scale)
-            odd = odd + sublane_tiles(odd_kernel_ref[at, :] * scale)
-            even = even + sublane_tiles(block * scale)
-        return own, odd, even
+            near = near + sublane_tiles(near_kernel_ref[at, :] * scale)
+            far = far + sublane_tiles(block * scale)
+        return own, near, far
 
     zero = jnp.zeros((8, SLAB), F32)
     sums = lax.fori_loop(0, 4, step, (zero, zero, zero))
@@ -241,12 +255,13 @@
     has_odd = flags[HAS_ODD] > 0
     own_weight, odd_weight, even_weight = (ref[...] for ref in weights)
     odd = jnp.where(has_odd, odd_weight / jnp.where(has_odd, odd, 1.0), 0.0)
-    return own_weight / own, odd, even_weight / even
+    even = even_weight / even
+    return own_weight / own, *regroup(flags, odd, even)
 
 
 def sweep_kernel(
     flags, partial_in, odd_in, even_in, a_in, b_in, own_weight, odd_weight, even_weight,
-    own_kernel_ref, odd_kernel_ref, even_kernel_ref, weight_ref, odd_joined, even_joined, row_ref,
+    own_kernel_ref, near_kernel_ref, far_kernel_ref, weight_ref, odd_joined, even_joined, row_ref,
     lane_ref, pair_ref, partial_ref, odd_ref, even_ref, a_ref, b_ref, flat_ref,
 ):
     pair_ref[0:HALF, :] = odd_joined[0:HALF, :]
@@ -254,7 +269,7 @@
     scales = column_scales(
         flags, partial_in, odd_in, even_in, a_in, b_in, (own_weight, odd_weight, even_weight)
     )
-    kernels = (own_kernel_ref, odd_kernel_ref, even_kernel_ref)
+    kernels = (own_kernel_ref, near_kernel_ref, far_kernel_ref)
 
     def step(i, carry):
         at = pl.ds(pl.multiple_of(i * LANES, LANES), LANES)
@@ -301,8 +316,8 @@
 
 def gradient_kernel(
     flags, partial_in, odd_in, even_in, a_in, b_in, own_weight, odd_weight, even_weight, row_ref,
-    lane_ref, own_kernel_ref, odd_kernel_ref, even_kernel_ref, own_columns_ref, odd_columns_ref,
-    even_columns_ref, rows_ref, odd_rows_ref, even_rows_ref, transposed_ref, treated_out,
+    lane_ref, own_kernel_ref, near_kernel_ref, far_kernel_ref, own_columns_ref, near_columns_ref,
+    far_columns_ref, rows_ref, odd_rows_ref, even_rows_ref, transposed_ref, treated_out,
     control_out,
 ):
     scales = column_scales(
@@ -312,9 +327,9 @@
     mass = jnp.zeros((QUARTER, LANES), F32)
     pulled = jnp.zeros((QUARTER, WIDTH), F32)
     for kernel_ref, scale, columns_ref in zip(
-        (own_kernel_ref, odd_kernel_ref, even_kernel_ref),
+        (own_kernel_ref, near_kernel_ref, far_kernel_ref),
         scales,
-        (own_columns_ref, odd_columns_ref, even_columns_ref),
+        (own_columns_ref, near_columns_ref, far_columns_ref),
         strict=True,
     ):
         transport = row_scale * kernel_ref[...] * scale
@@ -385,6 +400,7 @@
     toward_even = wide_index + 1 - 2 * odd
     values = (
         n,
+        n % 2,
         odd,
         jnp.logical_xor(wide_index % 4 >= 2, odd == 1).astype(jnp.int32),
         ((toward_odd >= 0) & (toward_odd < wide_count)).astype(jnp.int32),
@@ -398,10 +414,12 @@
         for at in (wide_index, toward_odd, toward_even)
     ]
 
-    odd_control = exchange(control, 1, True)
-    even_control = exchange(control, 1, False)
+    half = lax.dynamic_slice_in_dim(control, (n % 2) * HALF, HALF)
+    odd_control = exchange(half, 1, True)
+    even_control = exchange(half, 1, False)
     (own_columns,) = call(columns_kernel, [VMEM], [((SLAB, WIDTH), BF16)], [control])
 
+    treated_weight, flags, *weights = lax.optimization_barrier((treated_weight, flags, *weights))
     (message,) = call(
         pack_kernel,
         [VMEM] * 3,
@@ -429,19 +447,22 @@
         [flags, joined, joined_far, own_columns],
         [pltpu.VMEM((LANES, LANES), F32)],
     )
-    odd_columns, even_columns, odd_kernel, even_kernel, partial, *messages = call(
-        sides_kernel,
+    odd_control, even_control, _ = lax.optimization_barrier((odd_control, even_control, sums))
+    (near_columns,) = call(
+        near_columns_kernel, [VMEM] * 2, [((SLAB, WIDTH), BF16)], [odd_control, even_control]
+    )
+    far_columns = narrow_swap(near_columns, SWAP_CORE)
+    near_values, sums = call(
+        near_kernel,
+        [VMEM] * 4,
+        [((SLAB, SLAB), F32), ((SLAB, LANES), F32)],
+        [rows, near_columns, mask, sums],
+    )
+    far_values, partial, *messages = call(
+        far_kernel,
         [SMEM] + [VMEM] * 8,
-        [
-            ((SLAB, WIDTH), BF16),
-            ((SLAB, WIDTH), BF16),
-            ((SLAB, SLAB), F32),
-            ((SLAB, SLAB), F32),
-            ((8, SLAB), F32),
-            *MESSAGES,
-        ],
-        [flags, odd_control, even_control, rows, mask, own_kernel, sums, weight, pairs],
-        [pltpu.VMEM((SLAB, LANES), F32)],
+        [((SLAB, SLAB), F32), ((8, SLAB), F32), *MESSAGES],
+        [flags, rows, far_columns, mask, own_kernel, near_values, sums, weight, pairs],
     )
     first = trade(messages)
 
@@ -450,7 +471,7 @@
         [SMEM] + [VMEM] * 14,
         [((SLAB, LANES), F32), ((1, SLAB), F32), ((SLAB, WIDTH), BF16), ((8, SLAB), F32), *MESSAGES],
         [
-            flags, partial, *first, *weights, own_kernel, odd_kernel, even_kernel, weight,
+            flags, partial, *first, *weights, own_kernel, near_values, far_values, weight,
             odd_joined, even_joined,
         ],
         [pltpu.VMEM((8, LANES), F32)],
@@ -481,8 +502,8 @@
         compiler_params=pltpu.CompilerParams(vmem_limit_bytes=16 << 20),
         name="gradient_kernel",
     )(
-        flags, partial, *second, *weights, row_scale, lane_scale, own_kernel, odd_kernel,
-        even_kernel, own_columns, odd_columns, even_columns, rows, odd_rows, even_rows, transposed,
+        flags, partial, *second, *weights, row_scale, lane_scale, own_kernel, near_values,
+        far_values, own_columns, near_columns, far_columns, rows, odd_rows, even_rows, transposed,
     )
 
 

time: 115 us -> 119 us (1.035)
  the two profiles are of different devices: /device:TPU:150 before, /device:TPU:24 now
where the time goes in v4:
time: 119 us; the launch traced here: 118 us
  starting transfers between devices  70.6 us (59%)
  waiting for transfers between devices  22.7 us (19%)
  Pallas kernels  18.6 us (16%)
  local copies, waits for them, and re-layouts  5.34 us (4%)
    ppermute x12, starting transfers between devices, exchange(): return lax.ppermute(block, 'wide', both_ways(pairs, count))  62.2 us
    pallas_call x9, Pallas kernels, call(): pl.pallas_call(body, out_shape=tuple((jax.ShapeDtypeStruct(shape, dtype)...  15.1 us
    ppermute x12, waiting for transfers between devices, exchange(): return lax.ppermute(block, 'wide', both_ways(pairs, count))  15 us
    ppermute x4, starting transfers between devices, narrow_swap(): return lax.ppermute(block, 'narrow', pairs)  8.41 us
    ppermute x4, waiting for transfers between devices, narrow_swap(): return lax.ppermute(block, 'narrow', pairs)  7.63 us
    unnamed x8, local copies, waits for them, and re-layouts  3.53 us
    pallas_call x1, Pallas kernels, step(): pl.pallas_call(gradient_kernel, grid=(1,), out_shape=(jax.ShapeDtypeStruc...  3.48 us
  transfers between devices with their start and end apart: 16, of which 4 were waited for; matrix products, arithmetic and copies ran while one was open for 1% of the time, Pallas kernels for 9%

profile of v4, /device:TPU:24, one launch (start us, length us, event | category | flops | bytes accessed | tf_op | source)
XLA Modules:
  0.0 118.2 jit_solution(10089949340153164707)
XLA Ops:
  0.7 0.7 fusion
  1.4 0.0 copy-start.1
  1.4 0.9 copy-done.1
  2.4 0.0 copy-start.2
  2.4 0.7 copy-done.2
  3.1 0.0 copy-start.3
  3.1 0.7 copy-done.3
  3.7 0.1 shard_map.68.own_ref
  3.9 2.7 %collective-permute-start = (bf16[272,512]{1,0:T(8,128)(2,1)S(1)}, bf16[272,512]{1,0:T(8,128)(2,1)S(1)}, u32[]{:S(2)}, u32[]{:S(2)}) collective-permute-start(bf16[272,512]{1,0:T(8,128)(2,1)S(1)} %shard_map.68.own_ref), channel_id=1, source_target_pairs={{0,2},{2,0},{1,3},{3,1},{4,6},{6,4},{5,7},{7,5},{8,10},{10,8},{9,1... | collective-permute-start | bytes 835592 | tf_op jit(solution)/shard_map/ppermute | solution.py:38
  6.5 7.6 %collective-permute-done.y_ref = bf16[272,512]{1,0:T(8,128)(2,1)S(1)} collective-permute-done((bf16[272,512]{1,0:T(8,128)(2,1)S(1)}, bf16[272,512]{1,0:T(8,128)(2,1)S(1)}, u32[]{:S(2)}, u32[]{:S(2)}) %collective-permute-start) | collective-permute-done | bytes 278560 | tf_op jit(solution)/shard_map/ppermute | solution.py:38
  14.2 1.9 %collective-permute-start.1 = (bf16[544,512]{1,0:T(8,128)(2,1)S(1)}, bf16[544,512]{1,0:T(8,128)(2,1)S(1)}, u32[]{:S(2)}, u32[]{:S(2)}) collective-permute-start(bf16[544,512]{1,0:T(8,128)(2,1)S(1)} %shard_map.69.joined_ref), channel_id=1, source_target_pairs={{0,1},{1,0},{2,3},{3,2},{4,5},{5,4},{6,7},{7,6},{8,9},{9,8},{10,11... | collective-permute-start | bytes 1671176 | tf_op jit(solution)/shard_map/ppermute | solution.py:38
  16.1 1.1 constant_dynamic-slice_fusion
  17.2 3.8 %collective-permute-start.3 = (bf16[512,512]{1,0:T(8,128)(2,1)S(1)}, bf16[512,512]{1,0:T(8,128)(2,1)S(1)}, u32[]{:S(2)}, u32[]{:S(2)}) collective-permute-start(bf16[512,512]{1,0:T(8,128)(2,1)S(1)} %constant_dynamic-slice_fusion), channel_id=1, source_target_pairs={{0,4},{8,12},{16,20},{24,28},{32,36},{40,44},{48,52},{56,60},{64,6... | collective-permute-start | bytes 1572872 | tf_op jit(solution)/shard_map/ppermute | solution.py:47
  21.1 13.4 %collective-permute-start.2 = (bf16[512,512]{1,0:T(8,128)(2,1)S(1)}, bf16[512,512]{1,0:T(8,128)(2,1)S(1)}, u32[]{:S(2)}, u32[]{:S(2)}) collective-permute-start(bf16[512,512]{1,0:T(8,128)(2,1)S(1)} %constant_dynamic-slice_fusion), channel_id=1, source_target_pairs={{4,8},{12,16},{20,24},{28,32},{36,40},{44,48},{52,56},{60,64},{68,... | collective-permute-start | bytes 1572872 | tf_op jit(solution)/shard_map/ppermute | solution.py:47
  34.4 0.0 copy-start
  34.4 1.2 %copy-done = bf16[1024,512]{1,0:T(8,128)(2,1)S(1)} copy-done((bf16[1024,512]{1,0:T(8,128)(2,1)S(1)}, bf16[1024,512]{1,0:T(8,128)(2,1)}, u32[]{:S(2)}) %copy-start) | copy-done | bytes 1048600
  35.6 0.3 shard_map.70.columns_ref.own_columns_ref
  36.0 0.0 collective-permute-done.1.far_ref
  36.0 3.0 %shard_map.71 = (bf16[1024,512]{1,0:T(8,128)(2,1)S(1)}, f32[1024,1024]{1,0:T(8,128)S(1)}, f32[1024,128]{1,0:T(8,128)S(1)}, f32[8,3072]{1,0:T(8,128)S(1)}, f32[10...) custom-call(s32[8]{0:T(128)S(1)} %compare_select_fusion.4.flags, bf16[544,512]{1,0:T(8,128)(2,1)S(1)} %shard_map.69.joined_ref, ...), custom_call_target="tpu_custom_call" | custom-call | tf_op jit(solution)/shard_map/pallas_call | solution.py:371
  39.0 0.0 collective-permute-done.3.even_ref
  39.0 7.7 %collective-permute-done.2.odd_ref = bf16[512,512]{1,0:T(8,128)(2,1)S(1)} collective-permute-done((bf16[512,512]{1,0:T(8,128)(2,1)S(1)}, bf16[512,512]{1,0:T(8,128)(2,1)S(1)}, u32[]{:S(2)}, u32[]{:S(2)}) %collective-permute-start.2) | collective-permute-done | bytes 524320 | tf_op jit(solution)/shard_map/ppermute | solution.py:47
  46.7 0.3 shard_map.72.columns_ref.near_columns_ref
  47.1 1.9 %collective-permute-start.4 = (bf16[1024,512]{1,0:T(8,128)(2,1)S(1)}, bf16[1024,512]{1,0:T(8,128)(2,1)S(1)}, u32[]{:S(2)}, u32[]{:S(2)}) collective-permute-start(bf16[1024,512]{1,0:T(8,128)(2,1)S(1)} %shard_map.72.columns_ref.near_columns_ref), channel_id=1, source_target_pairs={{0,1},{1,0},{2,3},{3,2},{4,5},{5,4},{6,7},{7,6},{8,9},{9,8},{10,11... | collective-permute-start | bytes 3145736 | tf_op jit(solution)/shard_map/ppermute | solution.py:38
  49.0 1.9 %collective-permute-start.10 = (bf16[544,512]{1,0:T(8,128)(2,1)S(1)}, bf16[544,512]{1,0:T(8,128)(2,1)S(1)}, u32[]{:S(2)}, u32[]{:S(2)}) collective-permute-start(bf16[544,512]{1,0:T(8,128)(2,1)S(1)} %shard_map.69.joined_ref), channel_id=1, source_target_pairs={{0,4},{8,12},{16,20},{24,28},{32,36},{40,44},{48,52},{56,60},{64,6... | collective-permute-start | bytes 1671176 | tf_op jit(solution)/shard_map/ppermute | solution.py:47
  50.9 9.4 %collective-permute-start.9 = (bf16[544,512]{1,0:T(8,128)(2,1)S(1)}, bf16[544,512]{1,0:T(8,128)(2,1)S(1)}, u32[]{:S(2)}, u32[]{:S(2)}) collective-permute-start(bf16[544,512]{1,0:T(8,128)(2,1)S(1)} %shard_map.69.joined_ref), channel_id=1, source_target_pairs={{4,8},{12,16},{20,24},{28,32},{36,40},{44,48},{52,56},{60,64},{68,... | collective-permute-start | bytes 1671176 | tf_op jit(solution)/shard_map/ppermute | solution.py:47
  60.3 2.1 %shard_map.73 = (f32[1024,1024]{1,0:T(8,128)S(1)}, f32[1024,128]{1,0:T(8,128)S(1)}) custom-call(bf16[1024,512]{1,0:T(8,128)(2,1)S(1)} %get-tuple-element.36.rows_ref, bf16[1024,512]{1,0:T(8,128)(2,1)S(1)} %shard_map.72.columns_ref.near_columns_ref, f32[8,3072]{1,0:T(8,128)S(1)} %get-tuple-element.40.mask_ref, f32[1024,128]{1,0:T(8,128)S(1)} %get-tuple-element.37.before_ref), custom_call_target="tpu_custom_call" | custom-call | tf_op jit(solution)/shard_map/pallas_call | solution.py:371
  62.4 0.0 collective-permute-done.4.columns_ref.far_columns_ref
  62.4 4.1 %shard_map.74 = (f32[1024,1024]{1,0:T(8,128)S(1)}, f32[8,1024]{1,0:T(8,128)S(1)}, f32[4,1024]{1,0:T(4,128)S(1)}, f32[4,1024]{1,0:T(4,128)S(1)}, f32[1,1024]{1,0:T(1,128)S(1)}, /*index=5*/f32[1,1024]{1,0:T(1,128)S(1)}) custom-call(s32[8]{0:T(128)S(1)} %compare_select_fusion.4.flags, bf16[1024,512]{1,0:T(8,128)(2,1)S(1)} %get-tuple-element.36.rows_ref, ...), custom_call_target="tpu_custom_call" | custom-call | tf_op jit(solution)/shard_map/pallas_call | solution.py:371
  66.5 2.2 %collective-permute-start.5 = (f32[4,1024]{1,0:T(4,128)S(1)}, f32[4,1024]{1,0:T(4,128)S(1)}, u32[]{:S(2)}, u32[]{:S(2)}) collective-permute-start(f32[4,1024]{1,0:T(4,128)S(1)} %get-tuple-element.47), channel_id=1, source_target_pairs={{4,8},{12,16},{20,24},{28,32},{36,40},{44,48},{52,56},{60,64},{68,... | collective-permute-start | bytes 49160 | tf_op jit(solution)/shard_map/ppermute | solution.py:47
  68.7 1.9 %collective-permute-start.6 = (f32[4,1024]{1,0:T(4,128)S(1)}, f32[4,1024]{1,0:T(4,128)S(1)}, u32[]{:S(2)}, u32[]{:S(2)}) collective-permute-start(f32[4,1024]{1,0:T(4,128)S(1)} %get-tuple-element.48), channel_id=1, source_target_pairs={{0,4},{8,12},{16,20},{24,28},{32,36},{40,44},{48,52},{56,60},{64,6... | collective-permute-start | bytes 49160 | tf_op jit(solution)/shard_map/ppermute | solution.py:47
  70.7 10.8 %collective-permute-start.7 = (f32[1,1024]{1,0:T(1,128)S(1)}, f32[1,1024]{1,0:T(1,128)S(1)}, u32[]{:S(2)}, u32[]{:S(2)}) collective-permute-start(f32[1,1024]{1,0:T(1,128)S(1)} %get-tuple-element.49), channel_id=1, source_target_pairs={{8,16},{12,20},{24,32},{28,36},{40,48},{44,52},{56,64},{60,68},{72... | collective-permute-start | bytes 12296 | tf_op jit(solution)/shard_map/ppermute | solution.py:47
  81.5 0.0 collective-permute-done.10.even_joined
  81.5 1.9 %collective-permute-start.8 = (f32[1,1024]{1,0:T(1,128)S(1)}, f32[1,1024]{1,0:T(1,128)S(1)}, u32[]{:S(2)}, u32[]{:S(2)}) collective-permute-start(f32[1,1024]{1,0:T(1,128)S(1)} %get-tuple-element.50), channel_id=1, source_target_pairs={{0,8},{4,12},{16,24},{20,28},{32,40},{36,44},{48,56},{52,60},{64,7... | collective-permute-start | bytes 12296 | tf_op jit(solution)/shard_map/ppermute | solution.py:47
  83.4 0.0 collective-permute-done.9.odd_joined
  83.4 0.0 collective-permute-done.7.a_in
  83.5 4.5 %collective-permute-done.8.b_in = f32[1,1024]{1,0:T(1,128)S(1)} collective-permute-done((f32[1,1024]{1,0:T(1,128)S(1)}, f32[1,1024]{1,0:T(1,128)S(1)}, u32[]{:S(2)}, u32[]{:S(2)}) %collective-permute-start.8) | collective-permute-done | bytes 4128 | tf_op jit(solution)/shard_map/ppermute | solution.py:47
  87.9 0.0 collective-permute-done.5.odd_in
  87.9 0.0 collective-permute-done.6.even_in
  87.9 3.5 %shard_map.75 = (f32[1024,128]{1,0:T(8,128)S(1)}, f32[1,1024]{1,0:T(1,128)S(1)}, bf16[1024,512]{1,0:T(8,128)(2,1)S(1)}, f32[8,1024]{1,0:T(8,128)S(1)}, f32[4,102...) custom-call(s32[8]{0:T(128)S(1)} %compare_select_fusion.4.flags, ...), custom_call_target="tpu_custom_call" | custom-call | tf_op jit(solution)/shard_map/pallas_call | solution.py:371
  91.4 1.9 %collective-permute-start.15 = (bf16[1024,512]{1,0:T(8,128)(2,1)S(1)}, bf16[1024,512]{1,0:T(8,128)(2,1)S(1)}, u32[]{:S(2)}, u32[]{:S(2)}) collective-permute-start(bf16[1024,512]{1,0:T(8,128)(2,1)S(1)} %get-tuple-element.62.near_ref), channel_id=1, source_target_pairs={{0,1},{1,0},{2,3},{3,2},{4,5},{5,4},{6,7},{7,6},{8,9},{9,8},{10,11... | collective-permute-start | bytes 3145736 | tf_op jit(solution)/shard_map/ppermute | solution.py:38
  93.3 4.3 %collective-permute-start.11 = (f32[4,1024]{1,0:T(4,128)S(1)}, f32[4,1024]{1,0:T(4,128)S(1)}, u32[]{:S(2)}, u32[]{:S(2)}) collective-permute-start(f32[4,1024]{1,0:T(4,128)S(1)} %get-tuple-element.56), channel_id=1, source_target_pairs={{4,8},{12,16},{20,24},{28,32},{36,40},{44,48},{52,56},{60,64},{68,... | collective-permute-start | bytes 49160 | tf_op jit(solution)/shard_map/ppermute | solution.py:47
  97.6 1.9 %collective-permute-start.12 = (f32[4,1024]{1,0:T(4,128)S(1)}, f32[4,1024]{1,0:T(4,128)S(1)}, u32[]{:S(2)}, u32[]{:S(2)}) collective-permute-start(f32[4,1024]{1,0:T(4,128)S(1)} %get-tuple-element.57), channel_id=1, source_target_pairs={{0,4},{8,12},{16,20},{24,28},{32,36},{40,44},{48,52},{56,60},{64,6... | collective-permute-start | bytes 49160 | tf_op jit(solution)/shard_map/ppermute | solution.py:47
  99.5 8.7 %collective-permute-start.13 = (f32[1,1024]{1,0:T(1,128)S(1)}, f32[1,1024]{1,0:T(1,128)S(1)}, u32[]{:S(2)}, u32[]{:S(2)}) collective-permute-start(f32[1,1024]{1,0:T(1,128)S(1)} %get-tuple-element.58), channel_id=1, source_target_pairs={{8,16},{12,20},{24,32},{28,36},{40,48},{44,52},{56,64},{60,68},{72... | collective-permute-start | bytes 12296 | tf_op jit(solution)/shard_map/ppermute | solution.py:47
  108.3 1.9 %collective-permute-start.14 = (f32[1,1024]{1,0:T(1,128)S(1)}, f32[1,1024]{1,0:T(1,128)S(1)}, u32[]{:S(2)}, u32[]{:S(2)}) collective-permute-start(f32[1,1024]{1,0:T(1,128)S(1)} %get-tuple-element.59), channel_id=1, source_target_pairs={{0,8},{4,12},{16,24},{20,28},{32,40},{36,44},{48,56},{52,60},{64,7... | collective-permute-start | bytes 12296 | tf_op jit(solution)/shard_map/ppermute | solution.py:47
  110.2 0.0 collective-permute-done.15.far_ref
  110.2 1.6 %shard_map.76 = (bf16[1024,512]{1,0:T(8,128)(2,1)S(1)}, bf16[1024,512]{1,0:T(8,128)(2,1)S(1)}, f32[256,3072]{1,0:T(8,128)S(1)}) custom-call(s32[8]{0:T(128)S(1)} %compare_select_fusion.4.flags, bf16[1024,512]{1,0:T(8,128)(2,1)S(1)} %shard_map.70.columns_ref.own_columns_ref, bf16[1024,512]{1,0:T(8,128)(2,1)S(1)} %get-tuple-element.36.rows_ref, ...), custom_call_target="tpu_custom_call" | custom-call | tf_op jit(solution)/shard_map/pallas_call | solution.py:371
  111.8 0.0 collective-permute-done.13.a_in
  111.9 2.8 %collective-permute-done.14.b_in = f32[1,1024]{1,0:T(1,128)S(1)} collective-permute-done((f32[1,1024]{1,0:T(1,128)S(1)}, f32[1,1024]{1,0:T(1,128)S(1)}, u32[]{:S(2)}, u32[]{:S(2)}) %collective-permute-start.14) | collective-permute-done | bytes 4128 | tf_op jit(solution)/shard_map/ppermute | solution.py:47
  114.7 0.0 collective-permute-done.11.odd_in
  114.7 0.0 collective-permute-done.12.even_in
  114.7 3.5 %gradient_kernel.1 = (f32[256,512]{1,0:T(8,128)}, f32[256,512]{1,0:T(8,128)}) custom-call(s32[8]{0:T(128)S(1)} %compare_select_fusion.4.flags, f32[8,1024]{1,0:T(8,128)S(1)} %get-tuple-element.55.partial_in, f32[4,1024]{1,0:T(4,128)S(1)} %collective-permute-done.11.odd_in, f32[4,1024]{1,0:T(4,128)S(1)} %collective-permute-done.12.even_in, ...), custom_call_target="tpu_custom_call" | custom-call | tf_op jit(solution)/shard_map/gradient_kernel/pallas_call | solution.py:491
  (2 shorter events, 0.0 us)
Async XLA Ops:
  1.4 0.9 copy-start.1
  2.4 0.7 copy-start.2
  3.1 0.7 copy-start.3
  3.9 10.3 %collective-permute-start = (bf16[272,512]{1,0:T(8,128)(2,1)S(1)}, bf16[272,512]{1,0:T(8,128)(2,1)S(1)}, u32[]{:S(2)}, u32[]{:S(2)}) collective-permute-start(bf16[272,512]{1,0:T(8,128)(2,1)S(1)} %shard_map.68.own_ref), channel_id=1, source_target_pairs={{0,2},{2,0},{1,3},{3,1},{4,6},{6,4},{5,7},{7,5},{8,10},{10,8},{9,1... | collective-permute-start | bytes 835592 | tf_op jit(solution)/shard_map/ppermute | solution.py:38
  14.2 21.8 %collective-permute-start.1 = (bf16[544,512]{1,0:T(8,128)(2,1)S(1)}, bf16[544,512]{1,0:T(8,128)(2,1)S(1)}, u32[]{:S(2)}, u32[]{:S(2)}) collective-permute-start(bf16[544,512]{1,0:T(8,128)(2,1)S(1)} %shard_map.69.joined_ref), channel_id=1, source_target_pairs={{0,1},{1,0},{2,3},{3,2},{4,5},{5,4},{6,7},{7,6},{8,9},{9,8},{10,11... | collective-permute-start | bytes 1671176 | tf_op jit(solution)/shard_map/ppermute | solution.py:38
  17.2 21.8 %collective-permute-start.3 = (bf16[512,512]{1,0:T(8,128)(2,1)S(1)}, bf16[512,512]{1,0:T(8,128)(2,1)S(1)}, u32[]{:S(2)}, u32[]{:S(2)}) collective-permute-start(bf16[512,512]{1,0:T(8,128)(2,1)S(1)} %constant_dynamic-slice_fusion), channel_id=1, source_target_pairs={{0,4},{8,12},{16,20},{24,28},{32,36},{40,44},{48,52},{56,60},{64,6... | collective-permute-start | bytes 1572872 | tf_op jit(solution)/shard_map/ppermute | solution.py:47
  21.1 25.7 %collective-permute-start.2 = (bf16[512,512]{1,0:T(8,128)(2,1)S(1)}, bf16[512,512]{1,0:T(8,128)(2,1)S(1)}, u32[]{:S(2)}, u32[]{:S(2)}) collective-permute-start(bf16[512,512]{1,0:T(8,128)(2,1)S(1)} %constant_dynamic-slice_fusion), channel_id=1, source_target_pairs={{4,8},{12,16},{20,24},{28,32},{36,40},{44,48},{52,56},{60,64},{68,... | collective-permute-start | bytes 1572872 | tf_op jit(solution)/shard_map/ppermute | solution.py:47
  34.4 1.2 %copy-start = (bf16[1024,512]{1,0:T(8,128)(2,1)S(1)}, bf16[1024,512]{1,0:T(8,128)(2,1)}, u32[]{:S(2)}) copy-start(bf16[1024,512]{1,0:T(8,128)(2,1)} %control_ref.1) | copy-start | bytes 3145732
  47.1 15.3 %collective-permute-start.4 = (bf16[1024,512]{1,0:T(8,128)(2,1)S(1)}, bf16[1024,512]{1,0:T(8,128)(2,1)S(1)}, u32[]{:S(2)}, u32[]{:S(2)}) collective-permute-start(bf16[1024,512]{1,0:T(8,128)(2,1)S(1)} %shard_map.72.columns_ref.near_columns_ref), channel_id=1, source_target_pairs={{0,1},{1,0},{2,3},{3,2},{4,5},{5,4},{6,7},{7,6},{8,9},{9,8},{10,11... | collective-permute-start | bytes 3145736 | tf_op jit(solution)/shard_map/ppermute | solution.py:38
  49.0 32.5 %collective-permute-start.10 = (bf16[544,512]{1,0:T(8,128)(2,1)S(1)}, bf16[544,512]{1,0:T(8,128)(2,1)S(1)}, u32[]{:S(2)}, u32[]{:S(2)}) collective-permute-start(bf16[544,512]{1,0:T(8,128)(2,1)S(1)} %shard_map.69.joined_ref), channel_id=1, source_target_pairs={{0,4},{8,12},{16,20},{24,28},{32,36},{40,44},{48,52},{56,60},{64,6... | collective-permute-start | bytes 1671176 | tf_op jit(solution)/shard_map/ppermute | solution.py:47
  50.9 32.5 %collective-permute-start.9 = (bf16[544,512]{1,0:T(8,128)(2,1)S(1)}, bf16[544,512]{1,0:T(8,128)(2,1)S(1)}, u32[]{:S(2)}, u32[]{:S(2)}) collective-permute-start(bf16[544,512]{1,0:T(8,128)(2,1)S(1)} %shard_map.69.joined_ref), channel_id=1, source_target_pairs={{4,8},{12,16},{20,24},{28,32},{36,40},{44,48},{52,56},{60,64},{68,... | collective-permute-start | bytes 1671176 | tf_op jit(solution)/shard_map/ppermute | solution.py:47
  66.5 21.4 %collective-permute-start.5 = (f32[4,1024]{1,0:T(4,128)S(1)}, f32[4,1024]{1,0:T(4,128)S(1)}, u32[]{:S(2)}, u32[]{:S(2)}) collective-permute-start(f32[4,1024]{1,0:T(4,128)S(1)} %get-tuple-element.47), channel_id=1, source_target_pairs={{4,8},{12,16},{20,24},{28,32},{36,40},{44,48},{52,56},{60,64},{68,... | collective-permute-start | bytes 49160 | tf_op jit(solution)/shard_map/ppermute | solution.py:47
  68.7 19.2 %collective-permute-start.6 = (f32[4,1024]{1,0:T(4,128)S(1)}, f32[4,1024]{1,0:T(4,128)S(1)}, u32[]{:S(2)}, u32[]{:S(2)}) collective-permute-start(f32[4,1024]{1,0:T(4,128)S(1)} %get-tuple-element.48), channel_id=1, source_target_pairs={{0,4},{8,12},{16,20},{24,28},{32,36},{40,44},{48,52},{56,60},{64,6... | collective-permute-start | bytes 49160 | tf_op jit(solution)/shard_map/ppermute | solution.py:47
  70.7 12.8 %collective-permute-start.7 = (f32[1,1024]{1,0:T(1,128)S(1)}, f32[1,1024]{1,0:T(1,128)S(1)}, u32[]{:S(2)}, u32[]{:S(2)}) collective-permute-start(f32[1,1024]{1,0:T(1,128)S(1)} %get-tuple-element.49), channel_id=1, source_target_pairs={{8,16},{12,20},{24,32},{28,36},{40,48},{44,52},{56,64},{60,68},{72... | collective-permute-start | bytes 12296 | tf_op jit(solution)/shard_map/ppermute | solution.py:47
  81.5 6.4 %collective-permute-start.8 = (f32[1,1024]{1,0:T(1,128)S(1)}, f32[1,1024]{1,0:T(1,128)S(1)}, u32[]{:S(2)}, u32[]{:S(2)}) collective-permute-start(f32[1,1024]{1,0:T(1,128)S(1)} %get-tuple-element.50), channel_id=1, source_target_pairs={{0,8},{4,12},{16,24},{20,28},{32,40},{36,44},{48,56},{52,60},{64,7... | collective-permute-start | bytes 12296 | tf_op jit(solution)/shard_map/ppermute | solution.py:47
  91.4 18.8 %collective-permute-start.15 = (bf16[1024,512]{1,0:T(8,128)(2,1)S(1)}, bf16[1024,512]{1,0:T(8,128)(2,1)S(1)}, u32[]{:S(2)}, u32[]{:S(2)}) collective-permute-start(bf16[1024,512]{1,0:T(8,128)(2,1)S(1)} %get-tuple-element.62.near_ref), channel_id=1, source_target_pairs={{0,1},{1,0},{2,3},{3,2},{4,5},{5,4},{6,7},{7,6},{8,9},{9,8},{10,11... | collective-permute-start | bytes 3145736 | tf_op jit(solution)/shard_map/ppermute | solution.py:38
  93.3 21.4 %collective-permute-start.11 = (f32[4,1024]{1,0:T(4,128)S(1)}, f32[4,1024]{1,0:T(4,128)S(1)}, u32[]{:S(2)}, u32[]{:S(2)}) collective-permute-start(f32[4,1024]{1,0:T(4,128)S(1)} %get-tuple-element.56), channel_id=1, source_target_pairs={{4,8},{12,16},{20,24},{28,32},{36,40},{44,48},{52,56},{60,64},{68,... | collective-permute-start | bytes 49160 | tf_op jit(solution)/shard_map/ppermute | solution.py:47
  97.6 17.1 %collective-permute-start.12 = (f32[4,1024]{1,0:T(4,128)S(1)}, f32[4,1024]{1,0:T(4,128)S(1)}, u32[]{:S(2)}, u32[]{:S(2)}) collective-permute-start(f32[4,1024]{1,0:T(4,128)S(1)} %get-tuple-element.57), channel_id=1, source_target_pairs={{0,4},{8,12},{16,20},{24,28},{32,36},{40,44},{48,52},{56,60},{64,6... | collective-permute-start | bytes 49160 | tf_op jit(solution)/shard_map/ppermute | solution.py:47
  99.5 12.3 %collective-permute-start.13 = (f32[1,1024]{1,0:T(1,128)S(1)}, f32[1,1024]{1,0:T(1,128)S(1)}, u32[]{:S(2)}, u32[]{:S(2)}) collective-permute-start(f32[1,1024]{1,0:T(1,128)S(1)} %get-tuple-element.58), channel_id=1, source_target_pairs={{8,16},{12,20},{24,32},{28,36},{40,48},{44,52},{56,64},{60,68},{72... | collective-permute-start | bytes 12296 | tf_op jit(solution)/shard_map/ppermute | solution.py:47
  108.3 6.4 %collective-permute-start.14 = (f32[1,1024]{1,0:T(1,128)S(1)}, f32[1,1024]{1,0:T(1,128)S(1)}, u32[]{:S(2)}, u32[]{:S(2)}) collective-permute-start(f32[1,1024]{1,0:T(1,128)S(1)} %get-tuple-element.59), channel_id=1, source_target_pairs={{0,8},{4,12},{16,24},{20,28},{32,40},{36,44},{48,56},{52,60},{64,7... | collective-permute-start | bytes 12296 | tf_op jit(solution)/shard_map/ppermute | solution.py:47

commit v5 on v4

--- a/solution.py
+++ b/solution.py
@@ -25,6 +25,7 @@
 INFO = 16
 MESSAGE = QUARTER + INFO
 JOINED = 2 * MESSAGE
+LETTER = HALF + MESSAGE
 
 NARROW, CORE, ODD, A_EVEN, HAS_ODD = range(5)
 
@@ -106,16 +107,40 @@
     lax.fori_loop(0, 4, step, 0)
 
 
-def pack_kernel(treated_ref, weight_ref, band_ref, message_ref, info_ref):
-    message_ref[0:QUARTER, :] = normalize(treated_ref[...])
+def pack_kernel(
+    flags, treated_any, control_any, weight_any, band_any, letter_ref, message_ref, treated_ref,
+    weight_ref, band_ref, info_ref, sems,
+):
+    half = pl.ds(pl.multiple_of(flags[CORE] * HALF, HALF), HALF)
+    copies = [
+        pltpu.make_async_copy(source, target, sems.at[i])
+        for i, (source, target) in enumerate(
+            (
+                (treated_any, treated_ref),
+                (weight_any, weight_ref),
+                (band_any, band_ref),
+                (control_any.at[half, :], letter_ref.at[0:HALF, :]),
+            )
+        )
+    ]
+    for copy in copies:
+        copy.start()
     info_ref[...] = jnp.zeros_like(info_ref)
+    for copy in copies[:3]:
+        copy.wait()
+    rows = normalize(treated_ref[...])
     weight = weight_ref[...]
     for i in range(3):
         part = weight.astype(BF16).astype(F32)
         info_ref[0:2, i * LANES : (i + 1) * LANES] = part
         weight = weight - part
     info_ref[0:2, 3 * LANES : 3 * LANES + 24] = band_ref[...].astype(F32)
-    message_ref[QUARTER:MESSAGE, :] = info_ref[...].astype(BF16)
+    info = info_ref[...].astype(BF16)
+    message_ref[0:QUARTER, :] = rows
+    message_ref[QUARTER:MESSAGE, :] = info
+    letter_ref[HALF : HALF + QUARTER, :] = rows
+    letter_ref[HALF + QUARTER : LETTER, :] = info
+    copies[3].wait()
 
 
 def join_kernel(own_ref, y_ref, joined_ref):
@@ -125,13 +150,28 @@
     joined_ref[HALF + INFO : JOINED, :] = y_ref[QUARTER:MESSAGE, :]
 
 
-def columns_kernel(control_ref, columns_ref):
-    columns_ref[...] = normalize(control_ref[...])
-
-
-def near_columns_kernel(odd_ref, even_ref, columns_ref):
-    columns_ref[0:HALF, :] = normalize(odd_ref[...])
-    columns_ref[HALF:SLAB, :] = normalize(even_ref[...])
+def columns_kernel(control_any, columns_ref, control_ref, sems):
+    copies = [
+        pltpu.make_async_copy(
+            control_any.at[i * QUARTER : (i + 1) * QUARTER, :],
+            control_ref.at[i * QUARTER : (i + 1) * QUARTER, :],
+            sems.at[i],
+        )
+        for i in range(4)
+    ]
+    for copy in copies:
+        copy.start()
+    for i, copy in enumerate(copies):
+        copy.wait()
+        at = slice(i * QUARTER, (i + 1) * QUARTER)
+        columns_ref[at, :] = normalize(control_ref[at, :])
+
+
+def open_kernel(odd_ref, even_ref, columns_ref, quarters_ref):
+    columns_ref[0:HALF, :] = normalize(odd_ref[0:HALF, :])
+    columns_ref[HALF:SLAB, :] = normalize(even_ref[0:HALF, :])
+    quarters_ref[0:QUARTER, :] = odd_ref[HALF : HALF + QUARTER, :]
+    quarters_ref[QUARTER:HALF, :] = even_ref[HALF : HALF + QUARTER, :]
 
 
 def near_kernel(rows_ref, columns_ref, mask_ref, before_ref, kernel_ref, sums_ref):
@@ -261,11 +301,13 @@
 
 def sweep_kernel(
     flags, partial_in, odd_in, even_in, a_in, b_in, own_weight, odd_weight, even_weight,
-    own_kernel_ref, near_kernel_ref, far_kernel_ref, weight_ref, odd_joined, even_joined, row_ref,
+    own_kernel_ref, near_kernel_ref, far_kernel_ref, weight_ref, quarters_in, quarters_y, row_ref,
     lane_ref, pair_ref, partial_ref, odd_ref, even_ref, a_ref, b_ref, flat_ref,
 ):
-    pair_ref[0:HALF, :] = odd_joined[0:HALF, :]
-    pair_ref[HALF:SLAB, :] = even_joined[0:HALF, :]
+    for i, ref in enumerate((quarters_in, quarters_y)):
+        for j in range(2):
+            at = j * HALF + i * QUARTER
+            pair_ref[at : at + QUARTER, :] = ref[j * QUARTER : (j + 1) * QUARTER, :]
     scales = column_scales(
         flags, partial_in, odd_in, even_in, a_in, b_in, (own_weight, odd_weight, even_weight)
     )
@@ -364,6 +406,7 @@
 
 
 VMEM = pl.BlockSpec(memory_space=pltpu.VMEM)
+HBM = pl.BlockSpec(memory_space=pltpu.HBM)
 SMEM = pl.BlockSpec(memory_space=pltpu.SMEM)
 
 
@@ -414,24 +457,37 @@
         for at in (wide_index, toward_odd, toward_even)
     ]
 
-    half = lax.dynamic_slice_in_dim(control, (n % 2) * HALF, HALF)
-    odd_control = exchange(half, 1, True)
-    even_control = exchange(half, 1, False)
-    (own_columns,) = call(columns_kernel, [VMEM], [((SLAB, WIDTH), BF16)], [control])
-
-    treated_weight, flags, *weights = lax.optimization_barrier((treated_weight, flags, *weights))
-    (message,) = call(
+    treated, control, own_weight, own_band = (
+        pltpu.with_memory_space_constraint(x, pltpu.HBM)
+        for x in (treated, control, treated_weight.reshape(2, LANES), band)
+    )
+    letter, message = call(
         pack_kernel,
-        [VMEM] * 3,
-        [((MESSAGE, WIDTH), BF16)],
-        [treated, treated_weight.reshape(2, LANES), band],
-        [pltpu.VMEM((INFO, WIDTH), F32)],
-    )
+        [SMEM] + [HBM] * 4,
+        [((LETTER, WIDTH), BF16), ((MESSAGE, WIDTH), BF16)],
+        [flags, treated, control, own_weight, own_band],
+        [
+            pltpu.VMEM((QUARTER, WIDTH), BF16),
+            pltpu.VMEM((2, LANES), F32),
+            pltpu.VMEM((2, 24), jnp.int32),
+            pltpu.VMEM((INFO, WIDTH), F32),
+            pltpu.SemaphoreType.DMA((4,)),
+        ],
+    )
+    odd_letter = exchange(letter, 1, True)
+    even_letter = exchange(letter, 1, False)
+    control, *weights = lax.optimization_barrier((control, *weights))
+    (own_columns,) = call(
+        columns_kernel,
+        [HBM],
+        [((SLAB, WIDTH), BF16)],
+        [pltpu.with_memory_space_constraint(control, pltpu.HBM)],
+        [pltpu.VMEM((SLAB, WIDTH), BF16), pltpu.SemaphoreType.DMA((4,))],
+    )
+
     message_y = narrow_swap(message, SWAP_Y)
     (joined,) = call(join_kernel, [VMEM] * 2, [((JOINED, WIDTH), BF16)], [message, message_y])
     joined_far = narrow_swap(joined, SWAP_CORE)
-    odd_joined = exchange(joined, 1, True)
-    even_joined = exchange(joined, 1, False)
 
     rows, own_kernel, sums, mask, weight, pairs = call(
         prepare_kernel,
@@ -447,11 +503,15 @@
         [flags, joined, joined_far, own_columns],
         [pltpu.VMEM((LANES, LANES), F32)],
     )
-    odd_control, even_control, _ = lax.optimization_barrier((odd_control, even_control, sums))
-    (near_columns,) = call(
-        near_columns_kernel, [VMEM] * 2, [((SLAB, WIDTH), BF16)], [odd_control, even_control]
+    odd_letter, even_letter, _ = lax.optimization_barrier((odd_letter, even_letter, sums))
+    near_columns, quarters = call(
+        open_kernel,
+        [VMEM] * 2,
+        [((SLAB, WIDTH), BF16), ((HALF, WIDTH), BF16)],
+        [odd_letter, even_letter],
     )
     far_columns = narrow_swap(near_columns, SWAP_CORE)
+    quarters_y = narrow_swap(quarters, SWAP_Y)
     near_values, sums = call(
         near_kernel,
         [VMEM] * 4,
@@ -472,7 +532,7 @@
         [((SLAB, LANES), F32), ((1, SLAB), F32), ((SLAB, WIDTH), BF16), ((8, SLAB), F32), *MESSAGES],
         [
             flags, partial, *first, *weights, own_kernel, near_values, far_values, weight,
-            odd_joined, even_joined,
+            quarters, quarters_y,
         ],
         [pltpu.VMEM((8, LANES), F32)],
     )

time: 119 us -> 105 us (0.88)
  starting transfers between devices: 70.6 us -> 62.1 us
  local copies, waits for them, and re-layouts: 5.34 us -> 0.73 us
  waiting for transfers between devices: 22.7 us -> 19.8 us
  Pallas kernels: 18.6 us -> 21.2 us
    ppermute x12 -> x10, starting transfers between devices: 62.2 us -> 50.8 us  [exchange(): return lax.ppermute(block, 'wide', both_ways(pairs, count))]
    ppermute x4 -> x5, waiting for transfers between devices: 7.63 us -> 0.01 us  [narrow_swap(): return lax.ppermute(block, 'narrow', pairs)]
    ppermute x12 -> x10, waiting for transfers between devices: 15 us -> 19.8 us  [exchange(): return lax.ppermute(block, 'wide', both_ways(pairs, count))]
    unnamed x8 -> x0, local copies, waits for them, and re-layouts: 3.53 us -> none
    ppermute x4 -> x5, starting transfers between devices: 8.41 us -> 11.3 us  [narrow_swap(): return lax.ppermute(block, 'narrow', pairs)]
    pallas_call x9, Pallas kernels: 15.1 us -> 17.8 us  [call(): pl.pallas_call(body, out_shape=tuple((jax.ShapeDtypeStruct(shape, dtype)...]
  transfers between devices with their start and end apart: 16 -> 15, of which waited for: 4 -> 3; matrix products, arithmetic and copies ran while one was open for 1% -> 1% of each run, Pallas kernels for 9% -> 12%
where the time goes in v5:
time: 105 us
  starting transfers between devices  62.1 us (59%)
  Pallas kernels  21.2 us (20%)
  waiting for transfers between devices  19.8 us (19%)
    ppermute x10, starting transfers between devices, exchange(): return lax.ppermute(block, 'wide', both_ways(pairs, count))  50.8 us
    ppermute x10, waiting for transfers between devices, exchange(): return lax.ppermute(block, 'wide', both_ways(pairs, count))  19.8 us
    pallas_call x9, Pallas kernels, call(): pl.pallas_call(body, out_shape=tuple((jax.ShapeDtypeStruct(shape, dtype)...  17.8 us
    ppermute x5, starting transfers between devices, narrow_swap(): return lax.ppermute(block, 'narrow', pairs)  11.3 us
    pallas_call x1, Pallas kernels, step(): pl.pallas_call(gradient_kernel, grid=(1,), out_shape=(jax.ShapeDtypeStruc...  3.42 us
  transfers between devices with their start and end apart: 15, of which 3 were waited for; matrix products, arithmetic and copies ran while one was open for 1% of the time, Pallas kernels for 12%

profile of v5, /device:TPU:24, one launch (start us, length us, event | category | flops | bytes accessed | tf_op | source)
XLA Modules:
  0.0 104.8 jit_solution(12068594962439825680)
XLA Ops:
  0.7 1.7 %shard_map.68 = (bf16[784,512]{1,0:T(8,128)(2,1)S(1)}, bf16[272,512]{1,0:T(8,128)(2,1)S(1)}) custom-call(s32[8]{0:T(128)S(1)} %compare_select_fusion.4.flags, bf16[256,512]{1,0:T(8,128)(2,1)} %treated_any.1, bf16[1024,512]{1,0:T(8,128)(2,1)} %control_any.2, f32[2,128]{1,0:T(2,128)} %bitcast.10, s32[2,24]{1,0:T(2,128)} %band_any.1), custom_call_target="tpu_custom_call" | custom-call | tf_op jit(solution)/shard_map/pallas_call | solution.py:414
  2.4 2.7 %collective-permute-start = (bf16[272,512]{1,0:T(8,128)(2,1)S(1)}, bf16[272,512]{1,0:T(8,128)(2,1)S(1)}, u32[]{:S(2)}, u32[]{:S(2)}) collective-permute-start(bf16[272,512]{1,0:T(8,128)(2,1)S(1)} %get-tuple-element.37.own_ref), channel_id=1, source_target_pairs={{0,2},{2,0},{1,3},{3,1},{4,6},{6,4},{5,7},{7,5},{8,10},{10,8},{9,1... | collective-permute-start | bytes 835592 | tf_op jit(solution)/shard_map/ppermute | solution.py:39
  5.1 3.8 %collective-permute-start.3 = (bf16[784,512]{1,0:T(8,128)(2,1)S(1)}, bf16[784,512]{1,0:T(8,128)(2,1)S(1)}, u32[]{:S(2)}, u32[]{:S(2)}) collective-permute-start(bf16[784,512]{1,0:T(8,128)(2,1)S(1)} %get-tuple-element.40), channel_id=1, source_target_pairs={{0,4},{8,12},{16,20},{24,28},{32,36},{40,44},{48,52},{56,60},{64,6... | collective-permute-start | bytes 2408456 | tf_op jit(solution)/shard_map/ppermute | solution.py:48
  8.9 13.1 %collective-permute-start.2 = (bf16[784,512]{1,0:T(8,128)(2,1)S(1)}, bf16[784,512]{1,0:T(8,128)(2,1)S(1)}, u32[]{:S(2)}, u32[]{:S(2)}) collective-permute-start(bf16[784,512]{1,0:T(8,128)(2,1)S(1)} %get-tuple-element.40), channel_id=1, source_target_pairs={{4,8},{12,16},{20,24},{28,32},{36,40},{44,48},{52,56},{60,64},{68,... | collective-permute-start | bytes 2408456 | tf_op jit(solution)/shard_map/ppermute | solution.py:48
  22.0 0.0 collective-permute-done.y_ref
  22.1 1.9 %collective-permute-start.1 = (bf16[544,512]{1,0:T(8,128)(2,1)S(1)}, bf16[544,512]{1,0:T(8,128)(2,1)S(1)}, u32[]{:S(2)}, u32[]{:S(2)}) collective-permute-start(bf16[544,512]{1,0:T(8,128)(2,1)S(1)} %shard_map.69.joined_ref), channel_id=1, source_target_pairs={{0,1},{1,0},{2,3},{3,2},{4,5},{5,4},{6,7},{7,6},{8,9},{9,8},{10,11... | collective-permute-start | bytes 1671176 | tf_op jit(solution)/shard_map/ppermute | solution.py:39
  24.0 0.7 fusion
  24.7 1.5 %shard_map.70.columns_ref.own_columns_ref = bf16[1024,512]{1,0:T(8,128)(2,1)S(1)} custom-call(bf16[1024,512]{1,0:T(8,128)(2,1)} %control_any.2), custom_call_target="tpu_custom_call" | custom-call | tf_op jit(solution)/shard_map/pallas_call | solution.py:414
  26.3 0.0 collective-permute-done.1.far_ref
  26.3 3.0 %shard_map.71 = (bf16[1024,512]{1,0:T(8,128)(2,1)S(1)}, f32[1024,1024]{1,0:T(8,128)S(1)}, f32[1024,128]{1,0:T(8,128)S(1)}, f32[8,3072]{1,0:T(8,128)S(1)}, f32[10...) custom-call(s32[8]{0:T(128)S(1)} %compare_select_fusion.4.flags, bf16[544,512]{1,0:T(8,128)(2,1)S(1)} %shard_map.69.joined_ref, ...), custom_call_target="tpu_custom_call" | custom-call | tf_op jit(solution)/shard_map/pallas_call | solution.py:414
  29.2 0.0 collective-permute-done.3.even_ref
  29.2 10.2 %collective-permute-done.2.odd_ref = bf16[784,512]{1,0:T(8,128)(2,1)S(1)} collective-permute-done((bf16[784,512]{1,0:T(8,128)(2,1)S(1)}, bf16[784,512]{1,0:T(8,128)(2,1)S(1)}, u32[]{:S(2)}, u32[]{:S(2)}) %collective-permute-start.2) | collective-permute-done | bytes 802848 | tf_op jit(solution)/shard_map/ppermute | solution.py:48
  39.4 0.4 shard_map.72
  39.8 1.9 %collective-permute-start.4 = (bf16[1024,512]{1,0:T(8,128)(2,1)S(1)}, bf16[1024,512]{1,0:T(8,128)(2,1)S(1)}, u32[]{:S(2)}, u32[]{:S(2)}) collective-permute-start(bf16[1024,512]{1,0:T(8,128)(2,1)S(1)} %get-tuple-element.44.columns_ref.near_columns_ref), channel_id=1, source_target_pairs={{0,1},{1,0},{2,3},{3,2},{4,5},{5,4},{6,7},{7,6},{8,9},{9,8},{10,11... | collective-permute-start | bytes 3145736 | tf_op jit(solution)/shard_map/ppermute | solution.py:39
  41.7 2.9 %collective-permute-start.9 = (bf16[512,512]{1,0:T(8,128)(2,1)S(1)}, bf16[512,512]{1,0:T(8,128)(2,1)S(1)}, u32[]{:S(2)}, u32[]{:S(2)}) collective-permute-start(bf16[512,512]{1,0:T(8,128)(2,1)S(1)} %get-tuple-element.60.quarters_in), channel_id=1, source_target_pairs={{0,2},{2,0},{1,3},{3,1},{4,6},{6,4},{5,7},{7,5},{8,10},{10,8},{9,1... | collective-permute-start | bytes 1572872 | tf_op jit(solution)/shard_map/ppermute | solution.py:39
  44.6 2.1 %shard_map.73 = (f32[1024,1024]{1,0:T(8,128)S(1)}, f32[1024,128]{1,0:T(8,128)S(1)}) custom-call(bf16[1024,512]{1,0:T(8,128)(2,1)S(1)} %get-tuple-element.39.rows_ref, bf16[1024,512]{1,0:T(8,128)(2,1)S(1)} %get-tuple-element.44.columns_ref.near_columns_ref, f32[8,3072]{1,0:T(8,128)S(1)} %get-tuple-element.45.mask_ref, ...), custom_call_target="tpu_custom_call" | custom-call | tf_op jit(solution)/shard_map/pallas_call | solution.py:414
  46.7 0.0 collective-permute-done.4.columns_ref.far_columns_ref
  46.7 4.1 %shard_map.74 = (f32[1024,1024]{1,0:T(8,128)S(1)}, f32[8,1024]{1,0:T(8,128)S(1)}, f32[4,1024]{1,0:T(4,128)S(1)}, f32[4,1024]{1,0:T(4,128)S(1)}, f32[1,1024]{1,0:T(1,128)S(1)}, /*index=5*/f32[1,1024]{1,0:T(1,128)S(1)}) custom-call(s32[8]{0:T(128)S(1)} %compare_select_fusion.4.flags, bf16[1024,512]{1,0:T(8,128)(2,1)S(1)} %get-tuple-element.39.rows_ref, ...), custom_call_target="tpu_custom_call" | custom-call | tf_op jit(solution)/shard_map/pallas_call | solution.py:414
  50.8 9.9 %collective-permute-start.5 = (f32[4,1024]{1,0:T(4,128)S(1)}, f32[4,1024]{1,0:T(4,128)S(1)}, u32[]{:S(2)}, u32[]{:S(2)}) collective-permute-start(f32[4,1024]{1,0:T(4,128)S(1)} %get-tuple-element.52), channel_id=1, source_target_pairs={{4,8},{12,16},{20,24},{28,32},{36,40},{44,48},{52,56},{60,64},{68,... | collective-permute-start | bytes 49160 | tf_op jit(solution)/shard_map/ppermute | solution.py:48
  60.6 1.9 %collective-permute-start.6 = (f32[4,1024]{1,0:T(4,128)S(1)}, f32[4,1024]{1,0:T(4,128)S(1)}, u32[]{:S(2)}, u32[]{:S(2)}) collective-permute-start(f32[4,1024]{1,0:T(4,128)S(1)} %get-tuple-element.53), channel_id=1, source_target_pairs={{0,4},{8,12},{16,20},{24,28},{32,36},{40,44},{48,52},{56,60},{64,6... | collective-permute-start | bytes 49160 | tf_op jit(solution)/shard_map/ppermute | solution.py:48
  62.6 3.4 %collective-permute-start.7 = (f32[1,1024]{1,0:T(1,128)S(1)}, f32[1,1024]{1,0:T(1,128)S(1)}, u32[]{:S(2)}, u32[]{:S(2)}) collective-permute-start(f32[1,1024]{1,0:T(1,128)S(1)} %get-tuple-element.54), channel_id=1, source_target_pairs={{8,16},{12,20},{24,32},{28,36},{40,48},{44,52},{56,64},{60,68},{72... | collective-permute-start | bytes 12296 | tf_op jit(solution)/shard_map/ppermute | solution.py:48
  66.0 1.9 %collective-permute-start.8 = (f32[1,1024]{1,0:T(1,128)S(1)}, f32[1,1024]{1,0:T(1,128)S(1)}, u32[]{:S(2)}, u32[]{:S(2)}) collective-permute-start(f32[1,1024]{1,0:T(1,128)S(1)} %get-tuple-element.55), channel_id=1, source_target_pairs={{0,8},{4,12},{16,24},{20,28},{32,40},{36,44},{48,56},{52,60},{64,7... | collective-permute-start | bytes 12296 | tf_op jit(solution)/shard_map/ppermute | solution.py:48
  67.9 0.0 collective-permute-done.9.quarters_y
  67.9 6.8 %collective-permute-done.7.a_in = f32[1,1024]{1,0:T(1,128)S(1)} collective-permute-done((f32[1,1024]{1,0:T(1,128)S(1)}, f32[1,1024]{1,0:T(1,128)S(1)}, u32[]{:S(2)}, u32[]{:S(2)}) %collective-permute-start.7) | collective-permute-done | bytes 4128 | tf_op jit(solution)/shard_map/ppermute | solution.py:48
  74.7 0.0 collective-permute-done.8.b_in
  74.7 0.0 collective-permute-done.5.odd_in
  74.7 0.0 collective-permute-done.6.even_in
  74.7 3.4 %shard_map.75 = (f32[1024,128]{1,0:T(8,128)S(1)}, f32[1,1024]{1,0:T(1,128)S(1)}, bf16[1024,512]{1,0:T(8,128)(2,1)S(1)}, f32[8,1024]{1,0:T(8,128)S(1)}, f32[4,102...) custom-call(s32[8]{0:T(128)S(1)} %compare_select_fusion.4.flags, ...), custom_call_target="tpu_custom_call" | custom-call | tf_op jit(solution)/shard_map/pallas_call | solution.py:414
  78.1 1.9 %collective-permute-start.14 = (bf16[1024,512]{1,0:T(8,128)(2,1)S(1)}, bf16[1024,512]{1,0:T(8,128)(2,1)S(1)}, u32[]{:S(2)}, u32[]{:S(2)}) collective-permute-start(bf16[1024,512]{1,0:T(8,128)(2,1)S(1)} %get-tuple-element.68.near_ref), channel_id=1, source_target_pairs={{0,1},{1,0},{2,3},{3,2},{4,5},{5,4},{6,7},{7,6},{8,9},{9,8},{10,11... | collective-permute-start | bytes 3145736 | tf_op jit(solution)/shard_map/ppermute | solution.py:39
  80.0 7.3 %collective-permute-start.10 = (f32[4,1024]{1,0:T(4,128)S(1)}, f32[4,1024]{1,0:T(4,128)S(1)}, u32[]{:S(2)}, u32[]{:S(2)}) collective-permute-start(f32[4,1024]{1,0:T(4,128)S(1)} %get-tuple-element.62), channel_id=1, source_target_pairs={{4,8},{12,16},{20,24},{28,32},{36,40},{44,48},{52,56},{60,64},{68,... | collective-permute-start | bytes 49160 | tf_op jit(solution)/shard_map/ppermute | solution.py:48
  87.3 1.9 %collective-permute-start.11 = (f32[4,1024]{1,0:T(4,128)S(1)}, f32[4,1024]{1,0:T(4,128)S(1)}, u32[]{:S(2)}, u32[]{:S(2)}) collective-permute-start(f32[4,1024]{1,0:T(4,128)S(1)} %get-tuple-element.63), channel_id=1, source_target_pairs={{0,4},{8,12},{16,20},{24,28},{32,36},{40,44},{48,52},{56,60},{64,6... | collective-permute-start | bytes 49160 | tf_op jit(solution)/shard_map/ppermute | solution.py:48
  89.3 5.7 %collective-permute-start.12 = (f32[1,1024]{1,0:T(1,128)S(1)}, f32[1,1024]{1,0:T(1,128)S(1)}, u32[]{:S(2)}, u32[]{:S(2)}) collective-permute-start(f32[1,1024]{1,0:T(1,128)S(1)} %get-tuple-element.64), channel_id=1, source_target_pairs={{8,16},{12,20},{24,32},{28,36},{40,48},{44,52},{56,64},{60,68},{72... | collective-permute-start | bytes 12296 | tf_op jit(solution)/shard_map/ppermute | solution.py:48
  95.0 1.9 %collective-permute-start.13 = (f32[1,1024]{1,0:T(1,128)S(1)}, f32[1,1024]{1,0:T(1,128)S(1)}, u32[]{:S(2)}, u32[]{:S(2)}) collective-permute-start(f32[1,1024]{1,0:T(1,128)S(1)} %get-tuple-element.65), channel_id=1, source_target_pairs={{0,8},{4,12},{16,24},{20,28},{32,40},{36,44},{48,56},{52,60},{64,7... | collective-permute-start | bytes 12296 | tf_op jit(solution)/shard_map/ppermute | solution.py:48
  96.9 0.0 collective-permute-done.14.far_ref
  96.9 1.6 %shard_map.76 = (bf16[1024,512]{1,0:T(8,128)(2,1)S(1)}, bf16[1024,512]{1,0:T(8,128)(2,1)S(1)}, f32[256,3072]{1,0:T(8,128)S(1)}) custom-call(s32[8]{0:T(128)S(1)} %compare_select_fusion.4.flags, bf16[1024,512]{1,0:T(8,128)(2,1)S(1)} %shard_map.70.columns_ref.own_columns_ref, bf16[1024,512]{1,0:T(8,128)(2,1)S(1)} %get-tuple-element.39.rows_ref, ...), custom_call_target="tpu_custom_call" | custom-call | tf_op jit(solution)/shard_map/pallas_call | solution.py:414
  98.6 2.8 %collective-permute-done.12.a_in = f32[1,1024]{1,0:T(1,128)S(1)} collective-permute-done((f32[1,1024]{1,0:T(1,128)S(1)}, f32[1,1024]{1,0:T(1,128)S(1)}, u32[]{:S(2)}, u32[]{:S(2)}) %collective-permute-start.12) | collective-permute-done | bytes 4128 | tf_op jit(solution)/shard_map/ppermute | solution.py:48
  101.4 0.0 collective-permute-done.13.b_in
  101.4 0.0 collective-permute-done.10.odd_in
  101.4 0.0 collective-permute-done.11.even_in
  101.4 3.4 %gradient_kernel.1 = (f32[256,512]{1,0:T(8,128)}, f32[256,512]{1,0:T(8,128)}) custom-call(s32[8]{0:T(128)S(1)} %compare_select_fusion.4.flags, f32[8,1024]{1,0:T(8,128)S(1)} %get-tuple-element.61.partial_in, f32[4,1024]{1,0:T(4,128)S(1)} %collective-permute-done.10.odd_in, f32[4,1024]{1,0:T(4,128)S(1)} %collective-permute-done.11.even_in, ...), custom_call_target="tpu_custom_call" | custom-call | tf_op jit(solution)/shard_map/gradient_kernel/pallas_call | solution.py:551
  (2 shorter events, 0.0 us)
Async XLA Ops:
  2.4 19.6 %collective-permute-start = (bf16[272,512]{1,0:T(8,128)(2,1)S(1)}, bf16[272,512]{1,0:T(8,128)(2,1)S(1)}, u32[]{:S(2)}, u32[]{:S(2)}) collective-permute-start(bf16[272,512]{1,0:T(8,128)(2,1)S(1)} %get-tuple-element.37.own_ref), channel_id=1, source_target_pairs={{0,2},{2,0},{1,3},{3,1},{4,6},{6,4},{5,7},{7,5},{8,10},{10,8},{9,1... | collective-permute-start | bytes 835592 | tf_op jit(solution)/shard_map/ppermute | solution.py:39
  5.1 24.2 %collective-permute-start.3 = (bf16[784,512]{1,0:T(8,128)(2,1)S(1)}, bf16[784,512]{1,0:T(8,128)(2,1)S(1)}, u32[]{:S(2)}, u32[]{:S(2)}) collective-permute-start(bf16[784,512]{1,0:T(8,128)(2,1)S(1)} %get-tuple-element.40), channel_id=1, source_target_pairs={{0,4},{8,12},{16,20},{24,28},{32,36},{40,44},{48,52},{56,60},{64,6... | collective-permute-start | bytes 2408456 | tf_op jit(solution)/shard_map/ppermute | solution.py:48
  8.9 30.5 %collective-permute-start.2 = (bf16[784,512]{1,0:T(8,128)(2,1)S(1)}, bf16[784,512]{1,0:T(8,128)(2,1)S(1)}, u32[]{:S(2)}, u32[]{:S(2)}) collective-permute-start(bf16[784,512]{1,0:T(8,128)(2,1)S(1)} %get-tuple-element.40), channel_id=1, source_target_pairs={{4,8},{12,16},{20,24},{28,32},{36,40},{44,48},{52,56},{60,64},{68,... | collective-permute-start | bytes 2408456 | tf_op jit(solution)/shard_map/ppermute | solution.py:48
  22.1 4.2 %collective-permute-start.1 = (bf16[544,512]{1,0:T(8,128)(2,1)S(1)}, bf16[544,512]{1,0:T(8,128)(2,1)S(1)}, u32[]{:S(2)}, u32[]{:S(2)}) collective-permute-start(bf16[544,512]{1,0:T(8,128)(2,1)S(1)} %shard_map.69.joined_ref), channel_id=1, source_target_pairs={{0,1},{1,0},{2,3},{3,2},{4,5},{5,4},{6,7},{7,6},{8,9},{9,8},{10,11... | collective-permute-start | bytes 1671176 | tf_op jit(solution)/shard_map/ppermute | solution.py:39
  39.8 6.9 %collective-permute-start.4 = (bf16[1024,512]{1,0:T(8,128)(2,1)S(1)}, bf16[1024,512]{1,0:T(8,128)(2,1)S(1)}, u32[]{:S(2)}, u32[]{:S(2)}) collective-permute-start(bf16[1024,512]{1,0:T(8,128)(2,1)S(1)} %get-tuple-element.44.columns_ref.near_columns_ref), channel_id=1, source_target_pairs={{0,1},{1,0},{2,3},{3,2},{4,5},{5,4},{6,7},{7,6},{8,9},{9,8},{10,11... | collective-permute-start | bytes 3145736 | tf_op jit(solution)/shard_map/ppermute | solution.py:39
  41.7 26.2 %collective-permute-start.9 = (bf16[512,512]{1,0:T(8,128)(2,1)S(1)}, bf16[512,512]{1,0:T(8,128)(2,1)S(1)}, u32[]{:S(2)}, u32[]{:S(2)}) collective-permute-start(bf16[512,512]{1,0:T(8,128)(2,1)S(1)} %get-tuple-element.60.quarters_in), channel_id=1, source_target_pairs={{0,2},{2,0},{1,3},{3,1},{4,6},{6,4},{5,7},{7,5},{8,10},{10,8},{9,1... | collective-permute-start | bytes 1572872 | tf_op jit(solution)/shard_map/ppermute | solution.py:39
  50.8 23.9 %collective-permute-start.5 = (f32[4,1024]{1,0:T(4,128)S(1)}, f32[4,1024]{1,0:T(4,128)S(1)}, u32[]{:S(2)}, u32[]{:S(2)}) collective-permute-start(f32[4,1024]{1,0:T(4,128)S(1)} %get-tuple-element.52), channel_id=1, source_target_pairs={{4,8},{12,16},{20,24},{28,32},{36,40},{44,48},{52,56},{60,64},{68,... | collective-permute-start | bytes 49160 | tf_op jit(solution)/shard_map/ppermute | solution.py:48
  60.6 14.1 %collective-permute-start.6 = (f32[4,1024]{1,0:T(4,128)S(1)}, f32[4,1024]{1,0:T(4,128)S(1)}, u32[]{:S(2)}, u32[]{:S(2)}) collective-permute-start(f32[4,1024]{1,0:T(4,128)S(1)} %get-tuple-element.53), channel_id=1, source_target_pairs={{0,4},{8,12},{16,20},{24,28},{32,36},{40,44},{48,52},{56,60},{64,6... | collective-permute-start | bytes 49160 | tf_op jit(solution)/shard_map/ppermute | solution.py:48
  62.6 12.1 %collective-permute-start.7 = (f32[1,1024]{1,0:T(1,128)S(1)}, f32[1,1024]{1,0:T(1,128)S(1)}, u32[]{:S(2)}, u32[]{:S(2)}) collective-permute-start(f32[1,1024]{1,0:T(1,128)S(1)} %get-tuple-element.54), channel_id=1, source_target_pairs={{8,16},{12,20},{24,32},{28,36},{40,48},{44,52},{56,64},{60,68},{72... | collective-permute-start | bytes 12296 | tf_op jit(solution)/shard_map/ppermute | solution.py:48
  66.0 8.7 %collective-permute-start.8 = (f32[1,1024]{1,0:T(1,128)S(1)}, f32[1,1024]{1,0:T(1,128)S(1)}, u32[]{:S(2)}, u32[]{:S(2)}) collective-permute-start(f32[1,1024]{1,0:T(1,128)S(1)} %get-tuple-element.55), channel_id=1, source_target_pairs={{0,8},{4,12},{16,24},{20,28},{32,40},{36,44},{48,56},{52,60},{64,7... | collective-permute-start | bytes 12296 | tf_op jit(solution)/shard_map/ppermute | solution.py:48
  78.1 18.8 %collective-permute-start.14 = (bf16[1024,512]{1,0:T(8,128)(2,1)S(1)}, bf16[1024,512]{1,0:T(8,128)(2,1)S(1)}, u32[]{:S(2)}, u32[]{:S(2)}) collective-permute-start(bf16[1024,512]{1,0:T(8,128)(2,1)S(1)} %get-tuple-element.68.near_ref), channel_id=1, source_target_pairs={{0,1},{1,0},{2,3},{3,2},{4,5},{5,4},{6,7},{7,6},{8,9},{9,8},{10,11... | collective-permute-start | bytes 3145736 | tf_op jit(solution)/shard_map/ppermute | solution.py:39
  80.0 21.4 %collective-permute-start.10 = (f32[4,1024]{1,0:T(4,128)S(1)}, f32[4,1024]{1,0:T(4,128)S(1)}, u32[]{:S(2)}, u32[]{:S(2)}) collective-permute-start(f32[4,1024]{1,0:T(4,128)S(1)} %get-tuple-element.62), channel_id=1, source_target_pairs={{4,8},{12,16},{20,24},{28,32},{36,40},{44,48},{52,56},{60,64},{68,... | collective-permute-start | bytes 49160 | tf_op jit(solution)/shard_map/ppermute | solution.py:48
  87.3 14.1 %collective-permute-start.11 = (f32[4,1024]{1,0:T(4,128)S(1)}, f32[4,1024]{1,0:T(4,128)S(1)}, u32[]{:S(2)}, u32[]{:S(2)}) collective-permute-start(f32[4,1024]{1,0:T(4,128)S(1)} %get-tuple-element.63), channel_id=1, source_target_pairs={{0,4},{8,12},{16,20},{24,28},{32,36},{40,44},{48,52},{56,60},{64,6... | collective-permute-start | bytes 49160 | tf_op jit(solution)/shard_map/ppermute | solution.py:48
  89.3 12.1 %collective-permute-start.12 = (f32[1,1024]{1,0:T(1,128)S(1)}, f32[1,1024]{1,0:T(1,128)S(1)}, u32[]{:S(2)}, u32[]{:S(2)}) collective-permute-start(f32[1,1024]{1,0:T(1,128)S(1)} %get-tuple-element.64), channel_id=1, source_target_pairs={{8,16},{12,20},{24,32},{28,36},{40,48},{44,52},{56,64},{60,68},{72... | collective-permute-start | bytes 12296 | tf_op jit(solution)/shard_map/ppermute | solution.py:48
  95.0 6.4 %collective-permute-start.13 = (f32[1,1024]{1,0:T(1,128)S(1)}, f32[1,1024]{1,0:T(1,128)S(1)}, u32[]{:S(2)}, u32[]{:S(2)}) collective-permute-start(f32[1,1024]{1,0:T(1,128)S(1)} %get-tuple-element.65), channel_id=1, source_target_pairs={{0,8},{4,12},{16,24},{20,28},{32,40},{36,44},{48,56},{52,60},{64,7... | collective-permute-start | bytes 12296 | tf_op jit(solution)/shard_map/ppermute | solution.py:48

commit v6 on v5

--- a/solution.py
+++ b/solution.py
@@ -46,6 +46,22 @@
         (base + i, base + i + hops) for base in range(first, count, 2 * hops) for i in range(hops)
     ]
     return lax.ppermute(block, "wide", both_ways(pairs, count))
+
+
+def split_exchange(block, crossing):
+    count = lax.axis_size("wide")
+    narrow = lax.axis_size("narrow")
+    pairs = []
+    for n in range(narrow):
+        hops = 1 + n % 2
+        first = hops if crossing else 0
+        one = [
+            (base + i, base + i + hops)
+            for base in range(first, count, 2 * hops)
+            for i in range(hops)
+        ]
+        pairs += [(a * narrow + n, b * narrow + n) for a, b in both_ways(one, count)]
+    return lax.ppermute(block, ("wide", "narrow"), pairs)
 
 
 def normalize(features):
@@ -184,7 +200,7 @@
     flags, joined_ref, far_ref, columns_ref, rows_ref, kernel_ref, sums_ref, mask_ref, weight_ref,
     pair_ref, band_ref,
 ):
-    n, odd = flags[NARROW], flags[ODD]
+    n, odd, core = flags[NARROW], flags[ODD], flags[CORE]
     rows_ref[0:HALF, :] = joined_ref[0:HALF, :]
     rows_ref[HALF:SLAB, :] = far_ref[0:HALF, :]
 
@@ -203,7 +219,6 @@
     even_base = 16 - odd * 16
     lane = lax.broadcasted_iota(jnp.int32, (1, 3 * SLAB), 1)
     segment = lane // SLAB
-    core = flags[CORE]
     side = jnp.where(lane % SLAB < HALF, odd_base, even_base)
     side = side + 4 * jnp.where(segment == 1, core, 1 - core) + (lane % HALF) // LANES
     wanted = jnp.where(segment == 0, 8 + lane // LANES, side)
@@ -212,8 +227,10 @@
         band[:16], jnp.where(one_hot, 1.0, 0.0).astype(BF16), preferred_element_type=F32
     )[:8]
     place = lax.broadcasted_iota(jnp.int32, (16, LANES), 0)
-    base = jnp.where(place < 2, 8, jnp.where(place < 4, odd_base, even_base))
-    chosen = base + 2 * n + place % 2
+    base = jnp.where(place < 2, 8, jnp.where(place < 6, odd_base, even_base))
+    other = (place == 4) | (place == 5) | (place == 8) | (place == 9)
+    quarter = n + jnp.where(other, 1 - 2 * core, 0)
+    chosen = base + 2 * quarter + place % 2
     select = jnp.where(
         lax.broadcasted_iota(jnp.int32, (16, LANES), 1) == chosen, 1.0, 0.0
     ).astype(BF16)
@@ -224,7 +241,7 @@
     )
     pair_ref[...] = jnp.dot(
         by_block, jnp.where(spread, 1.0, 0.0).astype(BF16), preferred_element_type=F32
-    )[:8]
+    )
 
     fill_kernel(rows_ref, columns_ref, mask_ref, slice(0, SLAB), kernel_ref, sums_ref, None)
 
@@ -236,31 +253,47 @@
     return jnp.where(swap, high, low), jnp.where(swap, low, high)
 
 
-def finish_messages(flags, sums, first, second, partial_ref, odd_ref, even_ref, a_ref, b_ref):
+def finish_messages(flags, sums, first, second, partial_ref, cross_ref, inner_ref):
     own, near, far = (jnp.sum(part, axis=0, keepdims=True) for part in sums)
-    swap = flags[CORE] > 0
-    low = jnp.where(swap, far, near)
-    high = jnp.where(swap, near, far)
+    one = flags[CORE] > 0
+    low = jnp.where(one, far, near)
+    high = jnp.where(one, near, far)
     odd = jnp.concatenate([low[:, :HALF], high[:, :HALF]], axis=1)
     even = jnp.concatenate([low[:, HALF:], high[:, HALF:]], axis=1)
     partial_ref[...] = jnp.zeros_like(partial_ref)
     partial_ref[0:1, :] = own
     partial_ref[1:2, :] = odd
     partial_ref[2:3, :] = even
-    odd_ref[0:1, :] = own
-    odd_ref[1:2, :] = odd
-    odd_ref[2:4, :] = first
-    even_ref[0:1, :] = own
-    even_ref[1:2, :] = even
-    even_ref[2:4, :] = second
     a_even = flags[A_EVEN] > 0
-    a_ref[...] = jnp.where(a_even, even, odd)
-    b_ref[...] = jnp.where(a_even, odd, even)
+    for ref, side, along, distant in (
+        (cross_ref, odd, first, jnp.where(a_even, even, odd)),
+        (inner_ref, even, second, jnp.where(a_even, odd, even)),
+    ):
+        ref[...] = jnp.zeros_like(ref)
+        ref[0:1, :] = jnp.where(one, distant, own)
+        ref[1:2, :] = side
+        ref[2 : 2 + along.shape[0], :] = along
+
+
+def stack_kernel(cross_ref, inner_ref, both_ref):
+    both_ref[0:8, :] = cross_ref[...]
+    both_ref[8:16, :] = inner_ref[...]
+
+
+def received(flags, mine_ref, theirs_ref):
+    one = flags[CORE] > 0
+    mine, theirs = mine_ref[...], theirs_ref[...]
+    return jnp.where(one, theirs, mine), jnp.where(one, mine, theirs)
+
+
+def turned(flags, rows):
+    swapped = jnp.concatenate([rows[:, HALF:], rows[:, :HALF]], axis=1)
+    return jnp.where(flags[CORE] > 0, swapped, rows)
 
 
 def far_kernel(
     flags, rows_ref, columns_ref, mask_ref, own_kernel_ref, near_kernel_ref, before_ref,
-    weight_ref, pair_ref, kernel_ref, partial_ref, odd_ref, even_ref, a_ref, b_ref,
+    weight_ref, pair_ref, kernel_ref, partial_ref, cross_ref, inner_ref,
 ):
     def step(i, carry):
         own, near, far = carry
@@ -280,18 +313,17 @@
     zero = jnp.zeros((8, SLAB), F32)
     sums = lax.fori_loop(0, 4, step, (zero, zero, zero))
     finish_messages(
-        flags, sums, pair_ref[2:4, :], pair_ref[4:6, :], partial_ref, odd_ref, even_ref, a_ref,
-        b_ref,
-    )
-
-
-def column_scales(flags, partial_ref, odd_ref, even_ref, a_ref, b_ref, weights):
+        flags, sums, pair_ref[2:6, :], pair_ref[6:10, :], partial_ref, cross_ref, inner_ref
+    )
+
+
+def column_scales(flags, partial_ref, mine_ref, theirs_ref, weights):
     a_even = flags[A_EVEN] > 0
-    two_odd = jnp.where(a_even, b_ref[...], a_ref[...])
-    two_even = jnp.where(a_even, a_ref[...], b_ref[...])
-    own = partial_ref[0:1, :] + odd_ref[1:2, :] + even_ref[1:2, :]
-    odd = partial_ref[1:2, :] + odd_ref[0:1, :] + two_odd
-    even = partial_ref[2:3, :] + even_ref[0:1, :] + two_even
+    close, distant = received(flags, mine_ref, theirs_ref)
+    a, b = distant[0:1], distant[8:9]
+    own = partial_ref[0:1, :] + close[1:2] + close[9:10]
+    odd = partial_ref[1:2, :] + close[0:1] + jnp.where(a_even, b, a)
+    even = partial_ref[2:3, :] + close[8:9] + jnp.where(a_even, a, b)
     has_odd = flags[HAS_ODD] > 0
     own_weight, odd_weight, even_weight = (ref[...] for ref in weights)
     odd = jnp.where(has_odd, odd_weight / jnp.where(has_odd, odd, 1.0), 0.0)
@@ -300,16 +332,12 @@
 
 
 def sweep_kernel(
-    flags, partial_in, odd_in, even_in, a_in, b_in, own_weight, odd_weight, even_weight,
-    own_kernel_ref, near_kernel_ref, far_kernel_ref, weight_ref, quarters_in, quarters_y, row_ref,
-    lane_ref, pair_ref, partial_ref, odd_ref, even_ref, a_ref, b_ref, flat_ref,
+    flags, partial_in, mine_in, theirs_in, own_weight, odd_weight, even_weight, own_kernel_ref,
+    near_kernel_ref, far_kernel_ref, weight_ref, row_ref, lane_ref, partial_ref, cross_ref,
+    inner_ref, flat_ref,
 ):
-    for i, ref in enumerate((quarters_in, quarters_y)):
-        for j in range(2):
-            at = j * HALF + i * QUARTER
-            pair_ref[at : at + QUARTER, :] = ref[j * QUARTER : (j + 1) * QUARTER, :]
     scales = column_scales(
-        flags, partial_in, odd_in, even_in, a_in, b_in, (own_weight, odd_weight, even_weight)
+        flags, partial_in, mine_in, theirs_in, (own_weight, odd_weight, even_weight)
     )
     kernels = (own_kernel_ref, near_kernel_ref, far_kernel_ref)
 
@@ -330,12 +358,19 @@
     sums = lax.fori_loop(0, 8, step, (zero, zero, zero))
     for i in range(8):
         lane_ref[0:1, i * LANES : (i + 1) * LANES] = flat_ref[i : i + 1, :]
-    flat = jnp.broadcast_to(lane_ref[...], (2, SLAB))
-    finish_messages(flags, sums, flat, flat, partial_ref, odd_ref, even_ref, a_ref, b_ref)
+    flat = lane_ref[...]
+    finish_messages(flags, sums, flat, flat, partial_ref, cross_ref, inner_ref)
+
+
+def quarters_kernel(own_ref, y_ref, pair_ref):
+    for i, ref in enumerate((own_ref, y_ref)):
+        for j in range(2):
+            at = j * HALF + i * QUARTER
+            pair_ref[at : at + QUARTER, :] = ref[j * QUARTER : (j + 1) * QUARTER, :]
 
 
 def transposed_kernel(
-    flags, columns_ref, rows_ref, near_ref, far_ref, pair_ref, odd_in, even_in, odd_rows_ref,
+    flags, columns_ref, rows_ref, near_ref, far_ref, pair_ref, mine_in, theirs_in, odd_rows_ref,
     even_rows_ref, kernel_ref,
 ):
     own = columns_ref[pl.ds(pl.multiple_of(flags[NARROW] * QUARTER, QUARTER), QUARTER), :]
@@ -343,11 +378,15 @@
     odd_rows_ref[HALF:SLAB, :] = far_ref[0:HALF, :]
     even_rows_ref[0:HALF, :] = near_ref[HALF:SLAB, :]
     even_rows_ref[HALF:SLAB, :] = far_ref[HALF:SLAB, :]
+    one = flags[CORE] > 0
+    close, _ = received(flags, mine_in, theirs_in)
+    odd_pairs = turned(flags, jnp.where(one, close[4:6], close[2:4]))
+    even_pairs = turned(flags, jnp.where(one, close[12:14], close[10:12]))
     for i, (rows, top, bottom) in enumerate(
         (
             (rows_ref, pair_ref[0:1, :], pair_ref[1:2, :]),
-            (odd_rows_ref, odd_in[2:3, :], odd_in[3:4, :]),
-            (even_rows_ref, even_in[2:3, :], even_in[3:4, :]),
+            (odd_rows_ref, odd_pairs[0:1], odd_pairs[1:2]),
+            (even_rows_ref, even_pairs[0:1], even_pairs[1:2]),
         )
     ):
         values = jnp.exp(nt_dot(own, rows[...]) * SCALE)
@@ -357,14 +396,15 @@
 
 
 def gradient_kernel(
-    flags, partial_in, odd_in, even_in, a_in, b_in, own_weight, odd_weight, even_weight, row_ref,
-    lane_ref, own_kernel_ref, near_kernel_ref, far_kernel_ref, own_columns_ref, near_columns_ref,
+    flags, partial_in, mine_in, theirs_in, own_weight, odd_weight, even_weight, row_ref, lane_ref,
+    own_kernel_ref, near_kernel_ref, far_kernel_ref, own_columns_ref, near_columns_ref,
     far_columns_ref, rows_ref, odd_rows_ref, even_rows_ref, transposed_ref, treated_out,
     control_out,
 ):
     scales = column_scales(
-        flags, partial_in, odd_in, even_in, a_in, b_in, (own_weight, odd_weight, even_weight)
-    )
+        flags, partial_in, mine_in, theirs_in, (own_weight, odd_weight, even_weight)
+    )
+    close, _ = received(flags, mine_in, theirs_in)
     row_scale = row_ref[:, 0:1]
     mass = jnp.zeros((QUARTER, LANES), F32)
     pulled = jnp.zeros((QUARTER, WIDTH), F32)
@@ -397,7 +437,11 @@
     own_mass = upright(own_quarter(own_weight[...]))
     pushed = jnp.zeros((QUARTER, WIDTH), F32)
     for i, (scale, rows) in enumerate(
-        ((lane_ref[...], rows_ref), (odd_in[2:3, :], odd_rows_ref), (even_in[2:3, :], even_rows_ref))
+        (
+            (lane_ref[...], rows_ref),
+            (turned(flags, close[2:3]), odd_rows_ref),
+            (turned(flags, close[10:11]), even_rows_ref),
+        )
     ):
         transport = scale * transposed_ref[:, i * SLAB : (i + 1) * SLAB] * own_scale
         pushed = pushed + jnp.dot(transport.astype(BF16), rows[...], preferred_element_type=F32)
@@ -421,17 +465,14 @@
     )(*operands)
 
 
-MESSAGES = [((4, SLAB), F32), ((4, SLAB), F32), ((1, SLAB), F32), ((1, SLAB), F32)]
+MESSAGES = [((8, SLAB), F32), ((8, SLAB), F32)]
 
 
 def trade(messages):
-    odd, even, a, b = messages
-    return (
-        exchange(odd, 1, True),
-        exchange(even, 1, False),
-        exchange(a, 2, True),
-        exchange(b, 2, False),
-    )
+    cross = split_exchange(messages[0], True)
+    inner = split_exchange(messages[1], False)
+    (mine,) = call(stack_kernel, [VMEM] * 2, [((16, SLAB), F32)], [cross, inner])
+    return mine, narrow_swap(mine, SWAP_CORE)
 
 
 def step(treated, control, treated_weight, control_weight, band):
@@ -498,7 +539,7 @@
             ((SLAB, LANES), F32),
             ((8, 3 * SLAB), F32),
             ((SLAB, LANES), F32),
-            ((8, SLAB), F32),
+            ((16, SLAB), F32),
         ],
         [flags, joined, joined_far, own_columns],
         [pltpu.VMEM((LANES, LANES), F32)],
@@ -526,15 +567,15 @@
     )
     first = trade(messages)
 
-    row_scale, lane_scale, near_rows, partial, *messages = call(
+    row_scale, lane_scale, partial, *messages = call(
         sweep_kernel,
-        [SMEM] + [VMEM] * 14,
-        [((SLAB, LANES), F32), ((1, SLAB), F32), ((SLAB, WIDTH), BF16), ((8, SLAB), F32), *MESSAGES],
-        [
-            flags, partial, *first, *weights, own_kernel, near_values, far_values, weight,
-            quarters, quarters_y,
-        ],
+        [SMEM] + [VMEM] * 10,
+        [((SLAB, LANES), F32), ((1, SLAB), F32), ((8, SLAB), F32), *MESSAGES],
+        [flags, partial, *first, *weights, own_kernel, near_values, far_values, weight],
         [pltpu.VMEM((8, LANES), F32)],
+    )
+    (near_rows,) = call(
+        quarters_kernel, [VMEM] * 2, [((SLAB, WIDTH), BF16)], [quarters, quarters_y]
     )
     second = trade(messages)
     far_rows = narrow_swap(near_rows, SWAP_CORE)
@@ -543,7 +584,7 @@
         transposed_kernel,
         [SMEM] + [VMEM] * 7,
         [((SLAB, WIDTH), BF16), ((SLAB, WIDTH), BF16), ((QUARTER, 3 * SLAB), F32)],
-        [flags, own_columns, rows, near_rows, far_rows, pairs, first[0], first[1]],
+        [flags, own_columns, rows, near_rows, far_rows, pairs, *first],
     )
 
     top = pl.BlockSpec((QUARTER, SLAB), lambda i: (0, 0))
@@ -553,7 +594,7 @@
         grid=(1,),
         out_shape=(jax.ShapeDtypeStruct((QUARTER, WIDTH), F32),) * 2,
         in_specs=[
-            SMEM, whole(8, SLAB), whole(4, SLAB), whole(4, SLAB), whole(1, SLAB), whole(1, SLAB),
+            SMEM, whole(8, SLAB), whole(16, SLAB), whole(16, SLAB),
             whole(1, SLAB), whole(1, SLAB), whole(1, SLAB),
             pl.BlockSpec((QUARTER, LANES), lambda i: (0, 0)), whole(1, SLAB), top, top, top,
             *[whole(SLAB, WIDTH)] * 6, whole(QUARTER, 3 * SLAB),

time: 105 us -> 102 us (0.971); the launches traced: 105 us -> 100 us
  starting transfers between devices: 62.1 us -> 47.1 us
  waiting for transfers between devices: 19.8 us -> 30.4 us
    ppermute x10 -> x2, starting transfers between devices: 50.8 us -> 15.9 us  [exchange(): return lax.ppermute(block, 'wide', both_ways(pairs, count))]
    ppermute x0 -> x4, starting transfers between devices: none -> 16.1 us  [split_exchange(): return lax.ppermute(block, ('wide', 'narrow'), pairs)]
    ppermute x5 -> x7, waiting for transfers between devices: 0.01 us -> 10.6 us  [narrow_swap(): return lax.ppermute(block, 'narrow', pairs)]
    ppermute x0 -> x4, waiting for transfers between devices: none -> 8.1 us  [split_exchange(): return lax.ppermute(block, ('wide', 'narrow'), pairs)]
    ppermute x10 -> x2, waiting for transfers between devices: 19.8 us -> 11.8 us  [exchange(): return lax.ppermute(block, 'wide', both_ways(pairs, count))]
    ppermute x5 -> x7, starting transfers between devices: 11.3 us -> 15.1 us  [narrow_swap(): return lax.ppermute(block, 'narrow', pairs)]
    pallas_call x9 -> x12, Pallas kernels: 17.8 us -> 17.8 us  [call(): pl.pallas_call(body, out_shape=tuple((jax.ShapeDtypeStruct(shape, dtype)...]
  transfers between devices with their start and end apart: 15 -> 13, of which waited for: 3 -> 7; matrix products, arithmetic and copies ran while one was open for 1% -> 1% of each run, Pallas kernels for 12% -> 16%
where the time goes in v6:
time: 102 us; the launch traced here: 100 us
  starting transfers between devices  47.1 us (46%)
  waiting for transfers between devices  30.4 us (30%)
  Pallas kernels  21.2 us (21%)
    pallas_call x12, Pallas kernels, call(): pl.pallas_call(body, out_shape=tuple((jax.ShapeDtypeStruct(shape, dtype)...  17.8 us
    ppermute x4, starting transfers between devices, split_exchange(): return lax.ppermute(block, ('wide', 'narrow'), pairs)  16.1 us
    ppermute x2, starting transfers between devices, exchange(): return lax.ppermute(block, 'wide', both_ways(pairs, count))  15.9 us
    ppermute x7, starting transfers between devices, narrow_swap(): return lax.ppermute(block, 'narrow', pairs)  15.1 us
    ppermute x2, waiting for transfers between devices, exchange(): return lax.ppermute(block, 'wide', both_ways(pairs, count))  11.8 us
    ppermute x7, waiting for transfers between devices, narrow_swap(): return lax.ppermute(block, 'narrow', pairs)  10.6 us
    ppermute x4, waiting for transfers between devices, split_exchange(): return lax.ppermute(block, ('wide', 'narrow'), pairs)  8.1 us
    pallas_call x1, Pallas kernels, step(): pl.pallas_call(gradient_kernel, grid=(1,), out_shape=(jax.ShapeDtypeStruc...  3.45 us
  transfers between devices with their start and end apart: 13, of which 7 were waited for; matrix products, arithmetic and copies ran while one was open for 1% of the time, Pallas kernels for 16%

profile of v6, /device:TPU:24, one launch (start us, length us, event | category | flops | bytes accessed | tf_op | source)
XLA Modules:
  0.0 100.5 jit_solution(5594955081897686488)
XLA Ops:
  0.7 1.7 %shard_map.68 = (bf16[784,512]{1,0:T(8,128)(2,1)S(1)}, bf16[272,512]{1,0:T(8,128)(2,1)S(1)}) custom-call(s32[8]{0:T(128)S(1)} %compare_select_fusion.4.flags, bf16[256,512]{1,0:T(8,128)(2,1)} %treated_any.1, bf16[1024,512]{1,0:T(8,128)(2,1)} %control_any.2, f32[2,128]{1,0:T(2,128)} %bitcast.10, s32[2,24]{1,0:T(2,128)} %band_any.1), custom_call_target="tpu_custom_call" | custom-call | tf_op jit(solution)/shard_map/pallas_call | solution.py:458
  2.4 2.7 %collective-permute-start = (bf16[272,512]{1,0:T(8,128)(2,1)S(1)}, bf16[272,512]{1,0:T(8,128)(2,1)S(1)}, u32[]{:S(2)}, u32[]{:S(2)}) collective-permute-start(bf16[272,512]{1,0:T(8,128)(2,1)S(1)} %get-tuple-element.32.own_ref), channel_id=1, source_target_pairs={{0,2},{2,0},{1,3},{3,1},{4,6},{6,4},{5,7},{7,5},{8,10},{10,8},{9,1... | collective-permute-start | bytes 835592 | tf_op jit(solution)/shard_map/ppermute | solution.py:39
  5.1 14.0 %collective-permute-start.2 = (bf16[784,512]{1,0:T(8,128)(2,1)S(1)}, bf16[784,512]{1,0:T(8,128)(2,1)S(1)}, u32[]{:S(2)}, u32[]{:S(2)}) collective-permute-start(bf16[784,512]{1,0:T(8,128)(2,1)S(1)} %get-tuple-element.35), channel_id=1, source_target_pairs={{4,8},{12,16},{20,24},{28,32},{36,40},{44,48},{52,56},{60,64},{68,... | collective-permute-start | bytes 2408456 | tf_op jit(solution)/shard_map/ppermute | solution.py:48
  19.1 1.9 %collective-permute-start.3 = (bf16[784,512]{1,0:T(8,128)(2,1)S(1)}, bf16[784,512]{1,0:T(8,128)(2,1)S(1)}, u32[]{:S(2)}, u32[]{:S(2)}) collective-permute-start(bf16[784,512]{1,0:T(8,128)(2,1)S(1)} %get-tuple-element.35), channel_id=1, source_target_pairs={{0,4},{8,12},{16,20},{24,28},{32,36},{40,44},{48,52},{56,60},{64,6... | collective-permute-start | bytes 2408456 | tf_op jit(solution)/shard_map/ppermute | solution.py:48
  21.0 0.0 collective-permute-done.y_ref
  21.1 1.9 %collective-permute-start.1 = (bf16[544,512]{1,0:T(8,128)(2,1)S(1)}, bf16[544,512]{1,0:T(8,128)(2,1)S(1)}, u32[]{:S(2)}, u32[]{:S(2)}) collective-permute-start(bf16[544,512]{1,0:T(8,128)(2,1)S(1)} %shard_map.69.joined_ref), channel_id=1, source_target_pairs={{0,1},{1,0},{2,3},{3,2},{4,5},{5,4},{6,7},{7,6},{8,9},{9,8},{10,11... | collective-permute-start | bytes 1671176 | tf_op jit(solution)/shard_map/ppermute | solution.py:39
  23.0 0.7 fusion
  23.7 1.5 %shard_map.70.columns_ref.own_columns_ref = bf16[1024,512]{1,0:T(8,128)(2,1)S(1)} custom-call(bf16[1024,512]{1,0:T(8,128)(2,1)} %control_any.2), custom_call_target="tpu_custom_call" | custom-call | tf_op jit(solution)/shard_map/pallas_call | solution.py:458
  25.3 0.0 collective-permute-done.1.far_ref
  25.3 3.0 %shard_map.71 = (bf16[1024,512]{1,0:T(8,128)(2,1)S(1)}, f32[1024,1024]{1,0:T(8,128)S(1)}, f32[1024,128]{1,0:T(8,128)S(1)}, f32[8,3072]{1,0:T(8,128)S(1)}, f32[10...) custom-call(s32[8]{0:T(128)S(1)} %compare_select_fusion.4.flags, bf16[544,512]{1,0:T(8,128)(2,1)S(1)} %shard_map.69.joined_ref, ...), custom_call_target="tpu_custom_call" | custom-call | tf_op jit(solution)/shard_map/pallas_call | solution.py:458
  28.2 8.5 %collective-permute-done.2.odd_ref = bf16[784,512]{1,0:T(8,128)(2,1)S(1)} collective-permute-done((bf16[784,512]{1,0:T(8,128)(2,1)S(1)}, bf16[784,512]{1,0:T(8,128)(2,1)S(1)}, u32[]{:S(2)}, u32[]{:S(2)}) %collective-permute-start.2) | collective-permute-done | bytes 802848 | tf_op jit(solution)/shard_map/ppermute | solution.py:48
  36.8 3.3 %collective-permute-done.3.even_ref = bf16[784,512]{1,0:T(8,128)(2,1)S(1)} collective-permute-done((bf16[784,512]{1,0:T(8,128)(2,1)S(1)}, bf16[784,512]{1,0:T(8,128)(2,1)S(1)}, u32[]{:S(2)}, u32[]{:S(2)}) %collective-permute-start.3) | collective-permute-done | bytes 802848 | tf_op jit(solution)/shard_map/ppermute | solution.py:48
  40.0 0.4 shard_map.72
  40.4 2.9 %collective-permute-start.11 = (bf16[512,512]{1,0:T(8,128)(2,1)S(1)}, bf16[512,512]{1,0:T(8,128)(2,1)S(1)}, u32[]{:S(2)}, u32[]{:S(2)}) collective-permute-start(bf16[512,512]{1,0:T(8,128)(2,1)S(1)} %get-tuple-element.58.own_ref), channel_id=1, source_target_pairs={{0,2},{2,0},{1,3},{3,1},{4,6},{6,4},{5,7},{7,5},{8,10},{10,8},{9,1... | collective-permute-start | bytes 1572872 | tf_op jit(solution)/shard_map/ppermute | solution.py:39
  43.3 1.9 %collective-permute-start.4 = (bf16[1024,512]{1,0:T(8,128)(2,1)S(1)}, bf16[1024,512]{1,0:T(8,128)(2,1)S(1)}, u32[]{:S(2)}, u32[]{:S(2)}) collective-permute-start(bf16[1024,512]{1,0:T(8,128)(2,1)S(1)} %get-tuple-element.39.columns_ref.near_columns_ref), channel_id=1, source_target_pairs={{0,1},{1,0},{2,3},{3,2},{4,5},{5,4},{6,7},{7,6},{8,9},{9,8},{10,11... | collective-permute-start | bytes 3145736 | tf_op jit(solution)/shard_map/ppermute | solution.py:39
  45.2 9.3 %collective-permute-done.11.y_ref = bf16[512,512]{1,0:T(8,128)(2,1)S(1)} collective-permute-done((bf16[512,512]{1,0:T(8,128)(2,1)S(1)}, bf16[512,512]{1,0:T(8,128)(2,1)S(1)}, u32[]{:S(2)}, u32[]{:S(2)}) %collective-permute-start.11) | collective-permute-done | bytes 524320 | tf_op jit(solution)/shard_map/ppermute | solution.py:39
  54.6 0.1 shard_map.78.near_ref
  54.6 1.9 %collective-permute-start.12 = (bf16[1024,512]{1,0:T(8,128)(2,1)S(1)}, bf16[1024,512]{1,0:T(8,128)(2,1)S(1)}, u32[]{:S(2)}, u32[]{:S(2)}) collective-permute-start(bf16[1024,512]{1,0:T(8,128)(2,1)S(1)} %shard_map.78.near_ref), channel_id=1, source_target_pairs={{0,1},{1,0},{2,3},{3,2},{4,5},{5,4},{6,7},{7,6},{8,9},{9,8},{10,11... | collective-permute-start | bytes 3145736 | tf_op jit(solution)/shard_map/ppermute | solution.py:39
  56.6 2.1 %shard_map.73 = (f32[1024,1024]{1,0:T(8,128)S(1)}, f32[1024,128]{1,0:T(8,128)S(1)}) custom-call(bf16[1024,512]{1,0:T(8,128)(2,1)S(1)} %get-tuple-element.34.rows_ref, bf16[1024,512]{1,0:T(8,128)(2,1)S(1)} %get-tuple-element.39.columns_ref.near_columns_ref, f32[8,3072]{1,0:T(8,128)S(1)} %get-tuple-element.40.mask_ref, ...), custom_call_target="tpu_custom_call" | custom-call | tf_op jit(solution)/shard_map/pallas_call | solution.py:458
  58.6 0.0 collective-permute-done.4.columns_ref.far_columns_ref
  58.7 4.1 %shard_map.74 = (f32[1024,1024]{1,0:T(8,128)S(1)}, f32[8,1024]{1,0:T(8,128)S(1)}, f32[8,1024]{1,0:T(8,128)S(1)}, f32[8,1024]{1,0:T(8,128)S(1)}) custom-call(s32[8]{0:T(128)S(1)} %compare_select_fusion.4.flags, bf16[1024,512]{1,0:T(8,128)(2,1)S(1)} %get-tuple-element.34.rows_ref, bf16[1024,512]{1,0:T(8,128)(2,1)S(1)} %collective-permute-done.4.columns_ref.far_columns_ref, ...), custom_call_target="tpu_custom_call" | custom-call | tf_op jit(solution)/shard_map/pallas_call | solution.py:458
  62.7 6.3 %collective-permute-start.5 = (f32[8,1024]{1,0:T(8,128)S(1)}, f32[8,1024]{1,0:T(8,128)S(1)}, u32[]{:S(2)}, u32[]{:S(2)}) collective-permute-start(f32[8,1024]{1,0:T(8,128)S(1)} %get-tuple-element.47), channel_id=1, source_target_pairs={{4,8},{12,16},{20,24},{28,32},{36,40},{44,48},{52,56},{60,64},{68,... | collective-permute-start | bytes 98312 | tf_op jit(solution)/shard_map/ppermute | solution.py:64
  69.0 1.9 %collective-permute-start.6 = (f32[8,1024]{1,0:T(8,128)S(1)}, f32[8,1024]{1,0:T(8,128)S(1)}, u32[]{:S(2)}, u32[]{:S(2)}) collective-permute-start(f32[8,1024]{1,0:T(8,128)S(1)} %get-tuple-element.48), channel_id=1, source_target_pairs={{0,4},{8,12},{16,20},{24,28},{32,36},{40,44},{48,52},{56,60},{64,6... | collective-permute-start | bytes 98312 | tf_op jit(solution)/shard_map/ppermute | solution.py:64
  70.9 3.3 %collective-permute-done.5.cross_ref = f32[8,1024]{1,0:T(8,128)S(1)} collective-permute-done((f32[8,1024]{1,0:T(8,128)S(1)}, f32[8,1024]{1,0:T(8,128)S(1)}, u32[]{:S(2)}, u32[]{:S(2)}) %collective-permute-start.5) | collective-permute-done | bytes 32800 | tf_op jit(solution)/shard_map/ppermute | solution.py:64
  74.2 0.6 collective-permute-done.6.inner_ref
  74.8 1.9 %collective-permute-start.7 = (f32[16,1024]{1,0:T(8,128)S(1)}, f32[16,1024]{1,0:T(8,128)S(1)}, u32[]{:S(2)}, u32[]{:S(2)}) collective-permute-start(f32[16,1024]{1,0:T(8,128)S(1)} %shard_map.75.mine_in), channel_id=1, source_target_pairs={{0,1},{1,0},{2,3},{3,2},{4,5},{5,4},{6,7},{7,6},{8,9},{9,8},{10,11... | collective-permute-start | bytes 196616 | tf_op jit(solution)/shard_map/ppermute | solution.py:39
  76.7 1.2 %collective-permute-done.7.theirs_in = f32[16,1024]{1,0:T(8,128)S(1)} collective-permute-done((f32[16,1024]{1,0:T(8,128)S(1)}, f32[16,1024]{1,0:T(8,128)S(1)}, u32[]{:S(2)}, u32[]{:S(2)}) %collective-permute-start.7) | collective-permute-done | bytes 65568 | tf_op jit(solution)/shard_map/ppermute | solution.py:39
  78.0 3.3 %shard_map.76 = (f32[1024,128]{1,0:T(8,128)S(1)}, f32[1,1024]{1,0:T(1,128)S(1)}, f32[8,1024]{1,0:T(8,128)S(1)}, f32[8,1024]{1,0:T(8,128)S(1)}, f32[8,1024]{1,0:T(8,128)S(1)}) custom-call(s32[8]{0:T(128)S(1)} %compare_select_fusion.4.flags, f32[8,1024]{1,0:T(8,128)S(1)} %get-tuple-element.46.partial_in, f32[16,1024]{1,0:T(8,128)S(1)} %shard_map.75.mine_in, ...), custom_call_target="tpu_custom_call" | custom-call | tf_op jit(solution)/shard_map/pallas_call | solution.py:458
  81.3 6.0 %collective-permute-start.8 = (f32[8,1024]{1,0:T(8,128)S(1)}, f32[8,1024]{1,0:T(8,128)S(1)}, u32[]{:S(2)}, u32[]{:S(2)}) collective-permute-start(f32[8,1024]{1,0:T(8,128)S(1)} %get-tuple-element.54), channel_id=1, source_target_pairs={{4,8},{12,16},{20,24},{28,32},{36,40},{44,48},{52,56},{60,64},{68,... | collective-permute-start | bytes 98312 | tf_op jit(solution)/shard_map/ppermute | solution.py:64
  87.3 1.9 %collective-permute-start.9 = (f32[8,1024]{1,0:T(8,128)S(1)}, f32[8,1024]{1,0:T(8,128)S(1)}, u32[]{:S(2)}, u32[]{:S(2)}) collective-permute-start(f32[8,1024]{1,0:T(8,128)S(1)} %get-tuple-element.55), channel_id=1, source_target_pairs={{0,4},{8,12},{16,20},{24,28},{32,36},{40,44},{48,52},{56,60},{64,6... | collective-permute-start | bytes 98312 | tf_op jit(solution)/shard_map/ppermute | solution.py:64
  89.2 4.2 %collective-permute-done.8.cross_ref = f32[8,1024]{1,0:T(8,128)S(1)} collective-permute-done((f32[8,1024]{1,0:T(8,128)S(1)}, f32[8,1024]{1,0:T(8,128)S(1)}, u32[]{:S(2)}, u32[]{:S(2)}) %collective-permute-start.8) | collective-permute-done | bytes 32800 | tf_op jit(solution)/shard_map/ppermute | solution.py:64
  93.4 0.0 collective-permute-done.9.inner_ref
  93.4 1.9 %collective-permute-start.10 = (f32[16,1024]{1,0:T(8,128)S(1)}, f32[16,1024]{1,0:T(8,128)S(1)}, u32[]{:S(2)}, u32[]{:S(2)}) collective-permute-start(f32[16,1024]{1,0:T(8,128)S(1)} %shard_map.77.mine_in), channel_id=1, source_target_pairs={{0,1},{1,0},{2,3},{3,2},{4,5},{5,4},{6,7},{7,6},{8,9},{9,8},{10,11... | collective-permute-start | bytes 196616 | tf_op jit(solution)/shard_map/ppermute | solution.py:39
  95.4 0.0 collective-permute-done.12.far_ref
  95.4 1.6 %shard_map.79 = (bf16[1024,512]{1,0:T(8,128)(2,1)S(1)}, bf16[1024,512]{1,0:T(8,128)(2,1)S(1)}, f32[256,3072]{1,0:T(8,128)S(1)}) custom-call(s32[8]{0:T(128)S(1)} %compare_select_fusion.4.flags, bf16[1024,512]{1,0:T(8,128)(2,1)S(1)} %shard_map.70.columns_ref.own_columns_ref, bf16[1024,512]{1,0:T(8,128)(2,1)S(1)} %get-tuple-element.34.rows_ref, ...), custom_call_target="tpu_custom_call" | custom-call | tf_op jit(solution)/shard_map/pallas_call | solution.py:458
  97.0 0.0 collective-permute-done.10.theirs_in
  97.0 3.4 %gradient_kernel.1 = (f32[256,512]{1,0:T(8,128)}, f32[256,512]{1,0:T(8,128)}) custom-call(s32[8]{0:T(128)S(1)} %compare_select_fusion.4.flags, f32[8,1024]{1,0:T(8,128)S(1)} %get-tuple-element.53.partial_in, f32[16,1024]{1,0:T(8,128)S(1)} %shard_map.77.mine_in, f32[16,1024]{1,0:T(8,128)S(1)} %collective-permute-done.10.theirs_in, f32[1,1024]{1,0:T(1,128)S(1)} %bitcast.7, ...), custom_call_target="tpu_custom_call" | custom-call | tf_op jit(solution)/shard_map/gradient_kernel/pallas_call | solution.py:592
  (4 shorter events, 0.1 us)
Async XLA Ops:
  2.4 18.6 %collective-permute-start = (bf16[272,512]{1,0:T(8,128)(2,1)S(1)}, bf16[272,512]{1,0:T(8,128)(2,1)S(1)}, u32[]{:S(2)}, u32[]{:S(2)}) collective-permute-start(bf16[272,512]{1,0:T(8,128)(2,1)S(1)} %get-tuple-element.32.own_ref), channel_id=1, source_target_pairs={{0,2},{2,0},{1,3},{3,1},{4,6},{6,4},{5,7},{7,5},{8,10},{10,8},{9,1... | collective-permute-start | bytes 835592 | tf_op jit(solution)/shard_map/ppermute | solution.py:39
  5.1 31.7 %collective-permute-start.2 = (bf16[784,512]{1,0:T(8,128)(2,1)S(1)}, bf16[784,512]{1,0:T(8,128)(2,1)S(1)}, u32[]{:S(2)}, u32[]{:S(2)}) collective-permute-start(bf16[784,512]{1,0:T(8,128)(2,1)S(1)} %get-tuple-element.35), channel_id=1, source_target_pairs={{4,8},{12,16},{20,24},{28,32},{36,40},{44,48},{52,56},{60,64},{68,... | collective-permute-start | bytes 2408456 | tf_op jit(solution)/shard_map/ppermute | solution.py:48
  19.1 21.0 %collective-permute-start.3 = (bf16[784,512]{1,0:T(8,128)(2,1)S(1)}, bf16[784,512]{1,0:T(8,128)(2,1)S(1)}, u32[]{:S(2)}, u32[]{:S(2)}) collective-permute-start(bf16[784,512]{1,0:T(8,128)(2,1)S(1)} %get-tuple-element.35), channel_id=1, source_target_pairs={{0,4},{8,12},{16,20},{24,28},{32,36},{40,44},{48,52},{56,60},{64,6... | collective-permute-start | bytes 2408456 | tf_op jit(solution)/shard_map/ppermute | solution.py:48
  21.1 4.2 %collective-permute-start.1 = (bf16[544,512]{1,0:T(8,128)(2,1)S(1)}, bf16[544,512]{1,0:T(8,128)(2,1)S(1)}, u32[]{:S(2)}, u32[]{:S(2)}) collective-permute-start(bf16[544,512]{1,0:T(8,128)(2,1)S(1)} %shard_map.69.joined_ref), channel_id=1, source_target_pairs={{0,1},{1,0},{2,3},{3,2},{4,5},{5,4},{6,7},{7,6},{8,9},{9,8},{10,11... | collective-permute-start | bytes 1671176 | tf_op jit(solution)/shard_map/ppermute | solution.py:39
  40.4 14.1 %collective-permute-start.11 = (bf16[512,512]{1,0:T(8,128)(2,1)S(1)}, bf16[512,512]{1,0:T(8,128)(2,1)S(1)}, u32[]{:S(2)}, u32[]{:S(2)}) collective-permute-start(bf16[512,512]{1,0:T(8,128)(2,1)S(1)} %get-tuple-element.58.own_ref), channel_id=1, source_target_pairs={{0,2},{2,0},{1,3},{3,1},{4,6},{6,4},{5,7},{7,5},{8,10},{10,8},{9,1... | collective-permute-start | bytes 1572872 | tf_op jit(solution)/shard_map/ppermute | solution.py:39
  43.3 15.3 %collective-permute-start.4 = (bf16[1024,512]{1,0:T(8,128)(2,1)S(1)}, bf16[1024,512]{1,0:T(8,128)(2,1)S(1)}, u32[]{:S(2)}, u32[]{:S(2)}) collective-permute-start(bf16[1024,512]{1,0:T(8,128)(2,1)S(1)} %get-tuple-element.39.columns_ref.near_columns_ref), channel_id=1, source_target_pairs={{0,1},{1,0},{2,3},{3,2},{4,5},{5,4},{6,7},{7,6},{8,9},{9,8},{10,11... | collective-permute-start | bytes 3145736 | tf_op jit(solution)/shard_map/ppermute | solution.py:39
  54.6 40.8 %collective-permute-start.12 = (bf16[1024,512]{1,0:T(8,128)(2,1)S(1)}, bf16[1024,512]{1,0:T(8,128)(2,1)S(1)}, u32[]{:S(2)}, u32[]{:S(2)}) collective-permute-start(bf16[1024,512]{1,0:T(8,128)(2,1)S(1)} %shard_map.78.near_ref), channel_id=1, source_target_pairs={{0,1},{1,0},{2,3},{3,2},{4,5},{5,4},{6,7},{7,6},{8,9},{9,8},{10,11... | collective-permute-start | bytes 3145736 | tf_op jit(solution)/shard_map/ppermute | solution.py:39
  62.7 11.5 %collective-permute-start.5 = (f32[8,1024]{1,0:T(8,128)S(1)}, f32[8,1024]{1,0:T(8,128)S(1)}, u32[]{:S(2)}, u32[]{:S(2)}) collective-permute-start(f32[8,1024]{1,0:T(8,128)S(1)} %get-tuple-element.47), channel_id=1, source_target_pairs={{4,8},{12,16},{20,24},{28,32},{36,40},{44,48},{52,56},{60,64},{68,... | collective-permute-start | bytes 98312 | tf_op jit(solution)/shard_map/ppermute | solution.py:64
  69.0 5.8 %collective-permute-start.6 = (f32[8,1024]{1,0:T(8,128)S(1)}, f32[8,1024]{1,0:T(8,128)S(1)}, u32[]{:S(2)}, u32[]{:S(2)}) collective-permute-start(f32[8,1024]{1,0:T(8,128)S(1)} %get-tuple-element.48), channel_id=1, source_target_pairs={{0,4},{8,12},{16,20},{24,28},{32,36},{40,44},{48,52},{56,60},{64,6... | collective-permute-start | bytes 98312 | tf_op jit(solution)/shard_map/ppermute | solution.py:64
  74.8 3.1 %collective-permute-start.7 = (f32[16,1024]{1,0:T(8,128)S(1)}, f32[16,1024]{1,0:T(8,128)S(1)}, u32[]{:S(2)}, u32[]{:S(2)}) collective-permute-start(f32[16,1024]{1,0:T(8,128)S(1)} %shard_map.75.mine_in), channel_id=1, source_target_pairs={{0,1},{1,0},{2,3},{3,2},{4,5},{5,4},{6,7},{7,6},{8,9},{9,8},{10,11... | collective-permute-start | bytes 196616 | tf_op jit(solution)/shard_map/ppermute | solution.py:39
  81.3 12.1 %collective-permute-start.8 = (f32[8,1024]{1,0:T(8,128)S(1)}, f32[8,1024]{1,0:T(8,128)S(1)}, u32[]{:S(2)}, u32[]{:S(2)}) collective-permute-start(f32[8,1024]{1,0:T(8,128)S(1)} %get-tuple-element.54), channel_id=1, source_target_pairs={{4,8},{12,16},{20,24},{28,32},{36,40},{44,48},{52,56},{60,64},{68,... | collective-permute-start | bytes 98312 | tf_op jit(solution)/shard_map/ppermute | solution.py:64
  87.3 6.1 %collective-permute-start.9 = (f32[8,1024]{1,0:T(8,128)S(1)}, f32[8,1024]{1,0:T(8,128)S(1)}, u32[]{:S(2)}, u32[]{:S(2)}) collective-permute-start(f32[8,1024]{1,0:T(8,128)S(1)} %get-tuple-element.55), channel_id=1, source_target_pairs={{0,4},{8,12},{16,20},{24,28},{32,36},{40,44},{48,52},{56,60},{64,6... | collective-permute-start | bytes 98312 | tf_op jit(solution)/shard_map/ppermute | solution.py:64
  93.4 3.6 %collective-permute-start.10 = (f32[16,1024]{1,0:T(8,128)S(1)}, f32[16,1024]{1,0:T(8,128)S(1)}, u32[]{:S(2)}, u32[]{:S(2)}) collective-permute-start(f32[16,1024]{1,0:T(8,128)S(1)} %shard_map.77.mine_in), channel_id=1, source_target_pairs={{0,1},{1,0},{2,3},{3,2},{4,5},{5,4},{6,7},{7,6},{8,9},{9,8},{10,11... | collective-permute-start | bytes 196616 | tf_op jit(solution)/shard_map/ppermute | solution.py:39

commit v7 on v6

--- a/solution.py
+++ b/solution.py
@@ -25,14 +25,10 @@
 INFO = 16
 MESSAGE = QUARTER + INFO
 JOINED = 2 * MESSAGE
-LETTER = HALF + MESSAGE
-
-NARROW, CORE, ODD, A_EVEN, HAS_ODD = range(5)
-
-
-def both_ways(pairs, count):
-    kept = [(a, b) for a, b in pairs if b < count]
-    return kept + [(b, a) for a, b in kept]
+LETTER = HALF + QUARTER
+NOTE = 16
+
+NARROW, CORE, Y, ODD, A_EVEN, HAS_ODD, FLIPPED = range(7)
 
 
 def narrow_swap(block, pairs):
@@ -40,27 +36,18 @@
 
 
 def exchange(block, hops, crossing):
-    count = lax.axis_size("wide")
-    first = hops if crossing else 0
-    pairs = [
-        (base + i, base + i + hops) for base in range(first, count, 2 * hops) for i in range(hops)
-    ]
-    return lax.ppermute(block, "wide", both_ways(pairs, count))
-
-
-def split_exchange(block, crossing):
     count = lax.axis_size("wide")
     narrow = lax.axis_size("narrow")
     pairs = []
     for n in range(narrow):
-        hops = 1 + n % 2
-        first = hops if crossing else 0
-        one = [
-            (base + i, base + i + hops)
-            for base in range(first, count, 2 * hops)
-            for i in range(hops)
-        ]
-        pairs += [(a * narrow + n, b * narrow + n) for a, b in both_ways(one, count)]
+        far = hops[n % 2]
+        for base in range(far if crossing else 0, count, 2 * far):
+            for low in range(base, base + far):
+                high = low + far
+                if high < count:
+                    other = n ^ 2 if low < count // 2 <= high else n
+                    one, two = low * narrow + n, high * narrow + other
+                    pairs += [(one, two), (two, one)]
     return lax.ppermute(block, ("wide", "narrow"), pairs)
 
 
@@ -154,16 +141,14 @@
     info = info_ref[...].astype(BF16)
     message_ref[0:QUARTER, :] = rows
     message_ref[QUARTER:MESSAGE, :] = info
-    letter_ref[HALF : HALF + QUARTER, :] = rows
-    letter_ref[HALF + QUARTER : LETTER, :] = info
+    letter_ref[HALF:LETTER, :] = rows
     copies[3].wait()
 
 
-def join_kernel(own_ref, y_ref, joined_ref):
-    joined_ref[0:QUARTER, :] = own_ref[0:QUARTER, :]
-    joined_ref[QUARTER:HALF, :] = y_ref[0:QUARTER, :]
-    joined_ref[HALF : HALF + INFO, :] = own_ref[QUARTER:MESSAGE, :]
-    joined_ref[HALF + INFO : JOINED, :] = y_ref[QUARTER:MESSAGE, :]
+def join_kernel(flags, own_ref, y_ref, joined_ref):
+    for ref, y in ((own_ref, flags[Y]), (y_ref, 1 - flags[Y])):
+        joined_ref[pl.ds(pl.multiple_of(y * QUARTER, QUARTER), QUARTER), :] = ref[0:QUARTER, :]
+        joined_ref[pl.ds(pl.multiple_of(HALF + y * INFO, INFO), INFO), :] = ref[QUARTER:MESSAGE, :]
 
 
 def columns_kernel(control_any, columns_ref, control_ref, sems):
@@ -186,8 +171,8 @@
 def open_kernel(odd_ref, even_ref, columns_ref, quarters_ref):
     columns_ref[0:HALF, :] = normalize(odd_ref[0:HALF, :])
     columns_ref[HALF:SLAB, :] = normalize(even_ref[0:HALF, :])
-    quarters_ref[0:QUARTER, :] = odd_ref[HALF : HALF + QUARTER, :]
-    quarters_ref[QUARTER:HALF, :] = even_ref[HALF : HALF + QUARTER, :]
+    quarters_ref[0:QUARTER, :] = odd_ref[HALF:LETTER, :]
+    quarters_ref[QUARTER:HALF, :] = even_ref[HALF:LETTER, :]
 
 
 def near_kernel(rows_ref, columns_ref, mask_ref, before_ref, kernel_ref, sums_ref):
@@ -226,13 +211,11 @@
     mask_ref[...] = jnp.dot(
         band[:16], jnp.where(one_hot, 1.0, 0.0).astype(BF16), preferred_element_type=F32
     )[:8]
-    place = lax.broadcasted_iota(jnp.int32, (16, LANES), 0)
-    base = jnp.where(place < 2, 8, jnp.where(place < 6, odd_base, even_base))
-    other = (place == 4) | (place == 5) | (place == 8) | (place == 9)
-    quarter = n + jnp.where(other, 1 - 2 * core, 0)
-    chosen = base + 2 * quarter + place % 2
+    place = lax.broadcasted_iota(jnp.int32, (32, LANES), 0)
+    base = jnp.where(place < 8, odd_base, jnp.where(place < 16, even_base, 8 + 2 * n))
+    chosen = base + jnp.where(place < 16, place % 8, place % 2)
     select = jnp.where(
-        lax.broadcasted_iota(jnp.int32, (16, LANES), 1) == chosen, 1.0, 0.0
+        lax.broadcasted_iota(jnp.int32, (32, LANES), 1) == chosen, 1.0, 0.0
     ).astype(BF16)
     by_block = nt_dot(select, band).astype(BF16)
     spread = (
@@ -276,8 +259,8 @@
 
 
 def stack_kernel(cross_ref, inner_ref, both_ref):
-    both_ref[0:8, :] = cross_ref[...]
-    both_ref[8:16, :] = inner_ref[...]
+    both_ref[0:NOTE, :] = cross_ref[...]
+    both_ref[NOTE : 2 * NOTE, :] = inner_ref[...]
 
 
 def received(flags, mine_ref, theirs_ref):
@@ -313,17 +296,17 @@
     zero = jnp.zeros((8, SLAB), F32)
     sums = lax.fori_loop(0, 4, step, (zero, zero, zero))
     finish_messages(
-        flags, sums, pair_ref[2:6, :], pair_ref[6:10, :], partial_ref, cross_ref, inner_ref
+        flags, sums, pair_ref[0:8, :], pair_ref[8:16, :], partial_ref, cross_ref, inner_ref
     )
 
 
 def column_scales(flags, partial_ref, mine_ref, theirs_ref, weights):
     a_even = flags[A_EVEN] > 0
     close, distant = received(flags, mine_ref, theirs_ref)
-    a, b = distant[0:1], distant[8:9]
-    own = partial_ref[0:1, :] + close[1:2] + close[9:10]
+    a, b = distant[0:1], distant[NOTE : NOTE + 1]
+    own = partial_ref[0:1, :] + close[1:2] + close[NOTE + 1 : NOTE + 2]
     odd = partial_ref[1:2, :] + close[0:1] + jnp.where(a_even, b, a)
-    even = partial_ref[2:3, :] + close[8:9] + jnp.where(a_even, a, b)
+    even = partial_ref[2:3, :] + close[NOTE : NOTE + 1] + jnp.where(a_even, a, b)
     has_odd = flags[HAS_ODD] > 0
     own_weight, odd_weight, even_weight = (ref[...] for ref in weights)
     odd = jnp.where(has_odd, odd_weight / jnp.where(has_odd, odd, 1.0), 0.0)
@@ -362,11 +345,12 @@
     finish_messages(flags, sums, flat, flat, partial_ref, cross_ref, inner_ref)
 
 
-def quarters_kernel(own_ref, y_ref, pair_ref):
-    for i, ref in enumerate((own_ref, y_ref)):
-        for j in range(2):
-            at = j * HALF + i * QUARTER
-            pair_ref[at : at + QUARTER, :] = ref[j * QUARTER : (j + 1) * QUARTER, :]
+def quarters_kernel(flags, own_ref, y_ref, pair_ref):
+    y = flags[Y]
+    odd_y = jnp.where(flags[FLIPPED] > 0, 1 - y, y)
+    for ref, odd_at, even_at in ((own_ref, odd_y, y), (y_ref, 1 - odd_y, 1 - y)):
+        for at, first in ((odd_at * QUARTER, 0), (HALF + even_at * QUARTER, QUARTER)):
+            pair_ref[pl.ds(pl.multiple_of(at, QUARTER), QUARTER), :] = ref[first : first + QUARTER, :]
 
 
 def transposed_kernel(
@@ -378,13 +362,19 @@
     odd_rows_ref[HALF:SLAB, :] = far_ref[0:HALF, :]
     even_rows_ref[0:HALF, :] = near_ref[HALF:SLAB, :]
     even_rows_ref[HALF:SLAB, :] = far_ref[HALF:SLAB, :]
-    one = flags[CORE] > 0
+    n = flags[NARROW]
     close, _ = received(flags, mine_in, theirs_in)
-    odd_pairs = turned(flags, jnp.where(one, close[4:6], close[2:4]))
-    even_pairs = turned(flags, jnp.where(one, close[12:14], close[10:12]))
+
+    def pairs_of(first):
+        found = close[first : first + 2]
+        for i in range(1, 4):
+            found = jnp.where(n == i, close[first + 2 * i : first + 2 * i + 2], found)
+        return turned(flags, found)
+
+    odd_pairs, even_pairs = pairs_of(2), pairs_of(NOTE + 2)
     for i, (rows, top, bottom) in enumerate(
         (
-            (rows_ref, pair_ref[0:1, :], pair_ref[1:2, :]),
+            (rows_ref, pair_ref[16:17, :], pair_ref[17:18, :]),
             (odd_rows_ref, odd_pairs[0:1], odd_pairs[1:2]),
             (even_rows_ref, even_pairs[0:1], even_pairs[1:2]),
         )
@@ -405,7 +395,8 @@
         flags, partial_in, mine_in, theirs_in, (own_weight, odd_weight, even_weight)
     )
     close, _ = received(flags, mine_in, theirs_in)
-    row_scale = row_ref[:, 0:1]
+    mine = pl.ds(pl.multiple_of(flags[Y] * QUARTER, QUARTER), QUARTER)
+    row_scale = row_ref[mine, 0:1]
     mass = jnp.zeros((QUARTER, LANES), F32)
     pulled = jnp.zeros((QUARTER, WIDTH), F32)
     for kernel_ref, scale, columns_ref in zip(
@@ -414,13 +405,13 @@
         (own_columns_ref, near_columns_ref, far_columns_ref),
         strict=True,
     ):
-        transport = row_scale * kernel_ref[...] * scale
+        transport = row_scale * kernel_ref[mine, :] * scale
         mass = mass + lane_tiles(transport)
         pulled = pulled + jnp.dot(
             transport.astype(BF16), columns_ref[...], preferred_element_type=F32
         )
     mass = jnp.sum(mass, axis=1, keepdims=True)
-    treated_out[...] = mass * rows_ref[0:QUARTER, :].astype(F32) - pulled
+    treated_out[...] = mass * rows_ref[mine, :].astype(F32) - pulled
 
     n = flags[NARROW]
 
@@ -440,7 +431,7 @@
         (
             (lane_ref[...], rows_ref),
             (turned(flags, close[2:3]), odd_rows_ref),
-            (turned(flags, close[10:11]), even_rows_ref),
+            (turned(flags, close[NOTE + 2 : NOTE + 3]), even_rows_ref),
         )
     ):
         transport = scale * transposed_ref[:, i * SLAB : (i + 1) * SLAB] * own_scale
@@ -465,13 +456,13 @@
     )(*operands)
 
 
-MESSAGES = [((8, SLAB), F32), ((8, SLAB), F32)]
+MESSAGES = [((NOTE, SLAB), F32), ((NOTE, SLAB), F32)]
 
 
 def trade(messages):
-    cross = split_exchange(messages[0], True)
-    inner = split_exchange(messages[1], False)
-    (mine,) = call(stack_kernel, [VMEM] * 2, [((16, SLAB), F32)], [cross, inner])
+    cross = exchange(messages[0], (1, 2), True)
+    inner = exchange(messages[1], (1, 2), False)
+    (mine,) = call(stack_kernel, [VMEM] * 2, [((2 * NOTE, SLAB), F32)], [cross, inner])
     return mine, narrow_swap(mine, SWAP_CORE)
 
 
@@ -485,9 +476,11 @@
     values = (
         n,
         n % 2,
+        n // 2,
         odd,
         jnp.logical_xor(wide_index % 4 >= 2, odd == 1).astype(jnp.int32),
         ((toward_odd >= 0) & (toward_odd < wide_count)).astype(jnp.int32),
+        (jnp.minimum(wide_index, toward_odd) == wide_count // 2 - 1).astype(jnp.int32),
     )
     place = lax.iota(jnp.int32, 8)
     flags = jnp.zeros((8,), jnp.int32)
@@ -515,8 +508,8 @@
             pltpu.SemaphoreType.DMA((4,)),
         ],
     )
-    odd_letter = exchange(letter, 1, True)
-    even_letter = exchange(letter, 1, False)
+    odd_letter = exchange(letter, (1, 1), True)
+    even_letter = exchange(letter, (1, 1), False)
     control, *weights = lax.optimization_barrier((control, *weights))
     (own_columns,) = call(
         columns_kernel,
@@ -527,7 +520,9 @@
     )
 
     message_y = narrow_swap(message, SWAP_Y)
-    (joined,) = call(join_kernel, [VMEM] * 2, [((JOINED, WIDTH), BF16)], [message, message_y])
+    (joined,) = call(
+        join_kernel, [SMEM] + [VMEM] * 2, [((JOINED, WIDTH), BF16)], [flags, message, message_y]
+    )
     joined_far = narrow_swap(joined, SWAP_CORE)
 
     rows, own_kernel, sums, mask, weight, pairs = call(
@@ -539,7 +534,7 @@
             ((SLAB, LANES), F32),
             ((8, 3 * SLAB), F32),
             ((SLAB, LANES), F32),
-            ((16, SLAB), F32),
+            ((32, SLAB), F32),
         ],
         [flags, joined, joined_far, own_columns],
         [pltpu.VMEM((LANES, LANES), F32)],
@@ -575,7 +570,10 @@
         [pltpu.VMEM((8, LANES), F32)],
     )
     (near_rows,) = call(
-        quarters_kernel, [VMEM] * 2, [((SLAB, WIDTH), BF16)], [quarters, quarters_y]
+        quarters_kernel,
+        [SMEM] + [VMEM] * 2,
+        [((SLAB, WIDTH), BF16)],
+        [flags, quarters, quarters_y],
     )
     second = trade(messages)
     far_rows = narrow_swap(near_rows, SWAP_CORE)
@@ -587,24 +585,15 @@
         [flags, own_columns, rows, near_rows, far_rows, pairs, *first],
     )
 
-    top = pl.BlockSpec((QUARTER, SLAB), lambda i: (0, 0))
-    whole = lambda *shape: pl.BlockSpec(shape, lambda i: (0,) * len(shape))
-    return pl.pallas_call(
+    return call(
         gradient_kernel,
-        grid=(1,),
-        out_shape=(jax.ShapeDtypeStruct((QUARTER, WIDTH), F32),) * 2,
-        in_specs=[
-            SMEM, whole(8, SLAB), whole(16, SLAB), whole(16, SLAB),
-            whole(1, SLAB), whole(1, SLAB), whole(1, SLAB),
-            pl.BlockSpec((QUARTER, LANES), lambda i: (0, 0)), whole(1, SLAB), top, top, top,
-            *[whole(SLAB, WIDTH)] * 6, whole(QUARTER, 3 * SLAB),
+        [SMEM] + [VMEM] * 18,
+        [((QUARTER, WIDTH), F32)] * 2,
+        [
+            flags, partial, *second, *weights, row_scale, lane_scale, own_kernel, near_values,
+            far_values, own_columns, near_columns, far_columns, rows, odd_rows, even_rows,
+            transposed,
         ],
-        out_specs=(whole(QUARTER, WIDTH),) * 2,
-        compiler_params=pltpu.CompilerParams(vmem_limit_bytes=16 << 20),
-        name="gradient_kernel",
-    )(
-        flags, partial, *second, *weights, row_scale, lane_scale, own_kernel, near_values,
-        far_values, own_columns, near_columns, far_columns, rows, odd_rows, even_rows, transposed,
     )
 
 

time: 102 us -> 103 us (level)
  waiting for transfers between devices: 30.4 us -> 32 us
  starting transfers between devices: 47.1 us -> 45.6 us
  Pallas kernels: 21.2 us -> 22.4 us
    pallas_call x12 -> x13, Pallas kernels: 17.8 us -> 22.4 us  [call(): pl.pallas_call(body, out_shape=tuple((jax.ShapeDtypeStruct(shape, dtype)...]
    pallas_call x1 -> x0, Pallas kernels: 3.45 us -> none  [step(): pl.pallas_call(gradient_kernel, grid=(1,), out_shape=(jax.ShapeDtypeStruc...]
    ppermute x7, waiting for transfers between devices: 10.6 us -> 11.6 us  [narrow_swap(): return lax.ppermute(block, 'narrow', pairs)]
  transfers between devices with their start and end apart: 13 -> 13, of which waited for: 7 -> 6; matrix products, arithmetic and copies ran while one was open for 1% -> 1% of each run, Pallas kernels for 16% -> 17%
where the time goes in v7:
time: 103 us; the launch traced here: 102 us
  starting transfers between devices  45.6 us (44%)
  waiting for transfers between devices  32 us (31%)
  Pallas kernels  22.4 us (22%)
    ppermute x6, starting transfers between devices, exchange(): return lax.ppermute(block, ('wide', 'narrow'), pairs)  31.5 us
    pallas_call x13, Pallas kernels, call(): pl.pallas_call(body, out_shape=tuple((jax.ShapeDtypeStruct(shape, dtype)...  22.4 us
    ppermute x6, waiting for transfers between devices, exchange(): return lax.ppermute(block, ('wide', 'narrow'), pairs)  20.4 us
    ppermute x7, starting transfers between devices, narrow_swap(): return lax.ppermute(block, 'narrow', pairs)  14.2 us
    ppermute x7, waiting for transfers between devices, narrow_swap(): return lax.ppermute(block, 'narrow', pairs)  11.6 us
  transfers between devices with their start and end apart: 13, of which 6 were waited for; matrix products, arithmetic and copies ran while one was open for 1% of the time, Pallas kernels for 17%

profile of v7, /device:TPU:24, one launch (start us, length us, event | category | flops | bytes accessed | tf_op | source)
XLA Modules:
  0.0 101.7 jit_solution(4371485548928199067)
XLA Ops:
  0.7 1.7 %shard_map.68 = (bf16[768,512]{1,0:T(8,128)(2,1)S(1)}, bf16[272,512]{1,0:T(8,128)(2,1)S(1)}) custom-call(s32[8]{0:T(128)S(1)} %compare_select_fusion.6.flags, bf16[256,512]{1,0:T(8,128)(2,1)} %treated_any.1, bf16[1024,512]{1,0:T(8,128)(2,1)} %control_any.2, f32[2,128]{1,0:T(2,128)} %bitcast.10, s32[2,24]{1,0:T(2,128)} %band_any.1), custom_call_target="tpu_custom_call" | custom-call | tf_op jit(solution)/shard_map/pallas_call | solution.py:449
  2.4 2.7 %collective-permute-start = (bf16[272,512]{1,0:T(8,128)(2,1)S(1)}, bf16[272,512]{1,0:T(8,128)(2,1)S(1)}, u32[]{:S(2)}, u32[]{:S(2)}) collective-permute-start(bf16[272,512]{1,0:T(8,128)(2,1)S(1)} %get-tuple-element.32.own_ref), channel_id=1, source_target_pairs={{0,2},{2,0},{1,3},{3,1},{4,6},{6,4},{5,7},{7,5},{8,10},{10,8},{9,1... | collective-permute-start | bytes 835592 | tf_op jit(solution)/shard_map/ppermute | solution.py:35
  5.1 14.1 %collective-permute-start.2 = (bf16[768,512]{1,0:T(8,128)(2,1)S(1)}, bf16[768,512]{1,0:T(8,128)(2,1)S(1)}, u32[]{:S(2)}, u32[]{:S(2)}) collective-permute-start(bf16[768,512]{1,0:T(8,128)(2,1)S(1)} %get-tuple-element.35), channel_id=1, source_target_pairs={{4,8},{8,4},{12,16},{16,12},{20,24},{24,20},{28,32},{32,28},{36,40... | collective-permute-start | bytes 2359304 | tf_op jit(solution)/shard_map/ppermute | solution.py:51
  19.2 1.9 %collective-permute-start.3 = (bf16[768,512]{1,0:T(8,128)(2,1)S(1)}, bf16[768,512]{1,0:T(8,128)(2,1)S(1)}, u32[]{:S(2)}, u32[]{:S(2)}) collective-permute-start(bf16[768,512]{1,0:T(8,128)(2,1)S(1)} %get-tuple-element.35), channel_id=1, source_target_pairs={{0,4},{4,0},{8,12},{12,8},{16,20},{20,16},{24,28},{28,24},{32,36},... | collective-permute-start | bytes 2359304 | tf_op jit(solution)/shard_map/ppermute | solution.py:51
  21.1 0.0 collective-permute-done.y_ref
  21.1 0.6 shard_map.69.joined_ref
  21.7 1.9 %collective-permute-start.1 = (bf16[544,512]{1,0:T(8,128)(2,1)S(1)}, bf16[544,512]{1,0:T(8,128)(2,1)S(1)}, u32[]{:S(2)}, u32[]{:S(2)}) collective-permute-start(bf16[544,512]{1,0:T(8,128)(2,1)S(1)} %shard_map.69.joined_ref), channel_id=1, source_target_pairs={{0,1},{1,0},{2,3},{3,2},{4,5},{5,4},{6,7},{7,6},{8,9},{9,8},{10,11... | collective-permute-start | bytes 1671176 | tf_op jit(solution)/shard_map/ppermute | solution.py:35
  23.7 0.7 fusion
  24.4 1.5 %shard_map.70.columns_ref.own_columns_ref = bf16[1024,512]{1,0:T(8,128)(2,1)S(1)} custom-call(bf16[1024,512]{1,0:T(8,128)(2,1)} %control_any.2), custom_call_target="tpu_custom_call" | custom-call | tf_op jit(solution)/shard_map/pallas_call | solution.py:449
  25.9 0.0 collective-permute-done.1.far_ref
  25.9 3.0 %shard_map.71 = (bf16[1024,512]{1,0:T(8,128)(2,1)S(1)}, f32[1024,1024]{1,0:T(8,128)S(1)}, f32[1024,128]{1,0:T(8,128)S(1)}, f32[8,3072]{1,0:T(8,128)S(1)}, f32[10...) custom-call(s32[8]{0:T(128)S(1)} %compare_select_fusion.6.flags, bf16[544,512]{1,0:T(8,128)(2,1)S(1)} %shard_map.69.joined_ref, ...), custom_call_target="tpu_custom_call" | custom-call | tf_op jit(solution)/shard_map/pallas_call | solution.py:449
  28.9 7.5 %collective-permute-done.2.odd_ref = bf16[768,512]{1,0:T(8,128)(2,1)S(1)} collective-permute-done((bf16[768,512]{1,0:T(8,128)(2,1)S(1)}, bf16[768,512]{1,0:T(8,128)(2,1)S(1)}, u32[]{:S(2)}, u32[]{:S(2)}) %collective-permute-start.2) | collective-permute-done | bytes 786464 | tf_op jit(solution)/shard_map/ppermute | solution.py:51
  36.4 3.4 %collective-permute-done.3.even_ref = bf16[768,512]{1,0:T(8,128)(2,1)S(1)} collective-permute-done((bf16[768,512]{1,0:T(8,128)(2,1)S(1)}, bf16[768,512]{1,0:T(8,128)(2,1)S(1)}, u32[]{:S(2)}, u32[]{:S(2)}) %collective-permute-start.3) | collective-permute-done | bytes 786464 | tf_op jit(solution)/shard_map/ppermute | solution.py:51
  39.8 0.4 shard_map.72
  40.2 1.9 %collective-permute-start.11 = (bf16[512,512]{1,0:T(8,128)(2,1)S(1)}, bf16[512,512]{1,0:T(8,128)(2,1)S(1)}, u32[]{:S(2)}, u32[]{:S(2)}) collective-permute-start(bf16[512,512]{1,0:T(8,128)(2,1)S(1)} %get-tuple-element.58.own_ref), channel_id=1, source_target_pairs={{0,2},{2,0},{1,3},{3,1},{4,6},{6,4},{5,7},{7,5},{8,10},{10,8},{9,1... | collective-permute-start | bytes 1572872 | tf_op jit(solution)/shard_map/ppermute | solution.py:35
  42.1 1.9 %collective-permute-start.4 = (bf16[1024,512]{1,0:T(8,128)(2,1)S(1)}, bf16[1024,512]{1,0:T(8,128)(2,1)S(1)}, u32[]{:S(2)}, u32[]{:S(2)}) collective-permute-start(bf16[1024,512]{1,0:T(8,128)(2,1)S(1)} %get-tuple-element.39.columns_ref.near_columns_ref), channel_id=1, source_target_pairs={{0,1},{1,0},{2,3},{3,2},{4,5},{5,4},{6,7},{7,6},{8,9},{9,8},{10,11... | collective-permute-start | bytes 3145736 | tf_op jit(solution)/shard_map/ppermute | solution.py:35
  44.1 10.3 %collective-permute-done.11.y_ref = bf16[512,512]{1,0:T(8,128)(2,1)S(1)} collective-permute-done((bf16[512,512]{1,0:T(8,128)(2,1)S(1)}, bf16[512,512]{1,0:T(8,128)(2,1)S(1)}, u32[]{:S(2)}, u32[]{:S(2)}) %collective-permute-start.11) | collective-permute-done | bytes 524320 | tf_op jit(solution)/shard_map/ppermute | solution.py:35
  54.3 0.6 shard_map.78.near_ref
  55.0 1.9 %collective-permute-start.12 = (bf16[1024,512]{1,0:T(8,128)(2,1)S(1)}, bf16[1024,512]{1,0:T(8,128)(2,1)S(1)}, u32[]{:S(2)}, u32[]{:S(2)}) collective-permute-start(bf16[1024,512]{1,0:T(8,128)(2,1)S(1)} %shard_map.78.near_ref), channel_id=1, source_target_pairs={{0,1},{1,0},{2,3},{3,2},{4,5},{5,4},{6,7},{7,6},{8,9},{9,8},{10,11... | collective-permute-start | bytes 3145736 | tf_op jit(solution)/shard_map/ppermute | solution.py:35
  56.9 2.1 %shard_map.73 = (f32[1024,1024]{1,0:T(8,128)S(1)}, f32[1024,128]{1,0:T(8,128)S(1)}) custom-call(bf16[1024,512]{1,0:T(8,128)(2,1)S(1)} %get-tuple-element.34.rows_ref, bf16[1024,512]{1,0:T(8,128)(2,1)S(1)} %get-tuple-element.39.columns_ref.near_columns_ref, f32[8,3072]{1,0:T(8,128)S(1)} %get-tuple-element.40.mask_ref, ...), custom_call_target="tpu_custom_call" | custom-call | tf_op jit(solution)/shard_map/pallas_call | solution.py:449
  59.0 0.0 collective-permute-done.4.columns_ref.far_columns_ref
  59.0 4.1 %shard_map.74 = (f32[1024,1024]{1,0:T(8,128)S(1)}, f32[8,1024]{1,0:T(8,128)S(1)}, f32[16,1024]{1,0:T(8,128)S(1)}, f32[16,1024]{1,0:T(8,128)S(1)}) custom-call(s32[8]{0:T(128)S(1)} %compare_select_fusion.6.flags, bf16[1024,512]{1,0:T(8,128)(2,1)S(1)} %get-tuple-element.34.rows_ref, bf16[1024,512]{1,0:T(8,128)(2,1)S(1)} %collective-permute-done.4.columns_ref.far_columns_ref, ...), custom_call_target="tpu_custom_call" | custom-call | tf_op jit(solution)/shard_map/pallas_call | solution.py:449
  63.0 6.0 %collective-permute-start.5 = (f32[16,1024]{1,0:T(8,128)S(1)}, f32[16,1024]{1,0:T(8,128)S(1)}, u32[]{:S(2)}, u32[]{:S(2)}) collective-permute-start(f32[16,1024]{1,0:T(8,128)S(1)} %get-tuple-element.47), channel_id=1, source_target_pairs={{4,8},{8,4},{12,16},{16,12},{20,24},{24,20},{28,32},{32,28},{36,40... | collective-permute-start | bytes 196616 | tf_op jit(solution)/shard_map/ppermute | solution.py:51
  69.0 1.9 %collective-permute-start.6 = (f32[16,1024]{1,0:T(8,128)S(1)}, f32[16,1024]{1,0:T(8,128)S(1)}, u32[]{:S(2)}, u32[]{:S(2)}) collective-permute-start(f32[16,1024]{1,0:T(8,128)S(1)} %get-tuple-element.48), channel_id=1, source_target_pairs={{0,4},{4,0},{8,12},{12,8},{16,20},{20,16},{24,28},{28,24},{32,36},... | collective-permute-start | bytes 196616 | tf_op jit(solution)/shard_map/ppermute | solution.py:51
  71.0 4.6 %collective-permute-done.5.cross_ref = f32[16,1024]{1,0:T(8,128)S(1)} collective-permute-done((f32[16,1024]{1,0:T(8,128)S(1)}, f32[16,1024]{1,0:T(8,128)S(1)}, u32[]{:S(2)}, u32[]{:S(2)}) %collective-permute-start.5) | collective-permute-done | bytes 65568 | tf_op jit(solution)/shard_map/ppermute | solution.py:51
  75.6 0.0 collective-permute-done.6.inner_ref
  75.6 1.9 %collective-permute-start.7 = (f32[32,1024]{1,0:T(8,128)S(1)}, f32[32,1024]{1,0:T(8,128)S(1)}, u32[]{:S(2)}, u32[]{:S(2)}) collective-permute-start(f32[32,1024]{1,0:T(8,128)S(1)} %shard_map.75.mine_in), channel_id=1, source_target_pairs={{0,1},{1,0},{2,3},{3,2},{4,5},{5,4},{6,7},{7,6},{8,9},{9,8},{10,11... | collective-permute-start | bytes 393224 | tf_op jit(solution)/shard_map/ppermute | solution.py:35
  77.5 1.3 %collective-permute-done.7.theirs_in = f32[32,1024]{1,0:T(8,128)S(1)} collective-permute-done((f32[32,1024]{1,0:T(8,128)S(1)}, f32[32,1024]{1,0:T(8,128)S(1)}, u32[]{:S(2)}, u32[]{:S(2)}) %collective-permute-start.7) | collective-permute-done | bytes 131104 | tf_op jit(solution)/shard_map/ppermute | solution.py:35
  78.8 3.3 %shard_map.76 = (f32[1024,128]{1,0:T(8,128)S(1)}, f32[1,1024]{1,0:T(1,128)S(1)}, f32[8,1024]{1,0:T(8,128)S(1)}, f32[16,1024]{1,0:T(8,128)S(1)}, f32[16,1024]{1,0:T(8,128)S(1)}) custom-call(s32[8]{0:T(128)S(1)} %compare_select_fusion.6.flags, f32[8,1024]{1,0:T(8,128)S(1)} %get-tuple-element.46.partial_in, f32[32,1024]{1,0:T(8,128)S(1)} %shard_map.75.mine_in, ...), custom_call_target="tpu_custom_call" | custom-call | tf_op jit(solution)/shard_map/pallas_call | solution.py:449
  82.2 5.6 %collective-permute-start.8 = (f32[16,1024]{1,0:T(8,128)S(1)}, f32[16,1024]{1,0:T(8,128)S(1)}, u32[]{:S(2)}, u32[]{:S(2)}) collective-permute-start(f32[16,1024]{1,0:T(8,128)S(1)} %get-tuple-element.54), channel_id=1, source_target_pairs={{4,8},{8,4},{12,16},{16,12},{20,24},{24,20},{28,32},{32,28},{36,40... | collective-permute-start | bytes 196616 | tf_op jit(solution)/shard_map/ppermute | solution.py:51
  87.8 1.9 %collective-permute-start.9 = (f32[16,1024]{1,0:T(8,128)S(1)}, f32[16,1024]{1,0:T(8,128)S(1)}, u32[]{:S(2)}, u32[]{:S(2)}) collective-permute-start(f32[16,1024]{1,0:T(8,128)S(1)} %get-tuple-element.55), channel_id=1, source_target_pairs={{0,4},{4,0},{8,12},{12,8},{16,20},{20,16},{24,28},{28,24},{32,36},... | collective-permute-start | bytes 196616 | tf_op jit(solution)/shard_map/ppermute | solution.py:51
  89.8 4.9 %collective-permute-done.8.cross_ref = f32[16,1024]{1,0:T(8,128)S(1)} collective-permute-done((f32[16,1024]{1,0:T(8,128)S(1)}, f32[16,1024]{1,0:T(8,128)S(1)}, u32[]{:S(2)}, u32[]{:S(2)}) %collective-permute-start.8) | collective-permute-done | bytes 65568 | tf_op jit(solution)/shard_map/ppermute | solution.py:51
  94.7 0.0 collective-permute-done.9.inner_ref
  94.7 1.9 %collective-permute-start.10 = (f32[32,1024]{1,0:T(8,128)S(1)}, f32[32,1024]{1,0:T(8,128)S(1)}, u32[]{:S(2)}, u32[]{:S(2)}) collective-permute-start(f32[32,1024]{1,0:T(8,128)S(1)} %shard_map.77.mine_in), channel_id=1, source_target_pairs={{0,1},{1,0},{2,3},{3,2},{4,5},{5,4},{6,7},{7,6},{8,9},{9,8},{10,11... | collective-permute-start | bytes 393224 | tf_op jit(solution)/shard_map/ppermute | solution.py:35
  96.6 0.0 collective-permute-done.12.far_ref
  96.6 1.6 %shard_map.79 = (bf16[1024,512]{1,0:T(8,128)(2,1)S(1)}, bf16[1024,512]{1,0:T(8,128)(2,1)S(1)}, f32[256,3072]{1,0:T(8,128)S(1)}) custom-call(s32[8]{0:T(128)S(1)} %compare_select_fusion.6.flags, bf16[1024,512]{1,0:T(8,128)(2,1)S(1)} %shard_map.70.columns_ref.own_columns_ref, bf16[1024,512]{1,0:T(8,128)(2,1)S(1)} %get-tuple-element.34.rows_ref, ...), custom_call_target="tpu_custom_call" | custom-call | tf_op jit(solution)/shard_map/pallas_call | solution.py:449
  98.3 0.0 collective-permute-done.10.theirs_in
  98.3 3.5 %shard_map.80 = (f32[256,512]{1,0:T(8,128)}, f32[256,512]{1,0:T(8,128)}) custom-call(s32[8]{0:T(128)S(1)} %compare_select_fusion.6.flags, f32[8,1024]{1,0:T(8,128)S(1)} %get-tuple-element.53.partial_in, f32[32,1024]{1,0:T(8,128)S(1)} %shard_map.77.mine_in, f32[32,1024]{1,0:T(8,128)S(1)} %collective-permute-done.10.theirs_in, f32[1,1024]{1,0:T(1,128)S(1)} %bitcast.7, ...), custom_call_target="tpu_custom_call" | custom-call | tf_op jit(solution)/shard_map/pallas_call | solution.py:449
  (3 shorter events, 0.0 us)
Async XLA Ops:
  2.4 18.7 %collective-permute-start = (bf16[272,512]{1,0:T(8,128)(2,1)S(1)}, bf16[272,512]{1,0:T(8,128)(2,1)S(1)}, u32[]{:S(2)}, u32[]{:S(2)}) collective-permute-start(bf16[272,512]{1,0:T(8,128)(2,1)S(1)} %get-tuple-element.32.own_ref), channel_id=1, source_target_pairs={{0,2},{2,0},{1,3},{3,1},{4,6},{6,4},{5,7},{7,5},{8,10},{10,8},{9,1... | collective-permute-start | bytes 835592 | tf_op jit(solution)/shard_map/ppermute | solution.py:35
  5.1 31.3 %collective-permute-start.2 = (bf16[768,512]{1,0:T(8,128)(2,1)S(1)}, bf16[768,512]{1,0:T(8,128)(2,1)S(1)}, u32[]{:S(2)}, u32[]{:S(2)}) collective-permute-start(bf16[768,512]{1,0:T(8,128)(2,1)S(1)} %get-tuple-element.35), channel_id=1, source_target_pairs={{4,8},{8,4},{12,16},{16,12},{20,24},{24,20},{28,32},{32,28},{36,40... | collective-permute-start | bytes 2359304 | tf_op jit(solution)/shard_map/ppermute | solution.py:51
  19.2 20.6 %collective-permute-start.3 = (bf16[768,512]{1,0:T(8,128)(2,1)S(1)}, bf16[768,512]{1,0:T(8,128)(2,1)S(1)}, u32[]{:S(2)}, u32[]{:S(2)}) collective-permute-start(bf16[768,512]{1,0:T(8,128)(2,1)S(1)} %get-tuple-element.35), channel_id=1, source_target_pairs={{0,4},{4,0},{8,12},{12,8},{16,20},{20,16},{24,28},{28,24},{32,36},... | collective-permute-start | bytes 2359304 | tf_op jit(solution)/shard_map/ppermute | solution.py:51
  21.7 4.2 %collective-permute-start.1 = (bf16[544,512]{1,0:T(8,128)(2,1)S(1)}, bf16[544,512]{1,0:T(8,128)(2,1)S(1)}, u32[]{:S(2)}, u32[]{:S(2)}) collective-permute-start(bf16[544,512]{1,0:T(8,128)(2,1)S(1)} %shard_map.69.joined_ref), channel_id=1, source_target_pairs={{0,1},{1,0},{2,3},{3,2},{4,5},{5,4},{6,7},{7,6},{8,9},{9,8},{10,11... | collective-permute-start | bytes 1671176 | tf_op jit(solution)/shard_map/ppermute | solution.py:35
  40.2 14.1 %collective-permute-start.11 = (bf16[512,512]{1,0:T(8,128)(2,1)S(1)}, bf16[512,512]{1,0:T(8,128)(2,1)S(1)}, u32[]{:S(2)}, u32[]{:S(2)}) collective-permute-start(bf16[512,512]{1,0:T(8,128)(2,1)S(1)} %get-tuple-element.58.own_ref), channel_id=1, source_target_pairs={{0,2},{2,0},{1,3},{3,1},{4,6},{6,4},{5,7},{7,5},{8,10},{10,8},{9,1... | collective-permute-start | bytes 1572872 | tf_op jit(solution)/shard_map/ppermute | solution.py:35
  42.1 16.8 %collective-permute-start.4 = (bf16[1024,512]{1,0:T(8,128)(2,1)S(1)}, bf16[1024,512]{1,0:T(8,128)(2,1)S(1)}, u32[]{:S(2)}, u32[]{:S(2)}) collective-permute-start(bf16[1024,512]{1,0:T(8,128)(2,1)S(1)} %get-tuple-element.39.columns_ref.near_columns_ref), channel_id=1, source_target_pairs={{0,1},{1,0},{2,3},{3,2},{4,5},{5,4},{6,7},{7,6},{8,9},{9,8},{10,11... | collective-permute-start | bytes 3145736 | tf_op jit(solution)/shard_map/ppermute | solution.py:35
  55.0 41.7 %collective-permute-start.12 = (bf16[1024,512]{1,0:T(8,128)(2,1)S(1)}, bf16[1024,512]{1,0:T(8,128)(2,1)S(1)}, u32[]{:S(2)}, u32[]{:S(2)}) collective-permute-start(bf16[1024,512]{1,0:T(8,128)(2,1)S(1)} %shard_map.78.near_ref), channel_id=1, source_target_pairs={{0,1},{1,0},{2,3},{3,2},{4,5},{5,4},{6,7},{7,6},{8,9},{9,8},{10,11... | collective-permute-start | bytes 3145736 | tf_op jit(solution)/shard_map/ppermute | solution.py:35
  63.0 12.5 %collective-permute-start.5 = (f32[16,1024]{1,0:T(8,128)S(1)}, f32[16,1024]{1,0:T(8,128)S(1)}, u32[]{:S(2)}, u32[]{:S(2)}) collective-permute-start(f32[16,1024]{1,0:T(8,128)S(1)} %get-tuple-element.47), channel_id=1, source_target_pairs={{4,8},{8,4},{12,16},{16,12},{20,24},{24,20},{28,32},{32,28},{36,40... | collective-permute-start | bytes 196616 | tf_op jit(solution)/shard_map/ppermute | solution.py:51
  69.0 6.5 %collective-permute-start.6 = (f32[16,1024]{1,0:T(8,128)S(1)}, f32[16,1024]{1,0:T(8,128)S(1)}, u32[]{:S(2)}, u32[]{:S(2)}) collective-permute-start(f32[16,1024]{1,0:T(8,128)S(1)} %get-tuple-element.48), channel_id=1, source_target_pairs={{0,4},{4,0},{8,12},{12,8},{16,20},{20,16},{24,28},{28,24},{32,36},... | collective-permute-start | bytes 196616 | tf_op jit(solution)/shard_map/ppermute | solution.py:51
  75.6 3.2 %collective-permute-start.7 = (f32[32,1024]{1,0:T(8,128)S(1)}, f32[32,1024]{1,0:T(8,128)S(1)}, u32[]{:S(2)}, u32[]{:S(2)}) collective-permute-start(f32[32,1024]{1,0:T(8,128)S(1)} %shard_map.75.mine_in), channel_id=1, source_target_pairs={{0,1},{1,0},{2,3},{3,2},{4,5},{5,4},{6,7},{7,6},{8,9},{9,8},{10,11... | collective-permute-start | bytes 393224 | tf_op jit(solution)/shard_map/ppermute | solution.py:35
  82.2 12.5 %collective-permute-start.8 = (f32[16,1024]{1,0:T(8,128)S(1)}, f32[16,1024]{1,0:T(8,128)S(1)}, u32[]{:S(2)}, u32[]{:S(2)}) collective-permute-start(f32[16,1024]{1,0:T(8,128)S(1)} %get-tuple-element.54), channel_id=1, source_target_pairs={{4,8},{8,4},{12,16},{16,12},{20,24},{24,20},{28,32},{32,28},{36,40... | collective-permute-start | bytes 196616 | tf_op jit(solution)/shard_map/ppermute | solution.py:51
  87.8 6.9 %collective-permute-start.9 = (f32[16,1024]{1,0:T(8,128)S(1)}, f32[16,1024]{1,0:T(8,128)S(1)}, u32[]{:S(2)}, u32[]{:S(2)}) collective-permute-start(f32[16,1024]{1,0:T(8,128)S(1)} %get-tuple-element.55), channel_id=1, source_target_pairs={{0,4},{4,0},{8,12},{12,8},{16,20},{20,16},{24,28},{28,24},{32,36},... | collective-permute-start | bytes 196616 | tf_op jit(solution)/shard_map/ppermute | solution.py:51
  94.7 3.6 %collective-permute-start.10 = (f32[32,1024]{1,0:T(8,128)S(1)}, f32[32,1024]{1,0:T(8,128)S(1)}, u32[]{:S(2)}, u32[]{:S(2)}) collective-permute-start(f32[32,1024]{1,0:T(8,128)S(1)} %shard_map.77.mine_in), channel_id=1, source_target_pairs={{0,1},{1,0},{2,3},{3,2},{4,5},{5,4},{6,7},{7,6},{8,9},{9,8},{10,11... | collective-permute-start | bytes 393224 | tf_op jit(solution)/shard_map/ppermute | solution.py:35

commit v8 on v7

--- a/solution.py
+++ b/solution.py
@@ -107,7 +107,7 @@
             sums_ref[at, :] = sums
         return carry
 
-    lax.fori_loop(0, 4, step, 0)
+    lax.fori_loop(0, 4, step, 0, unroll=True)
 
 
 def pack_kernel(
@@ -294,7 +294,7 @@
         return own, near, far
 
     zero = jnp.zeros((8, SLAB), F32)
-    sums = lax.fori_loop(0, 4, step, (zero, zero, zero))
+    sums = lax.fori_loop(0, 4, step, (zero, zero, zero), unroll=True)
     finish_messages(
         flags, sums, pair_ref[0:8, :], pair_ref[8:16, :], partial_ref, cross_ref, inner_ref
     )
@@ -338,7 +338,7 @@
         )
 
     zero = jnp.zeros((8, SLAB), F32)
-    sums = lax.fori_loop(0, 8, step, (zero, zero, zero))
+    sums = lax.fori_loop(0, 8, step, (zero, zero, zero), unroll=True)
     for i in range(8):
         lane_ref[0:1, i * LANES : (i + 1) * LANES] = flat_ref[i : i + 1, :]
     flat = lane_ref[...]
@@ -353,43 +353,51 @@
             pair_ref[pl.ds(pl.multiple_of(at, QUARTER), QUARTER), :] = ref[first : first + QUARTER, :]
 
 
+def own_control(flags, columns_ref):
+    return columns_ref[pl.ds(pl.multiple_of(flags[NARROW] * QUARTER, QUARTER), QUARTER), :]
+
+
+def own_transposed_kernel(flags, columns_ref, rows_ref, pair_ref, kernel_ref):
+    values = jnp.exp(nt_dot(own_control(flags, columns_ref), rows_ref[...]) * SCALE)
+    kernel_ref[0:LANES, :] = values[:LANES] * pair_ref[16:17, :]
+    kernel_ref[LANES:QUARTER, :] = values[LANES:] * pair_ref[17:18, :]
+
+
+def push_kernel(lane_ref, kernel_ref, rows_ref, pushed_ref):
+    pushed_ref[...] = jnp.dot(
+        (lane_ref[...] * kernel_ref[...]).astype(BF16),
+        rows_ref[...],
+        preferred_element_type=F32,
+    )
+
+
 def transposed_kernel(
-    flags, columns_ref, rows_ref, near_ref, far_ref, pair_ref, mine_in, theirs_in, odd_rows_ref,
-    even_rows_ref, kernel_ref,
+    flags, columns_ref, near_ref, far_ref, mine_in, theirs_in, odd_rows_ref, even_rows_ref,
+    kernel_ref,
 ):
-    own = columns_ref[pl.ds(pl.multiple_of(flags[NARROW] * QUARTER, QUARTER), QUARTER), :]
+    own = own_control(flags, columns_ref)
     odd_rows_ref[0:HALF, :] = near_ref[0:HALF, :]
     odd_rows_ref[HALF:SLAB, :] = far_ref[0:HALF, :]
     even_rows_ref[0:HALF, :] = near_ref[HALF:SLAB, :]
     even_rows_ref[HALF:SLAB, :] = far_ref[HALF:SLAB, :]
     n = flags[NARROW]
     close, _ = received(flags, mine_in, theirs_in)
-
-    def pairs_of(first):
+    for i, (rows_ref, first) in enumerate(((odd_rows_ref, 2), (even_rows_ref, NOTE + 2))):
         found = close[first : first + 2]
-        for i in range(1, 4):
-            found = jnp.where(n == i, close[first + 2 * i : first + 2 * i + 2], found)
-        return turned(flags, found)
-
-    odd_pairs, even_pairs = pairs_of(2), pairs_of(NOTE + 2)
-    for i, (rows, top, bottom) in enumerate(
-        (
-            (rows_ref, pair_ref[16:17, :], pair_ref[17:18, :]),
-            (odd_rows_ref, odd_pairs[0:1], odd_pairs[1:2]),
-            (even_rows_ref, even_pairs[0:1], even_pairs[1:2]),
-        )
-    ):
-        values = jnp.exp(nt_dot(own, rows[...]) * SCALE)
+        for j in range(1, 4):
+            found = jnp.where(n == j, close[first + 2 * j : first + 2 * j + 2], found)
+        found = turned(flags, found)
+        values = jnp.exp(nt_dot(own, rows_ref[...]) * SCALE)
         lanes = slice(i * SLAB, (i + 1) * SLAB)
-        kernel_ref[0:LANES, lanes] = values[:LANES] * top
-        kernel_ref[LANES:QUARTER, lanes] = values[LANES:] * bottom
+        kernel_ref[0:LANES, lanes] = values[:LANES] * found[0:1]
+        kernel_ref[LANES:QUARTER, lanes] = values[LANES:] * found[1:2]
 
 
 def gradient_kernel(
-    flags, partial_in, mine_in, theirs_in, own_weight, odd_weight, even_weight, row_ref, lane_ref,
+    flags, partial_in, mine_in, theirs_in, own_weight, odd_weight, even_weight, row_ref,
     own_kernel_ref, near_kernel_ref, far_kernel_ref, own_columns_ref, near_columns_ref,
-    far_columns_ref, rows_ref, odd_rows_ref, even_rows_ref, transposed_ref, treated_out,
-    control_out,
+    far_columns_ref, rows_ref, pushed_ref, odd_rows_ref, even_rows_ref, transposed_ref,
+    treated_any, control_any, treated_out, control_out, sems,
 ):
     scales = column_scales(
         flags, partial_in, mine_in, theirs_in, (own_weight, odd_weight, even_weight)
@@ -412,6 +420,8 @@
         )
     mass = jnp.sum(mass, axis=1, keepdims=True)
     treated_out[...] = mass * rows_ref[mine, :].astype(F32) - pulled
+    treated_copy = pltpu.make_async_copy(treated_out, treated_any, sems.at[0])
+    treated_copy.start()
 
     n = flags[NARROW]
 
@@ -426,18 +436,17 @@
 
     own_scale = upright(own_quarter(scales[0]))
     own_mass = upright(own_quarter(own_weight[...]))
-    pushed = jnp.zeros((QUARTER, WIDTH), F32)
-    for i, (scale, rows) in enumerate(
-        (
-            (lane_ref[...], rows_ref),
-            (turned(flags, close[2:3]), odd_rows_ref),
-            (turned(flags, close[NOTE + 2 : NOTE + 3]), even_rows_ref),
-        )
-    ):
-        transport = scale * transposed_ref[:, i * SLAB : (i + 1) * SLAB] * own_scale
-        pushed = pushed + jnp.dot(transport.astype(BF16), rows[...], preferred_element_type=F32)
+    pushed = pushed_ref[...]
+    for i, (row, rows) in enumerate(((2, odd_rows_ref), (NOTE + 2, even_rows_ref))):
+        scale = turned(flags, close[row : row + 1])
+        transport = (scale * transposed_ref[:, i * SLAB : (i + 1) * SLAB]).astype(BF16)
+        pushed = pushed + jnp.dot(transport, rows[...], preferred_element_type=F32)
     at = pl.ds(pl.multiple_of(n * QUARTER, QUARTER), QUARTER)
-    control_out[...] = own_mass * own_columns_ref[at, :].astype(F32) - pushed
+    control_out[...] = own_mass * own_columns_ref[at, :].astype(F32) - own_scale * pushed
+    control_copy = pltpu.make_async_copy(control_out, control_any, sems.at[1])
+    control_copy.start()
+    treated_copy.wait()
+    control_copy.wait()
 
 
 VMEM = pl.BlockSpec(memory_space=pltpu.VMEM)
@@ -539,7 +548,15 @@
         [flags, joined, joined_far, own_columns],
         [pltpu.VMEM((LANES, LANES), F32)],
     )
-    odd_letter, even_letter, _ = lax.optimization_barrier((odd_letter, even_letter, sums))
+    (own_transposed,) = call(
+        own_transposed_kernel,
+        [SMEM] + [VMEM] * 3,
+        [((QUARTER, SLAB), F32)],
+        [flags, own_columns, rows, pairs],
+    )
+    odd_letter, even_letter, _, _ = lax.optimization_barrier(
+        (odd_letter, even_letter, sums, own_transposed)
+    )
     near_columns, quarters = call(
         open_kernel,
         [VMEM] * 2,
@@ -578,11 +595,17 @@
     second = trade(messages)
     far_rows = narrow_swap(near_rows, SWAP_CORE)
 
+    (pushed,) = call(
+        push_kernel,
+        [VMEM] * 3,
+        [((QUARTER, WIDTH), F32)],
+        [lane_scale, own_transposed, rows],
+    )
     odd_rows, even_rows, transposed = call(
         transposed_kernel,
-        [SMEM] + [VMEM] * 7,
-        [((SLAB, WIDTH), BF16), ((SLAB, WIDTH), BF16), ((QUARTER, 3 * SLAB), F32)],
-        [flags, own_columns, rows, near_rows, far_rows, pairs, *first],
+        [SMEM] + [VMEM] * 5,
+        [((SLAB, WIDTH), BF16), ((SLAB, WIDTH), BF16), ((QUARTER, 2 * SLAB), F32)],
+        [flags, own_columns, near_rows, far_rows, *first],
     )
 
     return call(
@@ -590,10 +613,15 @@
         [SMEM] + [VMEM] * 18,
         [((QUARTER, WIDTH), F32)] * 2,
         [
-            flags, partial, *second, *weights, row_scale, lane_scale, own_kernel, near_values,
-            far_values, own_columns, near_columns, far_columns, rows, odd_rows, even_rows,
-            transposed,
+            flags, partial, *second, *weights, row_scale, own_kernel, near_values, far_values,
+            own_columns, near_columns, far_columns, rows, pushed, odd_rows, even_rows, transposed,
         ],
+        [
+            pltpu.VMEM((QUARTER, WIDTH), F32),
+            pltpu.VMEM((QUARTER, WIDTH), F32),
+            pltpu.SemaphoreType.DMA((2,)),
+        ],
+        out_specs=(HBM, HBM),
     )
 
 

time: 103 us -> 103 us (level)
  starting transfers between devices: 45.6 us -> 50.1 us
  Pallas kernels: 22.4 us -> 19.9 us
  waiting for transfers between devices: 32 us -> 29.9 us
    ppermute x6, starting transfers between devices: 31.5 us -> 35.8 us  [exchange(): return lax.ppermute(block, ('wide', 'narrow'), pairs)]
    pallas_call x13 -> x15, Pallas kernels: 22.4 us -> 19.9 us  [call(): pl.pallas_call(body, out_shape=tuple((jax.ShapeDtypeStruct(shape, dtype)...]
    ppermute x6, waiting for transfers between devices: 20.4 us -> 18 us  [exchange(): return lax.ppermute(block, ('wide', 'narrow'), pairs)]
  transfers between devices with their start and end apart: 13 -> 13, of which waited for: 6 -> 6; matrix products, arithmetic and copies ran while one was open for 1% -> 1% of each run, Pallas kernels for 17% -> 14%
where the time goes in v8:
time: 103 us; the launch traced here: 102 us
  starting transfers between devices  50.1 us (49%)
  waiting for transfers between devices  29.9 us (29%)
  Pallas kernels  19.9 us (19%)
  between operations  1.12 us (1%)
    ppermute x6, starting transfers between devices, exchange(): return lax.ppermute(block, ('wide', 'narrow'), pairs)  35.8 us
    pallas_call x15, Pallas kernels, call(): pl.pallas_call(body, out_shape=tuple((jax.ShapeDtypeStruct(shape, dtype)...  19.9 us
    ppermute x6, waiting for transfers between devices, exchange(): return lax.ppermute(block, ('wide', 'narrow'), pairs)  18 us
    ppermute x7, starting transfers between devices, narrow_swap(): return lax.ppermute(block, 'narrow', pairs)  14.4 us
    ppermute x7, waiting for transfers between devices, narrow_swap(): return lax.ppermute(block, 'narrow', pairs)  11.9 us
  transfers between devices with their start and end apart: 13, of which 6 were waited for; matrix products, arithmetic and copies ran while one was open for 1% of the time, Pallas kernels for 14%

profile of v8, /device:TPU:24, one launch (start us, length us, event | category | flops | bytes accessed | tf_op | source)
XLA Modules:
  0.0 101.7 jit_solution(2233264067679565966)
XLA Ops:
  0.7 1.7 %shard_map.68 = (bf16[768,512]{1,0:T(8,128)(2,1)S(1)}, bf16[272,512]{1,0:T(8,128)(2,1)S(1)}) custom-call(s32[8]{0:T(128)S(1)} %compare_select_fusion.6.flags, bf16[256,512]{1,0:T(8,128)(2,1)} %treated_any.1, bf16[1024,512]{1,0:T(8,128)(2,1)} %control_any.2, f32[2,128]{1,0:T(2,128)} %bitcast.10, s32[2,24]{1,0:T(2,128)} %band_any.1), custom_call_target="tpu_custom_call" | custom-call | tf_op jit(solution)/shard_map/pallas_call | solution.py:458
  2.4 2.7 %collective-permute-start = (bf16[272,512]{1,0:T(8,128)(2,1)S(1)}, bf16[272,512]{1,0:T(8,128)(2,1)S(1)}, u32[]{:S(2)}, u32[]{:S(2)}) collective-permute-start(bf16[272,512]{1,0:T(8,128)(2,1)S(1)} %get-tuple-element.32.own_ref), channel_id=1, source_target_pairs={{0,2},{2,0},{1,3},{3,1},{4,6},{6,4},{5,7},{7,5},{8,10},{10,8},{9,1... | collective-permute-start | bytes 835592 | tf_op jit(solution)/shard_map/ppermute | solution.py:35
  5.1 3.8 %collective-permute-start.3 = (bf16[768,512]{1,0:T(8,128)(2,1)S(1)}, bf16[768,512]{1,0:T(8,128)(2,1)S(1)}, u32[]{:S(2)}, u32[]{:S(2)}) collective-permute-start(bf16[768,512]{1,0:T(8,128)(2,1)S(1)} %get-tuple-element.35), channel_id=1, source_target_pairs={{0,4},{4,0},{8,12},{12,8},{16,20},{20,16},{24,28},{28,24},{32,36},... | collective-permute-start | bytes 2359304 | tf_op jit(solution)/shard_map/ppermute | solution.py:51
  8.9 13.2 %collective-permute-start.2 = (bf16[768,512]{1,0:T(8,128)(2,1)S(1)}, bf16[768,512]{1,0:T(8,128)(2,1)S(1)}, u32[]{:S(2)}, u32[]{:S(2)}) collective-permute-start(bf16[768,512]{1,0:T(8,128)(2,1)S(1)} %get-tuple-element.35), channel_id=1, source_target_pairs={{4,8},{8,4},{12,16},{16,12},{20,24},{24,20},{28,32},{32,28},{36,40... | collective-permute-start | bytes 2359304 | tf_op jit(solution)/shard_map/ppermute | solution.py:51
  22.1 0.0 collective-permute-done.y_ref
  22.1 0.6 shard_map.69.joined_ref
  22.7 1.9 %collective-permute-start.1 = (bf16[544,512]{1,0:T(8,128)(2,1)S(1)}, bf16[544,512]{1,0:T(8,128)(2,1)S(1)}, u32[]{:S(2)}, u32[]{:S(2)}) collective-permute-start(bf16[544,512]{1,0:T(8,128)(2,1)S(1)} %shard_map.69.joined_ref), channel_id=1, source_target_pairs={{0,1},{1,0},{2,3},{3,2},{4,5},{5,4},{6,7},{7,6},{8,9},{9,8},{10,11... | collective-permute-start | bytes 1671176 | tf_op jit(solution)/shard_map/ppermute | solution.py:35
  24.7 0.7 fusion
  25.4 1.5 %shard_map.70.columns_ref.own_columns_ref = bf16[1024,512]{1,0:T(8,128)(2,1)S(1)} custom-call(bf16[1024,512]{1,0:T(8,128)(2,1)} %control_any.2), custom_call_target="tpu_custom_call" | custom-call | tf_op jit(solution)/shard_map/pallas_call | solution.py:458
  26.9 0.0 collective-permute-done.1.far_ref
  26.9 2.2 %shard_map.71 = (bf16[1024,512]{1,0:T(8,128)(2,1)S(1)}, f32[1024,1024]{1,0:T(8,128)S(1)}, f32[1024,128]{1,0:T(8,128)S(1)}, f32[8,3072]{1,0:T(8,128)S(1)}, f32[10...) custom-call(s32[8]{0:T(128)S(1)} %compare_select_fusion.6.flags, bf16[544,512]{1,0:T(8,128)(2,1)S(1)} %shard_map.69.joined_ref, ...), custom_call_target="tpu_custom_call" | custom-call | tf_op jit(solution)/shard_map/pallas_call | solution.py:458
  29.1 1.0 %shard_map.72.kernel_ref = f32[256,1024]{1,0:T(8,128)S(1)} custom-call(s32[8]{0:T(128)S(1)} %compare_select_fusion.6.flags, bf16[1024,512]{1,0:T(8,128)(2,1)S(1)} %shard_map.70.columns_ref.own_columns_ref, bf16[1024,512]{1,0:T(8,128)(2,1)S(1)} %get-tuple-element.34.rows_ref, f32[32,1024]{1,0:T(8,128)S(1)} %get-tuple-element.37.pair_ref), custom_call_target="tpu_custom_call" | custom-call | tf_op jit(solution)/shard_map/pallas_call | solution.py:458
  30.1 0.0 collective-permute-done.3.even_ref
  30.1 8.9 %collective-permute-done.2.odd_ref = bf16[768,512]{1,0:T(8,128)(2,1)S(1)} collective-permute-done((bf16[768,512]{1,0:T(8,128)(2,1)S(1)}, bf16[768,512]{1,0:T(8,128)(2,1)S(1)}, u32[]{:S(2)}, u32[]{:S(2)}) %collective-permute-start.2) | collective-permute-done | bytes 786464 | tf_op jit(solution)/shard_map/ppermute | solution.py:51
  39.1 0.4 shard_map.73
  39.5 1.9 %collective-permute-start.11 = (bf16[512,512]{1,0:T(8,128)(2,1)S(1)}, bf16[512,512]{1,0:T(8,128)(2,1)S(1)}, u32[]{:S(2)}, u32[]{:S(2)}) collective-permute-start(bf16[512,512]{1,0:T(8,128)(2,1)S(1)} %get-tuple-element.58.own_ref), channel_id=1, source_target_pairs={{0,2},{2,0},{1,3},{3,1},{4,6},{6,4},{5,7},{7,5},{8,10},{10,8},{9,1... | collective-permute-start | bytes 1572872 | tf_op jit(solution)/shard_map/ppermute | solution.py:35
  41.4 1.9 %collective-permute-start.4 = (bf16[1024,512]{1,0:T(8,128)(2,1)S(1)}, bf16[1024,512]{1,0:T(8,128)(2,1)S(1)}, u32[]{:S(2)}, u32[]{:S(2)}) collective-permute-start(bf16[1024,512]{1,0:T(8,128)(2,1)S(1)} %get-tuple-element.40.columns_ref.near_columns_ref), channel_id=1, source_target_pairs={{0,1},{1,0},{2,3},{3,2},{4,5},{5,4},{6,7},{7,6},{8,9},{9,8},{10,11... | collective-permute-start | bytes 3145736 | tf_op jit(solution)/shard_map/ppermute | solution.py:35
  43.3 10.6 %collective-permute-done.11.y_ref = bf16[512,512]{1,0:T(8,128)(2,1)S(1)} collective-permute-done((bf16[512,512]{1,0:T(8,128)(2,1)S(1)}, bf16[512,512]{1,0:T(8,128)(2,1)S(1)}, u32[]{:S(2)}, u32[]{:S(2)}) %collective-permute-start.11) | collective-permute-done | bytes 524320 | tf_op jit(solution)/shard_map/ppermute | solution.py:35
  53.9 0.6 shard_map.80.near_ref
  54.5 1.9 %collective-permute-start.12 = (bf16[1024,512]{1,0:T(8,128)(2,1)S(1)}, bf16[1024,512]{1,0:T(8,128)(2,1)S(1)}, u32[]{:S(2)}, u32[]{:S(2)}) collective-permute-start(bf16[1024,512]{1,0:T(8,128)(2,1)S(1)} %shard_map.80.near_ref), channel_id=1, source_target_pairs={{0,1},{1,0},{2,3},{3,2},{4,5},{5,4},{6,7},{7,6},{8,9},{9,8},{10,11... | collective-permute-start | bytes 3145736 | tf_op jit(solution)/shard_map/ppermute | solution.py:35
  56.4 1.3 %shard_map.74 = (f32[1024,1024]{1,0:T(8,128)S(1)}, f32[1024,128]{1,0:T(8,128)S(1)}) custom-call(bf16[1024,512]{1,0:T(8,128)(2,1)S(1)} %get-tuple-element.34.rows_ref, bf16[1024,512]{1,0:T(8,128)(2,1)S(1)} %get-tuple-element.40.columns_ref.near_columns_ref, f32[8,3072]{1,0:T(8,128)S(1)} %get-tuple-element.41.mask_ref, ...), custom_call_target="tpu_custom_call" | custom-call | tf_op jit(solution)/shard_map/pallas_call | solution.py:458
  57.8 0.0 collective-permute-done.4.columns_ref.far_columns_ref
  57.8 2.9 %shard_map.75 = (f32[1024,1024]{1,0:T(8,128)S(1)}, f32[8,1024]{1,0:T(8,128)S(1)}, f32[16,1024]{1,0:T(8,128)S(1)}, f32[16,1024]{1,0:T(8,128)S(1)}) custom-call(s32[8]{0:T(128)S(1)} %compare_select_fusion.6.flags, bf16[1024,512]{1,0:T(8,128)(2,1)S(1)} %get-tuple-element.34.rows_ref, bf16[1024,512]{1,0:T(8,128)(2,1)S(1)} %collective-permute-done.4.columns_ref.far_columns_ref, ...), custom_call_target="tpu_custom_call" | custom-call | tf_op jit(solution)/shard_map/pallas_call | solution.py:458
  60.6 8.8 %collective-permute-start.5 = (f32[16,1024]{1,0:T(8,128)S(1)}, f32[16,1024]{1,0:T(8,128)S(1)}, u32[]{:S(2)}, u32[]{:S(2)}) collective-permute-start(f32[16,1024]{1,0:T(8,128)S(1)} %get-tuple-element.47), channel_id=1, source_target_pairs={{4,8},{8,4},{12,16},{16,12},{20,24},{24,20},{28,32},{32,28},{36,40... | collective-permute-start | bytes 196616 | tf_op jit(solution)/shard_map/ppermute | solution.py:51
  69.4 1.9 %collective-permute-start.6 = (f32[16,1024]{1,0:T(8,128)S(1)}, f32[16,1024]{1,0:T(8,128)S(1)}, u32[]{:S(2)}, u32[]{:S(2)}) collective-permute-start(f32[16,1024]{1,0:T(8,128)S(1)} %get-tuple-element.48), channel_id=1, source_target_pairs={{0,4},{4,0},{8,12},{12,8},{16,20},{20,16},{24,28},{28,24},{32,36},... | collective-permute-start | bytes 196616 | tf_op jit(solution)/shard_map/ppermute | solution.py:51
  71.4 1.6 %collective-permute-done.5.cross_ref = f32[16,1024]{1,0:T(8,128)S(1)} collective-permute-done((f32[16,1024]{1,0:T(8,128)S(1)}, f32[16,1024]{1,0:T(8,128)S(1)}, u32[]{:S(2)}, u32[]{:S(2)}) %collective-permute-start.5) | collective-permute-done | bytes 65568 | tf_op jit(solution)/shard_map/ppermute | solution.py:51
  72.9 2.7 %collective-permute-done.6.inner_ref = f32[16,1024]{1,0:T(8,128)S(1)} collective-permute-done((f32[16,1024]{1,0:T(8,128)S(1)}, f32[16,1024]{1,0:T(8,128)S(1)}, u32[]{:S(2)}, u32[]{:S(2)}) %collective-permute-start.6) | collective-permute-done | bytes 65568 | tf_op jit(solution)/shard_map/ppermute | solution.py:51
  75.6 1.9 %collective-permute-start.7 = (f32[32,1024]{1,0:T(8,128)S(1)}, f32[32,1024]{1,0:T(8,128)S(1)}, u32[]{:S(2)}, u32[]{:S(2)}) collective-permute-start(f32[32,1024]{1,0:T(8,128)S(1)} %shard_map.76.mine_in), channel_id=1, source_target_pairs={{0,1},{1,0},{2,3},{3,2},{4,5},{5,4},{6,7},{7,6},{8,9},{9,8},{10,11... | collective-permute-start | bytes 393224 | tf_op jit(solution)/shard_map/ppermute | solution.py:35
  77.5 1.3 %collective-permute-done.7.theirs_in = f32[32,1024]{1,0:T(8,128)S(1)} collective-permute-done((f32[32,1024]{1,0:T(8,128)S(1)}, f32[32,1024]{1,0:T(8,128)S(1)}, u32[]{:S(2)}, u32[]{:S(2)}) %collective-permute-start.7) | collective-permute-done | bytes 131104 | tf_op jit(solution)/shard_map/ppermute | solution.py:35
  78.9 2.6 %shard_map.77 = (f32[1024,128]{1,0:T(8,128)S(1)}, f32[1,1024]{1,0:T(1,128)S(1)}, f32[8,1024]{1,0:T(8,128)S(1)}, f32[16,1024]{1,0:T(8,128)S(1)}, f32[16,1024]{1,0:T(8,128)S(1)}) custom-call(s32[8]{0:T(128)S(1)} %compare_select_fusion.6.flags, f32[8,1024]{1,0:T(8,128)S(1)} %get-tuple-element.46.partial_in, f32[32,1024]{1,0:T(8,128)S(1)} %shard_map.76.mine_in, ...), custom_call_target="tpu_custom_call" | custom-call | tf_op jit(solution)/shard_map/pallas_call | solution.py:458
  81.5 6.1 %collective-permute-start.8 = (f32[16,1024]{1,0:T(8,128)S(1)}, f32[16,1024]{1,0:T(8,128)S(1)}, u32[]{:S(2)}, u32[]{:S(2)}) collective-permute-start(f32[16,1024]{1,0:T(8,128)S(1)} %get-tuple-element.54), channel_id=1, source_target_pairs={{4,8},{8,4},{12,16},{16,12},{20,24},{24,20},{28,32},{32,28},{36,40... | collective-permute-start | bytes 196616 | tf_op jit(solution)/shard_map/ppermute | solution.py:51
  87.6 1.9 %collective-permute-start.9 = (f32[16,1024]{1,0:T(8,128)S(1)}, f32[16,1024]{1,0:T(8,128)S(1)}, u32[]{:S(2)}, u32[]{:S(2)}) collective-permute-start(f32[16,1024]{1,0:T(8,128)S(1)} %get-tuple-element.55), channel_id=1, source_target_pairs={{0,4},{4,0},{8,12},{12,8},{16,20},{20,16},{24,28},{28,24},{32,36},... | collective-permute-start | bytes 196616 | tf_op jit(solution)/shard_map/ppermute | solution.py:51
  89.6 4.8 %collective-permute-done.8.cross_ref = f32[16,1024]{1,0:T(8,128)S(1)} collective-permute-done((f32[16,1024]{1,0:T(8,128)S(1)}, f32[16,1024]{1,0:T(8,128)S(1)}, u32[]{:S(2)}, u32[]{:S(2)}) %collective-permute-start.8) | collective-permute-done | bytes 65568 | tf_op jit(solution)/shard_map/ppermute | solution.py:51
  94.4 0.0 collective-permute-done.9.inner_ref
  94.4 2.1 %collective-permute-start.10 = (f32[32,1024]{1,0:T(8,128)S(1)}, f32[32,1024]{1,0:T(8,128)S(1)}, u32[]{:S(2)}, u32[]{:S(2)}) collective-permute-start(f32[32,1024]{1,0:T(8,128)S(1)} %shard_map.78.mine_in), channel_id=1, source_target_pairs={{0,1},{1,0},{2,3},{3,2},{4,5},{5,4},{6,7},{7,6},{8,9},{9,8},{10,11... | collective-permute-start | bytes 393224 | tf_op jit(solution)/shard_map/ppermute | solution.py:35
  96.5 0.4 shard_map.79.pushed_ref
  96.9 0.0 collective-permute-done.12.far_ref
  97.0 1.3 %shard_map.81 = (bf16[1024,512]{1,0:T(8,128)(2,1)S(1)}, bf16[1024,512]{1,0:T(8,128)(2,1)S(1)}, f32[256,2048]{1,0:T(8,128)S(1)}) custom-call(s32[8]{0:T(128)S(1)} %compare_select_fusion.6.flags, bf16[1024,512]{1,0:T(8,128)(2,1)S(1)} %shard_map.70.columns_ref.own_columns_ref, bf16[1024,512]{1,0:T(8,128)(2,1)S(1)} %shard_map.80.near_ref, ...), custom_call_target="tpu_custom_call" | custom-call | tf_op jit(solution)/shard_map/pallas_call | solution.py:458
  98.3 0.0 collective-permute-done.10.theirs_in
  98.3 3.3 %shard_map.82 = (f32[256,512]{1,0:T(8,128)}, f32[256,512]{1,0:T(8,128)}) custom-call(s32[8]{0:T(128)S(1)} %compare_select_fusion.6.flags, f32[8,1024]{1,0:T(8,128)S(1)} %get-tuple-element.53.partial_in, f32[32,1024]{1,0:T(8,128)S(1)} %shard_map.78.mine_in, f32[32,1024]{1,0:T(8,128)S(1)} %collective-permute-done.10.theirs_in, f32[1,1024]{1,0:T(1,128)S(1)} %bitcast.7, ...), custom_call_target="tpu_custom_call" | custom-call | tf_op jit(solution)/shard_map/pallas_call | solution.py:458
  (3 shorter events, 0.0 us)
Async XLA Ops:
  2.4 19.7 %collective-permute-start = (bf16[272,512]{1,0:T(8,128)(2,1)S(1)}, bf16[272,512]{1,0:T(8,128)(2,1)S(1)}, u32[]{:S(2)}, u32[]{:S(2)}) collective-permute-start(bf16[272,512]{1,0:T(8,128)(2,1)S(1)} %get-tuple-element.32.own_ref), channel_id=1, source_target_pairs={{0,2},{2,0},{1,3},{3,1},{4,6},{6,4},{5,7},{7,5},{8,10},{10,8},{9,1... | collective-permute-start | bytes 835592 | tf_op jit(solution)/shard_map/ppermute | solution.py:35
  5.1 25.0 %collective-permute-start.3 = (bf16[768,512]{1,0:T(8,128)(2,1)S(1)}, bf16[768,512]{1,0:T(8,128)(2,1)S(1)}, u32[]{:S(2)}, u32[]{:S(2)}) collective-permute-start(bf16[768,512]{1,0:T(8,128)(2,1)S(1)} %get-tuple-element.35), channel_id=1, source_target_pairs={{0,4},{4,0},{8,12},{12,8},{16,20},{20,16},{24,28},{28,24},{32,36},... | collective-permute-start | bytes 2359304 | tf_op jit(solution)/shard_map/ppermute | solution.py:51
  8.9 30.2 %collective-permute-start.2 = (bf16[768,512]{1,0:T(8,128)(2,1)S(1)}, bf16[768,512]{1,0:T(8,128)(2,1)S(1)}, u32[]{:S(2)}, u32[]{:S(2)}) collective-permute-start(bf16[768,512]{1,0:T(8,128)(2,1)S(1)} %get-tuple-element.35), channel_id=1, source_target_pairs={{4,8},{8,4},{12,16},{16,12},{20,24},{24,20},{28,32},{32,28},{36,40... | collective-permute-start | bytes 2359304 | tf_op jit(solution)/shard_map/ppermute | solution.py:51
  22.7 4.2 %collective-permute-start.1 = (bf16[544,512]{1,0:T(8,128)(2,1)S(1)}, bf16[544,512]{1,0:T(8,128)(2,1)S(1)}, u32[]{:S(2)}, u32[]{:S(2)}) collective-permute-start(bf16[544,512]{1,0:T(8,128)(2,1)S(1)} %shard_map.69.joined_ref), channel_id=1, source_target_pairs={{0,1},{1,0},{2,3},{3,2},{4,5},{5,4},{6,7},{7,6},{8,9},{9,8},{10,11... | collective-permute-start | bytes 1671176 | tf_op jit(solution)/shard_map/ppermute | solution.py:35
  39.5 14.4 %collective-permute-start.11 = (bf16[512,512]{1,0:T(8,128)(2,1)S(1)}, bf16[512,512]{1,0:T(8,128)(2,1)S(1)}, u32[]{:S(2)}, u32[]{:S(2)}) collective-permute-start(bf16[512,512]{1,0:T(8,128)(2,1)S(1)} %get-tuple-element.58.own_ref), channel_id=1, source_target_pairs={{0,2},{2,0},{1,3},{3,1},{4,6},{6,4},{5,7},{7,5},{8,10},{10,8},{9,1... | collective-permute-start | bytes 1572872 | tf_op jit(solution)/shard_map/ppermute | solution.py:35
  41.4 16.4 %collective-permute-start.4 = (bf16[1024,512]{1,0:T(8,128)(2,1)S(1)}, bf16[1024,512]{1,0:T(8,128)(2,1)S(1)}, u32[]{:S(2)}, u32[]{:S(2)}) collective-permute-start(bf16[1024,512]{1,0:T(8,128)(2,1)S(1)} %get-tuple-element.40.columns_ref.near_columns_ref), channel_id=1, source_target_pairs={{0,1},{1,0},{2,3},{3,2},{4,5},{5,4},{6,7},{7,6},{8,9},{9,8},{10,11... | collective-permute-start | bytes 3145736 | tf_op jit(solution)/shard_map/ppermute | solution.py:35
  54.5 42.4 %collective-permute-start.12 = (bf16[1024,512]{1,0:T(8,128)(2,1)S(1)}, bf16[1024,512]{1,0:T(8,128)(2,1)S(1)}, u32[]{:S(2)}, u32[]{:S(2)}) collective-permute-start(bf16[1024,512]{1,0:T(8,128)(2,1)S(1)} %shard_map.80.near_ref), channel_id=1, source_target_pairs={{0,1},{1,0},{2,3},{3,2},{4,5},{5,4},{6,7},{7,6},{8,9},{9,8},{10,11... | collective-permute-start | bytes 3145736 | tf_op jit(solution)/shard_map/ppermute | solution.py:35
  60.6 12.3 %collective-permute-start.5 = (f32[16,1024]{1,0:T(8,128)S(1)}, f32[16,1024]{1,0:T(8,128)S(1)}, u32[]{:S(2)}, u32[]{:S(2)}) collective-permute-start(f32[16,1024]{1,0:T(8,128)S(1)} %get-tuple-element.47), channel_id=1, source_target_pairs={{4,8},{8,4},{12,16},{16,12},{20,24},{24,20},{28,32},{32,28},{36,40... | collective-permute-start | bytes 196616 | tf_op jit(solution)/shard_map/ppermute | solution.py:51
  69.4 6.2 %collective-permute-start.6 = (f32[16,1024]{1,0:T(8,128)S(1)}, f32[16,1024]{1,0:T(8,128)S(1)}, u32[]{:S(2)}, u32[]{:S(2)}) collective-permute-start(f32[16,1024]{1,0:T(8,128)S(1)} %get-tuple-element.48), channel_id=1, source_target_pairs={{0,4},{4,0},{8,12},{12,8},{16,20},{20,16},{24,28},{28,24},{32,36},... | collective-permute-start | bytes 196616 | tf_op jit(solution)/shard_map/ppermute | solution.py:51
  75.6 3.2 %collective-permute-start.7 = (f32[32,1024]{1,0:T(8,128)S(1)}, f32[32,1024]{1,0:T(8,128)S(1)}, u32[]{:S(2)}, u32[]{:S(2)}) collective-permute-start(f32[32,1024]{1,0:T(8,128)S(1)} %shard_map.76.mine_in), channel_id=1, source_target_pairs={{0,1},{1,0},{2,3},{3,2},{4,5},{5,4},{6,7},{7,6},{8,9},{9,8},{10,11... | collective-permute-start | bytes 393224 | tf_op jit(solution)/shard_map/ppermute | solution.py:35
  81.5 12.9 %collective-permute-start.8 = (f32[16,1024]{1,0:T(8,128)S(1)}, f32[16,1024]{1,0:T(8,128)S(1)}, u32[]{:S(2)}, u32[]{:S(2)}) collective-permute-start(f32[16,1024]{1,0:T(8,128)S(1)} %get-tuple-element.54), channel_id=1, source_target_pairs={{4,8},{8,4},{12,16},{16,12},{20,24},{24,20},{28,32},{32,28},{36,40... | collective-permute-start | bytes 196616 | tf_op jit(solution)/shard_map/ppermute | solution.py:51
  87.6 6.8 %collective-permute-start.9 = (f32[16,1024]{1,0:T(8,128)S(1)}, f32[16,1024]{1,0:T(8,128)S(1)}, u32[]{:S(2)}, u32[]{:S(2)}) collective-permute-start(f32[16,1024]{1,0:T(8,128)S(1)} %get-tuple-element.55), channel_id=1, source_target_pairs={{0,4},{4,0},{8,12},{12,8},{16,20},{20,16},{24,28},{28,24},{32,36},... | collective-permute-start | bytes 196616 | tf_op jit(solution)/shard_map/ppermute | solution.py:51
  94.4 3.9 %collective-permute-start.10 = (f32[32,1024]{1,0:T(8,128)S(1)}, f32[32,1024]{1,0:T(8,128)S(1)}, u32[]{:S(2)}, u32[]{:S(2)}) collective-permute-start(f32[32,1024]{1,0:T(8,128)S(1)} %shard_map.78.mine_in), channel_id=1, source_target_pairs={{0,1},{1,0},{2,3},{3,2},{4,5},{5,4},{6,7},{7,6},{8,9},{9,8},{10,11... | collective-permute-start | bytes 393224 | tf_op jit(solution)/shard_map/ppermute | solution.py:35

commit v9 on v8

--- a/solution.py
+++ b/solution.py
@@ -25,8 +25,7 @@
 INFO = 16
 MESSAGE = QUARTER + INFO
 JOINED = 2 * MESSAGE
-LETTER = HALF + QUARTER
-NOTE = 16
+NOTE = 4
 
 NARROW, CORE, Y, ODD, A_EVEN, HAS_ODD, FLIPPED = range(7)
 
@@ -122,7 +121,7 @@
                 (treated_any, treated_ref),
                 (weight_any, weight_ref),
                 (band_any, band_ref),
-                (control_any.at[half, :], letter_ref.at[0:HALF, :]),
+                (control_any.at[half, :], letter_ref),
             )
         )
     ]
@@ -141,7 +140,6 @@
     info = info_ref[...].astype(BF16)
     message_ref[0:QUARTER, :] = rows
     message_ref[QUARTER:MESSAGE, :] = info
-    letter_ref[HALF:LETTER, :] = rows
     copies[3].wait()
 
 
@@ -168,11 +166,14 @@
         columns_ref[at, :] = normalize(control_ref[at, :])
 
 
-def open_kernel(odd_ref, even_ref, columns_ref, quarters_ref):
-    columns_ref[0:HALF, :] = normalize(odd_ref[0:HALF, :])
-    columns_ref[HALF:SLAB, :] = normalize(even_ref[0:HALF, :])
-    quarters_ref[0:QUARTER, :] = odd_ref[HALF:LETTER, :]
-    quarters_ref[QUARTER:HALF, :] = even_ref[HALF:LETTER, :]
+def open_kernel(odd_ref, even_ref, columns_ref):
+    columns_ref[0:HALF, :] = normalize(odd_ref[...])
+    columns_ref[HALF:SLAB, :] = normalize(even_ref[...])
+
+
+def collect_kernel(odd_ref, even_ref, quarters_ref):
+    quarters_ref[0:QUARTER, :] = odd_ref[0:QUARTER, :]
+    quarters_ref[QUARTER:HALF, :] = even_ref[0:QUARTER, :]
 
 
 def near_kernel(rows_ref, columns_ref, mask_ref, before_ref, kernel_ref, sums_ref):
@@ -183,7 +184,7 @@
 
 def prepare_kernel(
     flags, joined_ref, far_ref, columns_ref, rows_ref, kernel_ref, sums_ref, mask_ref, weight_ref,
-    pair_ref, band_ref,
+    pair_ref, compact_ref, band_ref,
 ):
     n, odd, core = flags[NARROW], flags[ODD], flags[CORE]
     rows_ref[0:HALF, :] = joined_ref[0:HALF, :]
@@ -218,13 +219,27 @@
         lax.broadcasted_iota(jnp.int32, (32, LANES), 1) == chosen, 1.0, 0.0
     ).astype(BF16)
     by_block = nt_dot(select, band).astype(BF16)
+    shift = (
+        lax.broadcasted_iota(jnp.int32, (LANES, LANES), 0)
+        == lax.broadcasted_iota(jnp.int32, (LANES, LANES), 1) % 8
+    )
+    flat = jnp.dot(
+        by_block, jnp.where(shift, 1.0, 0.0).astype(BF16), preferred_element_type=F32
+    )
+    kept = lax.broadcasted_iota(jnp.int32, (8, LANES), 0) == (
+        lax.broadcasted_iota(jnp.int32, (8, LANES), 1) // 8
+    )
+    compact_ref[...] = jnp.zeros_like(compact_ref)
+    for i in range(2):
+        row = jnp.where(kept, flat[8 * i : 8 * i + 8], 0.0)
+        compact_ref[i : i + 1, 0:LANES] = jnp.sum(row, axis=0, keepdims=True)
     spread = (
         lax.broadcasted_iota(jnp.int32, (LANES, SLAB), 0)
         == lax.broadcasted_iota(jnp.int32, (LANES, SLAB), 1) // LANES
     )
     pair_ref[...] = jnp.dot(
         by_block, jnp.where(spread, 1.0, 0.0).astype(BF16), preferred_element_type=F32
-    )
+    )[16:24]
 
     fill_kernel(rows_ref, columns_ref, mask_ref, slice(0, SLAB), kernel_ref, sums_ref, None)
 
@@ -276,7 +291,7 @@
 
 def far_kernel(
     flags, rows_ref, columns_ref, mask_ref, own_kernel_ref, near_kernel_ref, before_ref,
-    weight_ref, pair_ref, kernel_ref, partial_ref, cross_ref, inner_ref,
+    weight_ref, compact_ref, kernel_ref, partial_ref, cross_ref, inner_ref,
 ):
     def step(i, carry):
         own, near, far = carry
@@ -296,7 +311,7 @@
     zero = jnp.zeros((8, SLAB), F32)
     sums = lax.fori_loop(0, 4, step, (zero, zero, zero), unroll=True)
     finish_messages(
-        flags, sums, pair_ref[0:8, :], pair_ref[8:16, :], partial_ref, cross_ref, inner_ref
+        flags, sums, compact_ref[0:1, :], compact_ref[1:2, :], partial_ref, cross_ref, inner_ref
     )
 
 
@@ -359,8 +374,8 @@
 
 def own_transposed_kernel(flags, columns_ref, rows_ref, pair_ref, kernel_ref):
     values = jnp.exp(nt_dot(own_control(flags, columns_ref), rows_ref[...]) * SCALE)
-    kernel_ref[0:LANES, :] = values[:LANES] * pair_ref[16:17, :]
-    kernel_ref[LANES:QUARTER, :] = values[LANES:] * pair_ref[17:18, :]
+    kernel_ref[0:LANES, :] = values[:LANES] * pair_ref[0:1, :]
+    kernel_ref[LANES:QUARTER, :] = values[LANES:] * pair_ref[1:2, :]
 
 
 def push_kernel(lane_ref, kernel_ref, rows_ref, pushed_ref):
@@ -382,11 +397,16 @@
     even_rows_ref[HALF:SLAB, :] = far_ref[HALF:SLAB, :]
     n = flags[NARROW]
     close, _ = received(flags, mine_in, theirs_in)
+    lane = lax.broadcasted_iota(jnp.int32, (16, LANES), 1)
+    wanted = (lane < 64) & (lane // 8 == 2 * n + lax.broadcasted_iota(jnp.int32, (16, LANES), 0))
+    spread = (
+        lax.broadcasted_iota(jnp.int32, (LANES, SLAB), 0) % 8
+        == lax.broadcasted_iota(jnp.int32, (LANES, SLAB), 1) // LANES
+    )
+    spread = jnp.where(spread, 1.0, 0.0).astype(BF16)
     for i, (rows_ref, first) in enumerate(((odd_rows_ref, 2), (even_rows_ref, NOTE + 2))):
-        found = close[first : first + 2]
-        for j in range(1, 4):
-            found = jnp.where(n == j, close[first + 2 * j : first + 2 * j + 2], found)
-        found = turned(flags, found)
+        compact = jnp.where(wanted, close[first : first + 1, :LANES], 0.0).astype(BF16)
+        found = turned(flags, jnp.dot(compact, spread, preferred_element_type=F32))
         values = jnp.exp(nt_dot(own, rows_ref[...]) * SCALE)
         lanes = slice(i * SLAB, (i + 1) * SLAB)
         kernel_ref[0:LANES, lanes] = values[:LANES] * found[0:1]
@@ -403,6 +423,11 @@
         flags, partial_in, mine_in, theirs_in, (own_weight, odd_weight, even_weight)
     )
     close, _ = received(flags, mine_in, theirs_in)
+    pushed = pushed_ref[...]
+    for i, (row, rows) in enumerate(((2, odd_rows_ref), (NOTE + 2, even_rows_ref))):
+        scale = turned(flags, close[row : row + 1])
+        transport = (scale * transposed_ref[:, i * SLAB : (i + 1) * SLAB]).astype(BF16)
+        pushed = pushed + jnp.dot(transport, rows[...], preferred_element_type=F32)
     mine = pl.ds(pl.multiple_of(flags[Y] * QUARTER, QUARTER), QUARTER)
     row_scale = row_ref[mine, 0:1]
     mass = jnp.zeros((QUARTER, LANES), F32)
@@ -436,11 +461,6 @@
 
     own_scale = upright(own_quarter(scales[0]))
     own_mass = upright(own_quarter(own_weight[...]))
-    pushed = pushed_ref[...]
-    for i, (row, rows) in enumerate(((2, odd_rows_ref), (NOTE + 2, even_rows_ref))):
-        scale = turned(flags, close[row : row + 1])
-        transport = (scale * transposed_ref[:, i * SLAB : (i + 1) * SLAB]).astype(BF16)
-        pushed = pushed + jnp.dot(transport, rows[...], preferred_element_type=F32)
     at = pl.ds(pl.multiple_of(n * QUARTER, QUARTER), QUARTER)
     control_out[...] = own_mass * own_columns_ref[at, :].astype(F32) - own_scale * pushed
     control_copy = pltpu.make_async_copy(control_out, control_any, sems.at[1])
@@ -507,7 +527,7 @@
     letter, message = call(
         pack_kernel,
         [SMEM] + [HBM] * 4,
-        [((LETTER, WIDTH), BF16), ((MESSAGE, WIDTH), BF16)],
+        [((HALF, WIDTH), BF16), ((MESSAGE, WIDTH), BF16)],
         [flags, treated, control, own_weight, own_band],
         [
             pltpu.VMEM((QUARTER, WIDTH), BF16),
@@ -528,13 +548,15 @@
         [pltpu.VMEM((SLAB, WIDTH), BF16), pltpu.SemaphoreType.DMA((4,))],
     )
 
+    odd_message = exchange(message, (1, 1), True)
+    even_message = exchange(message, (1, 1), False)
     message_y = narrow_swap(message, SWAP_Y)
     (joined,) = call(
         join_kernel, [SMEM] + [VMEM] * 2, [((JOINED, WIDTH), BF16)], [flags, message, message_y]
     )
     joined_far = narrow_swap(joined, SWAP_CORE)
 
-    rows, own_kernel, sums, mask, weight, pairs = call(
+    rows, own_kernel, sums, mask, weight, pairs, compact = call(
         prepare_kernel,
         [SMEM] + [VMEM] * 3,
         [
@@ -543,7 +565,8 @@
             ((SLAB, LANES), F32),
             ((8, 3 * SLAB), F32),
             ((SLAB, LANES), F32),
-            ((32, SLAB), F32),
+            ((8, SLAB), F32),
+            ((8, SLAB), F32),
         ],
         [flags, joined, joined_far, own_columns],
         [pltpu.VMEM((LANES, LANES), F32)],
@@ -554,16 +577,17 @@
         [((QUARTER, SLAB), F32)],
         [flags, own_columns, rows, pairs],
     )
-    odd_letter, even_letter, _, _ = lax.optimization_barrier(
-        (odd_letter, even_letter, sums, own_transposed)
-    )
-    near_columns, quarters = call(
+    odd_letter, even_letter, _ = lax.optimization_barrier((odd_letter, even_letter, sums))
+    (near_columns,) = call(
         open_kernel,
         [VMEM] * 2,
-        [((SLAB, WIDTH), BF16), ((HALF, WIDTH), BF16)],
+        [((SLAB, WIDTH), BF16)],
         [odd_letter, even_letter],
     )
     far_columns = narrow_swap(near_columns, SWAP_CORE)
+    (quarters,) = call(
+        collect_kernel, [VMEM] * 2, [((HALF, WIDTH), BF16)], [odd_message, even_message]
+    )
     quarters_y = narrow_swap(quarters, SWAP_Y)
     near_values, sums = call(
         near_kernel,
@@ -575,7 +599,7 @@
         far_kernel,
         [SMEM] + [VMEM] * 8,
         [((SLAB, SLAB), F32), ((8, SLAB), F32), *MESSAGES],
-        [flags, rows, far_columns, mask, own_kernel, near_values, sums, weight, pairs],
+        [flags, rows, far_columns, mask, own_kernel, near_values, sums, weight, compact],
     )
     first = trade(messages)
 

time: 103 us -> 94.2 us (0.915)
  waiting for transfers between devices: 29.9 us -> 16.3 us
  starting transfers between devices: 50.1 us -> 53.8 us
  Pallas kernels: 19.9 us -> 21 us
    ppermute x7, waiting for transfers between devices: 11.9 us -> 1.06 us  [narrow_swap(): return lax.ppermute(block, 'narrow', pairs)]
    ppermute x6 -> x8, waiting for transfers between devices: 18 us -> 15.2 us  [exchange(): return lax.ppermute(block, ('wide', 'narrow'), pairs)]
    ppermute x6 -> x8, starting transfers between devices: 35.8 us -> 37.9 us  [exchange(): return lax.ppermute(block, ('wide', 'narrow'), pairs)]
    ppermute x7, starting transfers between devices: 14.4 us -> 15.9 us  [narrow_swap(): return lax.ppermute(block, 'narrow', pairs)]
    pallas_call x15 -> x16, Pallas kernels: 19.9 us -> 21 us  [call(): pl.pallas_call(body, out_shape=tuple((jax.ShapeDtypeStruct(shape, dtype)...]
  transfers between devices with their start and end apart: 13 -> 15, of which waited for: 6 -> 5; matrix products, arithmetic and copies ran while one was open for 1% -> 1% of each run, Pallas kernels for 14% -> 16%
where the time goes in v9:
time: 94.2 us; the launch traced here: 93 us
  starting transfers between devices  53.8 us (57%)
  Pallas kernels  21 us (22%)
  waiting for transfers between devices  16.3 us (17%)
  between operations  1.15 us (1%)
    ppermute x8, starting transfers between devices, exchange(): return lax.ppermute(block, ('wide', 'narrow'), pairs)  37.9 us
    pallas_call x16, Pallas kernels, call(): pl.pallas_call(body, out_shape=tuple((jax.ShapeDtypeStruct(shape, dtype)...  21 us
    ppermute x7, starting transfers between devices, narrow_swap(): return lax.ppermute(block, 'narrow', pairs)  15.9 us
    ppermute x8, waiting for transfers between devices, exchange(): return lax.ppermute(block, ('wide', 'narrow'), pairs)  15.2 us
  transfers between devices with their start and end apart: 15, of which 5 were waited for; matrix products, arithmetic and copies ran while one was open for 1% of the time, Pallas kernels for 16%

profile of v9, /device:TPU:24, one launch (start us, length us, event | category | flops | bytes accessed | tf_op | source)
XLA Modules:
  0.0 93.0 jit_solution(13273314897422097470)
XLA Ops:
  0.7 2.5 %shard_map.68 = (bf16[512,512]{1,0:T(8,128)(2,1)}, bf16[272,512]{1,0:T(8,128)(2,1)S(1)}) custom-call(s32[8]{0:T(128)S(1)} %compare_select_fusion.6.flags, bf16[256,512]{1,0:T(8,128)(2,1)} %treated_any.1, bf16[1024,512]{1,0:T(8,128)(2,1)} %control_any.2, f32[2,128]{1,0:T(2,128)} %bitcast.10, s32[2,24]{1,0:T(2,128)} %band_any.1), custom_call_target="tpu_custom_call" | custom-call | tf_op jit(solution)/shard_map/pallas_call | solution.py:478
  3.2 2.7 %collective-permute-start = (bf16[272,512]{1,0:T(8,128)(2,1)S(1)}, bf16[272,512]{1,0:T(8,128)(2,1)S(1)}, u32[]{:S(2)}, u32[]{:S(2)}) collective-permute-start(bf16[272,512]{1,0:T(8,128)(2,1)S(1)} %get-tuple-element.31.own_ref), channel_id=1, source_target_pairs={{0,2},{2,0},{1,3},{3,1},{4,6},{6,4},{5,7},{7,5},{8,10},{10,8},{9,1... | collective-permute-start | bytes 835592 | tf_op jit(solution)/shard_map/ppermute | solution.py:34
  5.9 14.1 %collective-permute-start.11 = (bf16[272,512]{1,0:T(8,128)(2,1)S(1)}, bf16[272,512]{1,0:T(8,128)(2,1)S(1)}, u32[]{:S(2)}, u32[]{:S(2)}) collective-permute-start(bf16[272,512]{1,0:T(8,128)(2,1)S(1)} %get-tuple-element.31.own_ref), channel_id=1, source_target_pairs={{4,8},{8,4},{12,16},{16,12},{20,24},{24,20},{28,32},{32,28},{36,40... | collective-permute-start | bytes 835592 | tf_op jit(solution)/shard_map/ppermute | solution.py:50
  20.0 1.9 %collective-permute-start.12 = (bf16[272,512]{1,0:T(8,128)(2,1)S(1)}, bf16[272,512]{1,0:T(8,128)(2,1)S(1)}, u32[]{:S(2)}, u32[]{:S(2)}) collective-permute-start(bf16[272,512]{1,0:T(8,128)(2,1)S(1)} %get-tuple-element.31.own_ref), channel_id=1, source_target_pairs={{0,4},{4,0},{8,12},{12,8},{16,20},{20,16},{24,28},{28,24},{32,36},... | collective-permute-start | bytes 835592 | tf_op jit(solution)/shard_map/ppermute | solution.py:50
  21.9 0.0 collective-permute-done.y_ref
  21.9 0.6 shard_map.69.joined_ref
  22.5 1.9 %collective-permute-start.1 = (bf16[544,512]{1,0:T(8,128)(2,1)S(1)}, bf16[544,512]{1,0:T(8,128)(2,1)S(1)}, u32[]{:S(2)}, u32[]{:S(2)}) collective-permute-start(bf16[544,512]{1,0:T(8,128)(2,1)S(1)} %shard_map.69.joined_ref), channel_id=1, source_target_pairs={{0,1},{1,0},{2,3},{3,2},{4,5},{5,4},{6,7},{7,6},{8,9},{9,8},{10,11... | collective-permute-start | bytes 1671176 | tf_op jit(solution)/shard_map/ppermute | solution.py:34
  24.4 4.8 %collective-permute-start.2 = (bf16[512,512]{1,0:T(8,128)(2,1)}, bf16[512,512]{1,0:T(8,128)(2,1)S(1)}, u32[]{:S(2)}, u32[]{:S(2)}) collective-permute-start(bf16[512,512]{1,0:T(8,128)(2,1)} %get-tuple-element.34), channel_id=1, source_target_pairs={{4,8},{8,4},{12,16},{16,12},{20,24},{24,20},{28,32},{32,28},{36,40... | collective-permute-start | bytes 1572872 | tf_op jit(solution)/shard_map/ppermute | solution.py:50
  29.3 1.9 %collective-permute-start.3 = (bf16[512,512]{1,0:T(8,128)(2,1)}, bf16[512,512]{1,0:T(8,128)(2,1)S(1)}, u32[]{:S(2)}, u32[]{:S(2)}) collective-permute-start(bf16[512,512]{1,0:T(8,128)(2,1)} %get-tuple-element.34), channel_id=1, source_target_pairs={{0,4},{4,0},{8,12},{12,8},{16,20},{20,16},{24,28},{28,24},{32,36},... | collective-permute-start | bytes 1572872 | tf_op jit(solution)/shard_map/ppermute | solution.py:50
  31.2 0.0 collective-permute-done.11.odd_ref
  31.2 0.0 collective-permute-done.12.even_ref
  31.3 2.9 %collective-permute-start.13 = (bf16[512,512]{1,0:T(8,128)(2,1)S(1)}, bf16[512,512]{1,0:T(8,128)(2,1)S(1)}, u32[]{:S(2)}, u32[]{:S(2)}) collective-permute-start(bf16[512,512]{1,0:T(8,128)(2,1)S(1)} %shard_map.80.own_ref), channel_id=1, source_target_pairs={{0,2},{2,0},{1,3},{3,1},{4,6},{6,4},{5,7},{7,5},{8,10},{10,8},{9,1... | collective-permute-start | bytes 1572872 | tf_op jit(solution)/shard_map/ppermute | solution.py:34
  34.2 0.7 fusion
  34.9 1.5 %shard_map.70.columns_ref.own_columns_ref = bf16[1024,512]{1,0:T(8,128)(2,1)S(1)} custom-call(bf16[1024,512]{1,0:T(8,128)(2,1)} %control_any.2), custom_call_target="tpu_custom_call" | custom-call | tf_op jit(solution)/shard_map/pallas_call | solution.py:478
  36.5 0.0 collective-permute-done.1.far_ref
  36.5 2.2 %shard_map.71 = (bf16[1024,512]{1,0:T(8,128)(2,1)S(1)}, f32[1024,1024]{1,0:T(8,128)S(1)}, f32[1024,128]{1,0:T(8,128)S(1)}, f32[8,3072]{1,0:T(8,128)S(1)}, f32[10...) custom-call(s32[8]{0:T(128)S(1)} %compare_select_fusion.6.flags, ...), custom_call_target="tpu_custom_call" | custom-call | tf_op jit(solution)/shard_map/pallas_call | solution.py:478
  38.7 7.6 %collective-permute-done.2.odd_ref = bf16[512,512]{1,0:T(8,128)(2,1)S(1)} collective-permute-done((bf16[512,512]{1,0:T(8,128)(2,1)}, bf16[512,512]{1,0:T(8,128)(2,1)S(1)}, u32[]{:S(2)}, u32[]{:S(2)}) %collective-permute-start.2) | collective-permute-done | bytes 524320 | tf_op jit(solution)/shard_map/ppermute | solution.py:50
  46.3 0.0 collective-permute-done.3.even_ref
  46.3 0.3 shard_map.72.columns_ref.near_columns_ref
  46.7 1.9 %collective-permute-start.4 = (bf16[1024,512]{1,0:T(8,128)(2,1)S(1)}, bf16[1024,512]{1,0:T(8,128)(2,1)S(1)}, u32[]{:S(2)}, u32[]{:S(2)}) collective-permute-start(bf16[1024,512]{1,0:T(8,128)(2,1)S(1)} %shard_map.72.columns_ref.near_columns_ref), channel_id=1, source_target_pairs={{0,1},{1,0},{2,3},{3,2},{4,5},{5,4},{6,7},{7,6},{8,9},{9,8},{10,11... | collective-permute-start | bytes 3145736 | tf_op jit(solution)/shard_map/ppermute | solution.py:34
  48.6 0.0 collective-permute-done.13.y_ref
  48.6 0.6 shard_map.81.near_ref
  49.2 2.4 %collective-permute-start.14 = (bf16[1024,512]{1,0:T(8,128)(2,1)S(1)}, bf16[1024,512]{1,0:T(8,128)(2,1)S(1)}, u32[]{:S(2)}, u32[]{:S(2)}) collective-permute-start(bf16[1024,512]{1,0:T(8,128)(2,1)S(1)} %shard_map.81.near_ref), channel_id=1, source_target_pairs={{0,1},{1,0},{2,3},{3,2},{4,5},{5,4},{6,7},{7,6},{8,9},{9,8},{10,11... | collective-permute-start | bytes 3145736 | tf_op jit(solution)/shard_map/ppermute | solution.py:34
  51.6 1.3 %shard_map.73 = (f32[1024,1024]{1,0:T(8,128)S(1)}, f32[1024,128]{1,0:T(8,128)S(1)}) custom-call(bf16[1024,512]{1,0:T(8,128)(2,1)S(1)} %get-tuple-element.33.rows_ref, bf16[1024,512]{1,0:T(8,128)(2,1)S(1)} %shard_map.72.columns_ref.near_columns_ref, f32[8,3072]{1,0:T(8,128)S(1)} %get-tuple-element.38.mask_ref, f32[1024,128]{1,0:T(8,128)S(1)} %get-tuple-element.35.before_ref), custom_call_target="tpu_custom_call" | custom-call | tf_op jit(solution)/shard_map/pallas_call | solution.py:478
  53.0 0.0 collective-permute-done.4.columns_ref.far_columns_ref
  53.0 2.8 %shard_map.74 = (f32[1024,1024]{1,0:T(8,128)S(1)}, f32[8,1024]{1,0:T(8,128)S(1)}, f32[4,1024]{1,0:T(4,128)S(1)}, f32[4,1024]{1,0:T(4,128)S(1)}) custom-call(s32[8]{0:T(128)S(1)} %compare_select_fusion.6.flags, bf16[1024,512]{1,0:T(8,128)(2,1)S(1)} %get-tuple-element.33.rows_ref, bf16[1024,512]{1,0:T(8,128)(2,1)S(1)} %collective-permute-done.4.columns_ref.far_columns_ref, ...), custom_call_target="tpu_custom_call" | custom-call | tf_op jit(solution)/shard_map/pallas_call | solution.py:478
  55.8 5.6 %collective-permute-start.5 = (f32[4,1024]{1,0:T(4,128)S(1)}, f32[4,1024]{1,0:T(4,128)S(1)}, u32[]{:S(2)}, u32[]{:S(2)}) collective-permute-start(f32[4,1024]{1,0:T(4,128)S(1)} %get-tuple-element.45), channel_id=1, source_target_pairs={{4,8},{8,4},{12,16},{16,12},{20,24},{24,20},{28,32},{32,28},{36,40... | collective-permute-start | bytes 49160 | tf_op jit(solution)/shard_map/ppermute | solution.py:50
  61.4 1.9 %collective-permute-start.6 = (f32[4,1024]{1,0:T(4,128)S(1)}, f32[4,1024]{1,0:T(4,128)S(1)}, u32[]{:S(2)}, u32[]{:S(2)}) collective-permute-start(f32[4,1024]{1,0:T(4,128)S(1)} %get-tuple-element.46), channel_id=1, source_target_pairs={{0,4},{4,0},{8,12},{12,8},{16,20},{20,16},{24,28},{28,24},{32,36},... | collective-permute-start | bytes 49160 | tf_op jit(solution)/shard_map/ppermute | solution.py:50
  63.3 3.7 %collective-permute-done.5.cross_ref = f32[4,1024]{1,0:T(4,128)S(1)} collective-permute-done((f32[4,1024]{1,0:T(4,128)S(1)}, f32[4,1024]{1,0:T(4,128)S(1)}, u32[]{:S(2)}, u32[]{:S(2)}) %collective-permute-start.5) | collective-permute-done | bytes 16416 | tf_op jit(solution)/shard_map/ppermute | solution.py:50
  67.0 0.0 collective-permute-done.6.inner_ref
  67.1 2.0 %collective-permute-start.7 = (f32[8,1024]{1,0:T(8,128)S(1)}, f32[8,1024]{1,0:T(8,128)S(1)}, u32[]{:S(2)}, u32[]{:S(2)}) collective-permute-start(f32[8,1024]{1,0:T(8,128)S(1)} %shard_map.75.mine_in), channel_id=1, source_target_pairs={{0,1},{1,0},{2,3},{3,2},{4,5},{5,4},{6,7},{7,6},{8,9},{9,8},{10,11... | collective-permute-start | bytes 98312 | tf_op jit(solution)/shard_map/ppermute | solution.py:34
  69.1 1.0 %collective-permute-done.7.theirs_in = f32[8,1024]{1,0:T(8,128)S(1)} collective-permute-done((f32[8,1024]{1,0:T(8,128)S(1)}, f32[8,1024]{1,0:T(8,128)S(1)}, u32[]{:S(2)}, u32[]{:S(2)}) %collective-permute-start.7) | collective-permute-done | bytes 32800 | tf_op jit(solution)/shard_map/ppermute | solution.py:34
  70.1 2.6 %shard_map.76 = (f32[1024,128]{1,0:T(8,128)S(1)}, f32[1,1024]{1,0:T(1,128)S(1)}, f32[8,1024]{1,0:T(8,128)S(1)}, f32[4,1024]{1,0:T(4,128)S(1)}, f32[4,1024]{1,0:T(4,128)S(1)}) custom-call(s32[8]{0:T(128)S(1)} %compare_select_fusion.6.flags, f32[8,1024]{1,0:T(8,128)S(1)} %get-tuple-element.44.partial_in, f32[8,1024]{1,0:T(8,128)S(1)} %shard_map.75.mine_in, ...), custom_call_target="tpu_custom_call" | custom-call | tf_op jit(solution)/shard_map/pallas_call | solution.py:478
  72.8 5.7 %collective-permute-start.8 = (f32[4,1024]{1,0:T(4,128)S(1)}, f32[4,1024]{1,0:T(4,128)S(1)}, u32[]{:S(2)}, u32[]{:S(2)}) collective-permute-start(f32[4,1024]{1,0:T(4,128)S(1)} %get-tuple-element.52), channel_id=1, source_target_pairs={{4,8},{8,4},{12,16},{16,12},{20,24},{24,20},{28,32},{32,28},{36,40... | collective-permute-start | bytes 49160 | tf_op jit(solution)/shard_map/ppermute | solution.py:50
  78.5 1.9 %collective-permute-start.9 = (f32[4,1024]{1,0:T(4,128)S(1)}, f32[4,1024]{1,0:T(4,128)S(1)}, u32[]{:S(2)}, u32[]{:S(2)}) collective-permute-start(f32[4,1024]{1,0:T(4,128)S(1)} %get-tuple-element.53), channel_id=1, source_target_pairs={{0,4},{4,0},{8,12},{12,8},{16,20},{20,16},{24,28},{28,24},{32,36},... | collective-permute-start | bytes 49160 | tf_op jit(solution)/shard_map/ppermute | solution.py:50
  80.4 3.4 %collective-permute-done.8.cross_ref = f32[4,1024]{1,0:T(4,128)S(1)} collective-permute-done((f32[4,1024]{1,0:T(4,128)S(1)}, f32[4,1024]{1,0:T(4,128)S(1)}, u32[]{:S(2)}, u32[]{:S(2)}) %collective-permute-start.8) | collective-permute-done | bytes 16416 | tf_op jit(solution)/shard_map/ppermute | solution.py:50
  83.8 0.4 collective-permute-done.9.inner_ref
  84.3 2.1 %collective-permute-start.10 = (f32[8,1024]{1,0:T(8,128)S(1)}, f32[8,1024]{1,0:T(8,128)S(1)}, u32[]{:S(2)}, u32[]{:S(2)}) collective-permute-start(f32[8,1024]{1,0:T(8,128)S(1)} %shard_map.77.mine_in), channel_id=1, source_target_pairs={{0,1},{1,0},{2,3},{3,2},{4,5},{5,4},{6,7},{7,6},{8,9},{9,8},{10,11... | collective-permute-start | bytes 98312 | tf_op jit(solution)/shard_map/ppermute | solution.py:34
  86.4 1.0 %shard_map.78.kernel_ref = f32[256,1024]{1,0:T(8,128)S(1)} custom-call(s32[8]{0:T(128)S(1)} %compare_select_fusion.6.flags, bf16[1024,512]{1,0:T(8,128)(2,1)S(1)} %shard_map.70.columns_ref.own_columns_ref, bf16[1024,512]{1,0:T(8,128)(2,1)S(1)} %get-tuple-element.33.rows_ref, f32[8,1024]{1,0:T(8,128)S(1)} %get-tuple-element.56.pair_ref), custom_call_target="tpu_custom_call" | custom-call | tf_op jit(solution)/shard_map/pallas_call | solution.py:478
  87.4 0.4 shard_map.79.pushed_ref
  87.9 0.0 collective-permute-done.14.far_ref
  87.9 1.5 %shard_map.82 = (bf16[1024,512]{1,0:T(8,128)(2,1)S(1)}, bf16[1024,512]{1,0:T(8,128)(2,1)S(1)}, f32[256,2048]{1,0:T(8,128)S(1)}) custom-call(s32[8]{0:T(128)S(1)} %compare_select_fusion.6.flags, bf16[1024,512]{1,0:T(8,128)(2,1)S(1)} %shard_map.70.columns_ref.own_columns_ref, bf16[1024,512]{1,0:T(8,128)(2,1)S(1)} %shard_map.81.near_ref, ...), custom_call_target="tpu_custom_call" | custom-call | tf_op jit(solution)/shard_map/pallas_call | solution.py:478
  89.4 0.0 collective-permute-done.10.theirs_in
  89.4 3.4 %shard_map.83 = (f32[256,512]{1,0:T(8,128)}, f32[256,512]{1,0:T(8,128)}) custom-call(s32[8]{0:T(128)S(1)} %compare_select_fusion.6.flags, f32[8,1024]{1,0:T(8,128)S(1)} %get-tuple-element.51.partial_in, f32[8,1024]{1,0:T(8,128)S(1)} %shard_map.77.mine_in, f32[8,1024]{1,0:T(8,128)S(1)} %collective-permute-done.10.theirs_in, f32[1,1024]{1,0:T(1,128)S(1)} %bitcast.7, ...), custom_call_target="tpu_custom_call" | custom-call | tf_op jit(solution)/shard_map/pallas_call | solution.py:478
  (4 shorter events, 0.1 us)
Async XLA Ops:
  3.2 18.7 %collective-permute-start = (bf16[272,512]{1,0:T(8,128)(2,1)S(1)}, bf16[272,512]{1,0:T(8,128)(2,1)S(1)}, u32[]{:S(2)}, u32[]{:S(2)}) collective-permute-start(bf16[272,512]{1,0:T(8,128)(2,1)S(1)} %get-tuple-element.31.own_ref), channel_id=1, source_target_pairs={{0,2},{2,0},{1,3},{3,1},{4,6},{6,4},{5,7},{7,5},{8,10},{10,8},{9,1... | collective-permute-start | bytes 835592 | tf_op jit(solution)/shard_map/ppermute | solution.py:34
  5.9 25.3 %collective-permute-start.11 = (bf16[272,512]{1,0:T(8,128)(2,1)S(1)}, bf16[272,512]{1,0:T(8,128)(2,1)S(1)}, u32[]{:S(2)}, u32[]{:S(2)}) collective-permute-start(bf16[272,512]{1,0:T(8,128)(2,1)S(1)} %get-tuple-element.31.own_ref), channel_id=1, source_target_pairs={{4,8},{8,4},{12,16},{16,12},{20,24},{24,20},{28,32},{32,28},{36,40... | collective-permute-start | bytes 835592 | tf_op jit(solution)/shard_map/ppermute | solution.py:50
  20.0 11.3 %collective-permute-start.12 = (bf16[272,512]{1,0:T(8,128)(2,1)S(1)}, bf16[272,512]{1,0:T(8,128)(2,1)S(1)}, u32[]{:S(2)}, u32[]{:S(2)}) collective-permute-start(bf16[272,512]{1,0:T(8,128)(2,1)S(1)} %get-tuple-element.31.own_ref), channel_id=1, source_target_pairs={{0,4},{4,0},{8,12},{12,8},{16,20},{20,16},{24,28},{28,24},{32,36},... | collective-permute-start | bytes 835592 | tf_op jit(solution)/shard_map/ppermute | solution.py:50
  22.5 14.0 %collective-permute-start.1 = (bf16[544,512]{1,0:T(8,128)(2,1)S(1)}, bf16[544,512]{1,0:T(8,128)(2,1)S(1)}, u32[]{:S(2)}, u32[]{:S(2)}) collective-permute-start(bf16[544,512]{1,0:T(8,128)(2,1)S(1)} %shard_map.69.joined_ref), channel_id=1, source_target_pairs={{0,1},{1,0},{2,3},{3,2},{4,5},{5,4},{6,7},{7,6},{8,9},{9,8},{10,11... | collective-permute-start | bytes 1671176 | tf_op jit(solution)/shard_map/ppermute | solution.py:34
  24.4 21.9 %collective-permute-start.2 = (bf16[512,512]{1,0:T(8,128)(2,1)}, bf16[512,512]{1,0:T(8,128)(2,1)S(1)}, u32[]{:S(2)}, u32[]{:S(2)}) collective-permute-start(bf16[512,512]{1,0:T(8,128)(2,1)} %get-tuple-element.34), channel_id=1, source_target_pairs={{4,8},{8,4},{12,16},{16,12},{20,24},{24,20},{28,32},{32,28},{36,40... | collective-permute-start | bytes 1572872 | tf_op jit(solution)/shard_map/ppermute | solution.py:50
  29.3 17.0 %collective-permute-start.3 = (bf16[512,512]{1,0:T(8,128)(2,1)}, bf16[512,512]{1,0:T(8,128)(2,1)S(1)}, u32[]{:S(2)}, u32[]{:S(2)}) collective-permute-start(bf16[512,512]{1,0:T(8,128)(2,1)} %get-tuple-element.34), channel_id=1, source_target_pairs={{0,4},{4,0},{8,12},{12,8},{16,20},{20,16},{24,28},{28,24},{32,36},... | collective-permute-start | bytes 1572872 | tf_op jit(solution)/shard_map/ppermute | solution.py:50
  31.3 17.3 %collective-permute-start.13 = (bf16[512,512]{1,0:T(8,128)(2,1)S(1)}, bf16[512,512]{1,0:T(8,128)(2,1)S(1)}, u32[]{:S(2)}, u32[]{:S(2)}) collective-permute-start(bf16[512,512]{1,0:T(8,128)(2,1)S(1)} %shard_map.80.own_ref), channel_id=1, source_target_pairs={{0,2},{2,0},{1,3},{3,1},{4,6},{6,4},{5,7},{7,5},{8,10},{10,8},{9,1... | collective-permute-start | bytes 1572872 | tf_op jit(solution)/shard_map/ppermute | solution.py:34
  46.7 6.3 %collective-permute-start.4 = (bf16[1024,512]{1,0:T(8,128)(2,1)S(1)}, bf16[1024,512]{1,0:T(8,128)(2,1)S(1)}, u32[]{:S(2)}, u32[]{:S(2)}) collective-permute-start(bf16[1024,512]{1,0:T(8,128)(2,1)S(1)} %shard_map.72.columns_ref.near_columns_ref), channel_id=1, source_target_pairs={{0,1},{1,0},{2,3},{3,2},{4,5},{5,4},{6,7},{7,6},{8,9},{9,8},{10,11... | collective-permute-start | bytes 3145736 | tf_op jit(solution)/shard_map/ppermute | solution.py:34
  49.2 38.7 %collective-permute-start.14 = (bf16[1024,512]{1,0:T(8,128)(2,1)S(1)}, bf16[1024,512]{1,0:T(8,128)(2,1)S(1)}, u32[]{:S(2)}, u32[]{:S(2)}) collective-permute-start(bf16[1024,512]{1,0:T(8,128)(2,1)S(1)} %shard_map.81.near_ref), channel_id=1, source_target_pairs={{0,1},{1,0},{2,3},{3,2},{4,5},{5,4},{6,7},{7,6},{8,9},{9,8},{10,11... | collective-permute-start | bytes 3145736 | tf_op jit(solution)/shard_map/ppermute | solution.py:34
  55.8 11.2 %collective-permute-start.5 = (f32[4,1024]{1,0:T(4,128)S(1)}, f32[4,1024]{1,0:T(4,128)S(1)}, u32[]{:S(2)}, u32[]{:S(2)}) collective-permute-start(f32[4,1024]{1,0:T(4,128)S(1)} %get-tuple-element.45), channel_id=1, source_target_pairs={{4,8},{8,4},{12,16},{16,12},{20,24},{24,20},{28,32},{32,28},{36,40... | collective-permute-start | bytes 49160 | tf_op jit(solution)/shard_map/ppermute | solution.py:50
  61.4 5.6 %collective-permute-start.6 = (f32[4,1024]{1,0:T(4,128)S(1)}, f32[4,1024]{1,0:T(4,128)S(1)}, u32[]{:S(2)}, u32[]{:S(2)}) collective-permute-start(f32[4,1024]{1,0:T(4,128)S(1)} %get-tuple-element.46), channel_id=1, source_target_pairs={{0,4},{4,0},{8,12},{12,8},{16,20},{20,16},{24,28},{28,24},{32,36},... | collective-permute-start | bytes 49160 | tf_op jit(solution)/shard_map/ppermute | solution.py:50
  67.1 3.1 %collective-permute-start.7 = (f32[8,1024]{1,0:T(8,128)S(1)}, f32[8,1024]{1,0:T(8,128)S(1)}, u32[]{:S(2)}, u32[]{:S(2)}) collective-permute-start(f32[8,1024]{1,0:T(8,128)S(1)} %shard_map.75.mine_in), channel_id=1, source_target_pairs={{0,1},{1,0},{2,3},{3,2},{4,5},{5,4},{6,7},{7,6},{8,9},{9,8},{10,11... | collective-permute-start | bytes 98312 | tf_op jit(solution)/shard_map/ppermute | solution.py:34
  72.8 11.1 %collective-permute-start.8 = (f32[4,1024]{1,0:T(4,128)S(1)}, f32[4,1024]{1,0:T(4,128)S(1)}, u32[]{:S(2)}, u32[]{:S(2)}) collective-permute-start(f32[4,1024]{1,0:T(4,128)S(1)} %get-tuple-element.52), channel_id=1, source_target_pairs={{4,8},{8,4},{12,16},{16,12},{20,24},{24,20},{28,32},{32,28},{36,40... | collective-permute-start | bytes 49160 | tf_op jit(solution)/shard_map/ppermute | solution.py:50
  78.5 5.8 %collective-permute-start.9 = (f32[4,1024]{1,0:T(4,128)S(1)}, f32[4,1024]{1,0:T(4,128)S(1)}, u32[]{:S(2)}, u32[]{:S(2)}) collective-permute-start(f32[4,1024]{1,0:T(4,128)S(1)} %get-tuple-element.53), channel_id=1, source_target_pairs={{0,4},{4,0},{8,12},{12,8},{16,20},{20,16},{24,28},{28,24},{32,36},... | collective-permute-start | bytes 49160 | tf_op jit(solution)/shard_map/ppermute | solution.py:50
  84.3 5.1 %collective-permute-start.10 = (f32[8,1024]{1,0:T(8,128)S(1)}, f32[8,1024]{1,0:T(8,128)S(1)}, u32[]{:S(2)}, u32[]{:S(2)}) collective-permute-start(f32[8,1024]{1,0:T(8,128)S(1)} %shard_map.77.mine_in), channel_id=1, source_target_pairs={{0,1},{1,0},{2,3},{3,2},{4,5},{5,4},{6,7},{7,6},{8,9},{9,8},{10,11... | collective-permute-start | bytes 98312 | tf_op jit(solution)/shard_map/ppermute | solution.py:34

commit v10 on v9

--- a/solution.py
+++ b/solution.py
@@ -27,7 +27,7 @@
 JOINED = 2 * MESSAGE
 NOTE = 4
 
-NARROW, CORE, Y, ODD, A_EVEN, HAS_ODD, FLIPPED = range(7)
+NARROW, CORE, Y, ODD, A_EVEN, HAS_ODD, FLIPPED, WIDE, WIDE_ODD, WIDE_EVEN = range(10)
 
 
 def narrow_swap(block, pairs):
@@ -110,10 +110,11 @@
 
 
 def pack_kernel(
-    flags, treated_any, control_any, weight_any, band_any, letter_ref, message_ref, treated_ref,
-    weight_ref, band_ref, info_ref, sems,
+    flags, treated_any, control_any, weight_any, band_any, letter_ref, other_ref, message_ref,
+    treated_ref, weight_ref, band_ref, info_ref, sems,
 ):
     half = pl.ds(pl.multiple_of(flags[CORE] * HALF, HALF), HALF)
+    other = pl.ds(pl.multiple_of((1 - flags[CORE]) * HALF, HALF), HALF)
     copies = [
         pltpu.make_async_copy(source, target, sems.at[i])
         for i, (source, target) in enumerate(
@@ -122,6 +123,7 @@
                 (weight_any, weight_ref),
                 (band_any, band_ref),
                 (control_any.at[half, :], letter_ref),
+                (control_any.at[other, :], other_ref),
             )
         )
     ]
@@ -140,7 +142,8 @@
     info = info_ref[...].astype(BF16)
     message_ref[0:QUARTER, :] = rows
     message_ref[QUARTER:MESSAGE, :] = info
-    copies[3].wait()
+    for copy in copies[3:]:
+        copy.wait()
 
 
 def join_kernel(flags, own_ref, y_ref, joined_ref):
@@ -149,21 +152,26 @@
         joined_ref[pl.ds(pl.multiple_of(HALF + y * INFO, INFO), INFO), :] = ref[QUARTER:MESSAGE, :]
 
 
-def columns_kernel(control_any, columns_ref, control_ref, sems):
+def columns_kernel(
+    flags, letter_ref, other_ref, weight_any, columns_ref, own_ref, odd_ref, even_ref, fetched_ref,
+    sems,
+):
     copies = [
         pltpu.make_async_copy(
-            control_any.at[i * QUARTER : (i + 1) * QUARTER, :],
-            control_ref.at[i * QUARTER : (i + 1) * QUARTER, :],
+            weight_any.at[pl.ds(pl.multiple_of(flags[which] * 8, 8), 8), :],
+            fetched_ref.at[i],
             sems.at[i],
         )
-        for i in range(4)
+        for i, which in enumerate((WIDE, WIDE_ODD, WIDE_EVEN))
     ]
     for copy in copies:
         copy.start()
-    for i, copy in enumerate(copies):
+    for ref, half in ((letter_ref, flags[CORE]), (other_ref, 1 - flags[CORE])):
+        columns_ref[pl.ds(pl.multiple_of(half * HALF, HALF), HALF), :] = normalize(ref[...])
+    for i, (copy, ref) in enumerate(zip(copies, (own_ref, odd_ref, even_ref), strict=True)):
         copy.wait()
-        at = slice(i * QUARTER, (i + 1) * QUARTER)
-        columns_ref[at, :] = normalize(control_ref[at, :])
+        for j in range(8):
+            ref[0:1, j * LANES : (j + 1) * LANES] = fetched_ref[i, j : j + 1, :]
 
 
 def open_kernel(odd_ref, even_ref, columns_ref):
@@ -428,6 +436,23 @@
         scale = turned(flags, close[row : row + 1])
         transport = (scale * transposed_ref[:, i * SLAB : (i + 1) * SLAB]).astype(BF16)
         pushed = pushed + jnp.dot(transport, rows[...], preferred_element_type=F32)
+    n = flags[NARROW]
+
+    def own_quarter(row):
+        found = row[:, :QUARTER]
+        for i in range(1, 4):
+            found = jnp.where(n == i, row[:, i * QUARTER : (i + 1) * QUARTER], found)
+        return found
+
+    def upright(row):
+        return jnp.concatenate([to_column(row[:, :LANES]), to_column(row[:, LANES:])], axis=0)
+
+    own_scale = upright(own_quarter(scales[0]))
+    own_mass = upright(own_quarter(own_weight[...]))
+    at = pl.ds(pl.multiple_of(n * QUARTER, QUARTER), QUARTER)
+    control_out[...] = own_mass * own_columns_ref[at, :].astype(F32) - own_scale * pushed
+    control_copy = pltpu.make_async_copy(control_out, control_any, sems.at[1])
+    control_copy.start()
     mine = pl.ds(pl.multiple_of(flags[Y] * QUARTER, QUARTER), QUARTER)
     row_scale = row_ref[mine, 0:1]
     mass = jnp.zeros((QUARTER, LANES), F32)
@@ -448,23 +473,6 @@
     treated_copy = pltpu.make_async_copy(treated_out, treated_any, sems.at[0])
     treated_copy.start()
 
-    n = flags[NARROW]
-
-    def own_quarter(row):
-        found = row[:, :QUARTER]
-        for i in range(1, 4):
-            found = jnp.where(n == i, row[:, i * QUARTER : (i + 1) * QUARTER], found)
-        return found
-
-    def upright(row):
-        return jnp.concatenate([to_column(row[:, :LANES]), to_column(row[:, LANES:])], axis=0)
-
-    own_scale = upright(own_quarter(scales[0]))
-    own_mass = upright(own_quarter(own_weight[...]))
-    at = pl.ds(pl.multiple_of(n * QUARTER, QUARTER), QUARTER)
-    control_out[...] = own_mass * own_columns_ref[at, :].astype(F32) - own_scale * pushed
-    control_copy = pltpu.make_async_copy(control_out, control_any, sems.at[1])
-    control_copy.start()
     treated_copy.wait()
     control_copy.wait()
 
@@ -510,42 +518,42 @@
         jnp.logical_xor(wide_index % 4 >= 2, odd == 1).astype(jnp.int32),
         ((toward_odd >= 0) & (toward_odd < wide_count)).astype(jnp.int32),
         (jnp.minimum(wide_index, toward_odd) == wide_count // 2 - 1).astype(jnp.int32),
-    )
-    place = lax.iota(jnp.int32, 8)
-    flags = jnp.zeros((8,), jnp.int32)
+        wide_index,
+        jnp.clip(toward_odd, 0, wide_count - 1),
+        toward_even,
+    )
+    place = lax.iota(jnp.int32, 16)
+    flags = jnp.zeros((16,), jnp.int32)
     for i, value in enumerate(values):
         flags = jnp.where(place == i, value, flags)
-    weights = [
-        lax.dynamic_slice_in_dim(control_weight, jnp.maximum(at, 0) * SLAB, SLAB).reshape(1, SLAB)
-        for at in (wide_index, toward_odd, toward_even)
-    ]
-
-    treated, control, own_weight, own_band = (
+    treated, control, own_weight, own_band, column_weight = (
         pltpu.with_memory_space_constraint(x, pltpu.HBM)
-        for x in (treated, control, treated_weight.reshape(2, LANES), band)
-    )
-    letter, message = call(
+        for x in (
+            treated, control, treated_weight.reshape(2, LANES), band,
+            control_weight.reshape(-1, LANES),
+        )
+    )
+    letter, other, message = call(
         pack_kernel,
         [SMEM] + [HBM] * 4,
-        [((HALF, WIDTH), BF16), ((MESSAGE, WIDTH), BF16)],
+        [((HALF, WIDTH), BF16), ((HALF, WIDTH), BF16), ((MESSAGE, WIDTH), BF16)],
         [flags, treated, control, own_weight, own_band],
         [
             pltpu.VMEM((QUARTER, WIDTH), BF16),
             pltpu.VMEM((2, LANES), F32),
             pltpu.VMEM((2, 24), jnp.int32),
             pltpu.VMEM((INFO, WIDTH), F32),
-            pltpu.SemaphoreType.DMA((4,)),
+            pltpu.SemaphoreType.DMA((5,)),
         ],
     )
     odd_letter = exchange(letter, (1, 1), True)
     even_letter = exchange(letter, (1, 1), False)
-    control, *weights = lax.optimization_barrier((control, *weights))
-    (own_columns,) = call(
+    own_columns, *weights = call(
         columns_kernel,
-        [HBM],
-        [((SLAB, WIDTH), BF16)],
-        [pltpu.with_memory_space_constraint(control, pltpu.HBM)],
-        [pltpu.VMEM((SLAB, WIDTH), BF16), pltpu.SemaphoreType.DMA((4,))],
+        [SMEM] + [VMEM] * 2 + [HBM],
+        [((SLAB, WIDTH), BF16)] + [((1, SLAB), F32)] * 3,
+        [flags, letter, other, column_weight],
+        [pltpu.VMEM((3, 8, LANES), F32), pltpu.SemaphoreType.DMA((3,))],
     )
 
     odd_message = exchange(message, (1, 1), True)

time: 94.2 us -> 93.2 us (0.989)
  transfers between devices with their start and end apart: 15 -> 15, of which waited for: 5 -> 5; matrix products, arithmetic and copies ran while one was open for 1% -> 0% of each run, Pallas kernels for 16% -> 17%
where the time goes in v10:
time: 93.2 us; the launch traced here: 92.1 us
  starting transfers between devices  54.1 us (58%)
  Pallas kernels  20.4 us (22%)
  waiting for transfers between devices  16.4 us (18%)
  between operations  1.13 us (1%)
    ppermute x8, starting transfers between devices, exchange(): return lax.ppermute(block, ('wide', 'narrow'), pairs)  37.7 us
    pallas_call x16, Pallas kernels, call(): pl.pallas_call(body, out_shape=tuple((jax.ShapeDtypeStruct(shape, dtype)...  20.4 us
    ppermute x7, starting transfers between devices, narrow_swap(): return lax.ppermute(block, 'narrow', pairs)  16.4 us
    ppermute x8, waiting for transfers between devices, exchange(): return lax.ppermute(block, ('wide', 'narrow'), pairs)  15.6 us
  transfers between devices with their start and end apart: 15, of which 5 were waited for; matrix products, arithmetic and copies ran while one was open for 0% of the time, Pallas kernels for 17%

profile of v10, /device:TPU:24, one launch (start us, length us, event | category | flops | bytes accessed | tf_op | source)
XLA Modules:
  0.0 92.1 jit_solution(18246029234681400109)
XLA Ops:
  0.7 1.9 %shard_map.68 = (bf16[512,512]{1,0:T(8,128)(2,1)S(1)}, bf16[512,512]{1,0:T(8,128)(2,1)S(1)}, bf16[272,512]{1,0:T(8,128)(2,1)S(1)}) custom-call(s32[16]{0:T(128)S(1)} %compare_select_fusion.9.flags, bf16[256,512]{1,0:T(8,128)(2,1)} %treated_any.1, bf16[1024,512]{1,0:T(8,128)(2,1)} %control_any.1, f32[2,128]{1,0:T(2,128)} %bitcast.3, s32[2,24]{1,0:T(2,128)} %band_any.1), custom_call_target="tpu_custom_call" | custom-call | tf_op jit(solution)/shard_map/pallas_call | solution.py:486
  2.6 2.7 %collective-permute-start = (bf16[272,512]{1,0:T(8,128)(2,1)S(1)}, bf16[272,512]{1,0:T(8,128)(2,1)S(1)}, u32[]{:S(2)}, u32[]{:S(2)}) collective-permute-start(bf16[272,512]{1,0:T(8,128)(2,1)S(1)} %get-tuple-element.32.own_ref), channel_id=1, source_target_pairs={{0,2},{2,0},{1,3},{3,1},{4,6},{6,4},{5,7},{7,5},{8,10},{10,8},{9,1... | collective-permute-start | bytes 835592 | tf_op jit(solution)/shard_map/ppermute | solution.py:34
  5.3 14.1 %collective-permute-start.11 = (bf16[272,512]{1,0:T(8,128)(2,1)S(1)}, bf16[272,512]{1,0:T(8,128)(2,1)S(1)}, u32[]{:S(2)}, u32[]{:S(2)}) collective-permute-start(bf16[272,512]{1,0:T(8,128)(2,1)S(1)} %get-tuple-element.32.own_ref), channel_id=1, source_target_pairs={{4,8},{8,4},{12,16},{16,12},{20,24},{24,20},{28,32},{32,28},{36,40... | collective-permute-start | bytes 835592 | tf_op jit(solution)/shard_map/ppermute | solution.py:50
  19.4 1.9 %collective-permute-start.12 = (bf16[272,512]{1,0:T(8,128)(2,1)S(1)}, bf16[272,512]{1,0:T(8,128)(2,1)S(1)}, u32[]{:S(2)}, u32[]{:S(2)}) collective-permute-start(bf16[272,512]{1,0:T(8,128)(2,1)S(1)} %get-tuple-element.32.own_ref), channel_id=1, source_target_pairs={{0,4},{4,0},{8,12},{12,8},{16,20},{20,16},{24,28},{28,24},{32,36},... | collective-permute-start | bytes 835592 | tf_op jit(solution)/shard_map/ppermute | solution.py:50
  21.3 0.0 collective-permute-done.y_ref
  21.3 0.6 shard_map.69.joined_ref
  21.9 1.9 %collective-permute-start.1 = (bf16[544,512]{1,0:T(8,128)(2,1)S(1)}, bf16[544,512]{1,0:T(8,128)(2,1)S(1)}, u32[]{:S(2)}, u32[]{:S(2)}) collective-permute-start(bf16[544,512]{1,0:T(8,128)(2,1)S(1)} %shard_map.69.joined_ref), channel_id=1, source_target_pairs={{0,1},{1,0},{2,3},{3,2},{4,5},{5,4},{6,7},{7,6},{8,9},{9,8},{10,11... | collective-permute-start | bytes 1671176 | tf_op jit(solution)/shard_map/ppermute | solution.py:34
  23.8 4.8 %collective-permute-start.2 = (bf16[512,512]{1,0:T(8,128)(2,1)S(1)}, bf16[512,512]{1,0:T(8,128)(2,1)S(1)}, u32[]{:S(2)}, u32[]{:S(2)}) collective-permute-start(bf16[512,512]{1,0:T(8,128)(2,1)S(1)} %get-tuple-element.33.letter_ref), channel_id=1, source_target_pairs={{4,8},{8,4},{12,16},{16,12},{20,24},{24,20},{28,32},{32,28},{36,40... | collective-permute-start | bytes 1572872 | tf_op jit(solution)/shard_map/ppermute | solution.py:50
  28.7 1.9 %collective-permute-start.3 = (bf16[512,512]{1,0:T(8,128)(2,1)S(1)}, bf16[512,512]{1,0:T(8,128)(2,1)S(1)}, u32[]{:S(2)}, u32[]{:S(2)}) collective-permute-start(bf16[512,512]{1,0:T(8,128)(2,1)S(1)} %get-tuple-element.33.letter_ref), channel_id=1, source_target_pairs={{0,4},{4,0},{8,12},{12,8},{16,20},{20,16},{24,28},{28,24},{32,36},... | collective-permute-start | bytes 1572872 | tf_op jit(solution)/shard_map/ppermute | solution.py:50
  30.6 0.0 collective-permute-done.11.odd_ref
  30.6 0.0 collective-permute-done.12.even_ref
  30.7 2.9 %collective-permute-start.13 = (bf16[512,512]{1,0:T(8,128)(2,1)S(1)}, bf16[512,512]{1,0:T(8,128)(2,1)S(1)}, u32[]{:S(2)}, u32[]{:S(2)}) collective-permute-start(bf16[512,512]{1,0:T(8,128)(2,1)S(1)} %shard_map.80.own_ref), channel_id=1, source_target_pairs={{0,2},{2,0},{1,3},{3,1},{4,6},{6,4},{5,7},{7,5},{8,10},{10,8},{9,1... | collective-permute-start | bytes 1572872 | tf_op jit(solution)/shard_map/ppermute | solution.py:34
  33.6 1.5 %shard_map.70 = (bf16[1024,512]{1,0:T(8,128)(2,1)S(1)}, f32[1,1024]{1,0:T(1,128)S(1)}, f32[1,1024]{1,0:T(1,128)S(1)}, f32[1,1024]{1,0:T(1,128)S(1)}) custom-call(s32[16]{0:T(128)S(1)} %compare_select_fusion.9.flags, bf16[512,512]{1,0:T(8,128)(2,1)S(1)} %get-tuple-element.33.letter_ref, bf16[512,512]{1,0:T(8,128)(2,1)S(1)} %get-tuple-element.34.other_ref, ...), custom_call_target="tpu_custom_call" | custom-call | tf_op jit(solution)/shard_map/pallas_call | solution.py:486
  35.1 0.0 collective-permute-done.1.far_ref
  35.1 2.2 %shard_map.71 = (bf16[1024,512]{1,0:T(8,128)(2,1)S(1)}, f32[1024,1024]{1,0:T(8,128)S(1)}, f32[1024,128]{1,0:T(8,128)S(1)}, f32[8,3072]{1,0:T(8,128)S(1)}, f32[10...) custom-call(s32[16]{0:T(128)S(1)} %compare_select_fusion.9.flags, ...), custom_call_target="tpu_custom_call" | custom-call | tf_op jit(solution)/shard_map/pallas_call | solution.py:486
  37.3 8.1 %collective-permute-done.2.odd_ref = bf16[512,512]{1,0:T(8,128)(2,1)S(1)} collective-permute-done((bf16[512,512]{1,0:T(8,128)(2,1)S(1)}, bf16[512,512]{1,0:T(8,128)(2,1)S(1)}, u32[]{:S(2)}, u32[]{:S(2)}) %collective-permute-start.2) | collective-permute-done | bytes 524320 | tf_op jit(solution)/shard_map/ppermute | solution.py:50
  45.5 0.0 collective-permute-done.3.even_ref
  45.5 0.3 shard_map.72.columns_ref.near_columns_ref
  45.8 1.9 %collective-permute-start.4 = (bf16[1024,512]{1,0:T(8,128)(2,1)S(1)}, bf16[1024,512]{1,0:T(8,128)(2,1)S(1)}, u32[]{:S(2)}, u32[]{:S(2)}) collective-permute-start(bf16[1024,512]{1,0:T(8,128)(2,1)S(1)} %shard_map.72.columns_ref.near_columns_ref), channel_id=1, source_target_pairs={{0,1},{1,0},{2,3},{3,2},{4,5},{5,4},{6,7},{7,6},{8,9},{9,8},{10,11... | collective-permute-start | bytes 3145736 | tf_op jit(solution)/shard_map/ppermute | solution.py:34
  47.8 0.0 collective-permute-done.13.y_ref
  47.8 0.6 shard_map.81.near_ref
  48.4 2.4 %collective-permute-start.14 = (bf16[1024,512]{1,0:T(8,128)(2,1)S(1)}, bf16[1024,512]{1,0:T(8,128)(2,1)S(1)}, u32[]{:S(2)}, u32[]{:S(2)}) collective-permute-start(bf16[1024,512]{1,0:T(8,128)(2,1)S(1)} %shard_map.81.near_ref), channel_id=1, source_target_pairs={{0,1},{1,0},{2,3},{3,2},{4,5},{5,4},{6,7},{7,6},{8,9},{9,8},{10,11... | collective-permute-start | bytes 3145736 | tf_op jit(solution)/shard_map/ppermute | solution.py:34
  50.8 1.4 %shard_map.73 = (f32[1024,1024]{1,0:T(8,128)S(1)}, f32[1024,128]{1,0:T(8,128)S(1)}) custom-call(bf16[1024,512]{1,0:T(8,128)(2,1)S(1)} %get-tuple-element.36.rows_ref, bf16[1024,512]{1,0:T(8,128)(2,1)S(1)} %shard_map.72.columns_ref.near_columns_ref, f32[8,3072]{1,0:T(8,128)S(1)} %get-tuple-element.40.mask_ref, f32[1024,128]{1,0:T(8,128)S(1)} %get-tuple-element.37.before_ref), custom_call_target="tpu_custom_call" | custom-call | tf_op jit(solution)/shard_map/pallas_call | solution.py:486
  52.2 0.0 collective-permute-done.4.columns_ref.far_columns_ref
  52.2 2.9 %shard_map.74 = (f32[1024,1024]{1,0:T(8,128)S(1)}, f32[8,1024]{1,0:T(8,128)S(1)}, f32[4,1024]{1,0:T(4,128)S(1)}, f32[4,1024]{1,0:T(4,128)S(1)}) custom-call(s32[16]{0:T(128)S(1)} %compare_select_fusion.9.flags, bf16[1024,512]{1,0:T(8,128)(2,1)S(1)} %get-tuple-element.36.rows_ref, bf16[1024,512]{1,0:T(8,128)(2,1)S(1)} %collective-permute-done.4.columns_ref.far_columns_ref, ...), custom_call_target="tpu_custom_call" | custom-call | tf_op jit(solution)/shard_map/pallas_call | solution.py:486
  55.1 5.6 %collective-permute-start.5 = (f32[4,1024]{1,0:T(4,128)S(1)}, f32[4,1024]{1,0:T(4,128)S(1)}, u32[]{:S(2)}, u32[]{:S(2)}) collective-permute-start(f32[4,1024]{1,0:T(4,128)S(1)} %get-tuple-element.47), channel_id=1, source_target_pairs={{4,8},{8,4},{12,16},{16,12},{20,24},{24,20},{28,32},{32,28},{36,40... | collective-permute-start | bytes 49160 | tf_op jit(solution)/shard_map/ppermute | solution.py:50
  60.7 1.9 %collective-permute-start.6 = (f32[4,1024]{1,0:T(4,128)S(1)}, f32[4,1024]{1,0:T(4,128)S(1)}, u32[]{:S(2)}, u32[]{:S(2)}) collective-permute-start(f32[4,1024]{1,0:T(4,128)S(1)} %get-tuple-element.48), channel_id=1, source_target_pairs={{0,4},{4,0},{8,12},{12,8},{16,20},{20,16},{24,28},{28,24},{32,36},... | collective-permute-start | bytes 49160 | tf_op jit(solution)/shard_map/ppermute | solution.py:50
  62.6 3.7 %collective-permute-done.5.cross_ref = f32[4,1024]{1,0:T(4,128)S(1)} collective-permute-done((f32[4,1024]{1,0:T(4,128)S(1)}, f32[4,1024]{1,0:T(4,128)S(1)}, u32[]{:S(2)}, u32[]{:S(2)}) %collective-permute-start.5) | collective-permute-done | bytes 16416 | tf_op jit(solution)/shard_map/ppermute | solution.py:50
  66.3 0.0 collective-permute-done.6.inner_ref
  66.3 2.4 %collective-permute-start.7 = (f32[8,1024]{1,0:T(8,128)S(1)}, f32[8,1024]{1,0:T(8,128)S(1)}, u32[]{:S(2)}, u32[]{:S(2)}) collective-permute-start(f32[8,1024]{1,0:T(8,128)S(1)} %shard_map.75.mine_in), channel_id=1, source_target_pairs={{0,1},{1,0},{2,3},{3,2},{4,5},{5,4},{6,7},{7,6},{8,9},{9,8},{10,11... | collective-permute-start | bytes 98312 | tf_op jit(solution)/shard_map/ppermute | solution.py:34
  68.8 0.8 collective-permute-done.7.theirs_in
  69.6 2.6 %shard_map.76 = (f32[1024,128]{1,0:T(8,128)S(1)}, f32[1,1024]{1,0:T(1,128)S(1)}, f32[8,1024]{1,0:T(8,128)S(1)}, f32[4,1024]{1,0:T(4,128)S(1)}, f32[4,1024]{1,0:T(4,128)S(1)}) custom-call(s32[16]{0:T(128)S(1)} %compare_select_fusion.9.flags, f32[8,1024]{1,0:T(8,128)S(1)} %get-tuple-element.46.partial_in, f32[8,1024]{1,0:T(8,128)S(1)} %shard_map.75.mine_in, ...), custom_call_target="tpu_custom_call" | custom-call | tf_op jit(solution)/shard_map/pallas_call | solution.py:486
  72.3 5.5 %collective-permute-start.8 = (f32[4,1024]{1,0:T(4,128)S(1)}, f32[4,1024]{1,0:T(4,128)S(1)}, u32[]{:S(2)}, u32[]{:S(2)}) collective-permute-start(f32[4,1024]{1,0:T(4,128)S(1)} %get-tuple-element.54), channel_id=1, source_target_pairs={{4,8},{8,4},{12,16},{16,12},{20,24},{24,20},{28,32},{32,28},{36,40... | collective-permute-start | bytes 49160 | tf_op jit(solution)/shard_map/ppermute | solution.py:50
  77.8 1.9 %collective-permute-start.9 = (f32[4,1024]{1,0:T(4,128)S(1)}, f32[4,1024]{1,0:T(4,128)S(1)}, u32[]{:S(2)}, u32[]{:S(2)}) collective-permute-start(f32[4,1024]{1,0:T(4,128)S(1)} %get-tuple-element.55), channel_id=1, source_target_pairs={{0,4},{4,0},{8,12},{12,8},{16,20},{20,16},{24,28},{28,24},{32,36},... | collective-permute-start | bytes 49160 | tf_op jit(solution)/shard_map/ppermute | solution.py:50
  79.7 3.6 %collective-permute-done.8.cross_ref = f32[4,1024]{1,0:T(4,128)S(1)} collective-permute-done((f32[4,1024]{1,0:T(4,128)S(1)}, f32[4,1024]{1,0:T(4,128)S(1)}, u32[]{:S(2)}, u32[]{:S(2)}) %collective-permute-start.8) | collective-permute-done | bytes 16416 | tf_op jit(solution)/shard_map/ppermute | solution.py:50
  83.3 0.1 collective-permute-done.9.inner_ref
  83.4 2.2 %collective-permute-start.10 = (f32[8,1024]{1,0:T(8,128)S(1)}, f32[8,1024]{1,0:T(8,128)S(1)}, u32[]{:S(2)}, u32[]{:S(2)}) collective-permute-start(f32[8,1024]{1,0:T(8,128)S(1)} %shard_map.77.mine_in), channel_id=1, source_target_pairs={{0,1},{1,0},{2,3},{3,2},{4,5},{5,4},{6,7},{7,6},{8,9},{9,8},{10,11... | collective-permute-start | bytes 98312 | tf_op jit(solution)/shard_map/ppermute | solution.py:34
  85.6 1.0 %shard_map.78.kernel_ref = f32[256,1024]{1,0:T(8,128)S(1)} custom-call(s32[16]{0:T(128)S(1)} %compare_select_fusion.9.flags, bf16[1024,512]{1,0:T(8,128)(2,1)S(1)} %get-tuple-element.35.columns_ref.own_columns_ref, bf16[1024,512]{1,0:T(8,128)(2,1)S(1)} %get-tuple-element.36.rows_ref, f32[8,1024]{1,0:T(8,128)S(1)} %get-tuple-element.58.pair_ref), custom_call_target="tpu_custom_call" | custom-call | tf_op jit(solution)/shard_map/pallas_call | solution.py:486
  86.7 0.5 shard_map.79.pushed_ref
  87.1 0.0 collective-permute-done.14.far_ref
  87.2 1.5 %shard_map.82 = (bf16[1024,512]{1,0:T(8,128)(2,1)S(1)}, bf16[1024,512]{1,0:T(8,128)(2,1)S(1)}, f32[256,2048]{1,0:T(8,128)S(1)}) custom-call(s32[16]{0:T(128)S(1)} %compare_select_fusion.9.flags, bf16[1024,512]{1,0:T(8,128)(2,1)S(1)} %get-tuple-element.35.columns_ref.own_columns_ref, bf16[1024,512]{1,0:T(8,128)(2,1)S(1)} %shard_map.81.near_ref, ...), custom_call_target="tpu_custom_call" | custom-call | tf_op jit(solution)/shard_map/pallas_call | solution.py:486
  88.6 0.0 collective-permute-done.10.theirs_in
  88.7 3.3 %shard_map.83 = (f32[256,512]{1,0:T(8,128)}, f32[256,512]{1,0:T(8,128)}) custom-call(s32[16]{0:T(128)S(1)} %compare_select_fusion.9.flags, f32[8,1024]{1,0:T(8,128)S(1)} %get-tuple-element.53.partial_in, f32[8,1024]{1,0:T(8,128)S(1)} %shard_map.77.mine_in, f32[8,1024]{1,0:T(8,128)S(1)} %collective-permute-done.10.theirs_in, ...), custom_call_target="tpu_custom_call" | custom-call | tf_op jit(solution)/shard_map/pallas_call | solution.py:486
  (4 shorter events, 0.1 us)
Async XLA Ops:
  2.6 18.7 %collective-permute-start = (bf16[272,512]{1,0:T(8,128)(2,1)S(1)}, bf16[272,512]{1,0:T(8,128)(2,1)S(1)}, u32[]{:S(2)}, u32[]{:S(2)}) collective-permute-start(bf16[272,512]{1,0:T(8,128)(2,1)S(1)} %get-tuple-element.32.own_ref), channel_id=1, source_target_pairs={{0,2},{2,0},{1,3},{3,1},{4,6},{6,4},{5,7},{7,5},{8,10},{10,8},{9,1... | collective-permute-start | bytes 835592 | tf_op jit(solution)/shard_map/ppermute | solution.py:34
  5.3 25.3 %collective-permute-start.11 = (bf16[272,512]{1,0:T(8,128)(2,1)S(1)}, bf16[272,512]{1,0:T(8,128)(2,1)S(1)}, u32[]{:S(2)}, u32[]{:S(2)}) collective-permute-start(bf16[272,512]{1,0:T(8,128)(2,1)S(1)} %get-tuple-element.32.own_ref), channel_id=1, source_target_pairs={{4,8},{8,4},{12,16},{16,12},{20,24},{24,20},{28,32},{32,28},{36,40... | collective-permute-start | bytes 835592 | tf_op jit(solution)/shard_map/ppermute | solution.py:50
  19.4 11.3 %collective-permute-start.12 = (bf16[272,512]{1,0:T(8,128)(2,1)S(1)}, bf16[272,512]{1,0:T(8,128)(2,1)S(1)}, u32[]{:S(2)}, u32[]{:S(2)}) collective-permute-start(bf16[272,512]{1,0:T(8,128)(2,1)S(1)} %get-tuple-element.32.own_ref), channel_id=1, source_target_pairs={{0,4},{4,0},{8,12},{12,8},{16,20},{20,16},{24,28},{28,24},{32,36},... | collective-permute-start | bytes 835592 | tf_op jit(solution)/shard_map/ppermute | solution.py:50
  21.9 13.2 %collective-permute-start.1 = (bf16[544,512]{1,0:T(8,128)(2,1)S(1)}, bf16[544,512]{1,0:T(8,128)(2,1)S(1)}, u32[]{:S(2)}, u32[]{:S(2)}) collective-permute-start(bf16[544,512]{1,0:T(8,128)(2,1)S(1)} %shard_map.69.joined_ref), channel_id=1, source_target_pairs={{0,1},{1,0},{2,3},{3,2},{4,5},{5,4},{6,7},{7,6},{8,9},{9,8},{10,11... | collective-permute-start | bytes 1671176 | tf_op jit(solution)/shard_map/ppermute | solution.py:34
  23.8 21.6 %collective-permute-start.2 = (bf16[512,512]{1,0:T(8,128)(2,1)S(1)}, bf16[512,512]{1,0:T(8,128)(2,1)S(1)}, u32[]{:S(2)}, u32[]{:S(2)}) collective-permute-start(bf16[512,512]{1,0:T(8,128)(2,1)S(1)} %get-tuple-element.33.letter_ref), channel_id=1, source_target_pairs={{4,8},{8,4},{12,16},{16,12},{20,24},{24,20},{28,32},{32,28},{36,40... | collective-permute-start | bytes 1572872 | tf_op jit(solution)/shard_map/ppermute | solution.py:50
  28.7 16.8 %collective-permute-start.3 = (bf16[512,512]{1,0:T(8,128)(2,1)S(1)}, bf16[512,512]{1,0:T(8,128)(2,1)S(1)}, u32[]{:S(2)}, u32[]{:S(2)}) collective-permute-start(bf16[512,512]{1,0:T(8,128)(2,1)S(1)} %get-tuple-element.33.letter_ref), channel_id=1, source_target_pairs={{0,4},{4,0},{8,12},{12,8},{16,20},{20,16},{24,28},{28,24},{32,36},... | collective-permute-start | bytes 1572872 | tf_op jit(solution)/shard_map/ppermute | solution.py:50
  30.7 17.1 %collective-permute-start.13 = (bf16[512,512]{1,0:T(8,128)(2,1)S(1)}, bf16[512,512]{1,0:T(8,128)(2,1)S(1)}, u32[]{:S(2)}, u32[]{:S(2)}) collective-permute-start(bf16[512,512]{1,0:T(8,128)(2,1)S(1)} %shard_map.80.own_ref), channel_id=1, source_target_pairs={{0,2},{2,0},{1,3},{3,1},{4,6},{6,4},{5,7},{7,5},{8,10},{10,8},{9,1... | collective-permute-start | bytes 1572872 | tf_op jit(solution)/shard_map/ppermute | solution.py:34
  45.8 6.4 %collective-permute-start.4 = (bf16[1024,512]{1,0:T(8,128)(2,1)S(1)}, bf16[1024,512]{1,0:T(8,128)(2,1)S(1)}, u32[]{:S(2)}, u32[]{:S(2)}) collective-permute-start(bf16[1024,512]{1,0:T(8,128)(2,1)S(1)} %shard_map.72.columns_ref.near_columns_ref), channel_id=1, source_target_pairs={{0,1},{1,0},{2,3},{3,2},{4,5},{5,4},{6,7},{7,6},{8,9},{9,8},{10,11... | collective-permute-start | bytes 3145736 | tf_op jit(solution)/shard_map/ppermute | solution.py:34
  48.4 38.8 %collective-permute-start.14 = (bf16[1024,512]{1,0:T(8,128)(2,1)S(1)}, bf16[1024,512]{1,0:T(8,128)(2,1)S(1)}, u32[]{:S(2)}, u32[]{:S(2)}) collective-permute-start(bf16[1024,512]{1,0:T(8,128)(2,1)S(1)} %shard_map.81.near_ref), channel_id=1, source_target_pairs={{0,1},{1,0},{2,3},{3,2},{4,5},{5,4},{6,7},{7,6},{8,9},{9,8},{10,11... | collective-permute-start | bytes 3145736 | tf_op jit(solution)/shard_map/ppermute | solution.py:34
  55.1 11.2 %collective-permute-start.5 = (f32[4,1024]{1,0:T(4,128)S(1)}, f32[4,1024]{1,0:T(4,128)S(1)}, u32[]{:S(2)}, u32[]{:S(2)}) collective-permute-start(f32[4,1024]{1,0:T(4,128)S(1)} %get-tuple-element.47), channel_id=1, source_target_pairs={{4,8},{8,4},{12,16},{16,12},{20,24},{24,20},{28,32},{32,28},{36,40... | collective-permute-start | bytes 49160 | tf_op jit(solution)/shard_map/ppermute | solution.py:50
  60.7 5.6 %collective-permute-start.6 = (f32[4,1024]{1,0:T(4,128)S(1)}, f32[4,1024]{1,0:T(4,128)S(1)}, u32[]{:S(2)}, u32[]{:S(2)}) collective-permute-start(f32[4,1024]{1,0:T(4,128)S(1)} %get-tuple-element.48), channel_id=1, source_target_pairs={{0,4},{4,0},{8,12},{12,8},{16,20},{20,16},{24,28},{28,24},{32,36},... | collective-permute-start | bytes 49160 | tf_op jit(solution)/shard_map/ppermute | solution.py:50
  66.3 3.3 %collective-permute-start.7 = (f32[8,1024]{1,0:T(8,128)S(1)}, f32[8,1024]{1,0:T(8,128)S(1)}, u32[]{:S(2)}, u32[]{:S(2)}) collective-permute-start(f32[8,1024]{1,0:T(8,128)S(1)} %shard_map.75.mine_in), channel_id=1, source_target_pairs={{0,1},{1,0},{2,3},{3,2},{4,5},{5,4},{6,7},{7,6},{8,9},{9,8},{10,11... | collective-permute-start | bytes 98312 | tf_op jit(solution)/shard_map/ppermute | solution.py:34
  72.3 11.1 %collective-permute-start.8 = (f32[4,1024]{1,0:T(4,128)S(1)}, f32[4,1024]{1,0:T(4,128)S(1)}, u32[]{:S(2)}, u32[]{:S(2)}) collective-permute-start(f32[4,1024]{1,0:T(4,128)S(1)} %get-tuple-element.54), channel_id=1, source_target_pairs={{4,8},{8,4},{12,16},{16,12},{20,24},{24,20},{28,32},{32,28},{36,40... | collective-permute-start | bytes 49160 | tf_op jit(solution)/shard_map/ppermute | solution.py:50
  77.8 5.6 %collective-permute-start.9 = (f32[4,1024]{1,0:T(4,128)S(1)}, f32[4,1024]{1,0:T(4,128)S(1)}, u32[]{:S(2)}, u32[]{:S(2)}) collective-permute-start(f32[4,1024]{1,0:T(4,128)S(1)} %get-tuple-element.55), channel_id=1, source_target_pairs={{0,4},{4,0},{8,12},{12,8},{16,20},{20,16},{24,28},{28,24},{32,36},... | collective-permute-start | bytes 49160 | tf_op jit(solution)/shard_map/ppermute | solution.py:50
  83.4 5.2 %collective-permute-start.10 = (f32[8,1024]{1,0:T(8,128)S(1)}, f32[8,1024]{1,0:T(8,128)S(1)}, u32[]{:S(2)}, u32[]{:S(2)}) collective-permute-start(f32[8,1024]{1,0:T(8,128)S(1)} %shard_map.77.mine_in), channel_id=1, source_target_pairs={{0,1},{1,0},{2,3},{3,2},{4,5},{5,4},{6,7},{7,6},{8,9},{9,8},{10,11... | collective-permute-start | bytes 98312 | tf_op jit(solution)/shard_map/ppermute | solution.py:34

commit v11 on v10

--- a/solution.py
+++ b/solution.py
@@ -110,8 +110,9 @@
 
 
 def pack_kernel(
-    flags, treated_any, control_any, weight_any, band_any, letter_ref, other_ref, message_ref,
-    treated_ref, weight_ref, band_ref, info_ref, sems,
+    flags, treated_any, control_any, weight_any, band_any, columns_any, letter_ref, other_ref,
+    message_ref, own_ref, odd_ref, even_ref, treated_ref, weight_ref, band_ref, info_ref,
+    fetched_ref, sems,
 ):
     half = pl.ds(pl.multiple_of(flags[CORE] * HALF, HALF), HALF)
     other = pl.ds(pl.multiple_of((1 - flags[CORE]) * HALF, HALF), HALF)
@@ -124,6 +125,13 @@
                 (band_any, band_ref),
                 (control_any.at[half, :], letter_ref),
                 (control_any.at[other, :], other_ref),
+                *(
+                    (
+                        columns_any.at[pl.ds(pl.multiple_of(flags[which] * 8, 8), 8), :],
+                        fetched_ref.at[j],
+                    )
+                    for j, which in enumerate((WIDE, WIDE_ODD, WIDE_EVEN))
+                ),
             )
         )
     ]
@@ -144,6 +152,9 @@
     message_ref[QUARTER:MESSAGE, :] = info
     for copy in copies[3:]:
         copy.wait()
+    for i, ref in enumerate((own_ref, odd_ref, even_ref)):
+        for j in range(8):
+            ref[0:1, j * LANES : (j + 1) * LANES] = fetched_ref[i, j : j + 1, :]
 
 
 def join_kernel(flags, own_ref, y_ref, joined_ref):
@@ -152,26 +163,9 @@
         joined_ref[pl.ds(pl.multiple_of(HALF + y * INFO, INFO), INFO), :] = ref[QUARTER:MESSAGE, :]
 
 
-def columns_kernel(
-    flags, letter_ref, other_ref, weight_any, columns_ref, own_ref, odd_ref, even_ref, fetched_ref,
-    sems,
-):
-    copies = [
-        pltpu.make_async_copy(
-            weight_any.at[pl.ds(pl.multiple_of(flags[which] * 8, 8), 8), :],
-            fetched_ref.at[i],
-            sems.at[i],
-        )
-        for i, which in enumerate((WIDE, WIDE_ODD, WIDE_EVEN))
-    ]
-    for copy in copies:
-        copy.start()
+def columns_kernel(flags, letter_ref, other_ref, columns_ref):
     for ref, half in ((letter_ref, flags[CORE]), (other_ref, 1 - flags[CORE])):
         columns_ref[pl.ds(pl.multiple_of(half * HALF, HALF), HALF), :] = normalize(ref[...])
-    for i, (copy, ref) in enumerate(zip(copies, (own_ref, odd_ref, even_ref), strict=True)):
-        copy.wait()
-        for j in range(8):
-            ref[0:1, j * LANES : (j + 1) * LANES] = fetched_ref[i, j : j + 1, :]
 
 
 def open_kernel(odd_ref, even_ref, columns_ref):
@@ -533,27 +527,28 @@
             control_weight.reshape(-1, LANES),
         )
     )
-    letter, other, message = call(
+    letter, other, message, *weights = call(
         pack_kernel,
-        [SMEM] + [HBM] * 4,
-        [((HALF, WIDTH), BF16), ((HALF, WIDTH), BF16), ((MESSAGE, WIDTH), BF16)],
-        [flags, treated, control, own_weight, own_band],
+        [SMEM] + [HBM] * 5,
+        [((HALF, WIDTH), BF16), ((HALF, WIDTH), BF16), ((MESSAGE, WIDTH), BF16)]
+        + [((1, SLAB), F32)] * 3,
+        [flags, treated, control, own_weight, own_band, column_weight],
         [
             pltpu.VMEM((QUARTER, WIDTH), BF16),
             pltpu.VMEM((2, LANES), F32),
             pltpu.VMEM((2, 24), jnp.int32),
             pltpu.VMEM((INFO, WIDTH), F32),
-            pltpu.SemaphoreType.DMA((5,)),
+            pltpu.VMEM((3, 8, LANES), F32),
+            pltpu.SemaphoreType.DMA((8,)),
         ],
     )
     odd_letter = exchange(letter, (1, 1), True)
     even_letter = exchange(letter, (1, 1), False)
-    own_columns, *weights = call(
+    (own_columns,) = call(
         columns_kernel,
-        [SMEM] + [VMEM] * 2 + [HBM],
-        [((SLAB, WIDTH), BF16)] + [((1, SLAB), F32)] * 3,
-        [flags, letter, other, column_weight],
-        [pltpu.VMEM((3, 8, LANES), F32), pltpu.SemaphoreType.DMA((3,))],
+        [SMEM] + [VMEM] * 2,
+        [((SLAB, WIDTH), BF16)],
+        [flags, letter, other],
     )
 
     odd_message = exchange(message, (1, 1), True)

time: 93.2 us -> 93.2 us (level)
  transfers between devices with their start and end apart: 15 -> 15, of which waited for: 5 -> 5; matrix products, arithmetic and copies ran while one was open for 0% -> 0% of each run, Pallas kernels for 17% -> 16%
where the time goes in v11:
time: 93.2 us; the launch traced here: 92.1 us
  starting transfers between devices  54.1 us (58%)
  Pallas kernels  19.8 us (21%)
  waiting for transfers between devices  17.1 us (18%)
  between operations  1.13 us (1%)
    ppermute x8, starting transfers between devices, exchange(): return lax.ppermute(block, ('wide', 'narrow'), pairs)  37.7 us
    pallas_call x16, Pallas kernels, call(): pl.pallas_call(body, out_shape=tuple((jax.ShapeDtypeStruct(shape, dtype)...  19.8 us
    ppermute x7, starting transfers between devices, narrow_swap(): return lax.ppermute(block, 'narrow', pairs)  16.4 us
    ppermute x8, waiting for transfers between devices, exchange(): return lax.ppermute(block, ('wide', 'narrow'), pairs)  16.2 us
  transfers between devices with their start and end apart: 15, of which 5 were waited for; matrix products, arithmetic and copies ran while one was open for 0% of the time, Pallas kernels for 16%

profile of v11, /device:TPU:24, one launch (start us, length us, event | category | flops | bytes accessed | tf_op | source)
XLA Modules:
  0.0 92.1 jit_solution(18329583289694074015)
XLA Ops:
  0.7 1.9 %shard_map.68 = (bf16[512,512]{1,0:T(8,128)(2,1)S(1)}, bf16[512,512]{1,0:T(8,128)(2,1)S(1)}, bf16[272,512]{1,0:T(8,128)(2,1)S(1)}, f32[1,1024]{1,0:T(1,128)S(1)}...) custom-call(s32[16]{0:T(128)S(1)} %compare_select_fusion.9.flags, bf16[256,512]{1,0:T(8,128)(2,1)} %treated_any.1, ...), custom_call_target="tpu_custom_call" | custom-call | tf_op jit(solution)/shard_map/pallas_call | solution.py:480
  2.7 2.7 %collective-permute-start = (bf16[272,512]{1,0:T(8,128)(2,1)S(1)}, bf16[272,512]{1,0:T(8,128)(2,1)S(1)}, u32[]{:S(2)}, u32[]{:S(2)}) collective-permute-start(bf16[272,512]{1,0:T(8,128)(2,1)S(1)} %get-tuple-element.31.own_ref), channel_id=1, source_target_pairs={{0,2},{2,0},{1,3},{3,1},{4,6},{6,4},{5,7},{7,5},{8,10},{10,8},{9,1... | collective-permute-start | bytes 835592 | tf_op jit(solution)/shard_map/ppermute | solution.py:34
  5.3 14.1 %collective-permute-start.11 = (bf16[272,512]{1,0:T(8,128)(2,1)S(1)}, bf16[272,512]{1,0:T(8,128)(2,1)S(1)}, u32[]{:S(2)}, u32[]{:S(2)}) collective-permute-start(bf16[272,512]{1,0:T(8,128)(2,1)S(1)} %get-tuple-element.31.own_ref), channel_id=1, source_target_pairs={{4,8},{8,4},{12,16},{16,12},{20,24},{24,20},{28,32},{32,28},{36,40... | collective-permute-start | bytes 835592 | tf_op jit(solution)/shard_map/ppermute | solution.py:50
  19.4 1.9 %collective-permute-start.12 = (bf16[272,512]{1,0:T(8,128)(2,1)S(1)}, bf16[272,512]{1,0:T(8,128)(2,1)S(1)}, u32[]{:S(2)}, u32[]{:S(2)}) collective-permute-start(bf16[272,512]{1,0:T(8,128)(2,1)S(1)} %get-tuple-element.31.own_ref), channel_id=1, source_target_pairs={{0,4},{4,0},{8,12},{12,8},{16,20},{20,16},{24,28},{28,24},{32,36},... | collective-permute-start | bytes 835592 | tf_op jit(solution)/shard_map/ppermute | solution.py:50
  21.3 0.0 collective-permute-done.y_ref
  21.3 0.6 shard_map.69.joined_ref
  21.9 1.9 %collective-permute-start.1 = (bf16[544,512]{1,0:T(8,128)(2,1)S(1)}, bf16[544,512]{1,0:T(8,128)(2,1)S(1)}, u32[]{:S(2)}, u32[]{:S(2)}) collective-permute-start(bf16[544,512]{1,0:T(8,128)(2,1)S(1)} %shard_map.69.joined_ref), channel_id=1, source_target_pairs={{0,1},{1,0},{2,3},{3,2},{4,5},{5,4},{6,7},{7,6},{8,9},{9,8},{10,11... | collective-permute-start | bytes 1671176 | tf_op jit(solution)/shard_map/ppermute | solution.py:34
  23.9 4.8 %collective-permute-start.2 = (bf16[512,512]{1,0:T(8,128)(2,1)S(1)}, bf16[512,512]{1,0:T(8,128)(2,1)S(1)}, u32[]{:S(2)}, u32[]{:S(2)}) collective-permute-start(bf16[512,512]{1,0:T(8,128)(2,1)S(1)} %get-tuple-element.32.letter_ref), channel_id=1, source_target_pairs={{4,8},{8,4},{12,16},{16,12},{20,24},{24,20},{28,32},{32,28},{36,40... | collective-permute-start | bytes 1572872 | tf_op jit(solution)/shard_map/ppermute | solution.py:50
  28.7 1.9 %collective-permute-start.3 = (bf16[512,512]{1,0:T(8,128)(2,1)S(1)}, bf16[512,512]{1,0:T(8,128)(2,1)S(1)}, u32[]{:S(2)}, u32[]{:S(2)}) collective-permute-start(bf16[512,512]{1,0:T(8,128)(2,1)S(1)} %get-tuple-element.32.letter_ref), channel_id=1, source_target_pairs={{0,4},{4,0},{8,12},{12,8},{16,20},{20,16},{24,28},{28,24},{32,36},... | collective-permute-start | bytes 1572872 | tf_op jit(solution)/shard_map/ppermute | solution.py:50
  30.7 0.0 collective-permute-done.11.odd_ref
  30.7 0.0 collective-permute-done.12.even_ref
  30.7 2.9 %collective-permute-start.13 = (bf16[512,512]{1,0:T(8,128)(2,1)S(1)}, bf16[512,512]{1,0:T(8,128)(2,1)S(1)}, u32[]{:S(2)}, u32[]{:S(2)}) collective-permute-start(bf16[512,512]{1,0:T(8,128)(2,1)S(1)} %shard_map.80.own_ref), channel_id=1, source_target_pairs={{0,2},{2,0},{1,3},{3,1},{4,6},{6,4},{5,7},{7,5},{8,10},{10,8},{9,1... | collective-permute-start | bytes 1572872 | tf_op jit(solution)/shard_map/ppermute | solution.py:34
  33.6 0.9 shard_map.70.columns_ref.own_columns_ref
  34.5 0.0 collective-permute-done.1.far_ref
  34.5 2.2 %shard_map.71 = (bf16[1024,512]{1,0:T(8,128)(2,1)S(1)}, f32[1024,1024]{1,0:T(8,128)S(1)}, f32[1024,128]{1,0:T(8,128)S(1)}, f32[8,3072]{1,0:T(8,128)S(1)}, f32[10...) custom-call(s32[16]{0:T(128)S(1)} %compare_select_fusion.9.flags, ...), custom_call_target="tpu_custom_call" | custom-call | tf_op jit(solution)/shard_map/pallas_call | solution.py:480
  36.7 8.8 %collective-permute-done.2.odd_ref = bf16[512,512]{1,0:T(8,128)(2,1)S(1)} collective-permute-done((bf16[512,512]{1,0:T(8,128)(2,1)S(1)}, bf16[512,512]{1,0:T(8,128)(2,1)S(1)}, u32[]{:S(2)}, u32[]{:S(2)}) %collective-permute-start.2) | collective-permute-done | bytes 524320 | tf_op jit(solution)/shard_map/ppermute | solution.py:50
  45.5 0.0 collective-permute-done.3.even_ref
  45.5 0.3 shard_map.72.columns_ref.near_columns_ref
  45.9 1.9 %collective-permute-start.4 = (bf16[1024,512]{1,0:T(8,128)(2,1)S(1)}, bf16[1024,512]{1,0:T(8,128)(2,1)S(1)}, u32[]{:S(2)}, u32[]{:S(2)}) collective-permute-start(bf16[1024,512]{1,0:T(8,128)(2,1)S(1)} %shard_map.72.columns_ref.near_columns_ref), channel_id=1, source_target_pairs={{0,1},{1,0},{2,3},{3,2},{4,5},{5,4},{6,7},{7,6},{8,9},{9,8},{10,11... | collective-permute-start | bytes 3145736 | tf_op jit(solution)/shard_map/ppermute | solution.py:34
  47.8 0.0 collective-permute-done.13.y_ref
  47.8 0.6 shard_map.81.near_ref
  48.4 2.4 %collective-permute-start.14 = (bf16[1024,512]{1,0:T(8,128)(2,1)S(1)}, bf16[1024,512]{1,0:T(8,128)(2,1)S(1)}, u32[]{:S(2)}, u32[]{:S(2)}) collective-permute-start(bf16[1024,512]{1,0:T(8,128)(2,1)S(1)} %shard_map.81.near_ref), channel_id=1, source_target_pairs={{0,1},{1,0},{2,3},{3,2},{4,5},{5,4},{6,7},{7,6},{8,9},{9,8},{10,11... | collective-permute-start | bytes 3145736 | tf_op jit(solution)/shard_map/ppermute | solution.py:34
  50.8 1.4 %shard_map.73 = (f32[1024,1024]{1,0:T(8,128)S(1)}, f32[1024,128]{1,0:T(8,128)S(1)}) custom-call(bf16[1024,512]{1,0:T(8,128)(2,1)S(1)} %get-tuple-element.34.rows_ref, bf16[1024,512]{1,0:T(8,128)(2,1)S(1)} %shard_map.72.columns_ref.near_columns_ref, f32[8,3072]{1,0:T(8,128)S(1)} %get-tuple-element.38.mask_ref, f32[1024,128]{1,0:T(8,128)S(1)} %get-tuple-element.35.before_ref), custom_call_target="tpu_custom_call" | custom-call | tf_op jit(solution)/shard_map/pallas_call | solution.py:480
  52.2 0.0 collective-permute-done.4.columns_ref.far_columns_ref
  52.3 2.9 %shard_map.74 = (f32[1024,1024]{1,0:T(8,128)S(1)}, f32[8,1024]{1,0:T(8,128)S(1)}, f32[4,1024]{1,0:T(4,128)S(1)}, f32[4,1024]{1,0:T(4,128)S(1)}) custom-call(s32[16]{0:T(128)S(1)} %compare_select_fusion.9.flags, bf16[1024,512]{1,0:T(8,128)(2,1)S(1)} %get-tuple-element.34.rows_ref, bf16[1024,512]{1,0:T(8,128)(2,1)S(1)} %collective-permute-done.4.columns_ref.far_columns_ref, ...), custom_call_target="tpu_custom_call" | custom-call | tf_op jit(solution)/shard_map/pallas_call | solution.py:480
  55.2 5.6 %collective-permute-start.5 = (f32[4,1024]{1,0:T(4,128)S(1)}, f32[4,1024]{1,0:T(4,128)S(1)}, u32[]{:S(2)}, u32[]{:S(2)}) collective-permute-start(f32[4,1024]{1,0:T(4,128)S(1)} %get-tuple-element.45), channel_id=1, source_target_pairs={{4,8},{8,4},{12,16},{16,12},{20,24},{24,20},{28,32},{32,28},{36,40... | collective-permute-start | bytes 49160 | tf_op jit(solution)/shard_map/ppermute | solution.py:50
  60.7 1.9 %collective-permute-start.6 = (f32[4,1024]{1,0:T(4,128)S(1)}, f32[4,1024]{1,0:T(4,128)S(1)}, u32[]{:S(2)}, u32[]{:S(2)}) collective-permute-start(f32[4,1024]{1,0:T(4,128)S(1)} %get-tuple-element.46), channel_id=1, source_target_pairs={{0,4},{4,0},{8,12},{12,8},{16,20},{20,16},{24,28},{28,24},{32,36},... | collective-permute-start | bytes 49160 | tf_op jit(solution)/shard_map/ppermute | solution.py:50
  62.7 3.7 %collective-permute-done.5.cross_ref = f32[4,1024]{1,0:T(4,128)S(1)} collective-permute-done((f32[4,1024]{1,0:T(4,128)S(1)}, f32[4,1024]{1,0:T(4,128)S(1)}, u32[]{:S(2)}, u32[]{:S(2)}) %collective-permute-start.5) | collective-permute-done | bytes 16416 | tf_op jit(solution)/shard_map/ppermute | solution.py:50
  66.3 0.0 collective-permute-done.6.inner_ref
  66.4 2.4 %collective-permute-start.7 = (f32[8,1024]{1,0:T(8,128)S(1)}, f32[8,1024]{1,0:T(8,128)S(1)}, u32[]{:S(2)}, u32[]{:S(2)}) collective-permute-start(f32[8,1024]{1,0:T(8,128)S(1)} %shard_map.75.mine_in), channel_id=1, source_target_pairs={{0,1},{1,0},{2,3},{3,2},{4,5},{5,4},{6,7},{7,6},{8,9},{9,8},{10,11... | collective-permute-start | bytes 98312 | tf_op jit(solution)/shard_map/ppermute | solution.py:34
  68.8 0.8 collective-permute-done.7.theirs_in
  69.7 2.6 %shard_map.76 = (f32[1024,128]{1,0:T(8,128)S(1)}, f32[1,1024]{1,0:T(1,128)S(1)}, f32[8,1024]{1,0:T(8,128)S(1)}, f32[4,1024]{1,0:T(4,128)S(1)}, f32[4,1024]{1,0:T(4,128)S(1)}) custom-call(s32[16]{0:T(128)S(1)} %compare_select_fusion.9.flags, f32[8,1024]{1,0:T(8,128)S(1)} %get-tuple-element.44.partial_in, f32[8,1024]{1,0:T(8,128)S(1)} %shard_map.75.mine_in, ...), custom_call_target="tpu_custom_call" | custom-call | tf_op jit(solution)/shard_map/pallas_call | solution.py:480
  72.3 5.5 %collective-permute-start.8 = (f32[4,1024]{1,0:T(4,128)S(1)}, f32[4,1024]{1,0:T(4,128)S(1)}, u32[]{:S(2)}, u32[]{:S(2)}) collective-permute-start(f32[4,1024]{1,0:T(4,128)S(1)} %get-tuple-element.52), channel_id=1, source_target_pairs={{4,8},{8,4},{12,16},{16,12},{20,24},{24,20},{28,32},{32,28},{36,40... | collective-permute-start | bytes 49160 | tf_op jit(solution)/shard_map/ppermute | solution.py:50
  77.8 1.9 %collective-permute-start.9 = (f32[4,1024]{1,0:T(4,128)S(1)}, f32[4,1024]{1,0:T(4,128)S(1)}, u32[]{:S(2)}, u32[]{:S(2)}) collective-permute-start(f32[4,1024]{1,0:T(4,128)S(1)} %get-tuple-element.53), channel_id=1, source_target_pairs={{0,4},{4,0},{8,12},{12,8},{16,20},{20,16},{24,28},{28,24},{32,36},... | collective-permute-start | bytes 49160 | tf_op jit(solution)/shard_map/ppermute | solution.py:50
  79.8 3.6 %collective-permute-done.8.cross_ref = f32[4,1024]{1,0:T(4,128)S(1)} collective-permute-done((f32[4,1024]{1,0:T(4,128)S(1)}, f32[4,1024]{1,0:T(4,128)S(1)}, u32[]{:S(2)}, u32[]{:S(2)}) %collective-permute-start.8) | collective-permute-done | bytes 16416 | tf_op jit(solution)/shard_map/ppermute | solution.py:50
  83.4 0.1 collective-permute-done.9.inner_ref
  83.5 2.2 %collective-permute-start.10 = (f32[8,1024]{1,0:T(8,128)S(1)}, f32[8,1024]{1,0:T(8,128)S(1)}, u32[]{:S(2)}, u32[]{:S(2)}) collective-permute-start(f32[8,1024]{1,0:T(8,128)S(1)} %shard_map.77.mine_in), channel_id=1, source_target_pairs={{0,1},{1,0},{2,3},{3,2},{4,5},{5,4},{6,7},{7,6},{8,9},{9,8},{10,11... | collective-permute-start | bytes 98312 | tf_op jit(solution)/shard_map/ppermute | solution.py:34
  85.7 1.0 %shard_map.78.kernel_ref = f32[256,1024]{1,0:T(8,128)S(1)} custom-call(s32[16]{0:T(128)S(1)} %compare_select_fusion.9.flags, bf16[1024,512]{1,0:T(8,128)(2,1)S(1)} %shard_map.70.columns_ref.own_columns_ref, bf16[1024,512]{1,0:T(8,128)(2,1)S(1)} %get-tuple-element.34.rows_ref, f32[8,1024]{1,0:T(8,128)S(1)} %get-tuple-element.56.pair_ref), custom_call_target="tpu_custom_call" | custom-call | tf_op jit(solution)/shard_map/pallas_call | solution.py:480
  86.7 0.5 shard_map.79.pushed_ref
  87.2 0.0 collective-permute-done.14.far_ref
  87.2 1.5 %shard_map.82 = (bf16[1024,512]{1,0:T(8,128)(2,1)S(1)}, bf16[1024,512]{1,0:T(8,128)(2,1)S(1)}, f32[256,2048]{1,0:T(8,128)S(1)}) custom-call(s32[16]{0:T(128)S(1)} %compare_select_fusion.9.flags, bf16[1024,512]{1,0:T(8,128)(2,1)S(1)} %shard_map.70.columns_ref.own_columns_ref, bf16[1024,512]{1,0:T(8,128)(2,1)S(1)} %shard_map.81.near_ref, ...), custom_call_target="tpu_custom_call" | custom-call | tf_op jit(solution)/shard_map/pallas_call | solution.py:480
  88.7 0.0 collective-permute-done.10.theirs_in
  88.7 3.3 %shard_map.83 = (f32[256,512]{1,0:T(8,128)}, f32[256,512]{1,0:T(8,128)}) custom-call(s32[16]{0:T(128)S(1)} %compare_select_fusion.9.flags, f32[8,1024]{1,0:T(8,128)S(1)} %get-tuple-element.51.partial_in, f32[8,1024]{1,0:T(8,128)S(1)} %shard_map.77.mine_in, f32[8,1024]{1,0:T(8,128)S(1)} %collective-permute-done.10.theirs_in, ...), custom_call_target="tpu_custom_call" | custom-call | tf_op jit(solution)/shard_map/pallas_call | solution.py:480
  (4 shorter events, 0.1 us)
Async XLA Ops:
  2.7 18.7 %collective-permute-start = (bf16[272,512]{1,0:T(8,128)(2,1)S(1)}, bf16[272,512]{1,0:T(8,128)(2,1)S(1)}, u32[]{:S(2)}, u32[]{:S(2)}) collective-permute-start(bf16[272,512]{1,0:T(8,128)(2,1)S(1)} %get-tuple-element.31.own_ref), channel_id=1, source_target_pairs={{0,2},{2,0},{1,3},{3,1},{4,6},{6,4},{5,7},{7,5},{8,10},{10,8},{9,1... | collective-permute-start | bytes 835592 | tf_op jit(solution)/shard_map/ppermute | solution.py:34
  5.3 25.3 %collective-permute-start.11 = (bf16[272,512]{1,0:T(8,128)(2,1)S(1)}, bf16[272,512]{1,0:T(8,128)(2,1)S(1)}, u32[]{:S(2)}, u32[]{:S(2)}) collective-permute-start(bf16[272,512]{1,0:T(8,128)(2,1)S(1)} %get-tuple-element.31.own_ref), channel_id=1, source_target_pairs={{4,8},{8,4},{12,16},{16,12},{20,24},{24,20},{28,32},{32,28},{36,40... | collective-permute-start | bytes 835592 | tf_op jit(solution)/shard_map/ppermute | solution.py:50
  19.4 11.3 %collective-permute-start.12 = (bf16[272,512]{1,0:T(8,128)(2,1)S(1)}, bf16[272,512]{1,0:T(8,128)(2,1)S(1)}, u32[]{:S(2)}, u32[]{:S(2)}) collective-permute-start(bf16[272,512]{1,0:T(8,128)(2,1)S(1)} %get-tuple-element.31.own_ref), channel_id=1, source_target_pairs={{0,4},{4,0},{8,12},{12,8},{16,20},{20,16},{24,28},{28,24},{32,36},... | collective-permute-start | bytes 835592 | tf_op jit(solution)/shard_map/ppermute | solution.py:50
  21.9 12.6 %collective-permute-start.1 = (bf16[544,512]{1,0:T(8,128)(2,1)S(1)}, bf16[544,512]{1,0:T(8,128)(2,1)S(1)}, u32[]{:S(2)}, u32[]{:S(2)}) collective-permute-start(bf16[544,512]{1,0:T(8,128)(2,1)S(1)} %shard_map.69.joined_ref), channel_id=1, source_target_pairs={{0,1},{1,0},{2,3},{3,2},{4,5},{5,4},{6,7},{7,6},{8,9},{9,8},{10,11... | collective-permute-start | bytes 1671176 | tf_op jit(solution)/shard_map/ppermute | solution.py:34
  23.9 21.6 %collective-permute-start.2 = (bf16[512,512]{1,0:T(8,128)(2,1)S(1)}, bf16[512,512]{1,0:T(8,128)(2,1)S(1)}, u32[]{:S(2)}, u32[]{:S(2)}) collective-permute-start(bf16[512,512]{1,0:T(8,128)(2,1)S(1)} %get-tuple-element.32.letter_ref), channel_id=1, source_target_pairs={{4,8},{8,4},{12,16},{16,12},{20,24},{24,20},{28,32},{32,28},{36,40... | collective-permute-start | bytes 1572872 | tf_op jit(solution)/shard_map/ppermute | solution.py:50
  28.7 16.8 %collective-permute-start.3 = (bf16[512,512]{1,0:T(8,128)(2,1)S(1)}, bf16[512,512]{1,0:T(8,128)(2,1)S(1)}, u32[]{:S(2)}, u32[]{:S(2)}) collective-permute-start(bf16[512,512]{1,0:T(8,128)(2,1)S(1)} %get-tuple-element.32.letter_ref), channel_id=1, source_target_pairs={{0,4},{4,0},{8,12},{12,8},{16,20},{20,16},{24,28},{28,24},{32,36},... | collective-permute-start | bytes 1572872 | tf_op jit(solution)/shard_map/ppermute | solution.py:50
  30.7 17.1 %collective-permute-start.13 = (bf16[512,512]{1,0:T(8,128)(2,1)S(1)}, bf16[512,512]{1,0:T(8,128)(2,1)S(1)}, u32[]{:S(2)}, u32[]{:S(2)}) collective-permute-start(bf16[512,512]{1,0:T(8,128)(2,1)S(1)} %shard_map.80.own_ref), channel_id=1, source_target_pairs={{0,2},{2,0},{1,3},{3,1},{4,6},{6,4},{5,7},{7,5},{8,10},{10,8},{9,1... | collective-permute-start | bytes 1572872 | tf_op jit(solution)/shard_map/ppermute | solution.py:34
  45.9 6.4 %collective-permute-start.4 = (bf16[1024,512]{1,0:T(8,128)(2,1)S(1)}, bf16[1024,512]{1,0:T(8,128)(2,1)S(1)}, u32[]{:S(2)}, u32[]{:S(2)}) collective-permute-start(bf16[1024,512]{1,0:T(8,128)(2,1)S(1)} %shard_map.72.columns_ref.near_columns_ref), channel_id=1, source_target_pairs={{0,1},{1,0},{2,3},{3,2},{4,5},{5,4},{6,7},{7,6},{8,9},{9,8},{10,11... | collective-permute-start | bytes 3145736 | tf_op jit(solution)/shard_map/ppermute | solution.py:34
  48.4 38.7 %collective-permute-start.14 = (bf16[1024,512]{1,0:T(8,128)(2,1)S(1)}, bf16[1024,512]{1,0:T(8,128)(2,1)S(1)}, u32[]{:S(2)}, u32[]{:S(2)}) collective-permute-start(bf16[1024,512]{1,0:T(8,128)(2,1)S(1)} %shard_map.81.near_ref), channel_id=1, source_target_pairs={{0,1},{1,0},{2,3},{3,2},{4,5},{5,4},{6,7},{7,6},{8,9},{9,8},{10,11... | collective-permute-start | bytes 3145736 | tf_op jit(solution)/shard_map/ppermute | solution.py:34
  55.2 11.2 %collective-permute-start.5 = (f32[4,1024]{1,0:T(4,128)S(1)}, f32[4,1024]{1,0:T(4,128)S(1)}, u32[]{:S(2)}, u32[]{:S(2)}) collective-permute-start(f32[4,1024]{1,0:T(4,128)S(1)} %get-tuple-element.45), channel_id=1, source_target_pairs={{4,8},{8,4},{12,16},{16,12},{20,24},{24,20},{28,32},{32,28},{36,40... | collective-permute-start | bytes 49160 | tf_op jit(solution)/shard_map/ppermute | solution.py:50
  60.7 5.6 %collective-permute-start.6 = (f32[4,1024]{1,0:T(4,128)S(1)}, f32[4,1024]{1,0:T(4,128)S(1)}, u32[]{:S(2)}, u32[]{:S(2)}) collective-permute-start(f32[4,1024]{1,0:T(4,128)S(1)} %get-tuple-element.46), channel_id=1, source_target_pairs={{0,4},{4,0},{8,12},{12,8},{16,20},{20,16},{24,28},{28,24},{32,36},... | collective-permute-start | bytes 49160 | tf_op jit(solution)/shard_map/ppermute | solution.py:50
  66.4 3.3 %collective-permute-start.7 = (f32[8,1024]{1,0:T(8,128)S(1)}, f32[8,1024]{1,0:T(8,128)S(1)}, u32[]{:S(2)}, u32[]{:S(2)}) collective-permute-start(f32[8,1024]{1,0:T(8,128)S(1)} %shard_map.75.mine_in), channel_id=1, source_target_pairs={{0,1},{1,0},{2,3},{3,2},{4,5},{5,4},{6,7},{7,6},{8,9},{9,8},{10,11... | collective-permute-start | bytes 98312 | tf_op jit(solution)/shard_map/ppermute | solution.py:34
  72.3 11.1 %collective-permute-start.8 = (f32[4,1024]{1,0:T(4,128)S(1)}, f32[4,1024]{1,0:T(4,128)S(1)}, u32[]{:S(2)}, u32[]{:S(2)}) collective-permute-start(f32[4,1024]{1,0:T(4,128)S(1)} %get-tuple-element.52), channel_id=1, source_target_pairs={{4,8},{8,4},{12,16},{16,12},{20,24},{24,20},{28,32},{32,28},{36,40... | collective-permute-start | bytes 49160 | tf_op jit(solution)/shard_map/ppermute | solution.py:50
  77.8 5.6 %collective-permute-start.9 = (f32[4,1024]{1,0:T(4,128)S(1)}, f32[4,1024]{1,0:T(4,128)S(1)}, u32[]{:S(2)}, u32[]{:S(2)}) collective-permute-start(f32[4,1024]{1,0:T(4,128)S(1)} %get-tuple-element.53), channel_id=1, source_target_pairs={{0,4},{4,0},{8,12},{12,8},{16,20},{20,16},{24,28},{28,24},{32,36},... | collective-permute-start | bytes 49160 | tf_op jit(solution)/shard_map/ppermute | solution.py:50
  83.5 5.2 %collective-permute-start.10 = (f32[8,1024]{1,0:T(8,128)S(1)}, f32[8,1024]{1,0:T(8,128)S(1)}, u32[]{:S(2)}, u32[]{:S(2)}) collective-permute-start(f32[8,1024]{1,0:T(8,128)S(1)} %shard_map.77.mine_in), channel_id=1, source_target_pairs={{0,1},{1,0},{2,3},{3,2},{4,5},{5,4},{6,7},{7,6},{8,9},{9,8},{10,11... | collective-permute-start | bytes 98312 | tf_op jit(solution)/shard_map/ppermute | solution.py:34
